TPU v7x, 32 devices: a whole 2x2x4 slice. The times are simulated.
32 devices in a mesh: dp: 8 (over y, x, core), fsdp: 4 (over z).
Axes of the slice: x: 2, y: 2, z: 4, core: 2. Of those that a mesh axis runs over, the one named last changes fastest.
Arguments:
- patches: bfloat16 [2, 32, 256, 768], P(None, ('dp', 'fsdp')), may hold values from -6 to 6
- grid: int32 [2, 32, 4, 256], P(None, ('dp', 'fsdp')), may hold values from 0 to 63, as said below
- segments: int32 [2, 32, 256], P(None, ('dp', 'fsdp')), may hold values from 0 to 7, as said below
- text_ids: int32 [2, 32, 8, 16], P(None, ('dp', 'fsdp')), may hold values from 0 to 31999
- table: bfloat16 [32000, 768], P('fsdp'), may hold values from -6 to 6
- weights: float32 [26, 768, 768], P(None, 'fsdp')
- momenta: float32 [26, 768, 768], P(None, 'fsdp'), may hold values from -1.9073486e-05 to 1.9073486e-05
- gains: float32 [79, 768], replicated
- gains_m: float32 [79, 768], replicated, may hold values from -1.9073486e-05 to 1.9073486e-05
- gains_v: float32 [79, 768], replicated, may hold values from 1.7e-13 to 7e-13
- step: int32 [1], replicated, may hold values from 2 to 20
Outputs:
- loss: float32 [], replicated
- grad_norm: float32 [], replicated
- weights_new: float32 [26, 768, 768], P(None, 'fsdp')
- weights_low: bfloat16 [26, 768, 768], P(None, 'fsdp')
- momenta_new: float32 [26, 768, 768], P(None, 'fsdp')
- gains_new: float32 [79, 768], replicated
- gains_m_new: float32 [79, 768], replicated
- gains_v_new: float32 [79, 768], replicated
- final_shift_grad: float32 [768], replicated
Inputs may be any that keep to these rules, and one draw needn't show every extreme that they name: Rows 0 and 1 of grid are below rows 2 and 3 at the same patch; heights and widths are given per patch, 1 to 63. `segments`: slot numbers never fall along a sequence and start at 0; some slots may be empty.
All inputs are finite; a program needn't handle non-finite values.
Results may differ from a plain program's by a relative error of at most 0.015.
Values may be sent and summed in bfloat16 or wider, within the bound.
A program may use at most 384 MiB of HBM per device.

v0:
```python
import math

import jax
import jax.numpy as jnp
from jax import lax
from jax.sharding import PartitionSpec as P

D = 768
HEADS = 12
FF = 3072
LAYERS = 2
IMGS = 8
POS = 32
MB = 2
NS_ITERS = 5
HD = 64


HIGH = lax.Precision.HIGHEST
LOGIT_SCALE = 50.0
CLIP_LIMIT = 0.005
MOMENT = 0.95
MUON_RATE = 0.5
MUON_DECAY = 0.01
ADAM_RATE = 0.4
BETA_ONE = 0.9
BETA_TWO = 0.999
ADAM_EPS = 1e-08
ADAM_DECAY = 0.01
COEF_A = 3.4445
COEF_B = -4.775
COEF_C = 2.0315


def rounded(value):
    return value.astype(jnp.bfloat16)


def product(left, right, form):
    return jnp.einsum(form, left, right, preferred_element_type=jnp.float32)


def layer_norm(value, gain, shift):
    centred = value - jnp.mean(value, -1, keepdims=True)
    spread = jnp.mean(centred * centred, -1, keepdims=True)
    return centred * lax.rsqrt(spread + 1e-06) * gain + shift


def head_norm(value, gain):
    heads = value.reshape(value.shape[0], HEADS, HD)
    centred = heads - jnp.mean(heads, -1, keepdims=True)
    spread = jnp.mean(centred * centred, -1, keepdims=True)
    return centred * lax.rsqrt(spread + 1e-06) * gain.reshape(HEADS, HD)


def both_norms(query, key, gain_query, gain_key):
    return (head_norm(query, gain_query), head_norm(key, gain_key))


def unit_rows(value):
    return (
        value
        * lax.rsqrt(jnp.mean(value * value, -1, keepdims=True) + 1e-06)
        * (1.0 / math.sqrt(value.shape[-1]))
    )


def positions(grid):
    slots = jnp.arange(POS, dtype=jnp.int32)
    row_index = grid[0] * POS // grid[2]
    col_index = grid[1] * POS // grid[3]
    return (
        (row_index[:, None] == slots[None]).astype(jnp.float32),
        (col_index[:, None] == slots[None]).astype(jnp.float32),
    )


def pooling(segment):
    member = segment[None, :] == jnp.arange(IMGS, dtype=jnp.int32)[:, None]

    def pooled_of(final, query):
        split = final.reshape(-1, HEADS, HD)
        logits = jnp.einsum("shd,hd->hs", split, query.reshape(HEADS, HD), precision=HIGH) * (
            1.0 / math.sqrt(HD)
        )
        logits = jnp.where(member[:, None, :], logits[None], -1e30)
        share = jax.nn.softmax(logits, -1)
        return jnp.einsum("khs,shd->khd", share, split, precision=HIGH).reshape(IMGS, -1)

    return pooled_of


def fetch(blocks):
    return lax.all_gather(rounded(blocks), "fsdp", axis=1, tiled=True)


def fetch_again(blocks):
    return lax.all_gather(rounded(blocks), "fsdp", axis=1, tiled=True)


def masked_scores(query_low, key_low, same):
    scores = product(query_low, key_low, "shd,thd->hst") * (1.0 / math.sqrt(HD))
    return jnp.where(same[None], scores, -1e30)


def layer_forward(state, blocks, gains, same):
    heads_in, norm_one = jax.vjp(layer_norm, state, gains[0], gains[1])
    heads_low = rounded(heads_in)
    mixed = product(heads_low, blocks[0:3].reshape(3 * D, D), "sd,rd->sr")
    (query, key), norms_back = jax.vjp(
        both_norms, mixed[:, :D], mixed[:, D : 2 * D], gains[4], gains[5]
    )
    query_low = rounded(query)
    key_low = rounded(key)
    value_low = rounded(mixed[:, 2 * D :]).reshape(-1, HEADS, HD)
    scores = masked_scores(query_low, key_low, same)
    top = jax.scipy.special.logsumexp(scores, axis=-1, keepdims=True)
    weights_low = rounded(jnp.exp(scores - top))
    attended_low = rounded(product(weights_low, value_low, "hst,thd->shd").reshape(-1, D))
    state = state + product(attended_low, blocks[3], "sr,rd->sd")
    normed, norm_two = jax.vjp(layer_norm, state, gains[2], gains[3])
    normed_low = rounded(normed)
    hidden, gelu_back = jax.vjp(
        jax.nn.gelu, product(normed_low, blocks[4:8].reshape(FF, D), "sd,rd->sr")
    )
    hidden_low = rounded(hidden)
    state = state + product(hidden_low, blocks[8:12].reshape(FF, D), "sr,rd->sd")
    kept = (
        norm_one,
        heads_low,
        norms_back,
        query_low,
        key_low,
        value_low,
        top,
        attended_low,
        norm_two,
        normed_low,
        gelu_back,
        hidden_low,
    )
    return (state, kept)


def layer_backward(grad, kept, blocks, same):
    (
        norm_one,
        heads_low,
        norms_back,
        query_low,
        key_low,
        value_low,
        top,
        attended_low,
        norm_two,
        normed_low,
        gelu_back,
        hidden_low,
    ) = kept
    down = blocks[8:12].reshape(FF, D)
    upward = blocks[4:8].reshape(FF, D)
    grad_low = rounded(grad)
    grad_down = product(hidden_low, grad_low, "sr,sd->rd")
    (grad_hidden,) = gelu_back(product(grad_low, down, "sd,rd->sr"))
    hidden_grad = rounded(grad_hidden)
    grad_up = product(hidden_grad, normed_low, "sr,sd->rd")
    inner, gain_two, shift_two = norm_two(product(hidden_grad, upward, "sr,rd->sd"))
    grad = grad + inner
    grad_low = rounded(grad)
    grad_out = product(attended_low, grad_low, "sr,sd->rd")
    attended_grad = rounded(product(grad_low, blocks[3], "sd,rd->sr")).reshape(-1, HEADS, HD)
    weights = jnp.exp(masked_scores(query_low, key_low, same) - top)
    weights_low = rounded(weights)
    value_grad = product(weights_low, attended_grad, "hst,shd->thd")
    weight_grad = product(attended_grad, value_low, "shd,thd->hst")
    score_grad = weights * (weight_grad - jnp.sum(weights * weight_grad, -1, keepdims=True))
    score_low = rounded(score_grad * (1.0 / math.sqrt(HD)))
    query_grad = product(score_low, key_low, "hst,thd->shd")
    key_grad = product(score_low, query_low, "hst,shd->thd")
    query_in, key_in, gain_query, gain_key = norms_back((query_grad, key_grad))
    mixed_low = rounded(jnp.concatenate([query_in, key_in, value_grad.reshape(-1, D)], 1))
    grad_mixed = product(mixed_low, heads_low, "sr,sd->rd")
    inner, gain_one, shift_one = norm_one(
        product(mixed_low, blocks[0:3].reshape(3 * D, D), "sr,rd->sd")
    )
    grad = grad + inner
    block_grads = jnp.concatenate(
        [
            grad_mixed.reshape(3, D, D),
            grad_out[None],
            grad_up.reshape(4, D, D),
            grad_down.reshape(4, D, D),
        ],
        0,
    )
    gain_grads = jnp.stack([gain_one, shift_one, gain_two, shift_two, gain_query, gain_key])
    return (grad, block_grads, gain_grads)


def contrast_rows(scores, alive, own_live, offset):
    masked = jnp.where(alive[None, :] > 0, scores, -1e30)
    top = jax.scipy.special.logsumexp(masked, axis=1, keepdims=True)
    share = jnp.exp(masked - top)
    diagonal = jnp.diagonal(lax.dynamic_slice_in_dim(scores, offset, scores.shape[0], 1))
    term = jnp.sum((top[:, 0] - diagonal) * own_live)
    columns = jnp.arange(scores.shape[1], dtype=jnp.int32)
    target = (
        columns[None, :] == offset + jnp.arange(scores.shape[0], dtype=jnp.int32)[:, None]
    ).astype(jnp.float32)
    return (term, (share - target) * own_live[:, None], top[:, 0])


def collect(store, start, block_grads):
    reduced = lax.psum_scatter(
        block_grads.astype(jnp.bfloat16), "fsdp", scatter_dimension=1, tiled=True
    ).astype(jnp.float32)
    return store.at[start : start + block_grads.shape[0]].add(reduced)


def muon_groups():
    found = [(0, 1), (1, 1)]
    for index in range(LAYERS):
        base = 2 + 12 * index
        found = found + [(base, 3), (base + 3, 1), (base + 4, 4), (base + 8, 4)]
    return found


def local_grams(items):
    return jnp.stack([product(rounded(item), rounded(item), "brd,bre->de") for item in items])


def summed_grams(local):
    shares = lax.psum_scatter(
        local.astype(jnp.bfloat16), "fsdp", scatter_dimension=1, tiled=True
    ).astype(jnp.float32)
    return lax.all_gather(shares.astype(jnp.bfloat16), "fsdp", axis=1, tiled=True).astype(
        shares.dtype
    )


def per_device(
    patches, grid, segments, text_ids, table, weights, momenta, gains, gains_m, gains_v, step
):
    fin = 6 * LAYERS
    base = fin + 3
    slots = jnp.arange(IMGS, dtype=jnp.int32)
    live = jnp.any(segments[:, 0, None, :] == slots[None, :, None], -1).astype(jnp.float32)
    count = lax.psum(jnp.sum(live), ("dp", "fsdp"))
    factor = 1.0 / (2.0 * count)
    group_ids = lax.all_gather(text_ids, "fsdp", axis=1, tiled=True)
    flat_ids = jnp.transpose(group_ids, (1, 0, 2, 3)).reshape(-1, group_ids.shape[3])
    share_rows = table.shape[0]
    first_row = lax.axis_index("fsdp") * share_rows
    picked = flat_ids - first_row
    hits = jnp.sum(
        (picked[:, :, None] == jnp.arange(share_rows, dtype=jnp.int32)[None, None, :]).astype(
            jnp.int32
        ),
        1,
    )
    text_sum = lax.psum_scatter(
        jnp.dot(
            rounded(hits.astype(jnp.float32)), table, preferred_element_type=jnp.float32
        ).astype(jnp.bfloat16),
        "fsdp",
        scatter_dimension=0,
        tiled=True,
    ).astype(jnp.float32)
    text_low = rounded(unit_rows(text_sum / text_ids.shape[-1])).reshape(MB, IMGS, -1)
    me = lax.axis_index(("dp", "fsdp"))
    rows_local = weights.shape[1]
    store = jnp.zeros((weights.shape[0], rows_local, D), jnp.float32)
    gains_grad = jnp.zeros_like(gains)
    loss_part = jnp.float32(0.0)
    for part in range(MB):
        segment = segments[part, 0]
        same = segment[:, None] == segment[None, :]
        rows_hot, cols_hot = positions(grid[part, 0])
        patch_low = patches[part, 0]
        stem = fetch(weights[0:2])
        state = product(patch_low, stem[0], "sd,rd->sr")
        state = state + jnp.dot(rows_hot, gains[base : base + POS], precision=HIGH)
        state = state + jnp.dot(cols_hot, gains[base + POS : base + 2 * POS], precision=HIGH)
        saved = []
        for index in range(LAYERS):
            blocks = fetch(weights[2 + 12 * index : 14 + 12 * index])
            state, kept = layer_forward(state, blocks, gains[6 * index : 6 * index + 6], same)
            saved.append((kept, blocks))
        final, norm_final = jax.vjp(layer_norm, state, gains[fin], gains[fin + 1])
        pooled, pool_back = jax.vjp(pooling(segment), final, gains[fin + 2])
        pooled_low = rounded(pooled)
        embedded, unit_back = jax.vjp(unit_rows, product(pooled_low, stem[1], "kr,rd->kd"))
        image_low = rounded(embedded)
        own_text = text_low[part]
        images, texts, alive = (
            lax.all_gather(image_low, ("dp", "fsdp"), axis=0, tiled=True),
            lax.all_gather(own_text, ("dp", "fsdp"), axis=0, tiled=True),
            lax.all_gather(rounded(live[part]), ("dp", "fsdp"), axis=0, tiled=True),
        )
        alive = alive.astype(jnp.float32)
        forward = LOGIT_SCALE * product(image_low, texts, "kd,nd->kn")
        backward = LOGIT_SCALE * product(own_text, images, "kd,nd->kn")
        term_f, grad_f, tops_f = contrast_rows(forward, alive, live[part], me * IMGS)
        term_b, grad_b, tops_b = contrast_rows(backward, alive, live[part], me * IMGS)
        loss_part = loss_part + (term_f + term_b) * factor
        forward_low = rounded(grad_f * factor * LOGIT_SCALE)
        backward_low = rounded(grad_b * factor * LOGIT_SCALE)
        spread = product(backward_low, own_text, "kn,kd->nd")
        text_side = lax.psum_scatter(spread, ("dp", "fsdp"), scatter_dimension=0, tiled=True)
        image_grad = product(forward_low, texts, "kn,nd->kd") + text_side
        (embed_grad,) = unit_back(image_grad)
        embed_low = rounded(embed_grad)
        grad_pool = product(pooled_low, embed_low, "kr,kd->rd")
        final_grad, query_grad = pool_back(product(embed_low, stem[1], "kd,rd->kr"))
        grad, gain_final, shift_final = norm_final(final_grad)
        gains_grad = (
            gains_grad.at[fin]
            .add(gain_final)
            .at[fin + 1]
            .add(shift_final)
            .at[fin + 2]
            .add(query_grad)
        )
        for index in reversed(range(LAYERS)):
            kept, blocks = saved[index]
            blocks = fetch_again(weights[2 + 12 * index : 14 + 12 * index])
            grad, block_grads, gain_grads = layer_backward(grad, kept, blocks, same)
            store = collect(store, 2 + 12 * index, block_grads)
            gains_grad = gains_grad.at[6 * index : 6 * index + 6].add(gain_grads)
        grad_low = rounded(grad)
        grad_patch = product(grad_low, patch_low, "sr,sd->rd")
        store = collect(store, 0, jnp.stack([grad_patch, grad_pool]))
        gains_grad = gains_grad.at[base : base + POS].add(jnp.dot(rows_hot.T, grad, precision=HIGH))
        gains_grad = gains_grad.at[base + POS : base + 2 * POS].add(
            jnp.dot(cols_hot.T, grad, precision=HIGH)
        )
    shard_grads = lax.psum(store.astype(jnp.bfloat16), "dp").astype(jnp.float32)
    gains_grad, loss = lax.psum((gains_grad, loss_part), ("dp", "fsdp"))
    squares = lax.psum(jnp.sum(shard_grads * shard_grads), "fsdp")
    norm = jnp.sqrt(squares + jnp.sum(gains_grad * gains_grad))
    clip = jnp.minimum(1.0, CLIP_LIMIT / (norm + 1e-06))
    momenta_new = MOMENT * momenta + clip * shard_grads
    groups = muon_groups()
    current = [momenta_new[start : start + number] for start, number in groups]
    whole = summed_grams(local_grams(current))
    grams = []
    for place in range(len(groups)):
        size = jnp.sqrt(jnp.trace(whole[place])) + 1e-07
        current[place] = current[place] / size
        grams.append(whole[place] / (size * size))
    for turn in range(NS_ITERS):
        if turn > 0:
            whole = summed_grams(local_grams(current))
            grams = [whole[place] for place in range(len(groups))]
        for place in range(len(groups)):
            gram_low = rounded(grams[place])
            first = product(rounded(current[place]), gram_low, "brd,de->bre")
            second = product(rounded(first), gram_low, "brd,de->bre")
            current[place] = COEF_A * current[place] + COEF_B * first + COEF_C * second
    updated = []
    for place in range(len(groups)):
        start, number = groups[place]
        old = weights[start : start + number]
        updated.append(
            old * (1.0 - MUON_RATE * MUON_DECAY) - MUON_RATE * math.sqrt(number) * current[place]
        )
    weights_new = jnp.concatenate(updated, 0)
    grad_small = clip * gains_grad
    moment_one = BETA_ONE * gains_m + (1.0 - BETA_ONE) * grad_small
    moment_two = BETA_TWO * gains_v + (1.0 - BETA_TWO) * grad_small * grad_small
    count_steps = step[0].astype(jnp.float32)
    corrected_one = moment_one / (1.0 - jnp.power(BETA_ONE, count_steps))
    corrected_two = moment_two / (1.0 - jnp.power(BETA_TWO, count_steps))
    gains_new = gains - ADAM_RATE * (
        corrected_one / (jnp.sqrt(corrected_two) + ADAM_EPS) + ADAM_DECAY * gains
    )
    shift_grad = grad_small[fin + 1]
    return (
        loss,
        norm,
        weights_new,
        rounded(weights_new),
        momenta_new,
        gains_new,
        moment_one,
        moment_two,
        shift_grad,
    )


def solution(mesh):
    placed = (
        P(None, ("dp", "fsdp"), None, None),
        P(None, ("dp", "fsdp"), None, None),
        P(None, ("dp", "fsdp"), None),
        P(None, ("dp", "fsdp"), None, None),
        P("fsdp", None),
        P(None, "fsdp", None),
        P(None, "fsdp", None),
        P(),
        P(),
        P(),
        P(),
    )
    return jax.shard_map(
        per_device,
        mesh=mesh,
        in_specs=placed,
        out_specs=(
            P(),
            P(),
            P(None, "fsdp", None),
            P(None, "fsdp", None),
            P(None, "fsdp", None),
            P(),
            P(),
            P(),
            P(),
        ),
        check_vma=False,
    )
```

profile of v0, /device:TPU:0, one launch (start us, length us, event | category | flops | bytes accessed | tf_op | source)
XLA Modules:
  0.0 4878.5 jit_solution(1328657694093657984)
XLA Ops:
  7.2 15.0 all_gather.56
  22.3 13.9 convert_reduce_fusion
  36.2 7.1 convolution_convert_fusion.52
  43.3 9.6 convert.391
  54.9 6.8 fusion.839
  63.1 43.0 psum.35
  111.4 50.6 %all-reduce.4 = (bf16[256]{0:T(256)(128)(2,1)S(1)}, bf16[256]{0:T(256)(128)(2,1)S(1)}) all-reduce(bf16[256]{0:T(256)(128)(2,1)S(1)} %dynamic-update-slice.61, bf16[256]{0:T(256)(128)(2,1)S(1)} %dynamic-update-slice.60), channel_id=1, replica_groups=mesh['dp'=8,'fsdp'=4] {'dp','fsdp'}, use_global_device_ids=true, to_apply=%add.3 | all-reduce | flops 512 | bytes 2048
  169.4 113.7 %all_gather.60 = bf16[256,768]{1,0:T(8,128)(2,1)} all-gather(bf16[8,768]{1,0:T(8,128)(2,1)S(1)} %get-tuple-element.387), channel_id=1, replica_groups=mesh['dp'=8,'fsdp'=4] {'dp','fsdp'}, dimensions={0}, use_global_device_ids=true | all-gather | bytes 405504 | tf_op jit(solution)/shard_map/all_gather | solution.py:297
  283.1 101.7 %all_gather.57 = bf16[256,768]{1,0:T(8,128)(2,1)} all-gather(bf16[8,768]{1,0:T(8,128)(2,1)S(1)} %get-tuple-element.386), channel_id=1, replica_groups=mesh['dp'=8,'fsdp'=4] {'dp','fsdp'}, dimensions={0}, use_global_device_ids=true | all-gather | bytes 405504 | tf_op jit(solution)/shard_map/all_gather | solution.py:297
  420.8 6.7 fusion.838
  437.1 183.2 %all-gather.13.cloned.1.call-done = bf16[12,768,768]{2,1,0:T(8,128)(2,1)} async-done(((bf16[12,192,768]{2,1,0:T(8,128)(2,1)}), bf16[12,768,768]{2,1,0:T(8,128)(2,1)}) %all-gather.13.cloned.1.call-update) | async-done | bytes 14155792 | tf_op jit(solution)/shard_map/all_gather | solution.py:94
  657.8 6.6 fusion.837
  699.6 73.3 %all_gather.61 = bf16[256,768]{1,0:T(8,128)(2,1)} all-gather(bf16[8,768]{1,0:T(8,128)(2,1)S(1)} %multiply_convert_fusion.32), channel_id=1, replica_groups=mesh['dp'=8,'fsdp'=4] {'dp','fsdp'}, dimensions={0}, use_global_device_ids=true | all-gather | bytes 405504 | tf_op jit(solution)/shard_map/all_gather | solution.py:296
  783.8 66.9 %all_gather.58 = bf16[256,768]{1,0:T(8,128)(2,1)S(1)} all-gather(bf16[8,768]{1,0:T(8,128)(2,1)S(1)} %multiply_convert_fusion.33), channel_id=1, replica_groups=mesh['dp'=8,'fsdp'=4] {'dp','fsdp'}, dimensions={0}, use_global_device_ids=true | all-gather | bytes 405504 | tf_op jit(solution)/shard_map/all_gather | solution.py:296
  873.4 86.2 %reduce-scatter.17.cloned.1.call-done = f32[8,768]{1,0:T(8,128)} async-done(((f32[256,768]{1,0:T(8,128)}), f32[8,768]{1,0:T(8,128)}) %reduce-scatter.17.cloned.1.call-update) | async-done | bytes 24592 | tf_op jit(solution)/shard_map/reduce_scatter | solution.py:309
  972.5 87.5 %reduce-scatter.25.cloned.1.call-done = f32[8,768]{1,0:T(8,128)} async-done(((f32[256,768]{1,0:T(8,128)}), f32[8,768]{1,0:T(8,128)}) %reduce-scatter.25.cloned.1.call-update) | async-done | bytes 24592 | tf_op jit(solution)/shard_map/reduce_scatter | solution.py:309
  1073.2 6.0 fusion.21
  1096.8 7.8 multiply_reduce_fusion.37
  1104.5 7.9 multiply_reduce_fusion.36
  1133.3 8.8 multiply_reduce_fusion.18
  1144.4 8.7 multiply_reduce_fusion.17
  1162.5 8.6 pad_maximum_fusion
  1205.7 7.8 multiply_reduce_fusion.33
  1217.1 9.3 multiply_reduce_fusion.14
  1228.6 9.0 multiply_reduce_fusion.32
  1238.4 9.1 multiply_reduce_fusion.13
  1264.8 6.3 pad_maximum_fusion.1
  1294.2 6.4 pad_maximum_fusion.2
  1309.0 6.5 pad_maximum_fusion.3
  1319.6 88.0 %reduce-scatter.19.cloned.1.call-done = bf16[12,192,768]{2,1,0:T(8,128)(2,1)} async-done(((bf16[12,768,768]{2,1,0:T(8,128)(2,1)}), bf16[12,192,768]{2,1,0:T(8,128)(2,1)}) %reduce-scatter.19.cloned.1.call-update) | async-done | bytes 3538960 | tf_op jit(solution)/shard_map/reduce_scatter | solution.py:214
  1407.6 9.1 pad_convert_fusion
  1416.8 232.2 %reduce-scatter.21.cloned.1.call-done = bf16[12,192,768]{2,1,0:T(8,128)(2,1)} async-done(((bf16[12,768,768]{2,1,0:T(8,128)(2,1)}), bf16[12,192,768]{2,1,0:T(8,128)(2,1)}) %reduce-scatter.21.cloned.1.call-update) | async-done | bytes 3538960 | tf_op jit(solution)/shard_map/reduce_scatter | solution.py:214
  1649.0 5.7 convert_dynamic-update-slice_fusion
  1654.6 46.5 reduce-scatter.23.cloned.1.call-done
  1703.6 236.5 %reduce-scatter.27.cloned.1.call-done = bf16[12,192,768]{2,1,0:T(8,128)(2,1)} async-done(((bf16[12,768,768]{2,1,0:T(8,128)(2,1)}), bf16[12,192,768]{2,1,0:T(8,128)(2,1)}) %reduce-scatter.27.cloned.1.call-update) | async-done | bytes 3538960 | tf_op jit(solution)/shard_map/reduce_scatter | solution.py:214
  1940.2 7.7 fusion.7
  1947.9 233.1 %reduce-scatter.29.cloned.1.call-done = bf16[12,192,768]{2,1,0:T(8,128)(2,1)} async-done(((bf16[12,768,768]{2,1,0:T(8,128)(2,1)}), bf16[12,192,768]{2,1,0:T(8,128)(2,1)}) %reduce-scatter.29.cloned.1.call-update) | async-done | bytes 3538960 | tf_op jit(solution)/shard_map/reduce_scatter | solution.py:214
  2181.0 7.7 fusion.6
  2188.7 43.6 reduce-scatter.31.cloned.1.call-done
  2234.9 9.5 convert_element_type.1101
  2255.7 108.1 %all-reduce.8.cloned.1.call-done = bf16[26,192,768]{2,1,0:T(8,128)(2,1)} async-done(((bf16[26,192,768]{2,1,0:T(8,128)(2,1)}), bf16[26,192,768]{2,1,0:T(8,128)(2,1)}) %all-reduce.8.cloned.1.call-update) | async-done | bytes 7667728 | tf_op jit(solution)/shard_map/psum | solution.py:337
  2363.8 7.7 fusion.4
  2371.5 122.9 %all-reduce.10.cloned.1.call-done = f32[79,768]{1,0:T(8,128)} async-done(((f32[79,768]{1,0:T(8,128)}), f32[79,768]{1,0:T(8,128)}) %all-reduce.10.cloned.1.call-update) | async-done | bytes 242704 | tf_op jit(solution)/shard_map/psum | solution.py:338
  2496.0 12.6 psum.38
  2510.1 8.4 fusion.5
  2539.1 196.5 %reduce-scatter.33.cloned.1.call-done = bf16[10,192,768]{2,1,0:T(8,128)(2,1)} async-done(((bf16[10,768,768]{2,1,0:T(8,128)(2,1)}), bf16[10,192,768]{2,1,0:T(8,128)(2,1)}) %reduce-scatter.33.cloned.1.call-update) | async-done | bytes 2949136 | tf_op jit(solution)/shard_map/reduce_scatter | solution.py:233
  2736.1 207.5 %all-gather.15.cloned.1.call-done = bf16[10,768,768]{2,1,0:T(8,128)(2,1)} async-done(((bf16[10,192,768]{2,1,0:T(8,128)(2,1)}), bf16[10,768,768]{2,1,0:T(8,128)(2,1)}) %all-gather.15.cloned.1.call-update) | async-done | bytes 11796496 | tf_op jit(solution)/shard_map/all_gather | solution.py:236
  2943.6 6.3 convert_element_type.1113
  2952.8 4.9 copy-done
  2969.9 5.1 multiply_add_fusion.13
  2977.7 5.7 divide_convert_fusion.2
  2998.8 5.1 multiply_add_fusion.14
  3008.1 5.2 multiply_add_fusion.15
  3049.4 197.4 %reduce-scatter.35.cloned.1.call-done = bf16[10,192,768]{2,1,0:T(8,128)(2,1)} async-done(((bf16[10,768,768]{2,1,0:T(8,128)(2,1)}), bf16[10,192,768]{2,1,0:T(8,128)(2,1)}) %reduce-scatter.35.cloned.1.call-update) | async-done | bytes 2949136 | tf_op jit(solution)/shard_map/reduce_scatter | solution.py:233
  3246.9 207.9 %all-gather.17.cloned.1.call-done = bf16[10,768,768]{2,1,0:T(8,128)(2,1)} async-done(((bf16[10,192,768]{2,1,0:T(8,128)(2,1)}), bf16[10,768,768]{2,1,0:T(8,128)(2,1)}) %all-gather.17.cloned.1.call-update) | async-done | bytes 11796496 | tf_op jit(solution)/shard_map/all_gather | solution.py:236
  3502.3 197.4 %reduce-scatter.37.cloned.1.call-done = bf16[10,192,768]{2,1,0:T(8,128)(2,1)} async-done(((bf16[10,768,768]{2,1,0:T(8,128)(2,1)}), bf16[10,192,768]{2,1,0:T(8,128)(2,1)}) %reduce-scatter.37.cloned.1.call-update) | async-done | bytes 2949136 | tf_op jit(solution)/shard_map/reduce_scatter | solution.py:233
  3699.9 207.7 %all-gather.19.cloned.1.call-done = bf16[10,768,768]{2,1,0:T(8,128)(2,1)} async-done(((bf16[10,192,768]{2,1,0:T(8,128)(2,1)}), bf16[10,768,768]{2,1,0:T(8,128)(2,1)}) %all-gather.19.cloned.1.call-update) | async-done | bytes 11796496 | tf_op jit(solution)/shard_map/all_gather | solution.py:236
  3954.0 197.4 %reduce-scatter.39.cloned.1.call-done = bf16[10,192,768]{2,1,0:T(8,128)(2,1)} async-done(((bf16[10,768,768]{2,1,0:T(8,128)(2,1)}), bf16[10,192,768]{2,1,0:T(8,128)(2,1)}) %reduce-scatter.39.cloned.1.call-update) | async-done | bytes 2949136 | tf_op jit(solution)/shard_map/reduce_scatter | solution.py:233
  4151.9 207.6 %all-gather.21.cloned.1.call-done = bf16[10,768,768]{2,1,0:T(8,128)(2,1)} async-done(((bf16[10,192,768]{2,1,0:T(8,128)(2,1)}), bf16[10,768,768]{2,1,0:T(8,128)(2,1)}) %all-gather.21.cloned.1.call-update) | async-done | bytes 11796496 | tf_op jit(solution)/shard_map/all_gather | solution.py:236
  4404.9 197.4 %reduce-scatter.41.cloned.1.call-done = bf16[10,192,768]{2,1,0:T(8,128)(2,1)} async-done(((bf16[10,768,768]{2,1,0:T(8,128)(2,1)}), bf16[10,192,768]{2,1,0:T(8,128)(2,1)}) %reduce-scatter.41.cloned.1.call-update) | async-done | bytes 2949136 | tf_op jit(solution)/shard_map/reduce_scatter | solution.py:233
  4605.6 56.3 %psum.36 = f32[]{:T(128)} all-reduce(f32[]{:T(128)S(6)} %multiply.447), channel_id=1, replica_groups=mesh['dp'=8,'fsdp'=4] {'dp','fsdp'}, use_global_device_ids=true, to_apply=%region_68.69 | all-reduce | flops 1 | bytes 8 | tf_op jit(solution)/shard_map/psum | solution.py:338
  4664.8 146.5 %all-gather.23.cloned.1.call-done = bf16[10,768,768]{2,1,0:T(8,128)(2,1)} async-done(((bf16[10,192,768]{2,1,0:T(8,128)(2,1)}), bf16[10,768,768]{2,1,0:T(8,128)(2,1)}) %all-gather.23.cloned.1.call-update) | async-done | bytes 11796496 | tf_op jit(solution)/shard_map/all_gather | solution.py:236
  4844.5 5.5 subtract_dynamic-update-slice_fusion.2
  4860.5 9.5 convert_element_type.1268
  (1590 shorter events, 623.5 us)
Async XLA Ops:
  7.2 160.5 %reduce-scatter.15.cloned.1.call-start = ((), (), s32[]{:S(2)}) async-start(), calls=%async_computation.17 | async-start | bytes 122880 | tf_op jit(solution)/shard_map/reduce_scatter | solution.py:261
  43.3 341.5 %all-gather.9.cloned.1.call-start = ((), (), s32[]{:S(2)}) async-start(), calls=%async_computation.14 | async-start | bytes 2949120 | tf_op jit(solution)/shard_map/all_gather | solution.py:94
  54.9 338.3 %all-gather.11.cloned.1.call-start = ((), (), s32[]{:S(2)}) async-start(), calls=%async_computation.15 | async-start | bytes 17694720 | tf_op jit(solution)/shard_map/all_gather | solution.py:94
  61.7 44.5 copy-start.185
  61.7 100.8 %copy-start.378 = (s32[2,1,4,256]{3,2,1,0:T(4,128)S(1)}, s32[2,1,4,256]{3,2,1,0:T(4,128)}, u32[]{:S(2)}) copy-start(s32[2,1,4,256]{3,2,1,0:T(4,128)} %param.52) | copy-start | bytes 24580
  61.7 558.6 %all-gather.13.cloned.1.call-start = ((), (), s32[]{:S(2)}) async-start(), calls=%async_computation.16 | async-start | bytes 17694720 | tf_op jit(solution)/shard_map/all_gather | solution.py:94
  61.8 323.0 %copy-start.215 = (bf16[2,1,256,768]{3,2,1,0:T(8,128)(2,1)S(1)}, bf16[2,1,256,768]{3,2,1,0:T(8,128)(2,1)}, u32[]{:S(2)}) copy-start(bf16[2,1,256,768]{3,2,1,0:T(8,128)(2,1)} %param.51) | copy-start | bytes 2359300
  62.3 897.3 %reduce-scatter.17.cloned.1.call-start = ((), (), s32[]{:S(2)}) async-start(), calls=%async_computation.18 | async-start | bytes 811008 | tf_op jit(solution)/shard_map/reduce_scatter | solution.py:309
  106.2 62.4 %copy-start.423 = (f32[2,8]{1,0:T(2,128)}, f32[2,8]{1,0:T(2,128)S(1)}, u32[]{:S(2)}) copy-start(f32[2,8]{1,0:T(2,128)S(1)} %convert_element_type.1012) | copy-start | bytes 196
  106.9 61.7 %copy-start.358 = (f32[768]{0:T(1024)}, f32[768]{0:T(1024)S(1)}, u32[]{:S(2)}) copy-start(f32[768]{0:T(1024)S(1)} %get-tuple-element.303) | copy-start | bytes 9220
  106.9 531.2 %copy-start.258 = (f32[768]{0:T(1024)}, f32[768]{0:T(1024)S(1)}, u32[]{:S(2)}) copy-start(f32[768]{0:T(1024)S(1)} %get-tuple-element.312) | copy-start | bytes 9220
  164.9 222.4 %copy-start.424 = (s32[256]{0:T(256)}, s32[256]{0:T(256)S(1)}, u32[]{:S(2)}) copy-start(s32[256]{0:T(256)S(1)} %add_select_fusion.1) | copy-start | bytes 3076
  165.0 222.4 %copy-start.399 = (s32[256]{0:T(256)}, s32[256]{0:T(256)S(1)}, u32[]{:S(2)}) copy-start(s32[256]{0:T(256)S(1)} %add_select_fusion) | copy-start | bytes 3076
  165.0 224.7 %copy-start.426 = (s32[256]{0:T(256)}, s32[256]{0:T(256)S(1)}, u32[]{:S(2)}) copy-start(s32[256]{0:T(256)S(1)} %add_select_fusion.3) | copy-start | bytes 3076
  165.0 225.2 %copy-start.401 = (s32[256]{0:T(256)}, s32[256]{0:T(256)S(1)}, u32[]{:S(2)}) copy-start(s32[256]{0:T(256)S(1)} %add_select_fusion.2) | copy-start | bytes 3076
  169.4 218.0 %copy-start.225 = (bf16[16,768]{1,0:T(8,128)(2,1)}, bf16[16,768]{1,0:T(8,128)(2,1)S(1)}, u32[]{:S(2)}) copy-start(bf16[16,768]{1,0:T(8,128)(2,1)S(1)} %fusion.618) | copy-start | bytes 73732
  395.7 230.7 %copy-start.7 = (bf16[3,768,768]{2,1,0:T(8,128)(2,1)}, bf16[3,768,768]{2,1,0:T(8,128)(2,1)S(1)}, u32[]{:S(2)}) copy-start(bf16[3,768,768]{2,1,0:T(8,128)(2,1)S(1)} %slice.1080) | copy-start | bytes 10616836
  694.0 78.8 %copy-start.191 = (bf16[256,768]{1,0:T(8,128)(2,1)S(1)}, bf16[256,768]{1,0:T(8,128)(2,1)}, u32[]{:S(2)}) copy-start(bf16[256,768]{1,0:T(8,128)(2,1)} %all_gather.60) | copy-start | bytes 1179652
  695.5 367.5 %copy-start.34 = (f32[256,768]{0,1:T(8,128)}, f32[256,768]{0,1:T(8,128)S(1)}, u32[]{:S(2)}) copy-start(f32[256,768]{0,1:T(8,128)S(1)} %copy.126) | copy-start | bytes 2359300
  697.1 80.6 %copy-start.315 = (pred[8,256]{1,0:T(8,128)(4,1)S(1)}, pred[8,256]{1,0:T(8,128)(4,1)}, u32[]{:S(2)}) copy-start(pred[8,256]{1,0:T(8,128)(4,1)} %iota_compare_fusion.17) | copy-start | bytes 6148
  697.3 80.5 %copy-start.293 = (bf16[8,768]{1,0:T(8,128)(2,1)}, bf16[8,768]{1,0:T(8,128)(2,1)S(1)}, u32[]{:S(2)}) copy-start(bf16[8,768]{1,0:T(8,128)(2,1)S(1)} %convert_element_type.1065) | copy-start | bytes 36868
  773.7 77.0 %copy-start.192 = (bf16[256,768]{1,0:T(8,128)(2,1)S(1)}, bf16[256,768]{1,0:T(8,128)(2,1)}, u32[]{:S(2)}) copy-start(bf16[256,768]{1,0:T(8,128)(2,1)} %all_gather.57) | copy-start | bytes 1179652
  776.1 75.0 %copy-start.226 = (bf16[16,768]{1,0:T(8,128)(2,1)S(1)}, bf16[16,768]{1,0:T(8,128)(2,1)}, u32[]{:S(2)}) copy-start(bf16[16,768]{1,0:T(8,128)(2,1)} %copy-done.225) | copy-start | bytes 73732
  776.1 75.0 %copy-start.433 = (pred[256]{0:T(512)(128)(4,1)S(1)}, pred[256]{0:T(512)(128)(4,1)}, u32[]{:S(2)}) copy-start(pred[256]{0:T(512)(128)(4,1)} %convert_compare_fusion.1) | copy-start | bytes 772
  783.7 67.2 %copy-start.455 = (f32[8]{0:T(128)}, f32[8]{0:T(128)S(1)}, u32[]{:S(2)}) copy-start(f32[8]{0:T(128)S(1)} %get-tuple-element.470) | copy-start | bytes 100
  866.2 93.4 %copy-start.311 = (f32[8,256]{1,0:T(8,128)S(1)}, f32[8,256]{1,0:T(8,128)}, u32[]{:S(2)}) copy-start(f32[8,256]{1,0:T(8,128)} %copy-done.310) | copy-start | bytes 24580
  866.3 193.7 %reduce-scatter.25.cloned.1.call-start = ((), (), s32[]{:S(2)}) async-start(), calls=%async_computation.22 | async-start | bytes 811008 | tf_op jit(solution)/shard_map/reduce_scatter | solution.py:309
  867.7 96.2 %copy-start.316 = (pred[8,256]{1,0:T(8,128)(4,1)S(1)}, pred[8,256]{1,0:T(8,128)(4,1)}, u32[]{:S(2)}) copy-start(pred[8,256]{1,0:T(8,128)(4,1)} %iota_compare_fusion.17) | copy-start | bytes 6148
  873.2 90.7 %copy-start.377 = (f32[8,12]{0,1:T(8,128)S(1)}, f32[8,12]{0,1:T(8,128)}, u32[]{:S(2)}) copy-start(f32[8,12]{0,1:T(8,128)} %multiply_divide_fusion.1) | copy-start | bytes 1156
  873.2 534.4 %reduce-scatter.19.cloned.1.call-start = ((), (), s32[]{:S(2)}) async-start(), calls=%async_computation.19 | async-start | bytes 17694720 | tf_op jit(solution)/shard_map/reduce_scatter | solution.py:214
  962.0 98.0 %copy-start.309 = (f32[8,256]{1,0:T(8,128)S(1)}, f32[8,256]{1,0:T(8,128)}, u32[]{:S(2)}) copy-start(f32[8,256]{1,0:T(8,128)} %convolution_multiply_fusion.21) | copy-start | bytes 24580
  962.0 98.0 %copy-start.432 = (pred[256]{0:T(512)(128)(4,1)S(1)}, pred[256]{0:T(512)(128)(4,1)}, u32[]{:S(2)}) copy-start(pred[256]{0:T(512)(128)(4,1)} %convert_compare_fusion) | copy-start | bytes 772
  962.0 98.0 %copy-start.457 = (f32[8]{0:T(128)S(1)}, f32[8]{0:T(128)}, u32[]{:S(2)}) copy-start(f32[8]{0:T(128)} %get-tuple-element.432) | copy-start | bytes 100
  962.0 98.0 %copy-start.458 = (s32[8]{0:T(128)S(1)}, s32[8]{0:T(128)}, u32[]{:S(2)}) copy-start(s32[8]{0:T(128)} %iota_add_fusion) | copy-start | bytes 100
  962.0 98.0 %copy-start.459 = (f32[8]{0:T(128)S(1)}, f32[8]{0:T(128)}, u32[]{:S(2)}) copy-start(f32[8]{0:T(128)} %get-tuple-element.366) | copy-start | bytes 100
  963.9 97.2 %copy-start.454 = (f32[8]{0:T(128)S(1)}, f32[8]{0:T(128)}, u32[]{:S(2)}) copy-start(f32[8]{0:T(128)} %copy-done.453) | copy-start | bytes 100
  965.6 97.5 %copy-start.314 = (pred[8,256]{1,0:T(8,128)(4,1)S(1)}, pred[8,256]{1,0:T(8,128)(4,1)}, u32[]{:S(2)}) copy-start(pred[8,256]{1,0:T(8,128)(4,1)} %iota_compare_fusion.16) | copy-start | bytes 6148
  965.6 97.5 %copy-start.376 = (f32[8,12]{0,1:T(8,128)S(1)}, f32[8,12]{0,1:T(8,128)}, u32[]{:S(2)}) copy-start(f32[8,12]{0,1:T(8,128)} %multiply_divide_fusion) | copy-start | bytes 1156
  970.1 94.3 %copy-start.312 = (f32[12,64]{1,0:T(8,128)S(1)}, f32[12,64]{1,0:T(8,128)}, u32[]{:S(2)}) copy-start(f32[12,64]{1,0:T(8,128)} %reshape_squeeze.2) | copy-start | bytes 9220
  1073.1 16.5 copy-start.179
  1073.1 53.1 %copy-start.434 = (f32[256]{0:T(256)}, f32[256]{0:T(256)S(1)}, u32[]{:S(2)}) copy-start(f32[256]{0:T(256)S(1)} %negate_multiply_fusion.12) | copy-start | bytes 3076
  1171.2 477.8 %reduce-scatter.21.cloned.1.call-start = ((), (), s32[]{:S(2)}) async-start(), calls=%async_computation.20 | async-start | bytes 17694720 | tf_op jit(solution)/shard_map/reduce_scatter | solution.py:214
  1271.2 429.9 %reduce-scatter.23.cloned.1.call-start = ((), (), s32[]{:S(2)}) async-start(), calls=%async_computation.21 | async-start | bytes 2949120 | tf_op jit(solution)/shard_map/reduce_scatter | solution.py:214
  1284.8 655.3 %reduce-scatter.27.cloned.1.call-start = ((), (), s32[]{:S(2)}) async-start(), calls=%async_computation.23 | async-start | bytes 17694720 | tf_op jit(solution)/shard_map/reduce_scatter | solution.py:214
  1300.7 880.2 %reduce-scatter.29.cloned.1.call-start = ((), (), s32[]{:S(2)}) async-start(), calls=%async_computation.24 | async-start | bytes 17694720 | tf_op jit(solution)/shard_map/reduce_scatter | solution.py:214
  1315.5 916.8 %reduce-scatter.31.cloned.1.call-start = ((), (), s32[]{:S(2)}) async-start(), calls=%async_computation.25 | async-start | bytes 2949120 | tf_op jit(solution)/shard_map/reduce_scatter | solution.py:214
  1319.6 1044.2 %all-reduce.8.cloned.1.call-start = ((), (), s32[]{:S(2)}) async-start(), calls=%async_computation.26 | async-start | bytes 15335424 | tf_op jit(solution)/shard_map/psum | solution.py:337
  2244.7 249.7 %all-reduce.10.cloned.1.call-start = ((), (), s32[]{:S(2)}) async-start(), calls=%async_computation.27 | async-start | bytes 491520 | tf_op jit(solution)/shard_map/psum | solution.py:338
  2255.7 480.0 %reduce-scatter.33.cloned.1.call-start = ((), (), s32[]{:S(2)}) async-start(), calls=%async_computation.28 | async-start | bytes 14745600 | tf_op jit(solution)/shard_map/reduce_scatter | solution.py:233
  2518.5 18.4 copy-start.76
  2539.1 404.5 %all-gather.15.cloned.1.call-start = ((), (), s32[]{:S(2)}) async-start(), calls=%async_computation.29 | async-start | bytes 14745600 | tf_op jit(solution)/shard_map/all_gather | solution.py:236
  2735.7 511.2 %reduce-scatter.35.cloned.1.call-start = ((), (), s32[]{:S(2)}) async-start(), calls=%async_computation.30 | async-start | bytes 14745600 | tf_op jit(solution)/shard_map/reduce_scatter | solution.py:233
  2965.6 81.6 %copy-start.114 = (f32[4,192,768]{2,1,0:T(8,128)}, f32[4,192,768]{2,1,0:T(8,128)S(1)}, u32[]{:S(2)}) copy-start(f32[4,192,768]{2,1,0:T(8,128)S(1)} %multiply_add_fusion.12) | copy-start | bytes 7077892
  2986.4 57.1 %copy-start.130 = (f32[1,192,768]{2,1,0:T(8,128)}, f32[1,192,768]{2,1,0:T(8,128)S(1)}, u32[]{:S(2)}) copy-start(f32[1,192,768]{2,1,0:T(8,128)S(1)} %fusion.245) | copy-start | bytes 1769476
  3016.3 453.4 %copy-start.134 = (f32[1,192,768]{2,1,0:T(8,128)}, f32[1,192,768]{2,1,0:T(8,128)S(1)}, u32[]{:S(2)}) copy-start(f32[1,192,768]{2,1,0:T(8,128)S(1)} %fusion.244) | copy-start | bytes 1769476
  3049.3 405.4 %copy-start.184 = (f32[1,192,768]{2,1,0:T(8,128)S(1)}, f32[1,192,768]{2,1,0:T(8,128)}, u32[]{:S(2)}) copy-start(f32[1,192,768]{2,1,0:T(8,128)} %copy-done.183) | copy-start | bytes 1769476
  3049.3 405.4 %all-gather.17.cloned.1.call-start = ((), (), s32[]{:S(2)}) async-start(), calls=%async_computation.31 | async-start | bytes 14745600 | tf_op jit(solution)/shard_map/all_gather | solution.py:236
  3246.9 452.8 %reduce-scatter.37.cloned.1.call-start = ((), (), s32[]{:S(2)}) async-start(), calls=%async_computation.32 | async-start | bytes 14745600 | tf_op jit(solution)/shard_map/reduce_scatter | solution.py:233
  3502.2 405.4 %all-gather.19.cloned.1.call-start = ((), (), s32[]{:S(2)}) async-start(), calls=%async_computation.33 | async-start | bytes 14745600 | tf_op jit(solution)/shard_map/all_gather | solution.py:236
  3699.7 451.7 %reduce-scatter.39.cloned.1.call-start = ((), (), s32[]{:S(2)}) async-start(), calls=%async_computation.34 | async-start | bytes 14745600 | tf_op jit(solution)/shard_map/reduce_scatter | solution.py:233
  3953.9 405.6 %copy-start.140 = (f32[1,192,768]{2,1,0:T(8,128)S(1)}, f32[1,192,768]{2,1,0:T(8,128)}, u32[]{:S(2)}) copy-start(f32[1,192,768]{2,1,0:T(8,128)} %copy-done.139) | copy-start | bytes 1769476
  3953.9 405.6 %all-gather.21.cloned.1.call-start = ((), (), s32[]{:S(2)}) async-start(), calls=%async_computation.35 | async-start | bytes 14745600 | tf_op jit(solution)/shard_map/all_gather | solution.py:236
  4151.5 450.9 %reduce-scatter.41.cloned.1.call-start = ((), (), s32[]{:S(2)}) async-start(), calls=%async_computation.36 | async-start | bytes 14745600 | tf_op jit(solution)/shard_map/reduce_scatter | solution.py:233
  4404.9 406.4 %all-gather.23.cloned.1.call-start = ((), (), s32[]{:S(2)}) async-start(), calls=%async_computation.37 | async-start | bytes 14745600 | tf_op jit(solution)/shard_map/all_gather | solution.py:236
  (449 other events, 1417.6 us)
Sparse Core Ops, SparseCore 0:
  43.4 20.0 reduce-scatter.14
  65.1 49.6 all-gather.8
  117.1 258.9 all-gather.10
  378.1 242.1 all-gather.12
  866.4 93.1 reduce-scatter.16
  965.4 94.5 reduce-scatter.24
  1171.3 236.2 reduce-scatter.18
  1410.7 238.2 reduce-scatter.20
  1651.9 49.0 reduce-scatter.22
  1703.4 236.7 reduce-scatter.26
  1942.6 238.2 reduce-scatter.28
  2183.2 49.0 reduce-scatter.30
  2244.8 118.9 all-reduce.7
  2370.6 123.7 all-reduce.9
  2539.2 196.4 reduce-scatter.32
  2737.1 206.3 all-gather.14
  3049.5 197.3 reduce-scatter.34
  3248.3 206.3 all-gather.16
  3502.3 197.3 reduce-scatter.36
  3701.2 206.3 all-gather.18
  3954.1 197.3 reduce-scatter.38
  4153.1 206.3 all-gather.20
  4405.0 197.3 reduce-scatter.40
  4603.9 207.3 all-gather.22
where the time goes:
time: 4890 us; the launch traced here: 4880 us
  waiting for transfers between devices  3430 us (70%)
  blocking collectives  533 us (11%)
  matrix products  528 us (11%)
  other arithmetic  209 us (4%)
  local copies, waits for them, and re-layouts  139 us (3%)
    reduce_scatter x5, waiting for transfers between devices, summed_grams(): lax.psum_scatter(local.astype(jnp.bfloat16), 'fsdp', scatter_dimension=1,...  986 us
    all_gather x5, waiting for transfers between devices, summed_grams(): lax.all_gather(shares.astype(jnp.bfloat16), 'fsdp', axis=1, tiled=True)  977 us
    reduce_scatter x6, waiting for transfers between devices, collect(): lax.psum_scatter(block_grads.astype(jnp.bfloat16), 'fsdp', scatter_dimens...  880 us
    dot_general x240, matrix products, product(): return jnp.einsum(form, left, right, preferred_element_type=jnp.float32)  502 us
    all_gather x2, blocking collectives, per_device(): lax.all_gather(own_text, ('dp', 'fsdp'), axis=0, tiled=True)  215 us
    all_gather x3, waiting for transfers between devices, fetch(): return lax.all_gather(rounded(blocks), 'fsdp', axis=1, tiled=True)  183 us
    reduce_scatter x2, waiting for transfers between devices, per_device(): lax.psum_scatter(spread, ('dp', 'fsdp'), scatter_dimension=0, tiled=True)  174 us
    all_gather x2, blocking collectives, per_device(): lax.all_gather(image_low, ('dp', 'fsdp'), axis=0, tiled=True)  140 us
  transfers between devices with their start and end apart: 24, of which 21 were waited for; matrix products, arithmetic and copies ran while one was open for 6% of the time, Pallas kernels for 0%

commit v1 on v0

v1 whole, which is shorter than its diff:
```python
import functools
import math

import jax
import jax.numpy as jnp
import numpy as np
from jax import lax
from jax.sharding import PartitionSpec as P

D = 768
HEADS = 12
FF = 3072
LAYERS = 2
IMGS = 8
POS = 32
MB = 2
NS_ITERS = 5
HD = 64


HIGH = lax.Precision.HIGHEST
LOGIT_SCALE = 50.0
CLIP_LIMIT = 0.005
MOMENT = 0.95
MUON_RATE = 0.5
MUON_DECAY = 0.01
ADAM_RATE = 0.4
BETA_ONE = 0.9
BETA_TWO = 0.999
ADAM_EPS = 1e-08
ADAM_DECAY = 0.01
COEF_A = 3.4445
COEF_B = -4.775
COEF_C = 2.0315


def rounded(value):
    return value.astype(jnp.bfloat16)


def product(left, right, form):
    return jnp.einsum(form, left, right, preferred_element_type=jnp.float32)


def layer_norm(value, gain, shift):
    centred = value - jnp.mean(value, -1, keepdims=True)
    spread = jnp.mean(centred * centred, -1, keepdims=True)
    return centred * lax.rsqrt(spread + 1e-06) * gain + shift


def head_norm(value, gain):
    heads = value.reshape(value.shape[0], HEADS, HD)
    centred = heads - jnp.mean(heads, -1, keepdims=True)
    spread = jnp.mean(centred * centred, -1, keepdims=True)
    return centred * lax.rsqrt(spread + 1e-06) * gain.reshape(HEADS, HD)


def both_norms(query, key, gain_query, gain_key):
    return (head_norm(query, gain_query), head_norm(key, gain_key))


def unit_rows(value):
    return (
        value
        * lax.rsqrt(jnp.mean(value * value, -1, keepdims=True) + 1e-06)
        * (1.0 / math.sqrt(value.shape[-1]))
    )


def positions(grid):
    slots = jnp.arange(POS, dtype=jnp.int32)
    row_index = grid[0] * POS // grid[2]
    col_index = grid[1] * POS // grid[3]
    return (
        (row_index[:, None] == slots[None]).astype(jnp.float32),
        (col_index[:, None] == slots[None]).astype(jnp.float32),
    )


def pooling(segment):
    member = segment[None, :] == jnp.arange(IMGS, dtype=jnp.int32)[:, None]

    def pooled_of(final, query):
        split = final.reshape(-1, HEADS, HD)
        logits = jnp.einsum("shd,hd->hs", split, query.reshape(HEADS, HD), precision=HIGH) * (
            1.0 / math.sqrt(HD)
        )
        logits = jnp.where(member[:, None, :], logits[None], -1e30)
        share = jax.nn.softmax(logits, -1)
        return jnp.einsum("khs,shd->khd", share, split, precision=HIGH).reshape(IMGS, -1)

    return pooled_of


def fetch(blocks):
    return lax.all_gather(rounded(blocks), "fsdp", axis=1, tiled=True)


def masked_scores(query_low, key_low, same):
    scores = product(query_low, key_low, "bshd,bthd->bhst") * (1.0 / math.sqrt(HD))
    return jnp.where(same[:, None], scores, -1e30)


def layer_forward(state, blocks, gains, same):
    heads_in, norm_one = jax.vjp(layer_norm, state, gains[0], gains[1])
    heads_low = rounded(heads_in)
    mixed = product(heads_low, blocks[0:3].reshape(3 * D, D), "sd,rd->sr")
    (query, key), norms_back = jax.vjp(
        both_norms, mixed[:, :D], mixed[:, D : 2 * D], gains[4], gains[5]
    )
    query_low = rounded(query).reshape(MB, -1, HEADS, HD)
    key_low = rounded(key).reshape(MB, -1, HEADS, HD)
    value_low = rounded(mixed[:, 2 * D :]).reshape(MB, -1, HEADS, HD)
    scores = masked_scores(query_low, key_low, same)
    top = jax.scipy.special.logsumexp(scores, axis=-1, keepdims=True)
    weights_low = rounded(jnp.exp(scores - top))
    attended_low = rounded(product(weights_low, value_low, "bhst,bthd->bshd").reshape(-1, D))
    state = state + product(attended_low, blocks[3], "sr,rd->sd")
    normed, norm_two = jax.vjp(layer_norm, state, gains[2], gains[3])
    normed_low = rounded(normed)
    hidden, gelu_back = jax.vjp(
        jax.nn.gelu, product(normed_low, blocks[4:8].reshape(FF, D), "sd,rd->sr")
    )
    hidden_low = rounded(hidden)
    state = state + product(hidden_low, blocks[8:12].reshape(FF, D), "sr,rd->sd")
    kept = (
        norm_one,
        heads_low,
        norms_back,
        query_low,
        key_low,
        value_low,
        top,
        attended_low,
        norm_two,
        normed_low,
        gelu_back,
        hidden_low,
    )
    return (state, kept)


def layer_backward(grad, kept, blocks, same):
    (
        norm_one,
        heads_low,
        norms_back,
        query_low,
        key_low,
        value_low,
        top,
        attended_low,
        norm_two,
        normed_low,
        gelu_back,
        hidden_low,
    ) = kept
    down = blocks[8:12].reshape(FF, D)
    upward = blocks[4:8].reshape(FF, D)
    grad_low = rounded(grad)
    grad_down = rounded(product(hidden_low, grad_low, "sr,sd->rd"))
    (grad_hidden,) = gelu_back(product(grad_low, down, "sd,rd->sr"))
    hidden_grad = rounded(grad_hidden)
    grad_up = rounded(product(hidden_grad, normed_low, "sr,sd->rd"))
    inner, gain_two, shift_two = norm_two(product(hidden_grad, upward, "sr,rd->sd"))
    grad = grad + inner
    grad_low = rounded(grad)
    grad_out = rounded(product(attended_low, grad_low, "sr,sd->rd"))
    attended_grad = rounded(product(grad_low, blocks[3], "sd,rd->sr")).reshape(MB, -1, HEADS, HD)
    weights = jnp.exp(masked_scores(query_low, key_low, same) - top)
    weights_low = rounded(weights)
    value_grad = product(weights_low, attended_grad, "bhst,bshd->bthd")
    weight_grad = product(attended_grad, value_low, "bshd,bthd->bhst")
    score_grad = weights * (weight_grad - jnp.sum(weights * weight_grad, -1, keepdims=True))
    score_low = rounded(score_grad * (1.0 / math.sqrt(HD)))
    query_grad = product(score_low, key_low, "bhst,bthd->bshd").reshape(-1, HEADS, HD)
    key_grad = product(score_low, query_low, "bhst,bshd->bthd").reshape(-1, HEADS, HD)
    query_in, key_in, gain_query, gain_key = norms_back((query_grad, key_grad))
    mixed_low = rounded(jnp.concatenate([query_in, key_in, value_grad.reshape(-1, D)], 1))
    grad_mixed = rounded(product(mixed_low, heads_low, "sr,sd->rd"))
    inner, gain_one, shift_one = norm_one(
        product(mixed_low, blocks[0:3].reshape(3 * D, D), "sr,rd->sd")
    )
    grad = grad + inner
    block_grads = jnp.concatenate(
        [
            grad_mixed.reshape(3, D, D),
            grad_out[None],
            grad_up.reshape(4, D, D),
            grad_down.reshape(4, D, D),
        ],
        0,
    )
    gain_grads = jnp.stack([gain_one, shift_one, gain_two, shift_two, gain_query, gain_key])
    return (grad, block_grads, gain_grads)


def contrast_rows(scores, alive, own_live, offset):
    masked = jnp.where(alive[None, :] > 0, scores, -1e30)
    top = jax.scipy.special.logsumexp(masked, axis=1, keepdims=True)
    share = jnp.exp(masked - top)
    columns = jnp.arange(scores.shape[1], dtype=jnp.int32)
    target = (
        columns[None, :] == offset + jnp.arange(scores.shape[0], dtype=jnp.int32)[:, None]
    ).astype(jnp.float32)
    diagonal = jnp.sum(scores * target, 1)
    term = jnp.sum((top[:, 0] - diagonal) * own_live)
    return (term, (share - target) * own_live[:, None])


def muon_groups():
    found = [(0, 1), (1, 1)]
    for index in range(LAYERS):
        base = 2 + 12 * index
        found = found + [(base, 3), (base + 3, 1), (base + 4, 4), (base + 8, 4)]
    return found


def lane_plan(lanes):
    plan = [[] for _ in range(lanes)]
    for start, number in sorted(muon_groups(), key=lambda group: -group[1]):
        lane = min(range(lanes), key=lambda i: (sum(n for _, n in plan[i]), len(plan[i]), i))
        plan[lane].append((start, number))
    depth = max(len(entry) for entry in plan)
    widths = [
        max([entry[slot][1] for entry in plan if slot < len(entry)]) for slot in range(depth)
    ]
    return (plan, widths)


def lane_tables(plan, widths):
    index = np.zeros((len(plan), sum(widths)), np.int32)
    mask = np.zeros((len(plan), sum(widths)), np.float32)
    number = np.ones((len(plan), sum(widths)), np.float32)
    home = {}
    for lane, entry in enumerate(plan):
        first = 0
        for slot, width in enumerate(widths):
            if slot < len(entry):
                start, count = entry[slot]
                for place in range(count):
                    index[lane, first + place] = start + place
                    mask[lane, first + place] = 1.0
                    number[lane, first + place] = count
                    home[start + place] = (lane, first + place)
            first += width
    return (index, mask, number, home)


def orthogonal_factor(gram):
    size = jnp.sqrt(jnp.trace(gram)) + 1e-07
    state = gram / (size * size)
    total = None
    for turn in range(NS_ITERS):
        low = rounded(state)
        change = COEF_B * state + COEF_C * jnp.dot(low, low, preferred_element_type=jnp.float32)
        change_low = rounded(change)
        if total is None:
            total = COEF_A * jnp.eye(D, dtype=jnp.float32) + change
        else:
            total = COEF_A * total + jnp.dot(
                rounded(total), change_low, preferred_element_type=jnp.float32
            )
        if turn < NS_ITERS - 1:
            for _ in range(2):
                state = COEF_A * state + jnp.dot(
                    rounded(state), change_low, preferred_element_type=jnp.float32
                )
    return total / size


def per_device(
    patches, grid, segments, text_ids, table, weights, momenta, gains, gains_m, gains_v, step
):
    fin = 6 * LAYERS
    base = fin + 3
    lanes = lax.axis_size("dp")
    slots = jnp.arange(IMGS, dtype=jnp.int32)
    live = jnp.any(segments[:, 0, None, :] == slots[None, :, None], -1).astype(jnp.float32)
    count = lax.psum(jnp.sum(live), ("dp", "fsdp"))
    factor = 1.0 / (2.0 * count)
    group_ids = lax.all_gather(text_ids, "fsdp", axis=1, tiled=True)
    flat_ids = jnp.transpose(group_ids, (1, 0, 2, 3)).reshape(-1, group_ids.shape[3])
    share_rows = table.shape[0]
    first_row = lax.axis_index("fsdp") * share_rows
    picked = flat_ids - first_row
    hits = jnp.sum(
        (picked[:, :, None] == jnp.arange(share_rows, dtype=jnp.int32)[None, None, :]).astype(
            jnp.int32
        ),
        1,
    )
    text_sum = lax.psum_scatter(
        jnp.dot(
            rounded(hits.astype(jnp.float32)), table, preferred_element_type=jnp.float32
        ).astype(jnp.bfloat16),
        "fsdp",
        scatter_dimension=0,
        tiled=True,
    ).astype(jnp.float32)
    text_low = rounded(unit_rows(text_sum / text_ids.shape[-1])).reshape(MB, IMGS, -1)
    me = lax.axis_index(("dp", "fsdp"))
    rows_local = weights.shape[1]
    segment = segments[:, 0]
    same = segment[:, :, None] == segment[:, None, :]
    rows_hot, cols_hot = jax.vmap(positions)(grid[:, 0])
    rows_hot = rows_hot.reshape(-1, POS)
    cols_hot = cols_hot.reshape(-1, POS)
    patch_low = patches.reshape(-1, D)
    stem = fetch(weights[0:2])
    state = product(patch_low, stem[0], "sd,rd->sr")
    state = state + jnp.dot(rows_hot, gains[base : base + POS], precision=HIGH)
    state = state + jnp.dot(cols_hot, gains[base + POS : base + 2 * POS], precision=HIGH)
    saved = []
    for index in range(LAYERS):
        blocks = fetch(weights[2 + 12 * index : 14 + 12 * index])
        state, kept = layer_forward(state, blocks, gains[6 * index : 6 * index + 6], same)
        saved.append((kept, blocks))
    final, norm_final = jax.vjp(layer_norm, state, gains[fin], gains[fin + 1])

    def pool_all(values, query):
        split = values.reshape(MB, -1, D)
        return jnp.concatenate([pooling(segment[part])(split[part], query) for part in range(MB)])

    pooled, pool_back = jax.vjp(pool_all, final, gains[fin + 2])
    pooled_low = rounded(pooled)
    embedded, unit_back = jax.vjp(unit_rows, product(pooled_low, stem[1], "kr,rd->kd"))
    image_low = rounded(embedded)
    both = jnp.concatenate([image_low, text_low.reshape(MB * IMGS, D)], 0)
    whole = lax.all_gather(both, ("dp", "fsdp"), axis=0)
    alive = lax.all_gather(rounded(live), ("dp", "fsdp"), axis=1, tiled=True).astype(jnp.float32)
    loss_part = jnp.float32(0.0)
    image_grads = []
    spreads = []
    for part in range(MB):
        images = whole[:, part * IMGS : (part + 1) * IMGS].reshape(-1, D)
        texts = whole[:, (MB + part) * IMGS : (MB + part + 1) * IMGS].reshape(-1, D)
        own_image = image_low[part * IMGS : (part + 1) * IMGS]
        own_text = text_low[part]
        forward = LOGIT_SCALE * product(own_image, texts, "kd,nd->kn")
        backward = LOGIT_SCALE * product(own_text, images, "kd,nd->kn")
        term_f, grad_f = contrast_rows(forward, alive[part], live[part], me * IMGS)
        term_b, grad_b = contrast_rows(backward, alive[part], live[part], me * IMGS)
        loss_part = loss_part + (term_f + term_b) * factor
        forward_low = rounded(grad_f * factor * LOGIT_SCALE)
        backward_low = rounded(grad_b * factor * LOGIT_SCALE)
        spreads.append(product(backward_low, own_text, "kn,kd->nd"))
        image_grads.append(product(forward_low, texts, "kn,nd->kd"))
    spread = jnp.stack([value.reshape(-1, IMGS, D) for value in spreads], 1)
    text_side = lax.psum_scatter(spread, ("dp", "fsdp"), scatter_dimension=0)
    image_grad = jnp.concatenate(image_grads, 0) + text_side.reshape(MB * IMGS, D)
    (embed_grad,) = unit_back(image_grad)
    embed_low = rounded(embed_grad)
    grad_pool = rounded(product(pooled_low, embed_low, "kr,kd->rd"))
    final_grad, query_grad = pool_back(product(embed_low, stem[1], "kd,rd->kr"))
    grad, gain_final, shift_final = norm_final(final_grad)
    gain_parts = [None] * LAYERS
    shards = [None] * (LAYERS + 1)
    for index in reversed(range(LAYERS)):
        kept, blocks = saved[index]
        grad, block_grads, gain_parts[index] = layer_backward(grad, kept, blocks, same)
        shards[index + 1] = lax.psum(
            lax.psum_scatter(block_grads, "fsdp", scatter_dimension=1, tiled=True), "dp"
        )
    grad_low = rounded(grad)
    grad_patch = rounded(product(grad_low, patch_low, "sr,sd->rd"))
    shards[0] = lax.psum(
        lax.psum_scatter(
            jnp.stack([grad_patch, grad_pool]), "fsdp", scatter_dimension=1, tiled=True
        ),
        "dp",
    )
    grad_rows = jnp.dot(rows_hot.T, grad, precision=HIGH)
    grad_cols = jnp.dot(cols_hot.T, grad, precision=HIGH)
    gains_grad = jnp.concatenate(
        gain_parts
        + [jnp.stack([gain_final, shift_final, query_grad]), grad_rows, grad_cols],
        0,
    )
    gains_grad, loss = lax.psum((gains_grad, loss_part), ("dp", "fsdp"))
    shard_grads = jnp.concatenate(shards, 0).astype(jnp.float32)
    squares = lax.psum(jnp.sum(shard_grads * shard_grads), "fsdp")
    norm = jnp.sqrt(squares + jnp.sum(gains_grad * gains_grad))
    clip = jnp.minimum(1.0, CLIP_LIMIT / (norm + 1e-06))
    momenta_new = MOMENT * momenta + clip * shard_grads
    plan, widths = lane_plan(lanes)
    index, mask, number, home = lane_tables(plan, widths)
    lane = lax.axis_index("dp")
    own = jnp.stack(
        [
            lax.dynamic_index_in_dim(momenta_new, jnp.asarray(index)[lane, place], 0, False)
            * jnp.asarray(mask)[lane, place]
            for place in range(index.shape[1])
        ]
    )
    own_low = rounded(own)
    bounds = np.cumsum([0] + widths)
    grams = jnp.stack(
        [
            product(own_low[a:b], own_low[a:b], "brd,bre->de")
            for a, b in zip(bounds[:-1], bounds[1:])
        ]
    )
    grams = lax.psum(grams, "fsdp")
    turned = jnp.concatenate(
        [
            product(
                own_low[bounds[slot] : bounds[slot + 1]],
                rounded(orthogonal_factor(grams[slot])),
                "brd,de->bre",
            )
            for slot in range(len(widths))
        ],
        0,
    )
    spread_rows = lax.all_gather(rounded(turned), "dp", axis=0)
    current = jnp.stack(
        [spread_rows[home[block][0], home[block][1]] for block in range(weights.shape[0])]
    ).astype(jnp.float32)
    scale = np.ones((weights.shape[0], 1, 1), np.float32)
    for start, count_blocks in muon_groups():
        scale[start : start + count_blocks] = MUON_RATE * math.sqrt(count_blocks)
    weights_new = weights * (1.0 - MUON_RATE * MUON_DECAY) - jnp.asarray(scale) * current
    grad_small = clip * gains_grad
    moment_one = BETA_ONE * gains_m + (1.0 - BETA_ONE) * grad_small
    moment_two = BETA_TWO * gains_v + (1.0 - BETA_TWO) * grad_small * grad_small
    count_steps = step[0].astype(jnp.float32)
    corrected_one = moment_one / (1.0 - jnp.power(BETA_ONE, count_steps))
    corrected_two = moment_two / (1.0 - jnp.power(BETA_TWO, count_steps))
    gains_new = gains - ADAM_RATE * (
        corrected_one / (jnp.sqrt(corrected_two) + ADAM_EPS) + ADAM_DECAY * gains
    )
    shift_grad = grad_small[fin + 1]
    return (
        loss,
        norm,
        weights_new,
        rounded(weights_new),
        momenta_new,
        gains_new,
        moment_one,
        moment_two,
        shift_grad,
    )


def solution(mesh):
    placed = (
        P(None, ("dp", "fsdp"), None, None),
        P(None, ("dp", "fsdp"), None, None),
        P(None, ("dp", "fsdp"), None),
        P(None, ("dp", "fsdp"), None, None),
        P("fsdp", None),
        P(None, "fsdp", None),
        P(None, "fsdp", None),
        P(),
        P(),
        P(),
        P(),
    )
    return jax.shard_map(
        per_device,
        mesh=mesh,
        in_specs=placed,
        out_specs=(
            P(),
            P(),
            P(None, "fsdp", None),
            P(None, "fsdp", None),
            P(None, "fsdp", None),
            P(),
            P(),
            P(),
            P(),
        ),
        check_vma=False,
    )
```

time: 4890 us -> 2370 us (0.48)
  waiting for transfers between devices: 3430 us -> 1460 us
  blocking collectives: 533 us -> 174 us
  matrix products: 528 us -> 278 us
  local copies, waits for them, and re-layouts: 139 us -> 253 us
  other arithmetic: 209 us -> 152 us
    reduce_scatter x13 -> x4, waiting for transfers between devices: 2040 us -> 555 us  [the longest x2 481 us: per_device(): lax.psum_scatter(block_grads, 'fsdp', scatter_dimension=1, tiled=True)]
    all_gather x5 -> x2, waiting for transfers between devices: 977 us -> 24.3 us  [the longest x1 24.3 us: per_device(): spread_rows = lax.all_gather(rounded(turned), 'dp', axis=0)]
    dot_general x240 -> x53, matrix products: 502 us -> 204 us  [product(): return jnp.einsum(form, left, right, preferred_element_type=jnp.float32)]
    all_gather x3, waiting for transfers between devices: 183 us -> 479 us  [fetch(): return lax.all_gather(rounded(blocks), 'fsdp', axis=1, tiled=True)]
    all_gather x4 -> x1, blocking collectives: 356 us -> 68.5 us  [per_device(): lax.all_gather(rounded(live), ('dp', 'fsdp'), axis=1, tiled=True)]
    psum x1 -> x2, waiting for transfers between devices: 108 us -> 274 us  [the longest x1 169 us: per_device(): grams = lax.psum(grams, 'fsdp')]
    unnamed x1 -> x0, blocking collectives: 50.6 us -> none
    dot_general x4 -> x34, matrix products: 2.48 us -> 51.9 us  [the longest x10 20.1 us: orthogonal_factor(): jnp.dot(low, low, preferred_element_type=jnp.float32)]
  transfers between devices with their start and end apart: 24 -> 13, of which waited for: 21 -> 11; matrix products, arithmetic and copies ran while one was open for 6% -> 7% of each run, Pallas kernels for 0% -> 0%
where the time goes in v1:
time: 2370 us; the launch traced here: 2350 us
  waiting for transfers between devices  1460 us (62%)
  matrix products  278 us (12%)
  local copies, waits for them, and re-layouts  253 us (11%)
  blocking collectives  174 us (7%)
  other arithmetic  152 us (6%)
  between operations  36.1 us (2%)
    reduce_scatter x2, waiting for transfers between devices, per_device(): lax.psum_scatter(block_grads, 'fsdp', scatter_dimension=1, tiled=True)  481 us
    all_gather x3, waiting for transfers between devices, fetch(): return lax.all_gather(rounded(blocks), 'fsdp', axis=1, tiled=True)  479 us
    dot_general x53, matrix products, product(): return jnp.einsum(form, left, right, preferred_element_type=jnp.float32)  204 us
    psum x1, waiting for transfers between devices, per_device(): grams = lax.psum(grams, 'fsdp')  169 us
    psum x1, waiting for transfers between devices, per_device(): gains_grad, loss = lax.psum((gains_grad, loss_part), ('dp', 'fsdp'))  124 us
    psum x1, waiting for transfers between devices, per_device(): lax.psum(lax.psum_scatter(block_grads, 'fsdp', scatter_dimension=1, tiled...  105 us
    reduce_scatter x1, waiting for transfers between devices, per_device(): text_side = lax.psum_scatter(spread, ('dp', 'fsdp'), scatter_dimension=0)  72.4 us
    all_gather x1, blocking collectives, per_device(): lax.all_gather(rounded(live), ('dp', 'fsdp'), axis=1, tiled=True)  68.5 us
  transfers between devices with their start and end apart: 13, of which 11 were waited for; matrix products, arithmetic and copies ran while one was open for 7% of the time, Pallas kernels for 0%

profile of v1, /device:TPU:0, one launch (start us, length us, event | category | flops | bytes accessed | tf_op | source)
XLA Modules:
  0.0 2352.4 jit_solution(6298841848688018539)
XLA Ops:
  7.2 15.1 all_gather.29
  22.4 14.1 convert_reduce_fusion
  36.5 7.1 convolution_convert_fusion.17
  43.6 9.6 convert.64
  55.2 6.8 fusion.404
  70.2 44.0 %all-gather.8.cloned.1.call-done = bf16[2,768,768]{2,1,0:T(8,128)(2,1)} async-done(((bf16[2,192,768]{2,1,0:T(8,128)(2,1)}), bf16[2,768,768]{2,1,0:T(8,128)(2,1)}) %all-gather.8.cloned.1.call-update) | async-done | bytes 2359312 | tf_op jit(solution)/shard_map/all_gather | solution.py:96
  117.8 241.4 %all-gather.10.cloned.1.call-done = bf16[12,768,768]{2,1,0:T(8,128)(2,1)} async-done(((bf16[12,192,768]{2,1,0:T(8,128)(2,1)}), bf16[12,768,768]{2,1,0:T(8,128)(2,1)}) %all-gather.10.cloned.1.call-update) | async-done | bytes 14155792 | tf_op jit(solution)/shard_map/all_gather | solution.py:96
  381.9 3.5 fusion.20
  393.5 6.9 fusion.403
  405.3 3.9 fusion.413
  409.6 193.8 %all-gather.12.cloned.1.call-done = bf16[12,768,768]{2,1,0:T(8,128)(2,1)} async-done(((bf16[12,192,768]{2,1,0:T(8,128)(2,1)}), bf16[12,768,768]{2,1,0:T(8,128)(2,1)}) %all-gather.12.cloned.1.call-update) | async-done | bytes 14155792 | tf_op jit(solution)/shard_map/all_gather | solution.py:96
  619.3 3.1 reshape.997
  633.5 3.5 fusion.21
  644.6 4.3 fusion.68
  652.8 6.7 fusion.402
  664.5 3.9 fusion.415
  686.7 38.7 %psum.56 = f32[]{:T(128)} all-reduce(f32[]{:T(128)} %convert_reduce_fusion.1), channel_id=1, replica_groups=mesh['dp'=8,'fsdp'=4] {'dp','fsdp'}, use_global_device_ids=true, to_apply=%region_40.41 | all-reduce | flops 1 | bytes 8 | tf_op jit(solution)/shard_map/psum | solution.py:280
  726.5 68.5 %all-gather.1 = bf16[32,8,2]{1,2,0:T(2,128)(2,1)} all-gather(bf16[1,8,2]{1,2,0:T(2,128)(2,1)S(1)} %get-tuple-element.154), channel_id=1, replica_groups=mesh['dp'=8,'fsdp'=4] {'dp','fsdp'}, dimensions={0}, use_global_device_ids=true | all-gather | bytes 1056 | tf_op jit(solution)/shard_map/all_gather | solution.py:331
  816.1 3.2 copy.393
  825.1 3.1 copy.422
  836.3 72.4 %reduce-scatter.8.cloned.1.call-done = f32[1,2,8,768]{3,2,1,0:T(8,128)} async-done(((f32[32,2,8,768]{3,2,1,0:T(8,128)}), f32[1,2,8,768]{3,2,1,0:T(8,128)}) %reduce-scatter.8.cloned.1.call-update) | async-done | bytes 49168 | tf_op jit(solution)/shard_map/reduce_scatter | solution.py:350
  931.3 8.8 fusion.17
  940.2 3.4 multiply_reduce_fusion.4
  951.3 5.1 fusion.121
  956.4 13.7 fusion.25
  973.9 13.9 fusion.28
  991.5 5.3 fusion.69
  1035.8 8.4 fusion.49
  1044.2 4.6 multiply_reduce_fusion.5
  1050.5 8.4 fusion.10
  1059.0 3.5 multiply_reduce_fusion.8
  1068.1 5.0 fusion.118
  1073.1 11.6 fusion.33
  1088.6 13.8 fusion.36
  1106.2 5.3 fusion.70
  1122.2 3.4 multiply_reduce_fusion.6
  1139.1 3.1 copy.421
  1163.5 7.4 fusion.55
  1181.6 3.5 convolution_convert_fusion.5
  1185.2 3.3 convolution_convert_fusion.4
  1188.5 6.2 convolution_convert_fusion.3
  1194.7 6.3 pad_maximum_fusion
  1204.7 3.5 convolution_convert_fusion.2
  1208.2 3.3 convolution_convert_fusion.1
  1211.5 6.1 convolution_convert_fusion
  1217.6 6.3 pad_maximum_fusion.1
  1225.2 239.8 %reduce-scatter.12.cloned.1.call-done = bf16[12,192,768]{2,1,0:T(8,128)(2,1)} async-done(((bf16[12,768,768]{2,1,0:T(8,128)(2,1)}), bf16[12,192,768]{2,1,0:T(8,128)(2,1)}) %reduce-scatter.12.cloned.1.call-update) | async-done | bytes 3538960 | tf_op jit(solution)/shard_map/reduce_scatter | solution.py:363
  1465.0 241.4 %reduce-scatter.14.cloned.1.call-done = bf16[12,192,768]{2,1,0:T(8,128)(2,1)} async-done(((bf16[12,768,768]{2,1,0:T(8,128)(2,1)}), bf16[12,192,768]{2,1,0:T(8,128)(2,1)}) %reduce-scatter.14.cloned.1.call-update) | async-done | bytes 3538960 | tf_op jit(solution)/shard_map/reduce_scatter | solution.py:363
  1721.7 4.2 concatenate.54
  1725.9 105.3 %all-reduce.11.cloned.1.call-done = (bf16[12,192,768]{2,1,0:T(8,128)(2,1)}, bf16[12,192,768]{2,1,0:T(8,128)(2,1)}, bf16[2,192,768]{2,1,0:T(8,128)(2,1)}) async-done(((bf16[12,192,768]{2,1,0:T(8,128)(2,1)}, bf16[12,192,768]{2,1,0:T(8,128)(2,1)}, bf16[2,192,768]{2,1,0:T(8,128)(2,1)}), (bf16[12,192,768]{2,1,0:T(8,128)(2,1)}, bf16[12,192,768]{2,1,0:T(8,128)(2,1)}, ...) | async-done | bytes 7667728 | tf_op jit(solution)/shard_map/psum | solution.py:362
  1831.3 6.7 fusion.2
  1837.9 124.2 %all-reduce.7.cloned.1.call-done = f32[79,768]{1,0:T(8,128)} async-done(((f32[79,768]{1,0:T(8,128)}), f32[79,768]{1,0:T(8,128)}) %all-reduce.7.cloned.1.call-update) | async-done | bytes 242704 | tf_op jit(solution)/shard_map/psum | solution.py:380
  1963.7 12.4 psum.61
  1977.6 8.2 fusion.3
  1986.9 4.6 copy-done.15
  1998.4 168.9 %all-reduce.9.cloned.1.call-done = f32[2,768,768]{2,1,0:T(8,128)} async-done(((f32[2,768,768]{2,1,0:T(8,128)}), f32[2,768,768]{2,1,0:T(8,128)}) %all-reduce.9.cloned.1.call-update) | async-done | bytes 4718608 | tf_op jit(solution)/shard_map/psum | solution.py:404
  2167.3 3.1 fusion.43
  2171.2 4.4 multiply_add_fusion.23
  2184.8 4.4 multiply_add_fusion.11
  2224.0 4.8 fusion.65
  2228.8 5.0 fusion.105
  2238.4 39.7 %psum.57 = f32[]{:T(128)} all-reduce(f32[]{:T(128)S(6)} %multiply.259), channel_id=1, replica_groups=mesh['dp'=8,'fsdp'=4] {'dp','fsdp'}, use_global_device_ids=true, to_apply=%region_49.50 | all-reduce | flops 1 | bytes 8 | tf_op jit(solution)/shard_map/psum | solution.py:380
  2279.8 24.3 %all-gather.14.cloned.1.call-done = bf16[8,5,192,768]{3,2,1,0:T(8,128)(2,1)} async-done(((bf16[1,5,192,768]{3,2,1,0:T(8,128)(2,1)}), bf16[8,5,192,768]{3,2,1,0:T(8,128)(2,1)}) %all-gather.14.cloned.1.call-update) | async-done | bytes 11796496 | tf_op jit(solution)/shard_map/all_gather | solution.py:416
  2329.7 14.8 fusion.396
  (966 shorter events, 383.5 us)
Async XLA Ops:
  7.2 107.0 %copy-start = (bf16[2,1,256,768]{3,2,1,0:T(8,128)(2,1)S(1)}, bf16[2,1,256,768]{3,2,1,0:T(8,128)(2,1)}, u32[]{:S(2)}) copy-start(bf16[2,1,256,768]{3,2,1,0:T(8,128)(2,1)} %param.14) | copy-start | bytes 2359300
  7.2 61.3 %reduce-scatter.6.cloned.1.call-start = ((), (), s32[]{:S(2)}) async-start(), calls=%async_computation.8 | async-start | bytes 122880 | tf_op jit(solution)/shard_map/reduce_scatter | solution.py:293
  43.6 70.6 %all-gather.8.cloned.1.call-start = ((), (), s32[]{:S(2)}) async-start(), calls=%async_computation.5 | async-start | bytes 2949120 | tf_op jit(solution)/shard_map/all_gather | solution.py:96
  55.1 304.1 %all-gather.10.cloned.1.call-start = ((), (), s32[]{:S(2)}) async-start(), calls=%async_computation.6 | async-start | bytes 17694720 | tf_op jit(solution)/shard_map/all_gather | solution.py:96
  62.0 541.4 %all-gather.12.cloned.1.call-start = ((), (), s32[]{:S(2)}) async-start(), calls=%async_computation.7 | async-start | bytes 17694720 | tf_op jit(solution)/shard_map/all_gather | solution.py:96
  62.6 740.4 %all-gather.16.cloned.1.call-start = ((), (), s32[]{:S(2)}) async-start(), calls=%async_computation.16 | async-start | bytes 1622016 | tf_op jit(solution)/shard_map/all_gather | solution.py:330
  63.8 52.6 %copy-start.149 = (f32[768]{0:T(1024)}, f32[768]{0:T(1024)S(1)}, u32[]{:S(2)}) copy-start(f32[768]{0:T(1024)S(1)} %get-tuple-element.44) | copy-start | bytes 9220
  63.8 52.6 %copy-start.151 = (f32[768]{0:T(1024)}, f32[768]{0:T(1024)S(1)}, u32[]{:S(2)}) copy-start(f32[768]{0:T(1024)S(1)} %get-tuple-element.45) | copy-start | bytes 9220
  63.8 297.7 %copy-start.208 = (f32[768]{0:T(1024)}, f32[768]{0:T(1024)S(1)}, u32[]{:S(2)}) copy-start(f32[768]{0:T(1024)S(1)} %get-tuple-element.47) | copy-start | bytes 9220
  63.8 297.7 %copy-start.244 = (f32[768]{0:T(1024)}, f32[768]{0:T(1024)S(1)}, u32[]{:S(2)}) copy-start(f32[768]{0:T(1024)S(1)} %get-tuple-element.46) | copy-start | bytes 9220
  63.9 317.9 %copy-start.112 = (f32[12,64]{1,0:T(8,128)}, f32[12,64]{1,0:T(8,128)S(1)}, u32[]{:S(2)}) copy-start(f32[12,64]{1,0:T(8,128)S(1)} %mul.1256) | copy-start | bytes 9220
  64.0 317.9 %copy-start.114 = (f32[12,64]{1,0:T(8,128)}, f32[12,64]{1,0:T(8,128)S(1)}, u32[]{:S(2)}) copy-start(f32[12,64]{1,0:T(8,128)S(1)} %mul.1262) | copy-start | bytes 9220
  64.0 569.5 %copy-start.116 = (f32[12,64]{1,0:T(8,128)}, f32[12,64]{1,0:T(8,128)S(1)}, u32[]{:S(2)}) copy-start(f32[12,64]{1,0:T(8,128)S(1)} %mul.1285) | copy-start | bytes 9220
  64.1 569.4 %copy-start.118 = (f32[12,64]{1,0:T(8,128)}, f32[12,64]{1,0:T(8,128)S(1)}, u32[]{:S(2)}) copy-start(f32[12,64]{1,0:T(8,128)S(1)} %mul.1291) | copy-start | bytes 9220
  66.4 50.1 %copy-start.172 = (s32[512]{0:T(512)}, s32[512]{0:T(512)S(1)}, u32[]{:S(2)}) copy-start(s32[512]{0:T(512)S(1)} %add_select_fusion) | copy-start | bytes 6148
  117.4 244.0 %copy-start.11 = (f32[512,768]{1,0:T(8,128)}, f32[512,768]{1,0:T(8,128)S(1)}, u32[]{:S(2)}) copy-start(f32[512,768]{1,0:T(8,128)S(1)} %get-tuple-element.156) | copy-start | bytes 4718596
  117.4 244.0 %copy-start.174 = (f32[512]{0:T(512)}, f32[512]{0:T(512)S(1)}, u32[]{:S(2)}) copy-start(f32[512]{0:T(512)S(1)} %broadcast_multiply_fusion.11) | copy-start | bytes 6148
  117.7 243.7 %copy-start.186 = (f32[512]{0:T(512)}, f32[512]{0:T(512)S(1)}, u32[]{:S(2)}) copy-start(f32[512]{0:T(512)S(1)} %multiply_reduce_fusion.27) | copy-start | bytes 6148
  117.8 243.7 %copy-start.211 = (f32[512]{0:T(512)}, f32[512]{0:T(512)S(1)}, u32[]{:S(2)}) copy-start(f32[512]{0:T(512)S(1)} %fusion.319) | copy-start | bytes 6148
  409.2 196.5 %copy-start.30 = (f32[512,768]{1,0:T(8,128)}, f32[512,768]{1,0:T(8,128)S(1)}, u32[]{:S(2)}) copy-start(f32[512,768]{1,0:T(8,128)S(1)} %get-tuple-element.162) | copy-start | bytes 4718596
  409.2 196.4 %copy-start.177 = (f32[512]{0:T(512)}, f32[512]{0:T(512)S(1)}, u32[]{:S(2)}) copy-start(f32[512]{0:T(512)S(1)} %broadcast_multiply_fusion.9) | copy-start | bytes 6148
  409.5 196.1 %copy-start.190 = (f32[512]{0:T(512)}, f32[512]{0:T(512)S(1)}, u32[]{:S(2)}) copy-start(f32[512]{0:T(512)S(1)} %multiply_reduce_fusion.23) | copy-start | bytes 6148
  409.6 196.1 %copy-start.214 = (f32[512]{0:T(512)}, f32[512]{0:T(512)S(1)}, u32[]{:S(2)}) copy-start(f32[512]{0:T(512)S(1)} %fusion.321) | copy-start | bytes 6148
  409.6 196.1 %copy-start.202 = (f32[768]{0:T(1024)S(1)}, f32[768]{0:T(1024)}, u32[]{:S(2)}) copy-start(f32[768]{0:T(1024)} %get-tuple-element.41) | copy-start | bytes 9220
  409.6 196.1 %copy-start.240 = (f32[768]{0:T(1024)S(1)}, f32[768]{0:T(1024)}, u32[]{:S(2)}) copy-start(f32[768]{0:T(1024)} %get-tuple-element.40) | copy-start | bytes 9220
  615.7 12.2 copy-start.99
  672.2 242.2 %copy-start.16 = (f32[256,768]{0,1:T(8,128)}, f32[256,768]{0,1:T(8,128)S(1)}, u32[]{:S(2)}) copy-start(f32[256,768]{0,1:T(8,128)S(1)} %copy.377) | copy-start | bytes 2359300
  673.0 159.6 %copy-start.125 = (f32[8,12]{0,1:T(8,128)}, f32[8,12]{0,1:T(8,128)S(1)}, u32[]{:S(2)}) copy-start(f32[8,12]{0,1:T(8,128)S(1)} %fusion.201) | copy-start | bytes 1156
  679.0 154.2 %copy-start.126 = (f32[8,12]{0,1:T(8,128)}, f32[8,12]{0,1:T(8,128)S(1)}, u32[]{:S(2)}) copy-start(f32[8,12]{0,1:T(8,128)S(1)} %fusion.193) | copy-start | bytes 1156
  684.7 224.1 %reduce-scatter.8.cloned.1.call-start = ((), (), s32[]{:S(2)}) async-start(), calls=%async_computation.9 | async-start | bytes 1622016 | tf_op jit(solution)/shard_map/reduce_scatter | solution.py:350
  814.1 411.1 %reduce-scatter.10.cloned.1.call-start = ((), (), s32[]{:S(2)}) async-start(), calls=%async_computation.10 | async-start | bytes 2949120 | tf_op jit(solution)/shard_map/reduce_scatter | solution.py:368
  931.2 13.2 copy-start.49
  931.2 13.2 copy-start.223
  1035.8 14.7 slice-start.6
  1050.5 12.7 copy-start.51
  1178.1 286.9 %reduce-scatter.12.cloned.1.call-start = ((), (), s32[]{:S(2)}) async-start(), calls=%async_computation.11 | async-start | bytes 17694720 | tf_op jit(solution)/shard_map/reduce_scatter | solution.py:363
  1201.1 505.3 %reduce-scatter.14.cloned.1.call-start = ((), (), s32[]{:S(2)}) async-start(), calls=%async_computation.12 | async-start | bytes 17694720 | tf_op jit(solution)/shard_map/reduce_scatter | solution.py:363
  1224.0 607.3 %all-reduce.11.cloned.1.call-start = ((), (), s32[]{:S(2)}) async-start(), calls=%async_computation.17 | async-start | bytes 15335424 | tf_op jit(solution)/shard_map/psum | solution.py:362
  1706.4 12.4 copy-start.18
  1706.4 12.4 copy-start.148
  1706.4 13.3 copy-start.237
  1706.4 13.3 copy-start.236
  1706.4 13.3 copy-start.161
  1706.4 13.4 copy-start.235
  1706.4 13.4 copy-start.234
  1706.4 13.4 copy-start.233
  1706.5 13.4 copy-start.232
  1706.5 13.5 copy-start.159
  1706.5 13.5 copy-start.160
  1706.5 13.6 copy-start.231
  1706.5 13.6 copy-start.230
  1706.5 13.6 copy-start.197
  1706.5 13.6 copy-start.196
  1706.5 13.6 copy-start.173
  1706.6 14.3 copy-start.171
  1706.6 255.6 %all-reduce.7.cloned.1.call-start = ((), (), s32[]{:S(2)}) async-start(), calls=%async_computation.13 | async-start | bytes 491520 | tf_op jit(solution)/shard_map/psum | solution.py:380
  1725.9 441.4 %all-reduce.9.cloned.1.call-start = ((), (), s32[]{:S(2)}) async-start(), calls=%async_computation.14 | async-start | bytes 9437184 | tf_op jit(solution)/shard_map/psum | solution.py:404
  1831.3 146.3 %copy-start.66 = (bf16[2,192,768]{2,1,0:T(8,128)(2,1)S(1)}, bf16[2,192,768]{2,1,0:T(8,128)(2,1)}, u32[]{:S(2)}) copy-start(bf16[2,192,768]{2,1,0:T(8,128)(2,1)} %get-tuple-element.78) | copy-start | bytes 1769476
  1998.0 306.1 %all-gather.14.cloned.1.call-start = ((), (), s32[]{:S(2)}) async-start(), calls=%async_computation.15 | async-start | bytes 13271040 | tf_op jit(solution)/shard_map/all_gather | solution.py:416
  2233.8 44.4 %copy-start.67 = (f32[79,768]{1,0:T(8,128)S(1)}, f32[79,768]{1,0:T(8,128)}, u32[]{:S(2)}) copy-start(f32[79,768]{1,0:T(8,128)} %all-reduce.7.cloned.1.call-done) | copy-start | bytes 728068
  2233.8 44.3 %copy-start.69 = (f32[79,768]{1,0:T(8,128)S(1)}, f32[79,768]{1,0:T(8,128)}, u32[]{:S(2)}) copy-start(f32[79,768]{1,0:T(8,128)} %param.21) | copy-start | bytes 728068
  2233.8 44.3 %copy-start.103 = (f32[79,768]{1,0:T(8,128)S(1)}, f32[79,768]{1,0:T(8,128)}, u32[]{:S(2)}) copy-start(f32[79,768]{1,0:T(8,128)} %param.23) | copy-start | bytes 728068
  2233.8 44.3 %copy-start.104 = (f32[79,768]{1,0:T(8,128)S(1)}, f32[79,768]{1,0:T(8,128)}, u32[]{:S(2)}) copy-start(f32[79,768]{1,0:T(8,128)} %param.22) | copy-start | bytes 728068
  2329.7 14.8 copy-start.1
  (225 other events, 1039.5 us)
Sparse Core Ops, SparseCore 0:
  43.7 20.0 reduce-scatter.5
  65.4 48.7 all-gather.7
  116.4 242.7 all-gather.9
  361.3 242.1 all-gather.11
  684.8 53.2 all-gather.15
  814.2 94.5 reduce-scatter.7
  1178.2 46.9 reduce-scatter.9
  1228.2 236.7 reduce-scatter.11
  1468.0 238.2 reduce-scatter.13
  1710.3 120.9 all-reduce.10
  1838.3 123.8 all-reduce.6
  1998.1 169.2 all-reduce.8
  2235.2 68.7 all-gather.13

commit v2 on v1

--- a/solution.py
+++ b/solution.py
@@ -5,6 +5,8 @@
 import jax.numpy as jnp
 import numpy as np
 from jax import lax
+from jax.experimental import pallas as pl
+from jax.experimental.pallas import tpu as pltpu
 from jax.sharding import PartitionSpec as P
 
 D = 768
@@ -18,6 +20,8 @@
 HD = 64
 
 
+MESH = pl.DeviceIdType.MESH
+VMEM_LIMIT = 56 * 1024 * 1024
 HIGH = lax.Precision.HIGHEST
 LOGIT_SCALE = 50.0
 CLIP_LIMIT = 0.005
@@ -92,8 +96,525 @@
     return pooled_of
 
 
-def fetch(blocks):
-    return lax.all_gather(rounded(blocks), "fsdp", axis=1, tiled=True)
+def flip(index, bit):
+    return index + bit - 2 * bit * lax.rem(index // bit, 2)
+
+
+def greet(peers):
+    barrier = pltpu.get_barrier_semaphore()
+    for peer in peers:
+        pl.semaphore_signal(barrier, inc=1, device_id=peer, device_id_type=MESH)
+    pl.semaphore_wait(barrier, len(peers))
+
+
+def places():
+    d = lax.axis_index("dp")
+    z = lax.axis_index("fsdp")
+    return (d, z, [lax.rem(z + step, 4) for step in range(4)])
+
+
+def fetch_kernel(chunks, sizes, weights, *refs):
+    outs = refs[: len(sizes)]
+    full, low, load_sem, store_sem, send, recv = refs[len(sizes) :]
+    d, z, zs = places()
+    sib, near_x, near_y = flip(d, 1), flip(d, 2), flip(d, 4)
+    diagonal = flip(near_x, 4)
+    starts = [sum(chunk[3] for chunk in chunks[:k]) for k in range(len(chunks))]
+    loads = []
+    for k, (source, _, _, n) in enumerate(chunks):
+        loads.append(
+            pltpu.make_async_copy(
+                weights.at[pl.ds(source, n)], full.at[pl.ds(starts[k], n)], load_sem.at[k]
+            )
+        )
+        loads[k].start()
+    greet([(d, zs[1]), (d, zs[2]), (d, zs[3]), (sib, z), (near_x, z), (near_y, z)])
+    pending = []
+
+    def push(k, slot, first, n, zz, dd, to, source=None):
+        out = outs[chunks[k][1]]
+        rows = pl.ds(chunks[k][2] + first, n)
+        copy = pltpu.make_async_remote_copy(
+            src_ref=out.at[rows, zz, dd] if source is None else source,
+            dst_ref=out.at[rows, zz, dd],
+            send_sem=send.at[k, slot],
+            recv_sem=recv.at[k, slot],
+            device_id=to,
+            device_id_type=MESH,
+        )
+        copy.start()
+        pending.append(copy)
+        return copy
+
+    along_z = []
+    stores = []
+    for k, (_, out, offset, n) in enumerate(chunks):
+        loads[k].wait()
+
+        @pl.loop(starts[k], starts[k] + n)
+        def _(i):
+            low[i] = full[i].astype(low.dtype)
+
+        along_z.append(
+            [
+                push(k, o - 1, 0, n, z, d, (d, zs[o]), low.at[pl.ds(starts[k], n), d])
+                for o in (1, 2, 3)
+            ]
+        )
+        stores.append(
+            pltpu.make_async_copy(
+                low.at[pl.ds(starts[k], n)],
+                outs[out].at[pl.ds(offset, n), z],
+                store_sem.at[k],
+            )
+        )
+        stores[k].start()
+    along_x, along_y, turn_y, turn_x, last = {}, {}, {}, {}, []
+    count = len(chunks)
+    for step in range(count + 2):
+        if step < count:
+            k, n = step, chunks[step][3]
+            along_x[k], along_y[k] = [], []
+            for o in (1, 2, 3):
+                zz = zs[4 - o]
+                along_z[k][o - 1].wait_recv()
+                along_x[k].append(push(k, 2 + o, 0, n, zz, d, (near_x, z)))
+                along_y[k].append(push(k, 5 + o, 0, n, zz, d, (near_y, z)))
+                last.append(push(k, 14 + o, 0, n, zz, d, (sib, z)))
+        if 1 <= step <= count:
+            k, n = step - 1, chunks[step - 1][3]
+            half = n // 2
+            turn_y[k], turn_x[k] = [], []
+            for o in (1, 2, 3):
+                zz = zs[4 - o]
+                along_x[k][o - 1].wait_recv()
+                if half:
+                    turn_y[k].append(push(k, 8 + o, 0, half, zz, near_x, (near_y, z)))
+                last.append(push(k, 17 + o, 0, n, zz, near_x, (sib, z)))
+                along_y[k][o - 1].wait_recv()
+                turn_x[k].append(push(k, 11 + o, half, n - half, zz, near_y, (near_x, z)))
+                last.append(push(k, 20 + o, 0, n, zz, near_y, (sib, z)))
+        if step >= 2:
+            k, n = step - 2, chunks[step - 2][3]
+            for o in (1, 2, 3):
+                for copies in (turn_y[k], turn_x[k]):
+                    if copies:
+                        copies[o - 1].wait_recv()
+                last.append(push(k, 23 + o, 0, n, zs[4 - o], diagonal, (sib, z)))
+    for copy in last:
+        copy.wait_recv()
+    for copy in pending:
+        copy.wait_send()
+    for copy in stores:
+        copy.wait()
+
+
+def fetch(weights, pieces, collective):
+    depth, eighths = lax.axis_size("fsdp"), lax.axis_size("dp")
+    if depth != 4 or eighths != 8:
+        return [
+            lax.all_gather(rounded(weights[a : a + n]), "fsdp", axis=1, tiled=True)
+            for a, n in pieces
+        ]
+    blocks, rows, width = weights.shape
+    part = (eighths, rows // eighths, width)
+    chunks = []
+    for out, (a, n) in enumerate(pieces):
+        for first in range(0, n, 2):
+            chunks.append((a + first, out, first, min(2, n - first)))
+    total = sum(n for _, n in pieces)
+    outs = pl.pallas_call(
+        functools.partial(fetch_kernel, chunks, [n for _, n in pieces]),
+        out_shape=[
+            jax.ShapeDtypeStruct((n, depth) + part, jnp.bfloat16) for _, n in pieces
+        ],
+        in_specs=[pl.BlockSpec(memory_space=pl.ANY)],
+        out_specs=[pl.BlockSpec(memory_space=pl.ANY)] * len(pieces),
+        scratch_shapes=[
+            pltpu.VMEM((total,) + part, jnp.float32),
+            pltpu.VMEM((total,) + part, jnp.bfloat16),
+            pltpu.SemaphoreType.DMA((len(chunks),)),
+            pltpu.SemaphoreType.DMA((len(chunks),)),
+            pltpu.SemaphoreType.DMA((len(chunks), 27)),
+            pltpu.SemaphoreType.DMA((len(chunks), 27)),
+        ],
+        compiler_params=pltpu.CompilerParams(
+            collective_id=collective, has_side_effects=True, vmem_limit_bytes=VMEM_LIMIT
+        ),
+        name=f"fetch_{collective}",
+    )(weights.reshape((blocks,) + part))
+    return [out.reshape(-1, width, width) for out in outs]
+
+
+def share_kernel(own, out, send, recv):
+    d, z, zs = places()
+    sib, near_x, near_y = flip(d, 1), flip(d, 2), flip(d, 4)
+    diagonal = flip(near_x, 4)
+    greet(
+        [(d, zs[1]), (d, zs[2]), (d, zs[3]), (sib, z), (near_x, z), (near_y, z), (diagonal, z)]
+    )
+    out[d, z] = own[...]
+
+    def push(slot, source, target, to):
+        copy = pltpu.make_async_remote_copy(
+            src_ref=source,
+            dst_ref=target,
+            send_sem=send.at[slot],
+            recv_sem=recv.at[slot],
+            device_id=to,
+            device_id_type=MESH,
+        )
+        copy.start()
+        return copy
+
+    first = [push(o - 1, own, out.at[d, z], (d, zs[o])) for o in (1, 2, 3)]
+    for copy in first:
+        copy.wait_recv()
+    second = [
+        push(3 + i, out.at[d], out.at[d], (to, z)) for i, to in enumerate((near_x, near_y, diagonal))
+    ]
+    last = [push(6, out.at[d], out.at[d], (sib, z))]
+    for i, origin in enumerate((near_x, near_y, diagonal)):
+        second[i].wait_recv()
+        last.append(push(7 + i, out.at[origin], out.at[origin], (sib, z)))
+    for copy in last:
+        copy.wait_recv()
+    for copy in first + second + last:
+        copy.wait_send()
+
+
+def share(own, collective):
+    lanes, depth = lax.axis_size("dp"), lax.axis_size("fsdp")
+    if depth != 4 or lanes != 8:
+        return lax.all_gather(own, ("dp", "fsdp"), axis=0).reshape((lanes, depth) + own.shape)
+    return pl.pallas_call(
+        share_kernel,
+        out_shape=jax.ShapeDtypeStruct((lanes, depth) + own.shape, own.dtype),
+        in_specs=[pl.BlockSpec(memory_space=pltpu.VMEM)],
+        out_specs=pl.BlockSpec(memory_space=pltpu.VMEM),
+        scratch_shapes=[pltpu.SemaphoreType.DMA((10,)), pltpu.SemaphoreType.DMA((10,))],
+        compiler_params=pltpu.CompilerParams(collective_id=collective, has_side_effects=True),
+        name=f"share_{collective}",
+    )(own)
+
+
+def swap_kernel(parts, out, send, recv):
+    d, z, zs = places()
+    greet([(d, zs[1]), (d, zs[2]), (d, zs[3])])
+    out[z] = parts[z]
+    copies = []
+    for o in (1, 2, 3):
+        copies.append(
+            pltpu.make_async_remote_copy(
+                src_ref=parts.at[zs[o]],
+                dst_ref=out.at[z],
+                send_sem=send.at[o - 1],
+                recv_sem=recv.at[o - 1],
+                device_id=(d, zs[o]),
+                device_id_type=MESH,
+            )
+        )
+        copies[-1].start()
+    for copy in copies:
+        copy.wait()
+
+
+def swap(parts, collective):
+    depth = lax.axis_size("fsdp")
+    if depth != 4 or lax.axis_size("dp") != 8:
+        return lax.all_to_all(parts, "fsdp", 0, 0)
+    return pl.pallas_call(
+        swap_kernel,
+        out_shape=jax.ShapeDtypeStruct(parts.shape, parts.dtype),
+        in_specs=[pl.BlockSpec(memory_space=pltpu.VMEM)],
+        out_specs=pl.BlockSpec(memory_space=pltpu.VMEM),
+        scratch_shapes=[pltpu.SemaphoreType.DMA((3,)), pltpu.SemaphoreType.DMA((3,))],
+        compiler_params=pltpu.CompilerParams(collective_id=collective, has_side_effects=True),
+        name=f"swap_{collective}",
+    )(parts)
+
+
+class Reduction:
+    def __init__(self, source, start, first, n, buffers, k, semaphores, spots):
+        self.source, self.start, self.first, self.n, self.k = (source, start, first, n, k)
+        self.held, self.from_core, self.from_near, self.from_turn, self.ready, self.from_z = buffers
+        self.local_sem, self.send, self.recv = semaphores
+        self.spots = spots
+        self.rows = pl.ds(first, n)
+        self.started = []
+
+    def push(self, slot, source, target, to):
+        copy = pltpu.make_async_remote_copy(
+            src_ref=source,
+            dst_ref=target,
+            send_sem=self.send.at[self.k, slot],
+            recv_sem=self.recv.at[self.k, slot],
+            device_id=to,
+            device_id_type=MESH,
+        )
+        copy.start()
+        self.started.append(copy)
+        return copy
+
+    def begin(self):
+        d, z, zs, x, y, c = self.spots
+        blocks = pl.ds(self.start, self.n)
+        self.local = pltpu.make_async_copy(
+            self.source.at[blocks, :, :, :, c], self.held.at[self.rows], self.local_sem.at[self.k]
+        )
+        self.local.start()
+        self.core = self.push(
+            0,
+            self.source.at[blocks, :, :, :, 1 - c],
+            self.from_core.at[self.rows],
+            (flip(d, 1), z),
+        )
+
+    def add(self, count, place):
+        @pl.loop(0, self.n * count)
+        def _(i):
+            target, other = place(self.first + i // count, lax.rem(i, count))
+            total = self.held[target].astype(jnp.float32) + other.astype(jnp.float32)
+            self.held[target] = total.astype(self.held.dtype)
+
+    def across_plane(self):
+        d, z, zs, x, y, c = self.spots
+        self.local.wait()
+        self.core.wait_recv()
+
+        def place(b, i):
+            target = (b, i // 4, lax.rem(i // 2, 2), lax.rem(i, 2))
+            return (target, self.from_core[target])
+
+        self.add(16, place)
+        self.near = [
+            self.push(
+                1,
+                self.held.at[self.rows, 0:2, :, 1 - x],
+                self.from_near.at[self.rows, 0:2],
+                (flip(d, 2), z),
+            ),
+            self.push(
+                2,
+                self.held.at[self.rows, 2:4, 1 - y],
+                self.from_near.at[self.rows, 2:4],
+                (flip(d, 4), z),
+            ),
+        ]
+
+    def turn(self):
+        d, z, zs, x, y, c = self.spots
+
+        def place_a(b, i):
+            return ((b, i // 2, lax.rem(i, 2), x), self.from_near[b, i // 2, lax.rem(i, 2)])
+
+        def place_b(b, i):
+            return ((b, 2 + i // 2, y, lax.rem(i, 2)), self.from_near[b, 2 + i // 2, lax.rem(i, 2)])
+
+        self.near[0].wait_recv()
+        self.add(4, place_a)
+        a = self.push(
+            3,
+            self.held.at[self.rows, 0:2, 1 - y, x],
+            self.from_turn.at[self.rows, 0:2],
+            (flip(d, 4), z),
+        )
+        self.near[1].wait_recv()
+        self.add(4, place_b)
+        b = self.push(
+            4,
+            self.held.at[self.rows, 2:4, y, 1 - x],
+            self.from_turn.at[self.rows, 2:4],
+            (flip(d, 2), z),
+        )
+        self.turned = [a, b]
+
+    def along_z(self):
+        d, z, zs, x, y, c = self.spots
+        for copy in self.turned:
+            copy.wait_recv()
+
+        @pl.loop(0, self.n * 4)
+        def _(i):
+            b, zz = (self.first + i // 4, lax.rem(i, 4))
+            total = self.held[b, zz, y, x].astype(jnp.float32) + self.from_turn[b, zz].astype(
+                jnp.float32
+            )
+            self.ready[b, zz] = total.astype(self.ready.dtype)
+
+        self.spread = [
+            self.push(
+                4 + o,
+                self.ready.at[self.rows, zs[o]],
+                self.from_z.at[self.rows, o - 1],
+                (d, zs[o]),
+            )
+            for o in (1, 2, 3)
+        ]
+
+    def finish(self, out):
+        d, z, zs, x, y, c = self.spots
+        for copy in self.spread:
+            copy.wait_recv()
+
+        @pl.loop(self.first, self.first + self.n)
+        def _(b):
+            total = self.held[b, z, y, x].astype(jnp.float32) + self.from_turn[b, z].astype(
+                jnp.float32
+            )
+            for o in range(3):
+                total = total + self.from_z[b, o].astype(jnp.float32)
+            out[b] = total
+
+        for copy in self.started:
+            copy.wait_send()
+
+
+def reduce_kernel(chunks, sources, sets, *refs):
+    ins = refs[:sources]
+    outs = refs[sources : sources + sets]
+    buffers = [refs[sources + sets + 6 * i : sources + sets + 6 * i + 6] for i in range(sets)]
+    semaphores = refs[sources + 7 * sets :]
+    d, z, zs = places()
+    spots = (d, z, zs, lax.rem(d // 2, 2), d // 4, lax.rem(d, 2))
+    greet([(d, zs[1]), (d, zs[2]), (d, zs[3]), (flip(d, 1), z), (flip(d, 2), z), (flip(d, 4), z)])
+    work = []
+    for k, (source, start, first, n, which) in enumerate(chunks):
+        work.append(
+            Reduction(ins[source], start, first, n, buffers[which], k, semaphores, spots)
+        )
+        work[k].begin()
+    count = len(chunks)
+    for step in range(count + 3):
+        if step < count:
+            work[step].across_plane()
+        if 1 <= step <= count:
+            work[step - 1].turn()
+        if 2 <= step <= count + 1:
+            work[step - 2].along_z()
+        if step >= 3:
+            work[step - 3].finish(outs[chunks[step - 3][4]])
+
+
+def reduce_grads(grads, small, collective):
+    lanes, depth = lax.axis_size("dp"), lax.axis_size("fsdp")
+    rows = D // (lanes * depth)
+    tail = (depth, 2, 2, 2)
+    sources = [grad.reshape((-1,) + tail + (rows, D)) for grad in grads]
+    chunks = []
+    first = 0
+    for i, source in enumerate(sources):
+        for start in range(0, source.shape[0], 2):
+            n = min(2, source.shape[0] - start)
+            chunks.append((i, start, first, n, 0))
+            first += n
+    sets = [(first, (rows, D), jnp.bfloat16)]
+    if small is not None:
+        sources.append(small.reshape((1,) + tail + small.shape[1:]))
+        chunks.insert(1, (len(sources) - 1, 0, 0, 1, 1))
+        sets.append((1, small.shape[1:], jnp.float32))
+    scratch = []
+    for n, shape, kind in sets:
+        scratch += [
+            pltpu.VMEM((n, depth, 2, 2) + shape, kind),
+            pltpu.VMEM((n, depth, 2, 2) + shape, kind),
+            pltpu.VMEM((n, depth, 2) + shape, kind),
+            pltpu.VMEM((n, depth) + shape, kind),
+            pltpu.VMEM((n, depth) + shape, kind),
+            pltpu.VMEM((n, 3) + shape, kind),
+        ]
+    outs = pl.pallas_call(
+        functools.partial(reduce_kernel, chunks, len(sources), len(sets)),
+        out_shape=[jax.ShapeDtypeStruct((n,) + shape, jnp.float32) for n, shape, _ in sets],
+        in_specs=[pl.BlockSpec(memory_space=pl.ANY)] * len(sources),
+        out_specs=[pl.BlockSpec(memory_space=pltpu.VMEM)] * len(sets),
+        scratch_shapes=scratch
+        + [
+            pltpu.SemaphoreType.DMA((len(chunks),)),
+            pltpu.SemaphoreType.DMA((len(chunks), 8)),
+            pltpu.SemaphoreType.DMA((len(chunks), 8)),
+        ],
+        compiler_params=pltpu.CompilerParams(
+            collective_id=collective, has_side_effects=True, vmem_limit_bytes=VMEM_LIMIT
+        ),
+        name=f"reduce_{collective}",
+    )(*sources)
+    return (outs[0], outs[1] if small is not None else None)
+
+
+def spread_kernel(own, out, local_sem, send, recv):
+    d, z, _ = places()
+    sib, near_x, near_y = flip(d, 1), flip(d, 2), flip(d, 4)
+    diagonal = flip(near_x, 4)
+    greet([(sib, z), (near_x, z), (near_y, z)])
+    half = own.shape[0] // 2
+    first, second = (pl.ds(0, half), pl.ds(half, own.shape[0] - half))
+    started = []
+
+    def push(slot, origin, part, to, source=None):
+        copy = pltpu.make_async_remote_copy(
+            src_ref=out.at[part, origin] if source is None else source,
+            dst_ref=out.at[part, origin],
+            send_sem=send.at[slot],
+            recv_sem=recv.at[slot],
+            device_id=to,
+            device_id_type=MESH,
+        )
+        copy.start()
+        started.append(copy)
+        return copy
+
+    near = []
+    for i, part in enumerate((first, second)):
+        near.append(
+            [
+                push(2 * i, d, part, (near_x, z), own.at[part]),
+                push(2 * i + 1, d, part, (near_y, z), own.at[part]),
+            ]
+        )
+    keep = pltpu.make_async_copy(own, out.at[:, d], local_sem)
+    keep.start()
+    last = [push(4 + i, d, part, (sib, z), own.at[part]) for i, part in enumerate((first, second))]
+    near[0][0].wait_recv()
+    turn_y = push(6, near_x, first, (near_y, z))
+    last.append(push(7, near_x, first, (sib, z)))
+    near[1][1].wait_recv()
+    turn_x = push(8, near_y, second, (near_x, z))
+    last.append(push(9, near_y, second, (sib, z)))
+    near[0][1].wait_recv()
+    last.append(push(10, near_y, first, (sib, z)))
+    near[1][0].wait_recv()
+    last.append(push(11, near_x, second, (sib, z)))
+    turn_y.wait_recv()
+    last.append(push(12, diagonal, first, (sib, z)))
+    turn_x.wait_recv()
+    last.append(push(13, diagonal, second, (sib, z)))
+    for copy in last:
+        copy.wait_recv()
+    for copy in started:
+        copy.wait_send()
+    keep.wait()
+
+
+def spread(own, collective):
+    lanes = lax.axis_size("dp")
+    if lax.axis_size("fsdp") != 4 or lanes != 8:
+        return lax.all_gather(own, "dp", axis=1)
+    return pl.pallas_call(
+        spread_kernel,
+        out_shape=jax.ShapeDtypeStruct(own.shape[:1] + (lanes,) + own.shape[1:], own.dtype),
+        in_specs=[pl.BlockSpec(memory_space=pltpu.VMEM)],
+        out_specs=pl.BlockSpec(memory_space=pl.ANY),
+        scratch_shapes=[
+            pltpu.SemaphoreType.DMA,
+            pltpu.SemaphoreType.DMA((14,)),
+            pltpu.SemaphoreType.DMA((14,)),
+        ],
+        compiler_params=pltpu.CompilerParams(
+            collective_id=collective, has_side_effects=True, vmem_limit_bytes=VMEM_LIMIT
+        ),
+        name=f"spread_{collective}",
+    )(own)
 
 
 def masked_scores(query_low, key_low, same):
@@ -104,7 +625,7 @@
 def layer_forward(state, blocks, gains, same):
     heads_in, norm_one = jax.vjp(layer_norm, state, gains[0], gains[1])
     heads_low = rounded(heads_in)
-    mixed = product(heads_low, blocks[0:3].reshape(3 * D, D), "sd,rd->sr")
+    mixed = product(heads_low, blocks[0].reshape(3 * D, D), "sd,rd->sr")
     (query, key), norms_back = jax.vjp(
         both_norms, mixed[:, :D], mixed[:, D : 2 * D], gains[4], gains[5]
     )
@@ -115,14 +636,14 @@
     top = jax.scipy.special.logsumexp(scores, axis=-1, keepdims=True)
     weights_low = rounded(jnp.exp(scores - top))
     attended_low = rounded(product(weights_low, value_low, "bhst,bthd->bshd").reshape(-1, D))
-    state = state + product(attended_low, blocks[3], "sr,rd->sd")
+    state = state + product(attended_low, blocks[1].reshape(D, D), "sr,rd->sd")
     normed, norm_two = jax.vjp(layer_norm, state, gains[2], gains[3])
     normed_low = rounded(normed)
     hidden, gelu_back = jax.vjp(
-        jax.nn.gelu, product(normed_low, blocks[4:8].reshape(FF, D), "sd,rd->sr")
+        jax.nn.gelu, product(normed_low, blocks[2].reshape(FF, D), "sd,rd->sr")
     )
     hidden_low = rounded(hidden)
-    state = state + product(hidden_low, blocks[8:12].reshape(FF, D), "sr,rd->sd")
+    state = state + product(hidden_low, blocks[3].reshape(FF, D), "sr,rd->sd")
     kept = (
         norm_one,
         heads_low,
@@ -155,8 +676,8 @@
         gelu_back,
         hidden_low,
     ) = kept
-    down = blocks[8:12].reshape(FF, D)
-    upward = blocks[4:8].reshape(FF, D)
+    down = blocks[3].reshape(FF, D)
+    upward = blocks[2].reshape(FF, D)
     grad_low = rounded(grad)
     grad_down = rounded(product(hidden_low, grad_low, "sr,sd->rd"))
     (grad_hidden,) = gelu_back(product(grad_low, down, "sd,rd->sr"))
@@ -166,7 +687,7 @@
     grad = grad + inner
     grad_low = rounded(grad)
     grad_out = rounded(product(attended_low, grad_low, "sr,sd->rd"))
-    attended_grad = rounded(product(grad_low, blocks[3], "sd,rd->sr")).reshape(MB, -1, HEADS, HD)
+    attended_grad = rounded(product(grad_low, blocks[1].reshape(D, D), "sd,rd->sr")).reshape(MB, -1, HEADS, HD)
     weights = jnp.exp(masked_scores(query_low, key_low, same) - top)
     weights_low = rounded(weights)
     value_grad = product(weights_low, attended_grad, "bhst,bshd->bthd")
@@ -179,33 +700,22 @@
     mixed_low = rounded(jnp.concatenate([query_in, key_in, value_grad.reshape(-1, D)], 1))
     grad_mixed = rounded(product(mixed_low, heads_low, "sr,sd->rd"))
     inner, gain_one, shift_one = norm_one(
-        product(mixed_low, blocks[0:3].reshape(3 * D, D), "sr,rd->sd")
+        product(mixed_low, blocks[0].reshape(3 * D, D), "sr,rd->sd")
     )
     grad = grad + inner
-    block_grads = jnp.concatenate(
-        [
-            grad_mixed.reshape(3, D, D),
-            grad_out[None],
-            grad_up.reshape(4, D, D),
-            grad_down.reshape(4, D, D),
-        ],
-        0,
-    )
+    block_grads = [grad_mixed, grad_out, grad_up, grad_down]
     gain_grads = jnp.stack([gain_one, shift_one, gain_two, shift_two, gain_query, gain_key])
     return (grad, block_grads, gain_grads)
 
 
-def contrast_rows(scores, alive, own_live, offset):
+def contrast_rows(scores, alive, own_live, rows):
     masked = jnp.where(alive[None, :] > 0, scores, -1e30)
     top = jax.scipy.special.logsumexp(masked, axis=1, keepdims=True)
     share = jnp.exp(masked - top)
     columns = jnp.arange(scores.shape[1], dtype=jnp.int32)
-    target = (
-        columns[None, :] == offset + jnp.arange(scores.shape[0], dtype=jnp.int32)[:, None]
-    ).astype(jnp.float32)
+    target = (columns[None, :] == rows[:, None]).astype(jnp.float32)
     diagonal = jnp.sum(scores * target, 1)
-    term = jnp.sum((top[:, 0] - diagonal) * own_live)
-    return (term, (share - target) * own_live[:, None])
+    return ((top[:, 0] - diagonal) * own_live, (share - target) * own_live[:, None])
 
 
 def muon_groups():
@@ -277,43 +787,45 @@
     lanes = lax.axis_size("dp")
     slots = jnp.arange(IMGS, dtype=jnp.int32)
     live = jnp.any(segments[:, 0, None, :] == slots[None, :, None], -1).astype(jnp.float32)
-    count = lax.psum(jnp.sum(live), ("dp", "fsdp"))
-    factor = 1.0 / (2.0 * count)
-    group_ids = lax.all_gather(text_ids, "fsdp", axis=1, tiled=True)
-    flat_ids = jnp.transpose(group_ids, (1, 0, 2, 3)).reshape(-1, group_ids.shape[3])
+    depth = lax.axis_size("fsdp")
+    captions = MB * IMGS
+    ids = jnp.broadcast_to(text_ids.reshape(1, captions, -1), (depth, captions, text_ids.shape[3]))
+    ids = swap(ids, 10)
+    stem, *first_blocks = fetch(weights, [(0, 1), (2, 3), (5, 1), (6, 4), (10, 4)], 1)
+    flat_ids = ids.reshape(depth * captions, -1)
     share_rows = table.shape[0]
-    first_row = lax.axis_index("fsdp") * share_rows
-    picked = flat_ids - first_row
+    picked = flat_ids - lax.axis_index("fsdp") * share_rows
     hits = jnp.sum(
         (picked[:, :, None] == jnp.arange(share_rows, dtype=jnp.int32)[None, None, :]).astype(
             jnp.int32
         ),
         1,
     )
-    text_sum = lax.psum_scatter(
-        jnp.dot(
-            rounded(hits.astype(jnp.float32)), table, preferred_element_type=jnp.float32
-        ).astype(jnp.bfloat16),
-        "fsdp",
-        scatter_dimension=0,
-        tiled=True,
-    ).astype(jnp.float32)
-    text_low = rounded(unit_rows(text_sum / text_ids.shape[-1])).reshape(MB, IMGS, -1)
+    parts = jnp.dot(rounded(hits.astype(jnp.float32)), table, preferred_element_type=jnp.float32)
+    text_sum = jnp.sum(swap(parts.reshape(depth, captions, D), 11), 0)
+    text_low = rounded(unit_rows(text_sum / text_ids.shape[-1]))
     me = lax.axis_index(("dp", "fsdp"))
-    rows_local = weights.shape[1]
     segment = segments[:, 0]
     same = segment[:, :, None] == segment[:, None, :]
     rows_hot, cols_hot = jax.vmap(positions)(grid[:, 0])
     rows_hot = rows_hot.reshape(-1, POS)
     cols_hot = cols_hot.reshape(-1, POS)
     patch_low = patches.reshape(-1, D)
-    stem = fetch(weights[0:2])
     state = product(patch_low, stem[0], "sd,rd->sr")
     state = state + jnp.dot(rows_hot, gains[base : base + POS], precision=HIGH)
     state = state + jnp.dot(cols_hot, gains[base + POS : base + 2 * POS], precision=HIGH)
     saved = []
     for index in range(LAYERS):
-        blocks = fetch(weights[2 + 12 * index : 14 + 12 * index])
+        if index == 0:
+            blocks = first_blocks
+        else:
+            start = 2 + 12 * index
+            pieces = [(start, 3), (start + 3, 1), (start + 4, 4), (start + 8, 4)]
+            if index == 1:
+                pieces = pieces + [(1, 1)]
+            blocks = fetch(weights, pieces, 2 + index)
+            if index == 1:
+                pooling_matrix = blocks.pop()[0]
         state, kept = layer_forward(state, blocks, gains[6 * index : 6 * index + 6], same)
         saved.append((kept, blocks))
     final, norm_final = jax.vjp(layer_norm, state, gains[fin], gains[fin + 1])
@@ -324,52 +836,56 @@
 
     pooled, pool_back = jax.vjp(pool_all, final, gains[fin + 2])
     pooled_low = rounded(pooled)
-    embedded, unit_back = jax.vjp(unit_rows, product(pooled_low, stem[1], "kr,rd->kd"))
+    embedded, unit_back = jax.vjp(unit_rows, product(pooled_low, pooling_matrix, "kr,rd->kd"))
     image_low = rounded(embedded)
-    both = jnp.concatenate([image_low, text_low.reshape(MB * IMGS, D)], 0)
-    whole = lax.all_gather(both, ("dp", "fsdp"), axis=0)
-    alive = lax.all_gather(rounded(live), ("dp", "fsdp"), axis=1, tiled=True).astype(jnp.float32)
+    flags = jnp.broadcast_to(live.reshape(1, captions, 1), (1, captions, D)).astype(jnp.bfloat16)
+    both = jnp.concatenate([image_low[None], text_low[None], flags], 0).reshape(3 * captions, D)
+    whole = share(both, 8).reshape(-1, 3, MB, IMGS, D)
+    flags = whole[:, 2, :, :, 0].astype(jnp.float32)
+    count = jnp.sum(flags)
+    factor = 1.0 / (2.0 * count)
     loss_part = jnp.float32(0.0)
     image_grads = []
-    spreads = []
     for part in range(MB):
-        images = whole[:, part * IMGS : (part + 1) * IMGS].reshape(-1, D)
-        texts = whole[:, (MB + part) * IMGS : (MB + part + 1) * IMGS].reshape(-1, D)
+        images = whole[:, 0, part].reshape(-1, D)
+        texts = whole[:, 1, part].reshape(-1, D)
+        alive = flags[:, part].reshape(-1)
         own_image = image_low[part * IMGS : (part + 1) * IMGS]
-        own_text = text_low[part]
         forward = LOGIT_SCALE * product(own_image, texts, "kd,nd->kn")
-        backward = LOGIT_SCALE * product(own_text, images, "kd,nd->kn")
-        term_f, grad_f = contrast_rows(forward, alive[part], live[part], me * IMGS)
-        term_b, grad_b = contrast_rows(backward, alive[part], live[part], me * IMGS)
-        loss_part = loss_part + (term_f + term_b) * factor
+        backward = LOGIT_SCALE * product(texts, images, "kd,nd->kn")
+        own = me * IMGS + jnp.arange(IMGS, dtype=jnp.int32)
+        everyone = jnp.arange(alive.shape[0], dtype=jnp.int32)
+        term_f, grad_f = contrast_rows(forward, alive, live[part], own)
+        term_b, grad_b = contrast_rows(backward, alive, alive, everyone)
+        own_terms = jnp.sum(jnp.where((everyone // IMGS) == me, term_b, 0.0))
+        loss_part = loss_part + (jnp.sum(term_f) + own_terms) * factor
         forward_low = rounded(grad_f * factor * LOGIT_SCALE)
-        backward_low = rounded(grad_b * factor * LOGIT_SCALE)
-        spreads.append(product(backward_low, own_text, "kn,kd->nd"))
-        image_grads.append(product(forward_low, texts, "kn,nd->kd"))
-    spread = jnp.stack([value.reshape(-1, IMGS, D) for value in spreads], 1)
-    text_side = lax.psum_scatter(spread, ("dp", "fsdp"), scatter_dimension=0)
-    image_grad = jnp.concatenate(image_grads, 0) + text_side.reshape(MB * IMGS, D)
+        backward_low = rounded(
+            lax.dynamic_slice_in_dim(grad_b, me * IMGS, IMGS, 1) * factor * LOGIT_SCALE
+        )
+        image_grads.append(
+            product(forward_low, texts, "kn,nd->kd") + product(backward_low, texts, "nk,nd->kd")
+        )
+    image_grad = jnp.concatenate(image_grads, 0)
     (embed_grad,) = unit_back(image_grad)
     embed_low = rounded(embed_grad)
     grad_pool = rounded(product(pooled_low, embed_low, "kr,kd->rd"))
-    final_grad, query_grad = pool_back(product(embed_low, stem[1], "kd,rd->kr"))
+    final_grad, query_grad = pool_back(product(embed_low, pooling_matrix, "kd,rd->kr"))
     grad, gain_final, shift_final = norm_final(final_grad)
     gain_parts = [None] * LAYERS
-    shards = [None] * (LAYERS + 1)
+    block_grads = [None] * LAYERS
+    fast = depth == 4 and lanes == 8
+    slices = [None] * LAYERS
     for index in reversed(range(LAYERS)):
         kept, blocks = saved[index]
-        grad, block_grads, gain_parts[index] = layer_backward(grad, kept, blocks, same)
-        shards[index + 1] = lax.psum(
-            lax.psum_scatter(block_grads, "fsdp", scatter_dimension=1, tiled=True), "dp"
-        )
+        grad, block_grads[index], gain_parts[index] = layer_backward(grad, kept, blocks, same)
+        if index == 1:
+            block_grads[index].append(grad_pool)
+        if fast and index > 0:
+            slices[index], _ = reduce_grads(block_grads[index], None, 4 + index)
     grad_low = rounded(grad)
     grad_patch = rounded(product(grad_low, patch_low, "sr,sd->rd"))
-    shards[0] = lax.psum(
-        lax.psum_scatter(
-            jnp.stack([grad_patch, grad_pool]), "fsdp", scatter_dimension=1, tiled=True
-        ),
-        "dp",
-    )
+    block_grads[0].append(grad_patch)
     grad_rows = jnp.dot(rows_hot.T, grad, precision=HIGH)
     grad_cols = jnp.dot(cols_hot.T, grad, precision=HIGH)
     gains_grad = jnp.concatenate(
@@ -377,9 +893,33 @@
         + [jnp.stack([gain_final, shift_final, query_grad]), grad_rows, grad_cols],
         0,
     )
-    gains_grad, loss = lax.psum((gains_grad, loss_part), ("dp", "fsdp"))
-    shard_grads = jnp.concatenate(shards, 0).astype(jnp.float32)
-    squares = lax.psum(jnp.sum(shard_grads * shard_grads), "fsdp")
+    if fast:
+        width = 256
+        small = jnp.concatenate([gains_grad.reshape(-1), loss_part[None]])
+        small = jnp.pad(small, (0, lanes * depth * 8 * width - small.shape[0]))
+        slices[0], small = reduce_grads(
+            block_grads[0], small.reshape(lanes * depth, 8, width), 4
+        )
+        slices = jnp.concatenate(
+            [slices[0][12:], slices[1][12:]] + [values[:12] for values in slices], 0
+        )
+        squares = jnp.broadcast_to(jnp.sum(slices * slices), (8, width))
+        shared = share(jnp.concatenate([small[0], squares], 0), 9)
+        flat = jnp.transpose(shared[:, :, :8], (1, 0, 2, 3)).reshape(-1)
+        gains_grad, loss = (flat[: gains.size].reshape(gains.shape), flat[gains.size])
+        squares = jnp.sum(shared[:, :, 8, 0])
+        shard_grads = spread(rounded(slices), 12).reshape(weights.shape).astype(jnp.float32)
+    else:
+        stack = jnp.concatenate(
+            [block_grads[index].pop().reshape(1, D, D) for index in range(LAYERS)]
+            + [value.reshape(-1, D, D) for values in block_grads for value in values],
+            0,
+        )
+        shard_grads = lax.psum(
+            lax.psum_scatter(stack, "fsdp", scatter_dimension=1, tiled=True), "dp"
+        ).astype(jnp.float32)
+        gains_grad, loss = lax.psum((gains_grad, loss_part), ("dp", "fsdp"))
+        squares = lax.psum(jnp.sum(shard_grads * shard_grads), "fsdp")
     norm = jnp.sqrt(squares + jnp.sum(gains_grad * gains_grad))
     clip = jnp.minimum(1.0, CLIP_LIMIT / (norm + 1e-06))
     momenta_new = MOMENT * momenta + clip * shard_grads

time: 2370 us -> 1330 us (0.56)
  waiting for transfers between devices: 1460 us -> 237 us
  Pallas kernels: 0 us -> 405 us
  blocking collectives: 174 us -> 0 us
  local copies, waits for them, and re-layouts: 253 us -> 203 us
    reduce_scatter x5 -> x0, waiting for transfers between devices: 555 us -> none  [the longest x2 481 us: per_device(): lax.psum_scatter(block_grads, 'fsdp', scatter_dimension=1, tiled=True)]
    all_gather x4 -> x0, waiting for transfers between devices: 479 us -> none  [the longest x3 479 us: fetch(): return lax.all_gather(rounded(blocks), 'fsdp', axis=1, tiled=True)]
    pallas_call x0 -> x9, Pallas kernels: none -> 405 us  [the longest x2 168 us: reduce_grads(): pl.pallas_call(functools.partial(reduce_kernel, chunks, len(sources), len...]
    psum x2 -> x0, waiting for transfers between devices: 230 us -> none  [the longest x1 124 us: per_device(): gains_grad, loss = lax.psum((gains_grad, loss_part), ('dp', 'fsdp'))]
    psum x3 -> x0, blocking collectives: 90.9 us -> none  [the longest x1 39.7 us: per_device(): gains_grad, loss = lax.psum((gains_grad, loss_part), ('dp', 'fsdp'))]
    all_gather x2 -> x0, blocking collectives: 83.6 us -> none  [the longest x1 68.5 us: per_device(): lax.all_gather(rounded(live), ('dp', 'fsdp'), axis=1, tiled=True)]
    all_gather x1, waiting for transfers between devices: 24.3 us -> 65 us  [per_device(): spread_rows = lax.all_gather(rounded(turned), 'dp', axis=0)]
    unnamed x595 -> x615, local copies, waits for them, and re-layouts: 55.5 us -> 52 us
  transfers between devices with their start and end apart: 13 -> 2, of which waited for: 11 -> 2; matrix products, arithmetic and copies ran while one was open for 7% -> 0% of each run, Pallas kernels for 0% -> 0%
where the time goes in v2:
time: 1330 us; the launch traced here: 1320 us
  Pallas kernels  405 us (30%)
  matrix products  297 us (22%)
  waiting for transfers between devices  237 us (18%)
  local copies, waits for them, and re-layouts  203 us (15%)
  other arithmetic  140 us (11%)
  between operations  36.3 us (3%)
    dot_general x53, matrix products, product(): return jnp.einsum(form, left, right, preferred_element_type=jnp.float32)  225 us
    psum x1, waiting for transfers between devices, per_device(): grams = lax.psum(grams, 'fsdp')  172 us
    pallas_call x2, Pallas kernels, reduce_grads(): pl.pallas_call(functools.partial(reduce_kernel, chunks, len(sources), len...  168 us
    pallas_call x2, Pallas kernels, fetch(): pl.pallas_call(functools.partial(fetch_kernel, chunks, [n for _, n in pie...  144 us
    all_gather x1, waiting for transfers between devices, per_device(): spread_rows = lax.all_gather(rounded(turned), 'dp', axis=0)  65 us
    unnamed x615, local copies, waits for them, and re-layouts  52 us
    pallas_call x1, Pallas kernels, spread(): pl.pallas_call(spread_kernel, out_shape=jax.ShapeDtypeStruct(own.shape[:1...  39.2 us
    pallas_call x2, Pallas kernels, share(): pl.pallas_call(share_kernel, out_shape=jax.ShapeDtypeStruct((lanes, depth...  36.5 us
  transfers between devices with their start and end apart: 2, of which 2 were waited for; matrix products, arithmetic and copies ran while one was open for 0% of the time, Pallas kernels for 0%

profile of v2, /device:TPU:0, one launch (start us, length us, event | category | flops | bytes accessed | tf_op | source)
XLA Modules:
  0.0 1319.1 jit_solution(6476480309114386026)
XLA Ops:
  9.7 72.9 %fetch_1.1 = (bf16[1,4,8,24,768]{4,3,2,1,0:T(8,128)(2,1)}, bf16[3,4,8,24,768]{4,3,2,1,0:T(8,128)(2,1)}, bf16[1,4,8,24,768]{4,3,2,1,0:T(8,128)(2,1)}, bf16[4,4,8,...) custom-call(f32[26,8,24,768]{3,2,1,0:T(8,128)} %bitcast.545), custom_call_target="tpu_custom_call" | custom-call | tf_op jit(solution)/shard_map/fetch_1/pallas_call | solution.py:226
  99.3 3.1 reshape.1216
  106.0 71.3 %fetch_3.1 = (bf16[3,4,8,24,768]{4,3,2,1,0:T(8,128)(2,1)}, bf16[1,4,8,24,768]{4,3,2,1,0:T(8,128)(2,1)}, bf16[4,4,8,24,768]{4,3,2,1,0:T(8,128)(2,1)}, bf16[4,4,8,...) custom-call(f32[26,8,24,768]{3,2,1,0:T(8,128)} %bitcast.546), custom_call_target="tpu_custom_call" | custom-call | tf_op jit(solution)/shard_map/fetch_3/pallas_call | solution.py:226
  178.9 3.1 fusion.18
  185.3 4.6 fusion.61
  193.0 5.9 fusion.394
  199.0 3.9 fusion.415
  213.8 3.0 copy.281
  216.9 3.2 reshape.1224
  229.0 3.5 fusion.19
  239.5 4.3 fusion.62
  246.9 5.5 fusion.396
  252.5 3.9 fusion.417
  272.7 8.5 swap_10.1
  282.0 13.2 %convert_reduce_fusion = s32[64,8000]{1,0:T(8,128)} fusion(s32[64,16]{1,0:T(8,128)S(1)} %bitcast.650), kind=kLoop, calls=%fused_computation.2 | loop fusion | flops 24064000 | bytes 2052096 | tf_op jit(solution)/shard_map/reduce_sum | solution.py:798
  295.2 7.7 fusion.106
  302.9 8.9 swap_11.1
  314.4 23.9 %share_8.1 = bf16[8,4,48,768]{3,2,1,0:T(8,128)(2,1)} custom-call(bf16[48,768]{1,0:T(8,128)(2,1)} %bitcast.649), custom_call_target="tpu_custom_call" | custom-call | tf_op jit(solution)/shard_map/share_8/pallas_call | solution.py:290
  380.8 8.6 convolution_convert_fusion
  389.4 7.8 fusion.15
  397.3 4.9 convolution_convert_fusion.1
  402.2 3.4 multiply_reduce_fusion.5
  412.0 5.1 fusion.114
  417.1 13.6 %fusion.23 = f32[2,12,64,256]{3,2,1,0:T(8,128)} fusion(f32[2,12,256,256]{2,3,1,0:T(8,128)} %fusion.114, f32[2,12,256,256]{2,3,1,0:T(8,128)} %copy-done.7, f32[2,12,256]{2,1,0:T(8,128)S(1)} %copy-done.174, pred[2,256,256]{1,2,0:T(8,128)(4,1)S(1)} %broadcast_compare_fusion, f32[2,256,12,64]{1,0,3,2:T(2,128)} %reshape.1222, f32[12,64]{1,0:T(8,128)S(1)} %copy-done.119, ...), kind=kOutput, calls=%fused_computation.48 | convolution fusion | flops 220207360 | bytes 15936512 | tf_op jit(solution)/shard_map/bhst,bshd->bthd/dot_general | solution.py:46
  434.6 14.1 %fusion.26 = f32[2,12,64,256]{3,2,1,0:T(8,128)} fusion(f32[2,12,256,256]{2,3,1,0:T(8,128)} %fusion.114, f32[2,12,256,256]{2,3,1,0:T(8,128)} %copy-done.7, f32[2,12,256]{2,1,0:T(8,128)S(1)} %copy-done.174, pred[2,256,256]{1,2,0:T(8,128)(4,1)S(1)} %broadcast_compare_fusion, f32[2,256,12,64]{1,0,3,2:T(2,128)} %reshape.1224, f32[12,64]{1,0:T(8,128)S(1)} %copy-done.121, ...), kind=kOutput, calls=%fused_computation.49 | convolution fusion | flops 220207360 | bytes 15936512 | tf_op jit(solution)/shard_map/bhst,bthd->bshd/dot_general | solution.py:46
  452.3 5.4 fusion.63
  464.3 3.0 copy.320
  471.7 3.1 copy.324
  480.9 3.0 copy.309
  488.2 3.0 copy.313
  502.8 7.5 fusion.47
  510.4 4.6 convolution_convert_fusion.2
  515.0 81.4 %reduce_5.1 = f32[13,24,768]{2,1,0:T(8,128)} custom-call(bf16[3,4,2,2,2,24,768]{6,5,4,3,2,1,0:T(8,128)(2,1)} %bitcast.630, bf16[1,4,2,2,2,24,768]{6,5,4,3,2,1,0:T(8,128)(2,1)} %bitcast.616, bf16[4,4,2,2,2,24,768]{6,5,4,3,2,1,0:T(8,128)(2,1)} %bitcast.619, bf16[4,4,2,2,2,24,768]{6,5,4,3,2,1,0:T(8,128)(2,1)} %bitcast.618, ...), custom_call_target="tpu_custom_call" | custom-call | tf_op jit(solution)/shard_map/reduce_5/pallas_call | solution.py:526
  598.5 4.8 multiply_reduce_fusion.6
  605.2 9.6 fusion.8
  614.9 3.4 multiply_reduce_fusion.9
  622.8 5.2 fusion.111
  628.0 11.9 fusion.31
  645.0 14.1 %fusion.34 = f32[2,12,64,256]{3,2,1,0:T(8,128)} fusion(f32[2,12,256,256]{2,3,1,0:T(8,128)} %fusion.111, f32[2,12,256,256]{2,3,1,0:T(8,128)} %copy-done.6, f32[2,12,256]{2,1,0:T(8,128)} %copy-done.171, pred[2,256,256]{1,2,0:T(8,128)(4,1)S(1)} %broadcast_compare_fusion, f32[2,256,12,64]{1,0,3,2:T(2,128)} %reshape.1216, f32[12,64]{1,0:T(8,128)} %copy-done.115, ...), kind=kOutput, calls=%fused_computation.51 | convolution fusion | flops 220207360 | bytes 15936512 | tf_op jit(solution)/shard_map/bhst,bthd->bshd/dot_general | solution.py:46
  664.2 5.5 fusion.64
  671.1 3.0 copy.346
  679.3 3.4 multiply_reduce_fusion.7
  684.0 3.1 copy.353
  691.0 3.1 copy.345
  699.8 3.2 copy.338
  707.4 3.0 copy.342
  722.6 7.4 fusion.53
  739.5 7.5 convolution_convert_fusion.4
  747.0 4.0 convolution_convert_fusion.5
  751.0 5.1 convolution_convert_fusion.3
  765.4 86.4 %reduce_4.1 = (f32[13,24,768]{2,1,0:T(8,128)}, f32[1,8,256]{2,1,0:T(8,128)}) custom-call(bf16[3,4,2,2,2,24,768]{6,5,4,3,2,1,0:T(8,128)(2,1)} %bitcast.631, bf16[1,4,2,2,2,24,768]{6,5,4,3,2,1,0:T(8,128)(2,1)} %bitcast.629, bf16[4,4,2,2,2,24,768]{6,5,4,3,2,1,0:T(8,128)(2,1)} %bitcast.626, bf16[4,4,2,2,2,24,768]{6,5,4,3,2,1,0:T(8,128)(2,1)} %bitcast.627, ...), custom_call_target="tpu_custom_call" | custom-call | tf_op jit(solution)/shard_map/reduce_4/pallas_call | solution.py:526
  857.3 12.5 share_9.1
  879.5 39.2 %spread_12.1 = bf16[26,8,24,768]{3,2,1,0:T(8,128)(2,1)} custom-call(bf16[26,24,768]{2,1,0:T(8,128)(2,1)} %fusion.101.own), custom_call_target="tpu_custom_call" | custom-call | tf_op jit(solution)/shard_map/spread_12/pallas_call | solution.py:603
  921.6 10.8 convert_multiply_fusion
  932.3 16.4 %bitcast_add_fusion = f32[26,192,768]{2,1,0:T(8,128)} fusion(f32[26,8,24,768]{3,2,1,0:T(8,128)} %convert_multiply_fusion, f32[26,192,768]{2,1,0:T(8,128)} %param.20), kind=kLoop, calls=%fused_computation.4 | loop fusion | flops 7667712 | bytes 46006272 | tf_op jit(solution)/shard_map/add | solution.py:925
  954.5 4.3 multiply_convert_fusion.12
  962.7 171.6 %all-reduce.6.cloned.1.call-done = f32[2,768,768]{2,1,0:T(8,128)} async-done(((f32[2,768,768]{2,1,0:T(8,128)}), f32[2,768,768]{2,1,0:T(8,128)}) %all-reduce.6.cloned.1.call-update) | async-done | bytes 4718608 | tf_op jit(solution)/shard_map/psum | solution.py:944
  1134.3 3.1 fusion.41
  1138.2 4.4 multiply_add_fusion.23
  1151.8 4.4 multiply_add_fusion.11
  1191.2 4.9 fusion.59
  1196.1 5.0 fusion.98
  1205.3 65.0 %all-gather.2.cloned.1.call-done = bf16[8,5,192,768]{3,2,1,0:T(8,128)(2,1)} async-done(((bf16[1,5,192,768]{3,2,1,0:T(8,128)(2,1)}), bf16[8,5,192,768]{3,2,1,0:T(8,128)(2,1)}) %all-gather.2.cloned.1.call-update) | async-done | bytes 11796496 | tf_op jit(solution)/shard_map/all_gather | solution.py:956
  1296.0 14.7 %fusion.398 = (bf16[26,192,768]{2,1,0:T(8,128)(2,1)}, f32[26,192,768]{2,1,0:T(8,128)}) fusion(bf16[26,192,768]{2,1,0:T(8,128)(2,1)S(1)} %fusion.146, f32[26]{0:T(128)S(1)} %copy-done.256, f32[26,192,768]{2,1,0:T(8,128)} %param.19), kind=kLoop, calls=%fused_computation.730 | loop fusion | flops 19169280 | bytes 46006376 | tf_op jit(solution)/shard_map/convert_element_type | solution.py:42
  (993 shorter events, 323.6 us)
Async XLA Ops:
  7.2 77.0 %copy-start = (bf16[2,1,256,768]{3,2,1,0:T(8,128)(2,1)S(1)}, bf16[2,1,256,768]{3,2,1,0:T(8,128)(2,1)}, u32[]{:S(2)}) copy-start(bf16[2,1,256,768]{3,2,1,0:T(8,128)(2,1)} %param.14) | copy-start | bytes 2359300
  7.2 1127.1 %all-reduce.6.cloned.1.call-start = ((), (), s32[]{:S(2)}) async-start(), calls=%async_computation | async-start | bytes 9437184 | tf_op jit(solution)/shard_map/psum | solution.py:944
  9.7 72.9 %copy-start.56 = (f32[79,768]{1,0:T(8,128)S(1)}, f32[79,768]{1,0:T(8,128)}, u32[]{:S(2)}) copy-start(f32[79,768]{1,0:T(8,128)} %param.21) | copy-start | bytes 728068
  83.3 95.3 %copy-start.158 = (f32[768]{0:T(1024)}, f32[768]{0:T(1024)S(1)}, u32[]{:S(2)}) copy-start(f32[768]{0:T(1024)S(1)} %get-tuple-element.69) | copy-start | bytes 9220
  83.3 95.4 %copy-start.156 = (f32[768]{0:T(1024)}, f32[768]{0:T(1024)S(1)}, u32[]{:S(2)}) copy-start(f32[768]{0:T(1024)S(1)} %get-tuple-element.68) | copy-start | bytes 9220
  83.3 109.6 %copy-start.206 = (f32[768]{0:T(1024)}, f32[768]{0:T(1024)S(1)}, u32[]{:S(2)}) copy-start(f32[768]{0:T(1024)S(1)} %get-tuple-element.67) | copy-start | bytes 9220
  83.3 109.7 %copy-start.244 = (f32[768]{0:T(1024)}, f32[768]{0:T(1024)S(1)}, u32[]{:S(2)}) copy-start(f32[768]{0:T(1024)S(1)} %get-tuple-element.66) | copy-start | bytes 9220
  83.3 119.9 %copy-start.208 = (f32[768]{0:T(1024)}, f32[768]{0:T(1024)S(1)}, u32[]{:S(2)}) copy-start(f32[768]{0:T(1024)S(1)} %get-tuple-element.65) | copy-start | bytes 9220
  96.2 81.2 %copy-start.92 = (f32[512,12]{0,1:T(8,128)}, f32[512,12]{0,1:T(8,128)S(1)}, u32[]{:S(2)}) copy-start(f32[512,12]{0,1:T(8,128)S(1)} %multiply_reduce_fusion.27) | copy-start | bytes 73732
  99.3 78.0 %copy-start.90 = (f32[512,12]{0,1:T(8,128)}, f32[512,12]{0,1:T(8,128)S(1)}, u32[]{:S(2)}) copy-start(f32[512,12]{0,1:T(8,128)S(1)} %multiply_reduce_fusion.26) | copy-start | bytes 73732
  106.0 72.8 %copy-start.227 = (s32[2,1,256]{2,1,0:T(1,128)S(1)}, s32[2,1,256]{2,1,0:T(1,128)}, u32[]{:S(2)}) copy-start(s32[2,1,256]{2,1,0:T(1,128)} %param.16) | copy-start | bytes 6148
  106.0 72.9 %copy-start.18 = (f32[2,256,12,64]{1,0,3,2:T(2,128)S(1)}, f32[2,256,12,64]{1,0,3,2:T(2,128)}, u32[]{:S(2)}) copy-start(f32[2,256,12,64]{1,0,3,2:T(2,128)} %reshape.1218) | copy-start | bytes 4718596
  213.8 13.0 copy-start.94
  220.1 8.7 copy-start.162
  220.1 8.8 copy-start.160
  235.3 8.6 copy-start.173
  260.2 106.6 %copy-start.14 = (f32[256,768]{0,1:T(8,128)}, f32[256,768]{0,1:T(8,128)S(1)}, u32[]{:S(2)}) copy-start(f32[256,768]{0,1:T(8,128)S(1)} %copy.291) | copy-start | bytes 2359300
  262.4 9.7 copy-start.225
  271.3 31.6 %copy-start.247 = (f32[16]{0:T(128)}, f32[16]{0:T(128)S(1)}, u32[]{:S(2)}) copy-start(f32[16]{0:T(128)S(1)} %get-tuple-element.177) | copy-start | bytes 196
  295.2 17.8 %copy-start.251 = (pred[2,8]{1,0:T(4,128)(4,1)S(1)}, pred[2,8]{1,0:T(4,128)(4,1)}, u32[]{:S(2)}) copy-start(pred[2,8]{1,0:T(4,128)(4,1)} %fusion.250) | copy-start | bytes 52
  340.1 7.8 copy-start.140
  340.1 12.0 copy-start.131
  340.1 12.6 copy-start.165
  340.1 12.7 copy-start.129
  340.8 13.5 %copy-start.148 = (f32[32,2,8]{0,2,1:T(8,128)}, f32[32,2,8]{0,2,1:T(8,128)S(1)}, u32[]{:S(2)}) copy-start(f32[32,2,8]{0,2,1:T(8,128)S(1)} %convert_bitcast_fusion) | copy-start | bytes 6148
  342.1 13.4 %copy-start.215 = (f32[2,8]{1,0:T(2,128)S(1)}, f32[2,8]{1,0:T(2,128)}, u32[]{:S(2)}) copy-start(f32[2,8]{1,0:T(2,128)} %get-tuple-element.161) | copy-start | bytes 196
  343.0 15.2 %copy-start.249 = (pred[256]{0:T(512)(128)(4,1)}, pred[256]{0:T(512)(128)(4,1)S(1)}, u32[]{:S(2)}) copy-start(pred[256]{0:T(512)(128)(4,1)S(1)} %broadcast_compare_fusion.2) | copy-start | bytes 772
  345.7 14.0 %copy-start.212 = (f32[256]{0:T(256)}, f32[256]{0:T(256)S(1)}, u32[]{:S(2)}) copy-start(f32[256]{0:T(256)S(1)} %get-tuple-element.101) | copy-start | bytes 3076
  347.9 11.9 copy-start.250
  349.2 14.2 %copy-start.229 = (f32[256]{0:T(256)S(1)}, f32[256]{0:T(256)}, u32[]{:S(2)}) copy-start(f32[256]{0:T(256)} %copy-done.228) | copy-start | bytes 3076
  349.2 15.6 %copy-start.248 = (f32[16]{0:T(128)S(1)}, f32[16]{0:T(128)}, u32[]{:S(2)}) copy-start(f32[16]{0:T(128)} %copy-done.247) | copy-start | bytes 196
  352.0 9.0 copy-start.214
  352.0 14.8 %copy-start.125 = (f32[8,12]{0,1:T(8,128)S(1)}, f32[8,12]{0,1:T(8,128)}, u32[]{:S(2)}) copy-start(f32[8,12]{0,1:T(8,128)} %copy-done.124) | copy-start | bytes 1156
  352.0 14.8 %copy-start.147 = (pred[8,256]{1,0:T(8,128)(4,1)S(1)}, pred[8,256]{1,0:T(8,128)(4,1)}, u32[]{:S(2)}) copy-start(pred[8,256]{1,0:T(8,128)(4,1)} %copy-done.146) | copy-start | bytes 6148
  364.9 8.2 copy-start.123
  364.9 8.2 copy-start.145
  365.0 8.2 copy-start.169
  380.1 9.2 slice-start.12
  380.1 9.2 slice-start.16
  380.8 8.6 slice-start.13
  380.8 8.6 slice-start.17
  380.8 21.4 %slice-start.8 = ((s8[4718592]{0:T(1024)(128)(4,1)}), s8[4194304]{0:T(1024)(128)(4,1)S(1)}, s32[]{:S(2)}) async-start(s8[4718592]{0:T(1024)(128)(4,1)} %bitcast.682), calls=%async_computation.10 | async-start | bytes 8388608
  389.4 7.9 copy-start.38
  389.4 7.9 copy-start.189
  389.4 7.9 copy-start.211
  389.4 7.9 copy-start.224
  389.4 7.9 copy-start.246
  389.4 12.7 slice-start.9
  515.0 83.5 %copy-start.69 = (bf16[512,768]{1,0:T(8,128)(2,1)S(1)}, bf16[512,768]{1,0:T(8,128)(2,1)}, u32[]{:S(2)}) copy-start(bf16[512,768]{1,0:T(8,128)(2,1)} %copy-done.68) | copy-start | bytes 2359300
  603.4 11.4 slice-start.4
  605.1 13.9 %copy-start.47 = (f32[512,768]{1,0:T(8,128)}, f32[512,768]{1,0:T(8,128)S(1)}, u32[]{:S(2)}) copy-start(f32[512,768]{1,0:T(8,128)S(1)} %add_add_fusion.15) | copy-start | bytes 4718596
  605.1 9.7 copy-start.32
  605.1 9.7 copy-start.184
  605.2 9.7 copy-start.207
  605.2 9.7 copy-start.220
  605.2 9.7 slice-start.5
  722.6 7.7 copy-start.258
  739.5 11.5 slice-start.14
  853.9 18.5 %copy-start.253 = (s32[8,5]{1,0:T(8,128)S(1)}, s32[8,5]{1,0:T(8,128)}, u32[]{:S(2)}) copy-start(s32[8,5]{1,0:T(8,128)} %constant.263.clone) | copy-start | bytes 484
  879.5 41.4 %copy-start.252 = (f32[8,5]{1,0:T(8,128)S(1)}, f32[8,5]{1,0:T(8,128)}, u32[]{:S(2)}) copy-start(f32[8,5]{1,0:T(8,128)} %constant.264.clone) | copy-start | bytes 484
  962.4 307.9 %all-gather.2.cloned.1.call-start = ((), (), s32[]{:S(2)}) async-start(), calls=%async_computation.1 | async-start | bytes 13271040 | tf_op jit(solution)/shard_map/all_gather | solution.py:956
  1134.3 8.2 slice-start
  1148.5 7.6 slice-start.2
  1288.1 7.9 copy-start.256
  (223 other events, 809.8 us)
Sparse Core Ops, SparseCore 0:
  962.6 171.6 all-reduce.5
  1202.5 67.7 all-gather.1

commit v3 on v2

--- a/solution.py
+++ b/solution.py
@@ -50,17 +50,6 @@
     centred = value - jnp.mean(value, -1, keepdims=True)
     spread = jnp.mean(centred * centred, -1, keepdims=True)
     return centred * lax.rsqrt(spread + 1e-06) * gain + shift
-
-
-def head_norm(value, gain):
-    heads = value.reshape(value.shape[0], HEADS, HD)
-    centred = heads - jnp.mean(heads, -1, keepdims=True)
-    spread = jnp.mean(centred * centred, -1, keepdims=True)
-    return centred * lax.rsqrt(spread + 1e-06) * gain.reshape(HEADS, HD)
-
-
-def both_norms(query, key, gain_query, gain_key):
-    return (head_norm(query, gain_query), head_norm(key, gain_key))
 
 
 def unit_rows(value):
@@ -542,14 +531,14 @@
     return (outs[0], outs[1] if small is not None else None)
 
 
-def spread_kernel(own, out, local_sem, send, recv):
+def spread_stages(own, out, local_sem, send, recv):
     d, z, _ = places()
     sib, near_x, near_y = flip(d, 1), flip(d, 2), flip(d, 4)
     diagonal = flip(near_x, 4)
-    greet([(sib, z), (near_x, z), (near_y, z)])
     half = own.shape[0] // 2
-    first, second = (pl.ds(0, half), pl.ds(half, own.shape[0] - half))
+    parts = (pl.ds(0, half), pl.ds(half, own.shape[0] - half))
     started = []
+    last = []
 
     def push(slot, origin, part, to, source=None):
         copy = pltpu.make_async_remote_copy(
@@ -564,36 +553,50 @@
         started.append(copy)
         return copy
 
-    near = []
-    for i, part in enumerate((first, second)):
-        near.append(
-            [
-                push(2 * i, d, part, (near_x, z), own.at[part]),
-                push(2 * i + 1, d, part, (near_y, z), own.at[part]),
-            ]
-        )
     keep = pltpu.make_async_copy(own, out.at[:, d], local_sem)
-    keep.start()
-    last = [push(4 + i, d, part, (sib, z), own.at[part]) for i, part in enumerate((first, second))]
-    near[0][0].wait_recv()
-    turn_y = push(6, near_x, first, (near_y, z))
-    last.append(push(7, near_x, first, (sib, z)))
-    near[1][1].wait_recv()
-    turn_x = push(8, near_y, second, (near_x, z))
-    last.append(push(9, near_y, second, (sib, z)))
-    near[0][1].wait_recv()
-    last.append(push(10, near_y, first, (sib, z)))
-    near[1][0].wait_recv()
-    last.append(push(11, near_x, second, (sib, z)))
-    turn_y.wait_recv()
-    last.append(push(12, diagonal, first, (sib, z)))
-    turn_x.wait_recv()
-    last.append(push(13, diagonal, second, (sib, z)))
-    for copy in last:
-        copy.wait_recv()
-    for copy in started:
-        copy.wait_send()
-    keep.wait()
+    near = {}
+    turned = []
+
+    def begin():
+        for way, part in ((0, 0), (1, 1), (0, 1), (1, 0)):
+            near[way, part] = push(
+                2 * way + part, d, parts[part], ((near_x, near_y)[way], z), own.at[parts[part]]
+            )
+        keep.start()
+        last.extend([push(4 + i, d, parts[i], (sib, z), own.at[parts[i]]) for i in (0, 1)])
+
+    def forward():
+        near[0, 0].wait_recv()
+        turned.append(push(6, near_x, parts[0], (near_y, z)))
+        last.append(push(7, near_x, parts[0], (sib, z)))
+        near[1, 1].wait_recv()
+        turned.append(push(8, near_y, parts[1], (near_x, z)))
+        last.append(push(9, near_y, parts[1], (sib, z)))
+
+    def collect():
+        near[1, 0].wait_recv()
+        last.append(push(10, near_y, parts[0], (sib, z)))
+        near[0, 1].wait_recv()
+        last.append(push(11, near_x, parts[1], (sib, z)))
+        for i in (0, 1):
+            turned[i].wait_recv()
+            last.append(push(12 + i, diagonal, parts[i], (sib, z)))
+
+    def finish():
+        for copy in last:
+            copy.wait_recv()
+        for copy in started:
+            copy.wait_send()
+        keep.wait()
+
+    return (begin, forward, collect, finish)
+
+
+def spread_kernel(own, out, local_sem, send, recv):
+    d, z, _ = places()
+    greet([(flip(d, 1), z), (flip(d, 2), z), (flip(d, 4), z)])
+    for stage in spread_stages(own, out, local_sem, send, recv):
+        stage()
 
 
 def spread(own, collective):
@@ -617,26 +620,515 @@
     )(own)
 
 
-def masked_scores(query_low, key_low, same):
-    scores = product(query_low, key_low, "bshd,bthd->bhst") * (1.0 / math.sqrt(HD))
-    return jnp.where(same[:, None], scores, -1e30)
-
-
-def layer_forward(state, blocks, gains, same):
+def meet_kernel(own, parts, out, mine, local_sem, send, recv, part_send, part_recv):
+    d, z, zs = places()
+    sib, near_x, near_y = flip(d, 1), flip(d, 2), flip(d, 4)
+    diagonal = flip(near_x, 4)
+    others = [near_x, near_y, diagonal, sib, flip(near_x, 1), flip(near_y, 1), flip(diagonal, 1)]
+    greet([(d, zs[1]), (d, zs[2]), (d, zs[3])] + [(other, z) for other in others])
+    out[d, z] = own[...]
+
+    def push(slot, source, target, to, sems=(send, recv)):
+        copy = pltpu.make_async_remote_copy(
+            src_ref=source,
+            dst_ref=target,
+            send_sem=sems[0].at[slot],
+            recv_sem=sems[1].at[slot],
+            device_id=to,
+            device_id_type=MESH,
+        )
+        copy.start()
+        return copy
+
+    first = [push(o - 1, own, out.at[d, z], (d, zs[o])) for o in (1, 2, 3)]
+    moved = [
+        push(i, parts.at[other], mine.at[:, d], (other, z), (part_send, part_recv))
+        for i, other in enumerate(others)
+    ]
+    keep = pltpu.make_async_copy(parts.at[d], mine.at[:, d], local_sem)
+    keep.start()
+    for copy in first:
+        copy.wait_recv()
+    second = [push(3 + i, out.at[d], out.at[d], (to, z)) for i, to in enumerate(others[:3])]
+    last = [push(6, out.at[d], out.at[d], (sib, z))]
+    for i, origin in enumerate(others[:3]):
+        second[i].wait_recv()
+        last.append(push(7 + i, out.at[origin], out.at[origin], (sib, z)))
+    for copy in last + moved:
+        copy.wait_recv()
+    for copy in first + second + last + moved:
+        copy.wait_send()
+    keep.wait()
+
+
+def meet(own, parts, collective):
+    lanes, depth = lax.axis_size("dp"), lax.axis_size("fsdp")
+    rest = parts.shape[1:]
+    return pl.pallas_call(
+        meet_kernel,
+        out_shape=[
+            jax.ShapeDtypeStruct((lanes, depth) + own.shape, own.dtype),
+            jax.ShapeDtypeStruct(rest[:1] + (lanes,) + rest[1:], parts.dtype),
+        ],
+        in_specs=[pl.BlockSpec(memory_space=pltpu.VMEM)] * 2,
+        out_specs=[pl.BlockSpec(memory_space=pltpu.VMEM)] * 2,
+        scratch_shapes=[
+            pltpu.SemaphoreType.DMA,
+            pltpu.SemaphoreType.DMA((10,)),
+            pltpu.SemaphoreType.DMA((10,)),
+            pltpu.SemaphoreType.DMA((7,)),
+            pltpu.SemaphoreType.DMA((7,)),
+        ],
+        compiler_params=pltpu.CompilerParams(
+            collective_id=collective, has_side_effects=True, vmem_limit_bytes=VMEM_LIMIT
+        ),
+        name=f"meet_{collective}",
+    )(own, parts)
+
+
+GRAM_TILE = 128
+
+
+def gram_kernel(gram, own, total, shards, left, right, onward, back, sems, local_sem, send, recv):
+    d, z, _ = places()
+    up, down = (z + 1, z - 1)
+    two = jnp.logical_and(lax.rem(d, 2) == 1, d // 4 == 1)
+    sib, near_x, near_y = flip(d, 1), flip(d, 2), flip(d, 4)
+    greet([(d, lax.rem(z + step, 4)) for step in (1, 2, 3)] + [(sib, z), (near_x, z), (near_y, z)])
+    stages = spread_stages(own, shards, local_sem, send, recv)
+    stages[0]()
+    count = D // GRAM_TILE
+
+    def at(ref, slot, j):
+        return ref.at[slot, pl.ds(j * GRAM_TILE, GRAM_TILE), pl.ds(j * GRAM_TILE, D - j * GRAM_TILE)]
+
+    def copy(source, target, slot, j, way, to):
+        return pltpu.make_async_remote_copy(
+            src_ref=at(source, slot, j),
+            dst_ref=at(target, slot, j),
+            send_sem=sems.at[2 * way, slot, j],
+            recv_sem=sems.at[2 * way + 1, slot, j],
+            device_id=(d, to),
+            device_id_type=MESH,
+        )
+
+    def add(target, slot, j, *terms):
+        @pl.loop(0, GRAM_TILE // 16)
+        def _(i):
+            rows = pl.ds(pl.multiple_of(j * GRAM_TILE + i * 16, 16), 16)
+            columns = pl.ds(j * GRAM_TILE, D - j * GRAM_TILE)
+            value = terms[0][slot, rows, columns]
+            for term in terms[1:]:
+                value = value + term[slot, rows, columns]
+            target[slot, rows, columns] = value
+
+    def ends(slot):
+        @pl.when(z == 0)
+        def _():
+            for j in range(count):
+                copy(gram, left, slot, j, 0, up).start()
+
+        @pl.when(z == 3)
+        def _():
+            for j in range(count):
+                copy(gram, right, slot, j, 1, down).start()
+
+    def near(slot, j):
+        @pl.when(z == 1)
+        def _():
+            copy(onward, left, slot, j, 0, up).wait_recv()
+            add(onward, slot, j, gram, left)
+            copy(onward, left, slot, j, 0, up).start()
+
+        @pl.when(z == 2)
+        def _():
+            copy(back, right, slot, j, 1, down).wait_recv()
+            add(back, slot, j, gram, right)
+            copy(back, right, slot, j, 1, down).start()
+
+    def far(slot, j):
+        @pl.when(z == 1)
+        def _():
+            copy(back, right, slot, j, 1, down).wait_recv()
+            add(back, slot, j, gram, right)
+            copy(back, right, slot, j, 1, down).start()
+            add(total, slot, j, onward, right)
+
+        @pl.when(z == 2)
+        def _():
+            copy(onward, left, slot, j, 0, up).wait_recv()
+            add(onward, slot, j, gram, left)
+            copy(onward, left, slot, j, 0, up).start()
+            add(total, slot, j, onward, right)
+
+    def close(slot, j):
+        @pl.when(z == 3)
+        def _():
+            copy(gram, left, slot, j, 0, up).wait_recv()
+            add(total, slot, j, left, gram)
+
+        @pl.when(z == 0)
+        def _():
+            copy(gram, right, slot, j, 1, down).wait_recv()
+            add(total, slot, j, gram, right)
+
+    def finish(slot):
+        for j in range(count):
+            @pl.when(z == 0)
+            def _():
+                copy(gram, left, slot, j, 0, up).wait_send()
+
+            @pl.when(z == 3)
+            def _():
+                copy(gram, right, slot, j, 1, down).wait_send()
+
+            @pl.when(jnp.logical_and(z > 0, z < 3))
+            def _():
+                copy(onward, left, slot, j, 0, up).wait_send()
+                copy(back, right, slot, j, 1, down).wait_send()
+
+    def mirror(slot):
+        for i in range(count):
+            for j in range(i + 1, count):
+                block = total[slot, i * GRAM_TILE : (i + 1) * GRAM_TILE, j * GRAM_TILE : (j + 1) * GRAM_TILE]
+                total[slot, j * GRAM_TILE : (j + 1) * GRAM_TILE, i * GRAM_TILE : (i + 1) * GRAM_TILE] = block.T
+
+    ends(0)
+
+    @pl.when(two)
+    def _():
+        ends(1)
+
+    def guarded(action, item):
+        if item[0] == 0:
+            action(*item)
+        else:
+            pl.when(two)(lambda: action(*item))
+
+    skew = 2
+    items = [(slot, j) for slot in (0, 1) for j in range(count)]
+    for step in range(len(items) + skew):
+        if step < len(items):
+            guarded(near, items[step])
+        if step >= skew:
+            guarded(far, items[step - skew])
+            guarded(close, items[step - skew])
+        if step == 3:
+            stages[1]()
+        if step == count + 1:
+            stages[2]()
+
+    mirror(0)
+
+    @pl.when(two)
+    def _():
+        mirror(1)
+
+    finish(0)
+
+    @pl.when(two)
+    def _():
+        finish(1)
+
+    stages[3]()
+
+
+def sum_grams(grams, own, collective):
+    lanes = lax.axis_size("dp")
+    whole = pltpu.VMEM(grams.shape, jnp.float32)
+    return pl.pallas_call(
+        gram_kernel,
+        out_shape=[
+            jax.ShapeDtypeStruct(grams.shape, jnp.float32),
+            jax.ShapeDtypeStruct(own.shape[:1] + (lanes,) + own.shape[1:], own.dtype),
+        ],
+        in_specs=[pl.BlockSpec(memory_space=pltpu.VMEM)] * 2,
+        out_specs=[
+            pl.BlockSpec(memory_space=pltpu.VMEM),
+            pl.BlockSpec(memory_space=pl.ANY),
+        ],
+        scratch_shapes=[
+            whole,
+            whole,
+            whole,
+            whole,
+            pltpu.SemaphoreType.DMA((4, grams.shape[0], D // GRAM_TILE)),
+            pltpu.SemaphoreType.DMA,
+            pltpu.SemaphoreType.DMA((14,)),
+            pltpu.SemaphoreType.DMA((14,)),
+        ],
+        compiler_params=pltpu.CompilerParams(
+            collective_id=collective, has_side_effects=True, vmem_limit_bytes=VMEM_LIMIT
+        ),
+        name=f"gram_{collective}",
+    )(grams, own)
+
+
+def schulz_kernel(two, gram, rows, out, state, state_low, change, current):
+    tile = 256
+
+    def chain(slot, first, places_here, step):
+        total = jnp.zeros((1, 1), jnp.float32)
+        for t in range(0, D, tile):
+            value = gram[slot, t : t + tile, :]
+            line = lax.broadcasted_iota(jnp.int32, value.shape, 0) + t
+            column = lax.broadcasted_iota(jnp.int32, value.shape, 1)
+            total = total + jnp.sum(
+                jnp.where(line == column, value, 0.0), axis=(0, 1), keepdims=True
+            )
+        inverse = 1.0 / (jnp.sqrt(total) + 1e-07)
+
+        @pl.loop(0, D // tile)
+        def _(t):
+            part = pl.ds(pl.multiple_of(t * tile, tile), tile)
+            value = gram[slot, part, :] * (inverse * inverse)
+            state[part, :] = value
+            state_low[part, :] = value.astype(jnp.bfloat16)
+
+        for place in range(places_here):
+            current[first + place] = rows[first + place] * inverse
+
+        @pl.loop(0, NS_ITERS)
+        def _(turn):
+            @pl.loop(0, D // tile)
+            def _(t):
+                part = pl.ds(pl.multiple_of(t * tile, tile), tile)
+                square = jnp.dot(
+                    state_low[part, :], state_low[...], preferred_element_type=jnp.float32
+                )
+                change[part, :] = (COEF_B * state[part, :] + COEF_C * square).astype(jnp.bfloat16)
+
+            @pl.loop(first, first + places_here)
+            def _(place):
+                value = current[place]
+                current[place] = COEF_A * value + jnp.dot(
+                    value.astype(jnp.bfloat16), change[...], preferred_element_type=jnp.float32
+                )
+
+            @pl.when(turn < NS_ITERS - 1)
+            def _():
+                @pl.loop(0, D // tile)
+                def _(t):
+                    part = pl.ds(pl.multiple_of(t * tile, tile), tile)
+                    value = state[part, :]
+                    for _ in range(2):
+                        value = COEF_A * value + jnp.dot(
+                            value.astype(jnp.bfloat16),
+                            change[...],
+                            preferred_element_type=jnp.float32,
+                        )
+                    state[part, :] = value
+                    state_low[part, :] = value.astype(jnp.bfloat16)
+
+        for place in range(places_here):
+            out[first + place] = current[first + place].astype(jnp.bfloat16)
+
+    @pl.when(two[0] == 0)
+    def _():
+        chain(0, 0, 4, 0)
+
+    @pl.when(two[0] == 1)
+    def _():
+        chain(0, 0, 1, 0)
+        chain(1, 1, 1, 0)
+        for place in (2, 3):
+            out[place] = jnp.zeros(out.shape[1:], jnp.bfloat16)
+
+
+def schulz(two, grams, rows):
+    return pl.pallas_call(
+        schulz_kernel,
+        out_shape=jax.ShapeDtypeStruct(rows.shape, jnp.bfloat16),
+        in_specs=[
+            pl.BlockSpec(memory_space=pltpu.SMEM),
+            pl.BlockSpec(memory_space=pltpu.VMEM),
+            pl.BlockSpec(memory_space=pltpu.VMEM),
+        ],
+        out_specs=pl.BlockSpec(memory_space=pltpu.VMEM),
+        scratch_shapes=[
+            pltpu.VMEM((D, D), jnp.float32),
+            pltpu.VMEM((D, D), jnp.bfloat16),
+            pltpu.VMEM((D, D), jnp.bfloat16),
+            pltpu.VMEM(rows.shape, jnp.float32),
+        ],
+        compiler_params=pltpu.CompilerParams(vmem_limit_bytes=VMEM_LIMIT),
+        name="schulz",
+    )(two, grams, rows)
+
+
+def update_kernel(table, scale, clip, momenta, grads, weights, turned, momenta_new, weights_new, weights_low):
+    b = pl.program_id(0)
+    momenta_new[...] = MOMENT * momenta[...] + clip[0] * grads[...].astype(jnp.float32)
+    value = weights[...] * (1.0 - MUON_RATE * MUON_DECAY) - scale[b] * turned[0].astype(jnp.float32)
+    weights_new[...] = value
+    weights_low[...] = value.astype(jnp.bfloat16)
+
+
+def update(home, scale, clip, momenta, grads, weights, turned):
+    blocks, rows, width = weights.shape
+    table = np.array([home[block][1] for block in range(blocks)] + [home[block][0] for block in range(blocks)], np.int32)
+    block = pl.BlockSpec((1, rows, width), lambda b, *_: (b, 0, 0))
+    return pl.pallas_call(
+        update_kernel,
+        grid_spec=pltpu.PrefetchScalarGridSpec(
+            num_scalar_prefetch=3,
+            grid=(blocks,),
+            in_specs=[
+                block,
+                block,
+                block,
+                pl.BlockSpec(
+                    (1, 1, rows, width),
+                    lambda b, table, *_: (table[b], table[blocks + b], 0, 0),
+                ),
+            ],
+            out_specs=[block, block, block],
+        ),
+        out_shape=[
+            jax.ShapeDtypeStruct(weights.shape, jnp.float32),
+            jax.ShapeDtypeStruct(weights.shape, jnp.float32),
+            jax.ShapeDtypeStruct(weights.shape, jnp.bfloat16),
+        ],
+        compiler_params=pltpu.CompilerParams(vmem_limit_bytes=VMEM_LIMIT),
+        name="update",
+    )(jnp.asarray(table), jnp.asarray(scale), clip.reshape(1), momenta, grads, weights, turned)
+
+
+GROUP = 4 * HD
+
+
+def normed_head(value, gain):
+    centred = value - jnp.mean(value, 0, keepdims=True)
+    scale = lax.rsqrt(jnp.mean(centred * centred, 0, keepdims=True) + 1e-06)
+    centred = centred * scale
+    return (centred * gain, centred, scale)
+
+
+def contract_first(left, right):
+    return lax.dot_general(
+        left, right, (((0,), (0,)), ((), ())), preferred_element_type=jnp.float32
+    )
+
+
+def contract_last(left, right):
+    return lax.dot_general(
+        left, right, (((1,), (1,)), ((), ())), preferred_element_type=jnp.float32
+    )
+
+
+def head_shares(query_low, key_low, same):
+    scores = contract_first(key_low, query_low) * (1.0 / math.sqrt(HD))
+    scores = jnp.where(same, scores, -1e30)
+    exponent = jnp.exp(scores - jnp.max(scores, 0, keepdims=True))
+    return exponent * (1.0 / jnp.sum(exponent, 0, keepdims=True))
+
+
+def attend_kernel(query, key, value, gain_query, gain_key, rows, columns, out):
+    same = rows[0] == columns[0]
+    for head in range(GROUP // HD):
+        part = slice(head * HD, (head + 1) * HD)
+        query_low = normed_head(query[part], gain_query[part])[0].astype(jnp.bfloat16)
+        key_low = normed_head(key[part], gain_key[part])[0].astype(jnp.bfloat16)
+        share = head_shares(query_low, key_low, same).astype(jnp.bfloat16)
+        out[part] = jnp.dot(
+            value[part].astype(jnp.bfloat16), share, preferred_element_type=jnp.float32
+        ).astype(jnp.bfloat16)
+
+
+def attend_back_kernel(
+    query, key, value, gain_query, gain_key, rows, columns, grad, out, gain_out
+):
+    same = rows[0] == columns[0]
+    for head in range(GROUP // HD):
+        part = slice(head * HD, (head + 1) * HD)
+        query_value, query_unit, query_scale = normed_head(query[part], gain_query[part])
+        key_value, key_unit, key_scale = normed_head(key[part], gain_key[part])
+        query_low = query_value.astype(jnp.bfloat16)
+        key_low = key_value.astype(jnp.bfloat16)
+        value_low = value[part].astype(jnp.bfloat16)
+        grad_low = grad[part]
+        share = head_shares(query_low, key_low, same)
+        out[2, part] = contract_last(grad_low, share.astype(jnp.bfloat16)).astype(jnp.bfloat16)
+        share_grad = contract_first(value_low, grad_low)
+        total = jnp.sum(share * share_grad, 0, keepdims=True)
+        score_low = (share * (share_grad - total) * (1.0 / math.sqrt(HD))).astype(jnp.bfloat16)
+        query_grad = jnp.dot(key_low, score_low, preferred_element_type=jnp.float32)
+        key_grad = contract_last(query_low, score_low)
+        for place, (delta, unit, scale, gain) in enumerate(
+            (
+                (query_grad, query_unit, query_scale, gain_query[part]),
+                (key_grad, key_unit, key_scale, gain_key[part]),
+            )
+        ):
+            gain_out[0, place, part] = jnp.sum(delta * unit, 1, keepdims=True)
+            delta = delta * gain
+            delta = delta - jnp.mean(delta, 0, keepdims=True) - unit * jnp.mean(
+                delta * unit, 0, keepdims=True
+            )
+            out[place, part] = (delta * scale).astype(jnp.bfloat16)
+
+
+def attention_specs(length):
+    def rows_of(first):
+        return pl.BlockSpec((GROUP, length), lambda b, group: (first + group, b))
+
+    count = D // GROUP
+    gain = pl.BlockSpec((GROUP, 1), lambda b, group: (group, 0))
+    return [rows_of(0), rows_of(count), rows_of(2 * count), gain, gain] + [
+        pl.BlockSpec((1, length, 1), lambda b, group: (b, 0, 0)),
+        pl.BlockSpec((1, 1, length), lambda b, group: (b, 0, 0)),
+    ]
+
+
+def attention_operands(mixed, gains, segment):
+    return (
+        mixed,
+        mixed,
+        mixed,
+        gains[4][:, None],
+        gains[5][:, None],
+        segment[:, :, None],
+        segment[:, None, :],
+    )
+
+
+def attend(mixed, gains, segment):
+    parts, length = segment.shape
+    return pl.pallas_call(
+        attend_kernel,
+        grid=(parts, D // GROUP),
+        in_specs=attention_specs(length),
+        out_specs=pl.BlockSpec((GROUP, length), lambda b, group: (group, b)),
+        out_shape=jax.ShapeDtypeStruct((D, parts * length), jnp.bfloat16),
+        name="attend",
+    )(*attention_operands(mixed, gains, segment))
+
+
+def attend_back(mixed, gains, segment, grad):
+    parts, length = segment.shape
+    return pl.pallas_call(
+        attend_back_kernel,
+        grid=(parts, D // GROUP),
+        in_specs=attention_specs(length)
+        + [pl.BlockSpec((GROUP, length), lambda b, group: (group, b))],
+        out_specs=[
+            pl.BlockSpec((3, GROUP, length), lambda b, group: (0, group, b)),
+            pl.BlockSpec((1, 2, GROUP, 1), lambda b, group: (b, 0, group, 0)),
+        ],
+        out_shape=[
+            jax.ShapeDtypeStruct((3, D, parts * length), jnp.bfloat16),
+            jax.ShapeDtypeStruct((parts, 2, D, 1), jnp.float32),
+        ],
+        name="attend_back",
+    )(*attention_operands(mixed, gains, segment), grad)
+
+
+def layer_forward(state, blocks, gains, segment):
     heads_in, norm_one = jax.vjp(layer_norm, state, gains[0], gains[1])
     heads_low = rounded(heads_in)
-    mixed = product(heads_low, blocks[0].reshape(3 * D, D), "sd,rd->sr")
-    (query, key), norms_back = jax.vjp(
-        both_norms, mixed[:, :D], mixed[:, D : 2 * D], gains[4], gains[5]
-    )
-    query_low = rounded(query).reshape(MB, -1, HEADS, HD)
-    key_low = rounded(key).reshape(MB, -1, HEADS, HD)
-    value_low = rounded(mixed[:, 2 * D :]).reshape(MB, -1, HEADS, HD)
-    scores = masked_scores(query_low, key_low, same)
-    top = jax.scipy.special.logsumexp(scores, axis=-1, keepdims=True)
-    weights_low = rounded(jnp.exp(scores - top))
-    attended_low = rounded(product(weights_low, value_low, "bhst,bthd->bshd").reshape(-1, D))
-    state = state + product(attended_low, blocks[1].reshape(D, D), "sr,rd->sd")
+    mixed = product(blocks[0].reshape(3 * D, D), heads_low, "rd,sd->rs")
+    attended_low = attend(mixed, gains, segment)
+    state = state + product(attended_low, blocks[1].reshape(D, D), "rs,rd->sd")
     normed, norm_two = jax.vjp(layer_norm, state, gains[2], gains[3])
     normed_low = rounded(normed)
     hidden, gelu_back = jax.vjp(
@@ -647,11 +1139,7 @@
     kept = (
         norm_one,
         heads_low,
-        norms_back,
-        query_low,
-        key_low,
-        value_low,
-        top,
+        mixed,
         attended_low,
         norm_two,
         normed_low,
@@ -661,21 +1149,8 @@
     return (state, kept)
 
 
-def layer_backward(grad, kept, blocks, same):
-    (
-        norm_one,
-        heads_low,
-        norms_back,
-        query_low,
-        key_low,
-        value_low,
-        top,
-        attended_low,
-        norm_two,
-        normed_low,
-        gelu_back,
-        hidden_low,
-    ) = kept
+def layer_backward(grad, kept, blocks, gains, segment):
+    norm_one, heads_low, mixed, attended_low, norm_two, normed_low, gelu_back, hidden_low = kept
     down = blocks[3].reshape(FF, D)
     upward = blocks[2].reshape(FF, D)
     grad_low = rounded(grad)
@@ -686,25 +1161,21 @@
     inner, gain_two, shift_two = norm_two(product(hidden_grad, upward, "sr,rd->sd"))
     grad = grad + inner
     grad_low = rounded(grad)
-    grad_out = rounded(product(attended_low, grad_low, "sr,sd->rd"))
-    attended_grad = rounded(product(grad_low, blocks[1].reshape(D, D), "sd,rd->sr")).reshape(MB, -1, HEADS, HD)
-    weights = jnp.exp(masked_scores(query_low, key_low, same) - top)
-    weights_low = rounded(weights)
-    value_grad = product(weights_low, attended_grad, "bhst,bshd->bthd")
-    weight_grad = product(attended_grad, value_low, "bshd,bthd->bhst")
-    score_grad = weights * (weight_grad - jnp.sum(weights * weight_grad, -1, keepdims=True))
-    score_low = rounded(score_grad * (1.0 / math.sqrt(HD)))
-    query_grad = product(score_low, key_low, "bhst,bthd->bshd").reshape(-1, HEADS, HD)
-    key_grad = product(score_low, query_low, "bhst,bshd->bthd").reshape(-1, HEADS, HD)
-    query_in, key_in, gain_query, gain_key = norms_back((query_grad, key_grad))
-    mixed_low = rounded(jnp.concatenate([query_in, key_in, value_grad.reshape(-1, D)], 1))
-    grad_mixed = rounded(product(mixed_low, heads_low, "sr,sd->rd"))
+    grad_out = rounded(product(attended_low, grad_low, "rs,sd->rd"))
+    attended_grad = rounded(product(blocks[1].reshape(D, D), grad_low, "rd,sd->rs"))
+    mixed_low, head_gains = attend_back(mixed, gains, segment, attended_grad)
+    head_gains = jnp.sum(head_gains[..., 0], 0)
+    grad_mixed = rounded(product(mixed_low, heads_low, "krs,sd->krd"))
     inner, gain_one, shift_one = norm_one(
-        product(mixed_low, blocks[0].reshape(3 * D, D), "sr,rd->sd")
+        product(
+            mixed_low.reshape(3 * D, -1), blocks[0].reshape(3 * D, D), "rs,rd->sd"
+        )
     )
     grad = grad + inner
     block_grads = [grad_mixed, grad_out, grad_up, grad_down]
-    gain_grads = jnp.stack([gain_one, shift_one, gain_two, shift_two, gain_query, gain_key])
+    gain_grads = jnp.concatenate(
+        [jnp.stack([gain_one, shift_one, gain_two, shift_two]), head_gains], 0
+    )
     return (grad, block_grads, gain_grads)
 
 
@@ -731,11 +1202,20 @@
     for start, number in sorted(muon_groups(), key=lambda group: -group[1]):
         lane = min(range(lanes), key=lambda i: (sum(n for _, n in plan[i]), len(plan[i]), i))
         plan[lane].append((start, number))
+    plan.sort(key=lambda entry: (-entry[0][1] if entry else 0))
+    if lanes == 8:
+        plan = [plan[i] for i in (0, 1, 2, 3, 4, 6, 5, 7)]
     depth = max(len(entry) for entry in plan)
     widths = [
         max([entry[slot][1] for entry in plan if slot < len(entry)]) for slot in range(depth)
     ]
     return (plan, widths)
+
+
+def lane_blocks(plan):
+    rows = [[start + i for start, number in entry for i in range(number)] for entry in plan]
+    most = max(len(row) for row in rows)
+    return np.array([row + [-1] * (most - len(row)) for row in rows], np.int32)
 
 
 def lane_tables(plan, widths):
@@ -806,7 +1286,6 @@
     text_low = rounded(unit_rows(text_sum / text_ids.shape[-1]))
     me = lax.axis_index(("dp", "fsdp"))
     segment = segments[:, 0]
-    same = segment[:, :, None] == segment[:, None, :]
     rows_hot, cols_hot = jax.vmap(positions)(grid[:, 0])
     rows_hot = rows_hot.reshape(-1, POS)
     cols_hot = cols_hot.reshape(-1, POS)
@@ -826,7 +1305,7 @@
             blocks = fetch(weights, pieces, 2 + index)
             if index == 1:
                 pooling_matrix = blocks.pop()[0]
-        state, kept = layer_forward(state, blocks, gains[6 * index : 6 * index + 6], same)
+        state, kept = layer_forward(state, blocks, gains[6 * index : 6 * index + 6], segment)
         saved.append((kept, blocks))
     final, norm_final = jax.vjp(layer_norm, state, gains[fin], gains[fin + 1])
 
@@ -878,7 +1357,9 @@
     slices = [None] * LAYERS
     for index in reversed(range(LAYERS)):
         kept, blocks = saved[index]
-        grad, block_grads[index], gain_parts[index] = layer_backward(grad, kept, blocks, same)
+        grad, block_grads[index], gain_parts[index] = layer_backward(
+            grad, kept, blocks, gains[6 * index : 6 * index + 6], segment
+        )
         if index == 1:
             block_grads[index].append(grad_pool)
         if fast and index > 0:
@@ -893,6 +1374,12 @@
         + [jnp.stack([gain_final, shift_final, query_grad]), grad_rows, grad_cols],
         0,
     )
+    plan, widths = lane_plan(lanes)
+    index, mask, number, home = lane_tables(plan, widths)
+    lane = lax.axis_index("dp")
+    scale = np.ones((weights.shape[0],), np.float32)
+    for start, count_blocks in muon_groups():
+        scale[start : start + count_blocks] = MUON_RATE * math.sqrt(count_blocks)
     if fast:
         width = 256
         small = jnp.concatenate([gains_grad.reshape(-1), loss_part[None]])
@@ -900,15 +1387,62 @@
         slices[0], small = reduce_grads(
             block_grads[0], small.reshape(lanes * depth, 8, width), 4
         )
+        squares = jnp.sum(slices[0] * slices[0]) + jnp.sum(slices[1] * slices[1])
+        slices = [rounded(value) for value in slices]
         slices = jnp.concatenate(
             [slices[0][12:], slices[1][12:]] + [values[:12] for values in slices], 0
         )
-        squares = jnp.broadcast_to(jnp.sum(slices * slices), (8, width))
-        shared = share(jnp.concatenate([small[0], squares], 0), 9)
+        empty = jnp.zeros((1,) + slices.shape[1:], slices.dtype)
+        parts = jnp.concatenate(
+            [
+                slices[block : block + 1] if block >= 0 else empty
+                for block in lane_blocks(plan).reshape(-1)
+            ],
+            0,
+        ).reshape((lanes, -1) + slices.shape[1:])
+        squares = jnp.broadcast_to(squares, (8, width))
+        shared, mine = meet(jnp.concatenate([small[0], squares], 0), parts, 9)
         flat = jnp.transpose(shared[:, :, :8], (1, 0, 2, 3)).reshape(-1)
         gains_grad, loss = (flat[: gains.size].reshape(gains.shape), flat[gains.size])
         squares = jnp.sum(shared[:, :, 8, 0])
-        shard_grads = spread(rounded(slices), 12).reshape(weights.shape).astype(jnp.float32)
+        norm = jnp.sqrt(squares + jnp.sum(gains_grad * gains_grad))
+        clip = jnp.minimum(1.0, CLIP_LIMIT / (norm + 1e-06))
+        blocks_here = lane_blocks(plan)
+        own_momenta = jnp.stack(
+            [
+                jnp.where(
+                    jnp.asarray(blocks_here >= 0)[lane, place],
+                    lax.dynamic_index_in_dim(
+                        momenta, jnp.maximum(jnp.asarray(blocks_here)[lane, place], 0), 0, False
+                    ),
+                    0.0,
+                )
+                for place in range(blocks_here.shape[1])
+            ]
+        )
+        own = MOMENT * own_momenta + clip * mine.reshape(own_momenta.shape).astype(jnp.float32)
+        two = jnp.asarray(np.array([len(entry) > 1 for entry in plan], np.int32))[lane]
+        own_low = rounded(own)
+        first_low = jnp.concatenate(
+            [own_low[:1], jnp.where(two > 0, jnp.bfloat16(0), own_low[1:])], 0
+        )
+        grams = jnp.stack(
+            [
+                product(first_low, first_low, "brd,bre->de"),
+                product(own_low[1], own_low[1], "rd,re->de"),
+            ]
+        )
+        grams, shard_grads = sum_grams(grams, slices, 12)
+        turned = spread(schulz(two.reshape(1), grams, own), 13)
+        homes = {
+            int(block): (lane_of, place)
+            for lane_of, entry in enumerate(blocks_here)
+            for place, block in enumerate(entry)
+            if block >= 0
+        }
+        momenta_new, weights_new, weights_low = update(
+            homes, scale, clip, momenta, shard_grads.reshape(weights.shape), weights, turned
+        )
     else:
         stack = jnp.concatenate(
             [block_grads[index].pop().reshape(1, D, D) for index in range(LAYERS)]
@@ -920,47 +1454,42 @@
         ).astype(jnp.float32)
         gains_grad, loss = lax.psum((gains_grad, loss_part), ("dp", "fsdp"))
         squares = lax.psum(jnp.sum(shard_grads * shard_grads), "fsdp")
-    norm = jnp.sqrt(squares + jnp.sum(gains_grad * gains_grad))
-    clip = jnp.minimum(1.0, CLIP_LIMIT / (norm + 1e-06))
-    momenta_new = MOMENT * momenta + clip * shard_grads
-    plan, widths = lane_plan(lanes)
-    index, mask, number, home = lane_tables(plan, widths)
-    lane = lax.axis_index("dp")
-    own = jnp.stack(
-        [
-            lax.dynamic_index_in_dim(momenta_new, jnp.asarray(index)[lane, place], 0, False)
-            * jnp.asarray(mask)[lane, place]
-            for place in range(index.shape[1])
-        ]
-    )
-    own_low = rounded(own)
-    bounds = np.cumsum([0] + widths)
-    grams = jnp.stack(
-        [
-            product(own_low[a:b], own_low[a:b], "brd,bre->de")
-            for a, b in zip(bounds[:-1], bounds[1:])
-        ]
-    )
-    grams = lax.psum(grams, "fsdp")
-    turned = jnp.concatenate(
-        [
-            product(
-                own_low[bounds[slot] : bounds[slot + 1]],
-                rounded(orthogonal_factor(grams[slot])),
-                "brd,de->bre",
-            )
-            for slot in range(len(widths))
-        ],
-        0,
-    )
-    spread_rows = lax.all_gather(rounded(turned), "dp", axis=0)
-    current = jnp.stack(
-        [spread_rows[home[block][0], home[block][1]] for block in range(weights.shape[0])]
-    ).astype(jnp.float32)
-    scale = np.ones((weights.shape[0], 1, 1), np.float32)
-    for start, count_blocks in muon_groups():
-        scale[start : start + count_blocks] = MUON_RATE * math.sqrt(count_blocks)
-    weights_new = weights * (1.0 - MUON_RATE * MUON_DECAY) - jnp.asarray(scale) * current
+        norm = jnp.sqrt(squares + jnp.sum(gains_grad * gains_grad))
+        clip = jnp.minimum(1.0, CLIP_LIMIT / (norm + 1e-06))
+        momenta_new = MOMENT * momenta + clip * shard_grads
+        own = jnp.stack(
+            [
+                lax.dynamic_index_in_dim(momenta_new, jnp.asarray(index)[lane, place], 0, False)
+                * jnp.asarray(mask)[lane, place]
+                for place in range(index.shape[1])
+            ]
+        )
+        own_low = rounded(own)
+        bounds = np.cumsum([0] + widths)
+        grams = jnp.stack(
+            [
+                product(own_low[a:b], own_low[a:b], "brd,bre->de")
+                for a, b in zip(bounds[:-1], bounds[1:])
+            ]
+        )
+        grams = lax.psum(grams, "fsdp")
+        turned = jnp.concatenate(
+            [
+                product(
+                    own_low[bounds[slot] : bounds[slot + 1]],
+                    rounded(orthogonal_factor(grams[slot])),
+                    "brd,de->bre",
+                )
+                for slot in range(len(widths))
+            ],
+            0,
+        )
+        spread_rows = lax.all_gather(rounded(turned), "dp", axis=0)
+        current = jnp.stack(
+            [spread_rows[home[block][0], home[block][1]] for block in range(weights.shape[0])]
+        ).astype(jnp.float32)
+        weights_new = weights * (1.0 - MUON_RATE * MUON_DECAY) - jnp.asarray(scale)[:, None, None] * current
+        weights_low = rounded(weights_new)
     grad_small = clip * gains_grad
     moment_one = BETA_ONE * gains_m + (1.0 - BETA_ONE) * grad_small
     moment_two = BETA_TWO * gains_v + (1.0 - BETA_TWO) * grad_small * grad_small
@@ -975,7 +1504,7 @@
         loss,
         norm,
         weights_new,
-        rounded(weights_new),
+        weights_low,
         momenta_new,
         gains_new,
         moment_one,

time: 1330 us -> 900 us (0.68)
  waiting for transfers between devices: 237 us -> 0 us
  Pallas kernels: 405 us -> 630 us
  local copies, waits for them, and re-layouts: 203 us -> 31.4 us
  matrix products: 297 us -> 160 us
  other arithmetic: 140 us -> 53 us
  between operations: 36.3 us -> 14.3 us
    pallas_call x0 -> x8, Pallas kernels: none -> 210 us  [the longest x1 64.9 us: sum_grams(): pl.pallas_call(gram_kernel, out_shape=[jax.ShapeDtypeStruct(grams.shape,...]
    psum x1 -> x0, waiting for transfers between devices: 172 us -> none  [per_device(): grams = lax.psum(grams, 'fsdp')]
    dot_general x53 -> x39, matrix products: 225 us -> 135 us  [product(): return jnp.einsum(form, left, right, preferred_element_type=jnp.float32)]
    all_gather x1 -> x0, waiting for transfers between devices: 65 us -> none  [per_device(): spread_rows = lax.all_gather(rounded(turned), 'dp', axis=0)]
    dot_general x32 -> x0, matrix products: 50.6 us -> none  [the longest x10 20.1 us: orthogonal_factor(): jnp.dot(low, low, preferred_element_type=jnp.float32)]
    unnamed x615 -> x283, local copies, waits for them, and re-layouts: 52 us -> 6.84 us
    broadcast_in_dim x16 -> x0, local copies, waits for them, and re-layouts: 35.2 us -> none  [the longest x8 17.7 us: head_norm(): spread = jnp.mean(centred * centred, -1, keepdims=True)]
    reshape x22 -> x0, local copies, waits for them, and re-layouts: 34 us -> none  [the longest x4 10.7 us: head_norm(): heads = value.reshape(value.shape[0], HEADS, HD)]
  transfers between devices with their start and end apart: 2 -> 0, of which waited for: 2 -> 0; matrix products, arithmetic and copies ran while one was open for 0% -> 0% of each run, Pallas kernels for 0% -> 0%
where the time goes in v3:
time: 900 us; the launch traced here: 889 us
  Pallas kernels  630 us (70%)
  matrix products  160 us (18%)
  other arithmetic  53 us (6%)
  local copies, waits for them, and re-layouts  31.4 us (3%)
  between operations  14.3 us (2%)
    pallas_call x2, Pallas kernels, reduce_grads(): pl.pallas_call(functools.partial(reduce_kernel, chunks, len(sources), len...  165 us
    pallas_call x2, Pallas kernels, fetch(): pl.pallas_call(functools.partial(fetch_kernel, chunks, [n for _, n in pie...  144 us
    dot_general x39, matrix products, product(): return jnp.einsum(form, left, right, preferred_element_type=jnp.float32)  135 us
    pallas_call x1, Pallas kernels, spread(): pl.pallas_call(spread_kernel, out_shape=jax.ShapeDtypeStruct(own.shape[:1...  70.1 us
    pallas_call x1, Pallas kernels, sum_grams(): pl.pallas_call(gram_kernel, out_shape=[jax.ShapeDtypeStruct(grams.shape,...  64.9 us
    pallas_call x1, Pallas kernels, update(): pl.pallas_call(update_kernel, grid_spec=pltpu.PrefetchScalarGridSpec(num_...  35.8 us
    pallas_call x1, Pallas kernels, schulz(): pl.pallas_call(schulz_kernel, out_shape=jax.ShapeDtypeStruct(rows.shape,...  31.8 us
    pallas_call x2, Pallas kernels, attend_back(): pl.pallas_call(attend_back_kernel, grid=(parts, D // GROUP), in_specs=att...  29.7 us

profile of v3, /device:TPU:0, one launch (start us, length us, event | category | flops | bytes accessed | tf_op | source)
XLA Modules:
  0.0 889.4 jit_solution(15192430095889543454)
XLA Ops:
  0.7 72.9 %fetch_1.1 = (bf16[1,4,8,24,768]{4,3,2,1,0:T(8,128)(2,1)}, bf16[3,4,8,24,768]{4,3,2,1,0:T(8,128)(2,1)}, bf16[1,4,8,24,768]{4,3,2,1,0:T(8,128)(2,1)}, bf16[4,4,8,...) custom-call(f32[26,8,24,768]{3,2,1,0:T(8,128)} %bitcast.255), custom_call_target="tpu_custom_call" | custom-call | tf_op jit(solution)/shard_map/fetch_1/pallas_call | solution.py:215
  74.4 3.3 fusion.220
  81.3 4.5 convolution_bitcast_fusion.1.query.key.value
  88.5 11.3 %attend.2 = bf16[768,512]{1,0:T(8,128)(2,1)} custom-call(f32[2304,512]{1,0:T(8,128)} %convolution_bitcast_fusion.1.query.key.value, f32[2304,512]{1,0:T(8,128)} %convolution_bitcast_fusion.1.query.key.value, f32[2304,512]{1,0:T(8,128)} %convolution_bitcast_fusion.1.query.key.value, f32[768,1]{1,0:T(8,128)} %copy.100.gain_query, f32[768,1]{1,0:T(8,128)} %copy.101.gain_key, ...), custom_call_target="tpu_custom_call" | custom-call | tf_op jit(solution)/shard_map/attend/pallas_call | solution.py:1097
  99.8 2.4 fusion.216
  102.6 5.9 fusion.194
  108.6 3.9 fusion.217
  112.5 71.2 %fetch_3.1 = (bf16[3,4,8,24,768]{4,3,2,1,0:T(8,128)(2,1)}, bf16[1,4,8,24,768]{4,3,2,1,0:T(8,128)(2,1)}, bf16[4,4,8,24,768]{4,3,2,1,0:T(8,128)(2,1)}, bf16[4,4,8,...) custom-call(f32[26,8,24,768]{3,2,1,0:T(8,128)} %bitcast.256), custom_call_target="tpu_custom_call" | custom-call | tf_op jit(solution)/shard_map/fetch_3/pallas_call | solution.py:215
  184.1 6.5 convolution_bitcast_fusion.query.key.value
  192.5 11.3 %attend.3 = bf16[768,512]{1,0:T(8,128)(2,1)} custom-call(f32[2304,512]{1,0:T(8,128)} %convolution_bitcast_fusion.query.key.value, f32[2304,512]{1,0:T(8,128)} %convolution_bitcast_fusion.query.key.value, f32[2304,512]{1,0:T(8,128)} %convolution_bitcast_fusion.query.key.value, f32[768,1]{1,0:T(8,128)} %copy.81.gain_query, f32[768,1]{1,0:T(8,128)} %copy.82.gain_key, ...), custom_call_target="tpu_custom_call" | custom-call | tf_op jit(solution)/shard_map/attend/pallas_call | solution.py:1097
  203.8 2.4 fusion.218
  206.7 14.3 %fusion.195 = f32[512,3072]{1,0:T(8,128)S(1)} fusion(bf16[3072,768]{1,0:T(8,128)(2,1)} %bitcast.318, f32[512,768]{1,0:T(8,128)S(1)} %get-tuple-element.183, f32[768]{0:T(1024)S(1)} %get-tuple-element.142, f32[768]{0:T(1024)S(1)} %get-tuple-element.141, f32[512]{0:T(512)S(1)} %fusion.174, f32[512]{0:T(512)S(1)} %broadcast_multiply_fusion.3), kind=kOutput, calls=%fused_computation.423 | convolution fusion | flops 2417885184 | bytes 12593152 | tf_op jit(solution)/shard_map/sd,rd->sr/dot_general | solution.py:46
  221.0 3.8 fusion.219
  231.0 2.3 copy.86
  233.3 1.7 fusion.222
  235.2 1.9 fusion.24
  237.3 1.7 multiply_reduce_fusion.19
  239.9 8.1 swap_10.1
  248.8 13.0 %convert_reduce_fusion = s32[64,8000]{1,0:T(8,128)} fusion(s32[64,16]{1,0:T(8,128)S(1)} %bitcast.300), kind=kLoop, calls=%fused_computation | loop fusion | flops 24064000 | bytes 2052096 | tf_op jit(solution)/shard_map/reduce_sum | solution.py:1278
  261.9 7.7 fusion.25
  269.6 9.2 %swap_11.1 = f32[4,16,768]{2,1,0:T(8,128)} custom-call(f32[4,16,768]{2,1,0:T(8,128)} %bitcast.298), custom_call_target="tpu_custom_call" | custom-call | tf_op jit(solution)/shard_map/swap_11/pallas_call | solution.py:315
  280.7 24.0 %share_8.1 = bf16[8,4,48,768]{3,2,1,0:T(8,128)(2,1)} custom-call(bf16[48,768]{1,0:T(8,128)(2,1)} %bitcast.299), custom_call_target="tpu_custom_call" | custom-call | tf_op jit(solution)/shard_map/share_8/pallas_call | solution.py:279
  313.3 1.8 fusion.43
  315.1 2.0 fusion.205
  324.8 2.3 fusion.18
  327.1 2.3 copy.94
  329.4 1.7 fusion.62
  331.3 1.8 fusion.19
  333.1 2.3 copy.92
  338.4 9.6 %fusion.13 = bf16[512,3072]{1,0:T(8,128)(2,1)S(1)} fusion(f32[512,3072]{1,0:T(8,128)} %copy-done.117, bf16[3072,768]{1,0:T(8,128)(2,1)} %bitcast.322, f32[512,768]{1,0:T(8,128)S(1)} %get-tuple-element.108, f32[512]{0:T(512)S(1)} %negate_multiply_fusion.4), kind=kOutput, calls=%fused_computation.19 | convolution fusion | flops 2448162816 | bytes 15730688 | tf_op jit(solution)/shard_map/sd,rd->sr/dot_general | solution.py:46
  348.2 2.9 multiply_reduce_fusion
  353.1 1.7 fusion.16.grad
  354.8 14.8 %attend_back.2 = (bf16[3,768,512]{2,1,0:T(8,128)(2,1)}, f32[2,2,768,1]{3,2,1,0:T(8,128)}) custom-call(f32[2304,512]{1,0:T(8,128)} %convolution_bitcast_fusion.query.key.value, f32[2304,512]{1,0:T(8,128)} %convolution_bitcast_fusion.query.key.value, f32[2304,512]{1,0:T(8,128)} %convolution_bitcast_fusion.query.key.value, f32[768,1]{1,0:T(8,128)} %copy.81.gain_query, ...), custom_call_target="tpu_custom_call" | custom-call | tf_op jit(solution)/shard_map/attend_back/pallas_call | solution.py:1109
  369.6 5.7 multiply_reduce_fusion.1
  376.4 9.4 %fusion.6 = bf16[512,3072]{1,0:T(8,128)(2,1)S(1)} fusion(f32[512,3072]{1,0:T(8,128)} %copy-done.118, bf16[3072,768]{1,0:T(8,128)(2,1)} %bitcast.314, f32[512,768]{1,0:T(8,128)S(1)} %add_add_fusion.7), kind=kOutput, calls=%fused_computation.12 | convolution fusion | flops 2447769600 | bytes 15728640 | tf_op jit(solution)/shard_map/sd,rd->sr/dot_general | solution.py:46
  386.0 2.9 multiply_reduce_fusion.2
  391.1 1.7 fusion.17.grad
  392.9 14.9 %attend_back.3 = (bf16[3,768,512]{2,1,0:T(8,128)(2,1)}, f32[2,2,768,1]{3,2,1,0:T(8,128)}) custom-call(f32[2304,512]{1,0:T(8,128)} %convolution_bitcast_fusion.1.query.key.value, f32[2304,512]{1,0:T(8,128)} %convolution_bitcast_fusion.1.query.key.value, f32[2304,512]{1,0:T(8,128)} %convolution_bitcast_fusion.1.query.key.value, f32[768,1]{1,0:T(8,128)} %copy.100.gain_query, ...), custom_call_target="tpu_custom_call" | custom-call | tf_op jit(solution)/shard_map/attend_back/pallas_call | solution.py:1109
  407.9 5.8 convolution_convert_fusion.5
  413.7 1.8 convolution_convert_fusion.8
  415.5 4.7 convolution_convert_fusion.3
  420.2 5.3 convolution_convert_fusion.2
  425.6 2.4 multiply_reduce_fusion.3
  428.9 1.8 convolution_convert_fusion.7
  435.0 1.7 reduce_sum.685
  436.7 1.7 reduce_sum.690
  439.2 1.9 fusion.107
  443.9 86.0 %reduce_4.1 = (f32[13,24,768]{2,1,0:T(8,128)}, f32[1,8,256]{2,1,0:T(8,128)}) custom-call(bf16[3,4,2,2,2,24,768]{6,5,4,3,2,1,0:T(8,128)(2,1)} %bitcast.286, bf16[1,4,2,2,2,24,768]{6,5,4,3,2,1,0:T(8,128)(2,1)} %bitcast.283, bf16[4,4,2,2,2,24,768]{6,5,4,3,2,1,0:T(8,128)(2,1)} %bitcast.281, bf16[4,4,2,2,2,24,768]{6,5,4,3,2,1,0:T(8,128)(2,1)} %bitcast.282, ...), custom_call_target="tpu_custom_call" | custom-call | tf_op jit(solution)/shard_map/reduce_4/pallas_call | solution.py:515
  529.9 2.4 fusion.208
  532.3 4.0 convolution_convert_fusion.4
  536.3 1.8 convolution_convert_fusion.6
  538.2 4.7 convolution_convert_fusion.1
  542.9 5.1 convolution_convert_fusion
  549.5 79.1 %reduce_5.1 = f32[13,24,768]{2,1,0:T(8,128)} custom-call(bf16[3,4,2,2,2,24,768]{6,5,4,3,2,1,0:T(8,128)(2,1)} %bitcast.285, bf16[1,4,2,2,2,24,768]{6,5,4,3,2,1,0:T(8,128)(2,1)} %bitcast.275, bf16[4,4,2,2,2,24,768]{6,5,4,3,2,1,0:T(8,128)(2,1)} %bitcast.277, bf16[4,4,2,2,2,24,768]{6,5,4,3,2,1,0:T(8,128)(2,1)} %bitcast.278, ...), custom_call_target="tpu_custom_call" | custom-call | tf_op jit(solution)/shard_map/reduce_5/pallas_call | solution.py:515
  628.6 2.4 fusion.207
  634.1 25.0 %meet_9.1 = (f32[8,4,16,256]{3,2,1,0:T(8,128)}, bf16[4,8,24,768]{3,2,1,0:T(8,128)(2,1)}) custom-call(f32[16,256]{1,0:T(8,128)} %concatenate.34.own, bf16[8,4,24,768]{3,2,1,0:T(8,128)(2,1)} %bitcast.292), custom_call_target="tpu_custom_call" | custom-call | tf_op jit(solution)/shard_map/meet_9/pallas_call | solution.py:667
  664.5 1.6 convert_multiply_fusion
  670.0 4.5 dynamic-slice_select_fusion.3
  674.5 1.8 fusion.197
  679.4 2.5 pad_maximum_fusion.gram
  683.0 64.9 %gram_12.1 = (f32[2,768,768]{2,1,0:T(8,128)}, bf16[26,8,24,768]{3,2,1,0:T(8,128)(2,1)}) custom-call(f32[2,768,768]{2,1,0:T(8,128)} %pad_maximum_fusion.gram, bf16[26,24,768]{2,1,0:T(8,128)(2,1)} %pad_maximum_fusion.1.own), custom_call_target="tpu_custom_call" | custom-call | tf_op jit(solution)/shard_map/gram_12/pallas_call | solution.py:839
  747.9 31.8 %schulz.1.own = bf16[4,192,768]{2,1,0:T(8,128)(2,1)} custom-call(s32[1]{0:T(128)} %dynamic_slice.60.two, f32[2,768,768]{2,1,0:T(8,128)} %get-tuple-element.51.gram, f32[4,192,768]{2,1,0:T(8,128)} %get-tuple-element.96.rows), custom_call_target="tpu_custom_call" | custom-call | tf_op jit(solution)/shard_map/schulz/pallas_call | solution.py:939
  779.7 70.1 %spread_13.1.turned = bf16[4,8,192,768]{3,2,1,0:T(8,128)(2,1)} custom-call(bf16[4,192,768]{2,1,0:T(8,128)(2,1)} %schulz.1.own), custom_call_target="tpu_custom_call" | custom-call | tf_op jit(solution)/shard_map/spread_13/pallas_call | solution.py:606
  849.8 35.8 %update.1 = (f32[26,192,768]{2,1,0:T(8,128)}, f32[26,192,768]{2,1,0:T(8,128)}, bf16[26,192,768]{2,1,0:T(8,128)(2,1)}) custom-call(s32[52]{0:T(128)} %constant.242.clone.table, f32[26]{0:T(128)} %constant.243.clone.scale, f32[1]{0:T(128)} %bitcast.79.clip, f32[26,192,768]{2,1,0:T(8,128)} %momenta.1, bf16[26,192,768]{2,1,0:T(8,128)(2,1)} %bitcast.265, ...), custom_call_target="tpu_custom_call" | custom-call | tf_op jit(solution)/shard_map/update/pallas_call | solution.py:971
  (475 shorter events, 63.3 us)
Async XLA Ops:
  0.6 73.7 %copy-start = (bf16[2,1,256,768]{3,2,1,0:T(8,128)(2,1)S(1)}, bf16[2,1,256,768]{3,2,1,0:T(8,128)(2,1)}, u32[]{:S(2)}) copy-start(bf16[2,1,256,768]{3,2,1,0:T(8,128)(2,1)} %param.19) | copy-start | bytes 2359300
  0.7 72.9 %copy-start.46 = (s32[2,1,4,256]{3,2,1,0:T(4,128)S(1)}, s32[2,1,4,256]{3,2,1,0:T(4,128)}, u32[]{:S(2)}) copy-start(s32[2,1,4,256]{3,2,1,0:T(4,128)} %param.20) | copy-start | bytes 24580
  80.1 19.7 %copy-start.1 = (f32[512,768]{1,0:T(8,128)}, f32[512,768]{1,0:T(8,128)S(1)}, u32[]{:S(2)}) copy-start(f32[512,768]{1,0:T(8,128)S(1)} %get-tuple-element.177) | copy-start | bytes 4718596
  80.2 22.4 %copy-start.78 = (f32[768]{0:T(1024)}, f32[768]{0:T(1024)S(1)}, u32[]{:S(2)}) copy-start(f32[768]{0:T(1024)S(1)} %get-tuple-element.137) | copy-start | bytes 9220
  80.2 22.4 %copy-start.99 = (f32[768]{0:T(1024)}, f32[768]{0:T(1024)S(1)}, u32[]{:S(2)}) copy-start(f32[768]{0:T(1024)S(1)} %get-tuple-element.138) | copy-start | bytes 9220
  80.3 103.8 %copy-start.74 = (f32[768]{0:T(1024)}, f32[768]{0:T(1024)S(1)}, u32[]{:S(2)}) copy-start(f32[768]{0:T(1024)S(1)} %get-tuple-element.139) | copy-start | bytes 9220
  80.3 103.8 %copy-start.97 = (f32[768]{0:T(1024)}, f32[768]{0:T(1024)S(1)}, u32[]{:S(2)}) copy-start(f32[768]{0:T(1024)S(1)} %get-tuple-element.140) | copy-start | bytes 9220
  80.3 126.4 %copy-start.72 = (f32[768]{0:T(1024)}, f32[768]{0:T(1024)S(1)}, u32[]{:S(2)}) copy-start(f32[768]{0:T(1024)S(1)} %get-tuple-element.141) | copy-start | bytes 9220
  80.3 126.4 %copy-start.95 = (f32[768]{0:T(1024)}, f32[768]{0:T(1024)S(1)}, u32[]{:S(2)}) copy-start(f32[768]{0:T(1024)S(1)} %get-tuple-element.142) | copy-start | bytes 9220
  80.3 144.9 %copy-start.39 = (f32[768]{0:T(1024)}, f32[768]{0:T(1024)S(1)}, u32[]{:S(2)}) copy-start(f32[768]{0:T(1024)S(1)} %get-tuple-element.143) | copy-start | bytes 9220
  80.3 148.2 %copy-start.43 = (f32[768]{0:T(1024)}, f32[768]{0:T(1024)S(1)}, u32[]{:S(2)}) copy-start(f32[768]{0:T(1024)S(1)} %get-tuple-element.145) | copy-start | bytes 9220
  81.3 6.4 copy-start.33
  102.2 6.3 copy-start.13
  102.3 6.3 copy-start.60
  102.3 6.3 slice-start.2
  102.6 6.0 copy-start.64
  102.6 6.0 copy-start.88
  102.6 6.0 slice-start.3
  112.5 91.3 %copy-start.7 = (f32[512,768]{1,0:T(8,128)}, f32[512,768]{1,0:T(8,128)S(1)}, u32[]{:S(2)}) copy-start(f32[512,768]{1,0:T(8,128)S(1)} %get-tuple-element.181) | copy-start | bytes 4718596
  183.7 6.8 copy-start.54
  184.1 6.5 copy-start.66
  184.1 6.5 copy-start.82
  206.3 14.7 %copy-start.10 = (f32[512,768]{1,0:T(8,128)}, f32[512,768]{1,0:T(8,128)S(1)}, u32[]{:S(2)}) copy-start(f32[512,768]{1,0:T(8,128)S(1)} %get-tuple-element.183) | copy-start | bytes 4718596
  206.3 14.7 %copy-start.56 = (f32[512]{0:T(512)}, f32[512]{0:T(512)S(1)}, u32[]{:S(2)}) copy-start(f32[512]{0:T(512)S(1)} %broadcast_multiply_fusion.3) | copy-start | bytes 6148
  206.3 14.7 %slice-start.6 = ((s8[4718592]{0:T(1024)(128)(4,1)}), s8[4194304]{0:T(1024)(128)(4,1)S(1)}, s32[]{:S(2)}) async-start(s8[4718592]{0:T(1024)(128)(4,1)} %bitcast.323), calls=%async_computation.6 | async-start | bytes 8388608
  206.6 14.4 %copy-start.68 = (f32[512]{0:T(512)}, f32[512]{0:T(512)S(1)}, u32[]{:S(2)}) copy-start(f32[512]{0:T(512)S(1)} %multiply_reduce_fusion.10) | copy-start | bytes 6148
  206.6 14.3 %copy-start.84 = (f32[512]{0:T(512)}, f32[512]{0:T(512)S(1)}, u32[]{:S(2)}) copy-start(f32[512]{0:T(512)S(1)} %fusion.174) | copy-start | bytes 6148
  206.7 14.4 %slice-start.7 = ((s8[4718592]{0:T(1024)(128)(4,1)}), s8[524288]{0:T(1024)(128)(4,1)S(1)}, s32[]{:S(2)}) async-start(s8[4718592]{0:T(1024)(128)(4,1)} %bitcast.323), calls=%async_computation.7 | async-start | bytes 1048576
  233.3 6.0 copy-start.90
  238.9 41.0 %copy-start.105 = (f32[16]{0:T(128)}, f32[16]{0:T(128)S(1)}, u32[]{:S(2)}) copy-start(f32[16]{0:T(128)S(1)} %get-tuple-element.186) | copy-start | bytes 196
  306.4 6.9 copy-start.107
  337.8 10.3 %slice-start.4 = ((s8[4718592]{0:T(1024)(128)(4,1)}), s8[4194304]{0:T(1024)(128)(4,1)S(1)}, s32[]{:S(2)}) async-start(s8[4718592]{0:T(1024)(128)(4,1)} %bitcast.319), calls=%async_computation.4 | async-start | bytes 8388608
  338.4 13.4 %copy-start.19 = (f32[512,768]{1,0:T(8,128)}, f32[512,768]{1,0:T(8,128)S(1)}, u32[]{:S(2)}) copy-start(f32[512,768]{1,0:T(8,128)S(1)} %get-tuple-element.108) | copy-start | bytes 4718596
  338.4 9.7 %copy-start.11 = (f32[512,768]{1,0:T(8,128)S(1)}, f32[512,768]{1,0:T(8,128)}, u32[]{:S(2)}) copy-start(f32[512,768]{1,0:T(8,128)} %copy-done.10) | copy-start | bytes 4718596
  338.4 9.7 %copy-start.57 = (f32[512]{0:T(512)S(1)}, f32[512]{0:T(512)}, u32[]{:S(2)}) copy-start(f32[512]{0:T(512)} %copy-done.56) | copy-start | bytes 6148
  338.4 9.7 %copy-start.73 = (f32[768]{0:T(1024)S(1)}, f32[768]{0:T(1024)}, u32[]{:S(2)}) copy-start(f32[768]{0:T(1024)} %copy-done.72) | copy-start | bytes 9220
  338.4 9.7 %copy-start.85 = (f32[512]{0:T(512)S(1)}, f32[512]{0:T(512)}, u32[]{:S(2)}) copy-start(f32[512]{0:T(512)} %copy-done.84) | copy-start | bytes 6148
  338.4 9.7 %slice-start.5 = ((s8[4718592]{0:T(1024)(128)(4,1)}), s8[524288]{0:T(1024)(128)(4,1)S(1)}, s32[]{:S(2)}) async-start(s8[4718592]{0:T(1024)(128)(4,1)} %bitcast.319), calls=%async_computation.5 | async-start | bytes 1048576
  353.1 22.9 %copy-start.3 = (f32[512,768]{1,0:T(8,128)}, f32[512,768]{1,0:T(8,128)S(1)}, u32[]{:S(2)}) copy-start(f32[512,768]{1,0:T(8,128)S(1)} %add_add_fusion.8) | copy-start | bytes 4718596
  354.8 14.8 %copy-start.55 = (f32[512]{0:T(512)S(1)}, f32[512]{0:T(512)}, u32[]{:S(2)}) copy-start(f32[512]{0:T(512)} %copy-done.54) | copy-start | bytes 6148
  354.8 14.8 %copy-start.75 = (f32[768]{0:T(1024)S(1)}, f32[768]{0:T(1024)}, u32[]{:S(2)}) copy-start(f32[768]{0:T(1024)} %copy-done.74) | copy-start | bytes 9220
  354.8 14.8 %copy-start.83 = (f32[512]{0:T(512)S(1)}, f32[512]{0:T(512)}, u32[]{:S(2)}) copy-start(f32[512]{0:T(512)} %copy-done.82) | copy-start | bytes 6148
  376.0 9.8 %slice-start = ((s8[4718592]{0:T(1024)(128)(4,1)}), s8[4194304]{0:T(1024)(128)(4,1)S(1)}, s32[]{:S(2)}) async-start(s8[4718592]{0:T(1024)(128)(4,1)} %bitcast.311), calls=%async_computation | async-start | bytes 8388608
  376.3 13.3 %copy-start.21 = (f32[512,768]{1,0:T(8,128)}, f32[512,768]{1,0:T(8,128)S(1)}, u32[]{:S(2)}) copy-start(f32[512,768]{1,0:T(8,128)S(1)} %add_add_fusion.7) | copy-start | bytes 4718596
  376.4 9.5 %copy-start.14 = (f32[512,768]{1,0:T(8,128)S(1)}, f32[512,768]{1,0:T(8,128)}, u32[]{:S(2)}) copy-start(f32[512,768]{1,0:T(8,128)} %copy-done.13) | copy-start | bytes 4718596
  376.4 9.5 %copy-start.61 = (f32[512]{0:T(512)S(1)}, f32[512]{0:T(512)}, u32[]{:S(2)}) copy-start(f32[512]{0:T(512)} %copy-done.60) | copy-start | bytes 6148
  376.4 9.5 %copy-start.79 = (f32[768]{0:T(1024)S(1)}, f32[768]{0:T(1024)}, u32[]{:S(2)}) copy-start(f32[768]{0:T(1024)} %copy-done.78) | copy-start | bytes 9220
  376.4 9.5 %copy-start.89 = (f32[512]{0:T(512)S(1)}, f32[512]{0:T(512)}, u32[]{:S(2)}) copy-start(f32[512]{0:T(512)} %copy-done.88) | copy-start | bytes 6148
  376.4 9.5 %slice-start.1 = ((s8[4718592]{0:T(1024)(128)(4,1)}), s8[524288]{0:T(1024)(128)(4,1)S(1)}, s32[]{:S(2)}) async-start(s8[4718592]{0:T(1024)(128)(4,1)} %bitcast.311), calls=%async_computation.1 | async-start | bytes 1048576
  392.9 15.0 %copy-start.2 = (f32[512,768]{1,0:T(8,128)S(1)}, f32[512,768]{1,0:T(8,128)}, u32[]{:S(2)}) copy-start(f32[512,768]{1,0:T(8,128)} %copy-done.1) | copy-start | bytes 4718596
  392.9 15.0 %copy-start.59 = (f32[512]{0:T(512)S(1)}, f32[512]{0:T(512)}, u32[]{:S(2)}) copy-start(f32[512]{0:T(512)} %copy-done.58) | copy-start | bytes 6148
  392.9 15.0 %copy-start.77 = (f32[768]{0:T(1024)S(1)}, f32[768]{0:T(1024)}, u32[]{:S(2)}) copy-start(f32[768]{0:T(1024)} %copy-done.76) | copy-start | bytes 9220
  392.9 15.0 %copy-start.87 = (f32[512]{0:T(512)S(1)}, f32[512]{0:T(512)}, u32[]{:S(2)}) copy-start(f32[512]{0:T(512)} %copy-done.86) | copy-start | bytes 6148
  392.9 15.0 %copy-start.102 = (f32[768]{0:T(1024)S(1)}, f32[768]{0:T(1024)}, u32[]{:S(2)}) copy-start(f32[768]{0:T(1024)} %copy-done.101) | copy-start | bytes 9220
  407.9 7.6 copy-start.122
  407.9 12.3 %slice-start.10 = ((s8[6291456]{0:T(1024)(128)(4,1)}), s8[4194304]{0:T(1024)(128)(4,1)S(1)}, s32[]{:S(2)}) async-start(s8[6291456]{0:T(1024)(128)(4,1)} %bitcast.335), calls=%async_computation.10 | async-start | bytes 8388608
  443.9 88.4 %copy-start.9 = (f32[512,768]{1,0:T(8,128)S(1)}, f32[512,768]{1,0:T(8,128)}, u32[]{:S(2)}) copy-start(f32[512,768]{1,0:T(8,128)} %copy-done.7) | copy-start | bytes 4718596
  443.9 88.4 %copy-start.98 = (f32[768]{0:T(1024)S(1)}, f32[768]{0:T(1024)}, u32[]{:S(2)}) copy-start(f32[768]{0:T(1024)} %copy-done.97) | copy-start | bytes 9220
  443.9 88.4 %copy-start.114 = (bf16[3,768,512]{2,1,0:T(8,128)(2,1)S(1)}, bf16[3,768,512]{2,1,0:T(8,128)(2,1)}, u32[]{:S(2)}) copy-start(bf16[3,768,512]{2,1,0:T(8,128)(2,1)} %get-tuple-element.42) | copy-start | bytes 7077892
  532.3 10.6 %slice-start.8 = ((s8[6291456]{0:T(1024)(128)(4,1)}), s8[4194304]{0:T(1024)(128)(4,1)S(1)}, s32[]{:S(2)}) async-start(s8[6291456]{0:T(1024)(128)(4,1)} %bitcast.333), calls=%async_computation.8 | async-start | bytes 8388608
  549.5 82.8 %copy-start.91 = (f32[1,8,256]{2,1,0:T(8,128)S(1)}, f32[1,8,256]{2,1,0:T(8,128)}, u32[]{:S(2)}) copy-start(f32[1,8,256]{2,1,0:T(8,128)} %get-tuple-element.46) | copy-start | bytes 24580
  849.8 36.7 %copy-start.30 = (f32[79,768]{1,0:T(8,128)S(1)}, f32[79,768]{1,0:T(8,128)}, u32[]{:S(2)}) copy-start(f32[79,768]{1,0:T(8,128)} %param.26) | copy-start | bytes 728068
  849.8 36.7 %copy-start.31 = (f32[79,768]{1,0:T(8,128)S(1)}, f32[79,768]{1,0:T(8,128)}, u32[]{:S(2)}) copy-start(f32[79,768]{1,0:T(8,128)} %param.28) | copy-start | bytes 728068
  849.8 36.7 %copy-start.32 = (f32[79,768]{1,0:T(8,128)S(1)}, f32[79,768]{1,0:T(8,128)}, u32[]{:S(2)}) copy-start(f32[79,768]{1,0:T(8,128)} %param.27) | copy-start | bytes 728068
  (71 other events, 220.9 us)

commit v4 on v3

--- a/solution.py
+++ b/solution.py
@@ -46,12 +46,6 @@
     return jnp.einsum(form, left, right, preferred_element_type=jnp.float32)
 
 
-def layer_norm(value, gain, shift):
-    centred = value - jnp.mean(value, -1, keepdims=True)
-    spread = jnp.mean(centred * centred, -1, keepdims=True)
-    return centred * lax.rsqrt(spread + 1e-06) * gain + shift
-
-
 def unit_rows(value):
     return (
         value
@@ -70,21 +64,6 @@
     )
 
 
-def pooling(segment):
-    member = segment[None, :] == jnp.arange(IMGS, dtype=jnp.int32)[:, None]
-
-    def pooled_of(final, query):
-        split = final.reshape(-1, HEADS, HD)
-        logits = jnp.einsum("shd,hd->hs", split, query.reshape(HEADS, HD), precision=HIGH) * (
-            1.0 / math.sqrt(HD)
-        )
-        logits = jnp.where(member[:, None, :], logits[None], -1e30)
-        share = jax.nn.softmax(logits, -1)
-        return jnp.einsum("khs,shd->khd", share, split, precision=HIGH).reshape(IMGS, -1)
-
-    return pooled_of
-
-
 def flip(index, bit):
     return index + bit - 2 * bit * lax.rem(index // bit, 2)
 
@@ -102,9 +81,12 @@
     return (d, z, [lax.rem(z + step, 4) for step in range(4)])
 
 
-def fetch_kernel(chunks, sizes, weights, *refs):
+def fetch_kernel(chunks, sizes, later, weights, ids, *refs):
     outs = refs[: len(sizes)]
-    full, low, load_sem, store_sem, send, recv = refs[len(sizes) :]
+    all_ids, slices = refs[len(sizes) : len(sizes) + 2]
+    full, low, held, load_sem, store_sem, send, recv, later_sem, id_send, id_recv = refs[
+        len(sizes) + 2 :
+    ]
     d, z, zs = places()
     sib, near_x, near_y = flip(d, 1), flip(d, 2), flip(d, 4)
     diagonal = flip(near_x, 4)
@@ -117,8 +99,30 @@
             )
         )
         loads[k].start()
+    later_loads = [
+        pltpu.make_async_copy(
+            weights.at[pl.ds(first, n), d], held.at[pl.ds(place, n)], later_sem.at[i]
+        )
+        for i, (first, place, n) in enumerate(later)
+    ]
+    for copy in later_loads:
+        copy.start()
     greet([(d, zs[1]), (d, zs[2]), (d, zs[3]), (sib, z), (near_x, z), (near_y, z)])
     pending = []
+    all_ids[z] = ids[...]
+    id_copies = []
+    for o in (1, 2, 3):
+        id_copies.append(
+            pltpu.make_async_remote_copy(
+                src_ref=ids,
+                dst_ref=all_ids.at[z],
+                send_sem=id_send.at[o - 1],
+                recv_sem=id_recv.at[o - 1],
+                device_id=(d, zs[o]),
+                device_id_type=MESH,
+            )
+        )
+        id_copies[-1].start()
 
     def push(k, slot, first, n, zz, dd, to, source=None):
         out = outs[chunks[k][1]]
@@ -158,6 +162,13 @@
             )
         )
         stores[k].start()
+    for copy in later_loads:
+        copy.wait()
+
+    @pl.loop(0, held.shape[0])
+    def _(i):
+        slices[i] = held[i].astype(slices.dtype)
+
     along_x, along_y, turn_y, turn_x, last = {}, {}, {}, {}, []
     count = len(chunks)
     for step in range(count + 2):
@@ -196,15 +207,21 @@
         copy.wait_send()
     for copy in stores:
         copy.wait()
-
-
-def fetch(weights, pieces, collective):
+    for copy in id_copies:
+        copy.wait()
+
+
+def fetch(weights, pieces, later, ids, collective):
     depth, eighths = lax.axis_size("fsdp"), lax.axis_size("dp")
     if depth != 4 or eighths != 8:
-        return [
-            lax.all_gather(rounded(weights[a : a + n]), "fsdp", axis=1, tiled=True)
-            for a, n in pieces
-        ]
+        return (
+            [
+                lax.all_gather(rounded(weights[a : a + n]), "fsdp", axis=1, tiled=True)
+                for a, n in pieces
+            ],
+            lax.all_gather(ids, "fsdp", axis=0),
+            jnp.concatenate([rounded(weights[a : a + n]) for a, n in later], 0),
+        )
     blocks, rows, width = weights.shape
     part = (eighths, rows // eighths, width)
     chunks = []
@@ -212,79 +229,116 @@
         for first in range(0, n, 2):
             chunks.append((a + first, out, first, min(2, n - first)))
     total = sum(n for _, n in pieces)
+    later_places = []
+    for a, n in later:
+        later_places.append((a, sum(m for _, _, m in later_places), n))
+    later_total = sum(n for _, n in later)
     outs = pl.pallas_call(
-        functools.partial(fetch_kernel, chunks, [n for _, n in pieces]),
+        functools.partial(fetch_kernel, chunks, [n for _, n in pieces], later_places),
         out_shape=[
             jax.ShapeDtypeStruct((n, depth) + part, jnp.bfloat16) for _, n in pieces
+        ]
+        + [
+            jax.ShapeDtypeStruct((depth,) + ids.shape, ids.dtype),
+            jax.ShapeDtypeStruct((later_total,) + part[1:], jnp.bfloat16),
         ],
-        in_specs=[pl.BlockSpec(memory_space=pl.ANY)],
-        out_specs=[pl.BlockSpec(memory_space=pl.ANY)] * len(pieces),
+        in_specs=[pl.BlockSpec(memory_space=pl.ANY), pl.BlockSpec(memory_space=pltpu.VMEM)],
+        out_specs=[pl.BlockSpec(memory_space=pl.ANY)] * len(pieces)
+        + [pl.BlockSpec(memory_space=pltpu.VMEM)] * 2,
         scratch_shapes=[
             pltpu.VMEM((total,) + part, jnp.float32),
             pltpu.VMEM((total,) + part, jnp.bfloat16),
+            pltpu.VMEM((later_total,) + part[1:], jnp.float32),
             pltpu.SemaphoreType.DMA((len(chunks),)),
             pltpu.SemaphoreType.DMA((len(chunks),)),
             pltpu.SemaphoreType.DMA((len(chunks), 27)),
             pltpu.SemaphoreType.DMA((len(chunks), 27)),
+            pltpu.SemaphoreType.DMA((len(later),)),
+            pltpu.SemaphoreType.DMA((3,)),
+            pltpu.SemaphoreType.DMA((3,)),
         ],
         compiler_params=pltpu.CompilerParams(
             collective_id=collective, has_side_effects=True, vmem_limit_bytes=VMEM_LIMIT
         ),
         name=f"fetch_{collective}",
-    )(weights.reshape((blocks,) + part))
-    return [out.reshape(-1, width, width) for out in outs]
-
-
-def share_kernel(own, out, send, recv):
+    )(weights.reshape((blocks,) + part), ids)
+    return ([out.reshape(-1, width, width) for out in outs[:-2]], outs[-2], outs[-1])
+
+
+def gather_later(own):
+    depth, eighths = lax.axis_size("fsdp"), lax.axis_size("dp")
+    if depth != 4 or eighths != 8:
+        return lax.all_gather(own, "fsdp", axis=1, tiled=True)
+    return lax.all_gather(own, ("fsdp", "dp"), axis=1).reshape(-1, D, D)
+
+
+def share_kernel(count, *refs):
+    owns, outs, (send, recv) = (refs[:count], refs[count : 2 * count], refs[2 * count :])
     d, z, zs = places()
     sib, near_x, near_y = flip(d, 1), flip(d, 2), flip(d, 4)
     diagonal = flip(near_x, 4)
     greet(
         [(d, zs[1]), (d, zs[2]), (d, zs[3]), (sib, z), (near_x, z), (near_y, z), (diagonal, z)]
     )
-    out[d, z] = own[...]
-
-    def push(slot, source, target, to):
-        copy = pltpu.make_async_remote_copy(
-            src_ref=source,
-            dst_ref=target,
-            send_sem=send.at[slot],
-            recv_sem=recv.at[slot],
-            device_id=to,
-            device_id_type=MESH,
-        )
-        copy.start()
-        return copy
-
-    first = [push(o - 1, own, out.at[d, z], (d, zs[o])) for o in (1, 2, 3)]
-    for copy in first:
-        copy.wait_recv()
-    second = [
-        push(3 + i, out.at[d], out.at[d], (to, z)) for i, to in enumerate((near_x, near_y, diagonal))
-    ]
-    last = [push(6, out.at[d], out.at[d], (sib, z))]
+    for own, out in zip(owns, outs):
+        out[d, z] = own[...]
+    started = []
+
+    def push(slot, origin, to, first=False):
+        copies = []
+        for i in range(count):
+            copies.append(
+                pltpu.make_async_remote_copy(
+                    src_ref=owns[i] if first else outs[i].at[origin],
+                    dst_ref=outs[i].at[origin, z] if first else outs[i].at[origin],
+                    send_sem=send.at[i, slot],
+                    recv_sem=recv.at[i, slot],
+                    device_id=to,
+                    device_id_type=MESH,
+                )
+            )
+            copies[-1].start()
+        started.extend(copies)
+        return copies
+
+    def arrive(copies):
+        for copy in copies:
+            copy.wait_recv()
+
+    first = [push(o - 1, d, (d, zs[o]), True) for o in (1, 2, 3)]
+    for copies in first:
+        arrive(copies)
+    second = [push(3 + i, d, (to, z)) for i, to in enumerate((near_x, near_y, diagonal))]
+    last = [push(6, d, (sib, z))]
     for i, origin in enumerate((near_x, near_y, diagonal)):
-        second[i].wait_recv()
-        last.append(push(7 + i, out.at[origin], out.at[origin], (sib, z)))
-    for copy in last:
-        copy.wait_recv()
-    for copy in first + second + last:
+        arrive(second[i])
+        last.append(push(7 + i, origin, (sib, z)))
+    for copies in last:
+        arrive(copies)
+    for copy in started:
         copy.wait_send()
 
 
-def share(own, collective):
+def share(owns, collective):
     lanes, depth = lax.axis_size("dp"), lax.axis_size("fsdp")
     if depth != 4 or lanes != 8:
-        return lax.all_gather(own, ("dp", "fsdp"), axis=0).reshape((lanes, depth) + own.shape)
+        return [
+            lax.all_gather(own, ("dp", "fsdp"), axis=0).reshape((lanes, depth) + own.shape)
+            for own in owns
+        ]
+    count = len(owns)
     return pl.pallas_call(
-        share_kernel,
-        out_shape=jax.ShapeDtypeStruct((lanes, depth) + own.shape, own.dtype),
-        in_specs=[pl.BlockSpec(memory_space=pltpu.VMEM)],
-        out_specs=pl.BlockSpec(memory_space=pltpu.VMEM),
-        scratch_shapes=[pltpu.SemaphoreType.DMA((10,)), pltpu.SemaphoreType.DMA((10,))],
+        functools.partial(share_kernel, count),
+        out_shape=[jax.ShapeDtypeStruct((lanes, depth) + own.shape, own.dtype) for own in owns],
+        in_specs=[pl.BlockSpec(memory_space=pltpu.VMEM)] * count,
+        out_specs=[pl.BlockSpec(memory_space=pltpu.VMEM)] * count,
+        scratch_shapes=[
+            pltpu.SemaphoreType.DMA((count, 10)),
+            pltpu.SemaphoreType.DMA((count, 10)),
+        ],
         compiler_params=pltpu.CompilerParams(collective_id=collective, has_side_effects=True),
         name=f"share_{collective}",
-    )(own)
+    )(*owns)
 
 
 def swap_kernel(parts, out, send, recv):
@@ -363,8 +417,7 @@
         @pl.loop(0, self.n * count)
         def _(i):
             target, other = place(self.first + i // count, lax.rem(i, count))
-            total = self.held[target].astype(jnp.float32) + other.astype(jnp.float32)
-            self.held[target] = total.astype(self.held.dtype)
+            self.held[target] = self.held[target] + other
 
     def across_plane(self):
         d, z, zs, x, y, c = self.spots
@@ -426,10 +479,7 @@
         @pl.loop(0, self.n * 4)
         def _(i):
             b, zz = (self.first + i // 4, lax.rem(i, 4))
-            total = self.held[b, zz, y, x].astype(jnp.float32) + self.from_turn[b, zz].astype(
-                jnp.float32
-            )
-            self.ready[b, zz] = total.astype(self.ready.dtype)
+            self.ready[b, zz] = self.held[b, zz, y, x] + self.from_turn[b, zz]
 
         self.spread = [
             self.push(
@@ -592,34 +642,6 @@
     return (begin, forward, collect, finish)
 
 
-def spread_kernel(own, out, local_sem, send, recv):
-    d, z, _ = places()
-    greet([(flip(d, 1), z), (flip(d, 2), z), (flip(d, 4), z)])
-    for stage in spread_stages(own, out, local_sem, send, recv):
-        stage()
-
-
-def spread(own, collective):
-    lanes = lax.axis_size("dp")
-    if lax.axis_size("fsdp") != 4 or lanes != 8:
-        return lax.all_gather(own, "dp", axis=1)
-    return pl.pallas_call(
-        spread_kernel,
-        out_shape=jax.ShapeDtypeStruct(own.shape[:1] + (lanes,) + own.shape[1:], own.dtype),
-        in_specs=[pl.BlockSpec(memory_space=pltpu.VMEM)],
-        out_specs=pl.BlockSpec(memory_space=pl.ANY),
-        scratch_shapes=[
-            pltpu.SemaphoreType.DMA,
-            pltpu.SemaphoreType.DMA((14,)),
-            pltpu.SemaphoreType.DMA((14,)),
-        ],
-        compiler_params=pltpu.CompilerParams(
-            collective_id=collective, has_side_effects=True, vmem_limit_bytes=VMEM_LIMIT
-        ),
-        name=f"spread_{collective}",
-    )(own)
-
-
 def meet_kernel(own, parts, out, mine, local_sem, send, recv, part_send, part_recv):
     d, z, zs = places()
     sib, near_x, near_y = flip(d, 1), flip(d, 2), flip(d, 4)
@@ -956,6 +978,32 @@
     )(two, grams, rows)
 
 
+def spread_kernel(own, out, local_sem, send, recv):
+    d, z, _ = places()
+    greet([(flip(d, 1), z), (flip(d, 2), z), (flip(d, 4), z)])
+    for stage in spread_stages(own, out, local_sem, send, recv):
+        stage()
+
+
+def spread(own, collective):
+    lanes = lax.axis_size("dp")
+    return pl.pallas_call(
+        spread_kernel,
+        out_shape=jax.ShapeDtypeStruct(own.shape[:1] + (lanes,) + own.shape[1:], own.dtype),
+        in_specs=[pl.BlockSpec(memory_space=pltpu.VMEM)],
+        out_specs=pl.BlockSpec(memory_space=pl.ANY),
+        scratch_shapes=[
+            pltpu.SemaphoreType.DMA,
+            pltpu.SemaphoreType.DMA((14,)),
+            pltpu.SemaphoreType.DMA((14,)),
+        ],
+        compiler_params=pltpu.CompilerParams(
+            collective_id=collective, has_side_effects=True, vmem_limit_bytes=VMEM_LIMIT
+        ),
+        name=f"spread_{collective}",
+    )(own)
+
+
 def update_kernel(table, scale, clip, momenta, grads, weights, turned, momenta_new, weights_new, weights_low):
     b = pl.program_id(0)
     momenta_new[...] = MOMENT * momenta[...] + clip[0] * grads[...].astype(jnp.float32)
@@ -1023,68 +1071,124 @@
     return exponent * (1.0 / jnp.sum(exponent, 0, keepdims=True))
 
 
-def attend_kernel(query, key, value, gain_query, gain_key, rows, columns, out):
-    same = rows[0] == columns[0]
-    for head in range(GROUP // HD):
-        part = slice(head * HD, (head + 1) * HD)
-        query_low = normed_head(query[part], gain_query[part])[0].astype(jnp.bfloat16)
-        key_low = normed_head(key[part], gain_key[part])[0].astype(jnp.bfloat16)
-        share = head_shares(query_low, key_low, same).astype(jnp.bfloat16)
-        out[part] = jnp.dot(
-            value[part].astype(jnp.bfloat16), share, preferred_element_type=jnp.float32
-        ).astype(jnp.bfloat16)
-
-
-def attend_back_kernel(
-    query, key, value, gain_query, gain_key, rows, columns, grad, out, gain_out
+TILE = 256
+SLOPE = math.sqrt(2.0 / math.pi)
+CUBIC = 0.044715
+
+
+def tile_of(t, size=TILE):
+    return pl.ds(pl.multiple_of(t * size, size), size)
+
+
+def row_norm(value):
+    centred = value - jnp.mean(value, -1, keepdims=True)
+    scale = lax.rsqrt(jnp.mean(centred * centred, -1, keepdims=True) + 1e-06)
+    return (centred * scale, scale)
+
+
+def gelu_parts(value):
+    square = value * value
+    bend = jnp.tanh(SLOPE * value * (1.0 + CUBIC * square))
+    half = 0.5 + 0.5 * bend
+    slope = half + 0.5 * value * (1.0 - bend * bend) * SLOPE * (1.0 + 3.0 * CUBIC * square)
+    return (value * half, slope)
+
+
+def load_all(pairs, sem):
+    copies = [
+        pltpu.make_async_copy(source, target, sem.at[i])
+        for i, (source, target) in enumerate(pairs)
+    ]
+    for copy in copies:
+        copy.start()
+    return copies
+
+
+def norm_rows(source, gains, first, target):
+    gain, shift = (gains[first : first + 1], gains[first + 1 : first + 2])
+
+    @pl.loop(0, source.shape[0] // 64)
+    def _(t):
+        part = tile_of(t, 64)
+        target[part] = (row_norm(source[part])[0] * gain + shift).astype(target.dtype)
+
+
+def forward_kernel(
+    state,
+    gains,
+    gain_query,
+    gain_key,
+    rows,
+    columns,
+    mixing,
+    mixing_out,
+    upward,
+    down,
+    state_out,
+    middle,
+    mixed,
+    heads_low,
+    attended,
+    normed_low,
+    mixing_held,
+    out_held,
+    up_held,
+    down_held,
+    hidden,
+    sem,
 ):
-    same = rows[0] == columns[0]
-    for head in range(GROUP // HD):
-        part = slice(head * HD, (head + 1) * HD)
-        query_value, query_unit, query_scale = normed_head(query[part], gain_query[part])
-        key_value, key_unit, key_scale = normed_head(key[part], gain_key[part])
-        query_low = query_value.astype(jnp.bfloat16)
-        key_low = key_value.astype(jnp.bfloat16)
-        value_low = value[part].astype(jnp.bfloat16)
-        grad_low = grad[part]
-        share = head_shares(query_low, key_low, same)
-        out[2, part] = contract_last(grad_low, share.astype(jnp.bfloat16)).astype(jnp.bfloat16)
-        share_grad = contract_first(value_low, grad_low)
-        total = jnp.sum(share * share_grad, 0, keepdims=True)
-        score_low = (share * (share_grad - total) * (1.0 / math.sqrt(HD))).astype(jnp.bfloat16)
-        query_grad = jnp.dot(key_low, score_low, preferred_element_type=jnp.float32)
-        key_grad = contract_last(query_low, score_low)
-        for place, (delta, unit, scale, gain) in enumerate(
-            (
-                (query_grad, query_unit, query_scale, gain_query[part]),
-                (key_grad, key_unit, key_scale, gain_key[part]),
-            )
-        ):
-            gain_out[0, place, part] = jnp.sum(delta * unit, 1, keepdims=True)
-            delta = delta * gain
-            delta = delta - jnp.mean(delta, 0, keepdims=True) - unit * jnp.mean(
-                delta * unit, 0, keepdims=True
-            )
-            out[place, part] = (delta * scale).astype(jnp.bfloat16)
-
-
-def attention_specs(length):
-    def rows_of(first):
-        return pl.BlockSpec((GROUP, length), lambda b, group: (first + group, b))
-
-    count = D // GROUP
-    gain = pl.BlockSpec((GROUP, 1), lambda b, group: (group, 0))
-    return [rows_of(0), rows_of(count), rows_of(2 * count), gain, gain] + [
-        pl.BlockSpec((1, length, 1), lambda b, group: (b, 0, 0)),
-        pl.BlockSpec((1, 1, length), lambda b, group: (b, 0, 0)),
-    ]
-
-
-def attention_operands(mixed, gains, segment):
+    loads = load_all(
+        [(mixing, mixing_held), (mixing_out, out_held), (upward, up_held), (down, down_held)], sem
+    )
+    norm_rows(state, gains, 0, heads_low)
+    loads[0].wait()
+
+    @pl.loop(0, 3 * D // TILE)
+    def _(t):
+        mixed[tile_of(t)] = contract_last(mixing_held[tile_of(t)], heads_low[...])
+
+    parts, length = (rows.shape[0], rows.shape[1])
+    for b in range(parts):
+        same = rows[b] == columns[b]
+        tokens = slice(b * length, (b + 1) * length)
+
+        @pl.loop(0, D // GROUP)
+        def _(group):
+            for head in range(GROUP // HD):
+                first = group * GROUP + head * HD
+                part = pl.ds(pl.multiple_of(first, HD), HD)
+                query, key, value = [
+                    mixed[pl.ds(pl.multiple_of(place * D + first, HD), HD), tokens]
+                    for place in range(3)
+                ]
+                query_low = normed_head(query, gain_query[part])[0].astype(jnp.bfloat16)
+                key_low = normed_head(key, gain_key[part])[0].astype(jnp.bfloat16)
+                share = head_shares(query_low, key_low, same).astype(jnp.bfloat16)
+                attended[part, tokens] = jnp.dot(
+                    value.astype(jnp.bfloat16), share, preferred_element_type=jnp.float32
+                ).astype(jnp.bfloat16)
+
+    loads[1].wait()
+    for t in range(state.shape[0] // TILE):
+        part = slice(t * TILE, (t + 1) * TILE)
+        middle[part] = state[part] + contract_first(attended[:, part], out_held[...])
+    norm_rows(middle, gains, 2, normed_low)
+    loads[2].wait()
+
+    @pl.loop(0, FF // TILE)
+    def _(t):
+        value = contract_last(up_held[tile_of(t)], normed_low[...])
+        hidden[tile_of(t)] = gelu_parts(value)[0].astype(jnp.bfloat16)
+
+    loads[3].wait()
+    for t in range(state.shape[0] // TILE):
+        part = slice(t * TILE, (t + 1) * TILE)
+        state_out[part] = middle[part] + contract_first(hidden[:, part], down_held[...])
+
+
+def attention_operands(gains, segment):
     return (
-        mixed,
-        mixed,
-        mixed,
+        jnp.pad(gains[:4], ((0, 4), (0, 0))),
         gains[4][:, None],
         gains[5][:, None],
         segment[:, :, None],
@@ -1092,101 +1196,479 @@
     )
 
 
-def attend(mixed, gains, segment):
-    parts, length = segment.shape
+def whole(*memory):
+    kinds = {"v": pltpu.VMEM, "a": pl.ANY}
+    return [pl.BlockSpec(memory_space=kinds[kind]) for kind in memory[0]]
+
+
+def layer_forward(state, blocks, gains, segment):
+    tokens = state.shape[0]
+    weights = [block.reshape(-1, D) for block in blocks]
+    state_out, middle, mixed, heads_low, attended, normed_low = pl.pallas_call(
+        forward_kernel,
+        out_shape=[
+            jax.ShapeDtypeStruct((tokens, D), jnp.float32),
+            jax.ShapeDtypeStruct((tokens, D), jnp.float32),
+            jax.ShapeDtypeStruct((3 * D, tokens), jnp.float32),
+            jax.ShapeDtypeStruct((tokens, D), jnp.bfloat16),
+            jax.ShapeDtypeStruct((D, tokens), jnp.bfloat16),
+            jax.ShapeDtypeStruct((tokens, D), jnp.bfloat16),
+        ],
+        in_specs=whole("vvvvvvaaaa"),
+        out_specs=whole("vvvvvv"),
+        scratch_shapes=[pltpu.VMEM(weight.shape, jnp.bfloat16) for weight in weights]
+        + [pltpu.VMEM((FF, tokens), jnp.bfloat16), pltpu.SemaphoreType.DMA((4,))],
+        compiler_params=pltpu.CompilerParams(vmem_limit_bytes=VMEM_LIMIT),
+        name="layer_forward",
+    )(state, *attention_operands(gains, segment), *weights)
+    return (state_out, (state, middle, mixed, heads_low, attended, normed_low))
+
+
+def backward_kernel(
+    grad,
+    middle,
+    normed_low,
+    gains,
+    gain_query,
+    gain_key,
+    rows,
+    columns,
+    state,
+    mixed,
+    heads_low,
+    attended,
+    mixing,
+    mixing_out,
+    upward,
+    down,
+    grad_out,
+    gain_out,
+    head_gain_out,
+    grad_mixing,
+    grad_mixing_out,
+    grad_up,
+    grad_down,
+    state_held,
+    mixed_held,
+    heads_held,
+    attended_held,
+    mixing_held,
+    out_held,
+    up_held,
+    down_held,
+    low,
+    inner,
+    hidden_grad,
+    mixed_low,
+    attended_grad,
+    made_up,
+    made_down,
+    made_mixing,
+    made_out,
+    sem,
+    store_sem,
+):
+    loads = load_all(
+        [
+            (upward, up_held),
+            (down, down_held),
+            (mixing_out, out_held),
+            (attended, attended_held),
+            (mixed, mixed_held),
+            (heads_low, heads_held),
+            (mixing, mixing_held),
+            (state, state_held),
+        ],
+        sem,
+    )
+    stores = [
+        pltpu.make_async_copy(made_up, grad_up, store_sem.at[0]),
+        pltpu.make_async_copy(made_down, grad_down, store_sem.at[1]),
+        pltpu.make_async_copy(made_out, grad_mixing_out, store_sem.at[2]),
+        pltpu.make_async_copy(made_mixing, grad_mixing, store_sem.at[3]),
+    ]
+    tokens = grad.shape[0]
+    gain_out[...] = jnp.zeros_like(gain_out)
+
+    @pl.loop(0, tokens // 64)
+    def _(t):
+        low[tile_of(t, 64)] = grad[tile_of(t, 64)].astype(jnp.bfloat16)
+
+    loads[0].wait()
+    loads[1].wait()
+
+    @pl.loop(0, FF // TILE)
+    def _(t):
+        part = tile_of(t)
+        value, slope = gelu_parts(contract_last(up_held[part], normed_low[...]))
+        delta = (contract_last(down_held[part], low[...]) * slope).astype(jnp.bfloat16)
+        hidden_grad[part] = delta
+        made_down[part] = jnp.dot(
+            value.astype(jnp.bfloat16), low[...], preferred_element_type=jnp.float32
+        ).astype(jnp.bfloat16)
+        made_up[part] = jnp.dot(
+            delta, normed_low[...], preferred_element_type=jnp.float32
+        ).astype(jnp.bfloat16)
+
+    stores[0].start()
+    stores[1].start()
+    for t in range(tokens // TILE):
+        part = slice(t * TILE, (t + 1) * TILE)
+        inner[part] = contract_first(hidden_grad[:, part], up_held[...])
+
+    def norm_back(source, first, previous, target, target_low):
+        gain = gains[first : first + 1]
+
+        @pl.loop(0, tokens // 64)
+        def _(t):
+            part = tile_of(t, 64)
+            unit, scale = row_norm(source[part])
+            delta = inner[part]
+            gain_out[first : first + 1] += jnp.sum(delta * unit, 0, keepdims=True)
+            gain_out[first + 1 : first + 2] += jnp.sum(delta, 0, keepdims=True)
+            delta = delta * gain
+            delta = delta - jnp.mean(delta, -1, keepdims=True) - unit * jnp.mean(
+                delta * unit, -1, keepdims=True
+            )
+            value = previous[part] + delta * scale
+            target[part] = value
+            if target_low is not None:
+                target_low[part] = value.astype(jnp.bfloat16)
+
+    norm_back(middle, 2, grad, grad_out, low)
+    loads[2].wait()
+    loads[3].wait()
+
+    @pl.loop(0, D // TILE)
+    def _(t):
+        part = tile_of(t)
+        made_out[part] = jnp.dot(
+            attended_held[part], low[...], preferred_element_type=jnp.float32
+        ).astype(jnp.bfloat16)
+        attended_grad[part] = contract_last(out_held[part], low[...]).astype(jnp.bfloat16)
+
+    stores[2].start()
+    loads[4].wait()
+    parts, length = (rows.shape[0], rows.shape[1])
+    for b in range(parts):
+        same = rows[b] == columns[b]
+        span = slice(b * length, (b + 1) * length)
+
+        @pl.loop(0, D // GROUP)
+        def _(group):
+            for head in range(GROUP // HD):
+                first = group * GROUP + head * HD
+                part = pl.ds(pl.multiple_of(first, HD), HD)
+                where = [pl.ds(pl.multiple_of(place * D + first, HD), HD) for place in range(3)]
+                query, key, value = [mixed_held[at, span] for at in where]
+                query_value, query_unit, query_scale = normed_head(query, gain_query[part])
+                key_value, key_unit, key_scale = normed_head(key, gain_key[part])
+                query_low = query_value.astype(jnp.bfloat16)
+                key_low = key_value.astype(jnp.bfloat16)
+                value_low = value.astype(jnp.bfloat16)
+                out_low = attended_grad[part, span]
+                share = head_shares(query_low, key_low, same)
+                mixed_low[where[2], span] = contract_last(
+                    out_low, share.astype(jnp.bfloat16)
+                ).astype(jnp.bfloat16)
+                share_grad = contract_first(value_low, out_low)
+                total = jnp.sum(share * share_grad, 0, keepdims=True)
+                score_low = (share * (share_grad - total) * (1.0 / math.sqrt(HD))).astype(
+                    jnp.bfloat16
+                )
+                query_grad = jnp.dot(key_low, score_low, preferred_element_type=jnp.float32)
+                key_grad = contract_last(query_low, score_low)
+                for place, (delta, unit, scale, gain) in enumerate(
+                    (
+                        (query_grad, query_unit, query_scale, gain_query[part]),
+                        (key_grad, key_unit, key_scale, gain_key[part]),
+                    )
+                ):
+                    head_gain_out[b, place, part] = jnp.sum(delta * unit, 1, keepdims=True)
+                    delta = delta * gain
+                    delta = delta - jnp.mean(delta, 0, keepdims=True) - unit * jnp.mean(
+                        delta * unit, 0, keepdims=True
+                    )
+                    mixed_low[where[place], span] = (delta * scale).astype(jnp.bfloat16)
+
+    loads[5].wait()
+
+    @pl.loop(0, 3 * D // TILE)
+    def _(t):
+        part = tile_of(t)
+        made_mixing[part] = jnp.dot(
+            mixed_low[part], heads_held[...], preferred_element_type=jnp.float32
+        ).astype(jnp.bfloat16)
+
+    stores[3].start()
+    loads[6].wait()
+    for t in range(tokens // TILE):
+        part = slice(t * TILE, (t + 1) * TILE)
+        inner[part] = contract_first(mixed_low[:, part], mixing_held[...])
+    loads[7].wait()
+    norm_back(state_held, 0, grad_out, grad_out, None)
+    for copy in stores:
+        copy.wait()
+
+
+def layer_backward(grad, kept, blocks, gains, segment):
+    state, middle, mixed, heads_low, attended, normed_low = kept
+    tokens = grad.shape[0]
+    weights = [block.reshape(-1, D) for block in blocks]
+    low = jnp.bfloat16
+    grad, gain_grads, head_gains, *block_grads = pl.pallas_call(
+        backward_kernel,
+        out_shape=[
+            jax.ShapeDtypeStruct((tokens, D), jnp.float32),
+            jax.ShapeDtypeStruct((8, D), jnp.float32),
+            jax.ShapeDtypeStruct((segment.shape[0], 2, D, 1), jnp.float32),
+        ]
+        + [jax.ShapeDtypeStruct(weight.shape, low) for weight in weights],
+        in_specs=whole("vvvvvvvvaaaaaaaa"),
+        out_specs=whole("vvvaaaa"),
+        scratch_shapes=[
+            pltpu.VMEM(state.shape, jnp.float32),
+            pltpu.VMEM(mixed.shape, jnp.float32),
+            pltpu.VMEM(heads_low.shape, low),
+            pltpu.VMEM(attended.shape, low),
+        ]
+        + [pltpu.VMEM(weight.shape, low) for weight in weights]
+        + [
+            pltpu.VMEM((tokens, D), low),
+            pltpu.VMEM((tokens, D), jnp.float32),
+            pltpu.VMEM((FF, tokens), low),
+            pltpu.VMEM((3 * D, tokens), low),
+            pltpu.VMEM((D, tokens), low),
+            pltpu.VMEM((FF, D), low),
+            pltpu.VMEM((FF, D), low),
+            pltpu.VMEM((3 * D, D), low),
+            pltpu.VMEM((D, D), low),
+            pltpu.SemaphoreType.DMA((8,)),
+            pltpu.SemaphoreType.DMA((4,)),
+        ],
+        compiler_params=pltpu.CompilerParams(vmem_limit_bytes=60 * 1024 * 1024),
+        name="layer_backward",
+    )(grad, middle, normed_low, *attention_operands(gains, segment), state, mixed, heads_low, attended, *weights)
+    gain_grads = jnp.concatenate([gain_grads[:4], jnp.sum(head_gains[..., 0], 0)], 0)
+    return (grad, block_grads, gain_grads)
+
+
+HEAD_LANES = 128
+
+
+def full_dot(left, right):
+    return jnp.dot(left, right, preferred_element_type=jnp.float32, precision=HIGH)
+
+
+def head_marks():
+    entry = lax.broadcasted_iota(jnp.int32, (D, HEAD_LANES), 0)
+    lane = lax.broadcasted_iota(jnp.int32, (D, HEAD_LANES), 1)
+    return (entry // HD == lane).astype(jnp.float32)
+
+
+def full_dot_last(left, right):
+    return lax.dot_general(
+        left,
+        right,
+        (((1,), (1,)), ((), ())),
+        preferred_element_type=jnp.float32,
+        precision=HIGH,
+    )
+
+
+def pool_sequence(state, gains, rows, columns):
+    unit, scale = row_norm(state)
+    final = unit * gains[0:1] + gains[1:2]
+    marks = head_marks()
+    logits = full_dot(final * gains[2:3], marks) * (1.0 / math.sqrt(HD))
+    slot = lax.broadcasted_iota(jnp.int32, (rows.shape[0], IMGS), 1)
+    member = (rows == slot).astype(jnp.float32)
+    slot = lax.broadcasted_iota(jnp.int32, (IMGS, columns.shape[1]), 0)
+    member_rows = (columns == slot).astype(jnp.float32)
+    tops = jnp.zeros_like(logits)
+    for k in range(IMGS):
+        here = rows == k
+        top = jnp.max(jnp.where(here, logits, -1e30), 0, keepdims=True)
+        tops = jnp.where(here, top, tops)
+    exponent = jnp.exp(logits - tops)
+    share = exponent / full_dot(member, full_dot(member_rows, exponent))
+    spread_share = full_dot_last(share, marks)
+    dead = (jnp.sum(member_rows, 1, keepdims=True) == 0.0).astype(jnp.float32)
+    pooled = full_dot(member_rows, spread_share * final) + dead * jnp.mean(
+        final, 0, keepdims=True
+    )
+    return (unit, scale, final, marks, member, member_rows, share, spread_share, dead, pooled)
+
+
+def unit_scale(value):
+    return lax.rsqrt(jnp.mean(value * value, -1, keepdims=True) + 1e-06)
+
+
+def pool_kernel(state, gains, rows, columns, matrix, pooled_low, embedded, image_low):
+    parts, length = (rows.shape[0], rows.shape[1])
+    for b in range(parts):
+        pooled = pool_sequence(
+            state[b * length : (b + 1) * length], gains[...], rows[b], columns[b]
+        )[-1]
+        pooled_low[b] = pooled.astype(jnp.bfloat16)
+        value = jnp.dot(
+            pooled.astype(jnp.bfloat16), matrix[...], preferred_element_type=jnp.float32
+        )
+        embedded[b] = value
+        image_low[b] = (value * unit_scale(value) * (1.0 / math.sqrt(D))).astype(jnp.bfloat16)
+
+
+def pool_forward(state, gains, segment, matrix):
+    parts = segment.shape[0]
+    shape = (parts, IMGS, D)
     return pl.pallas_call(
-        attend_kernel,
-        grid=(parts, D // GROUP),
-        in_specs=attention_specs(length),
-        out_specs=pl.BlockSpec((GROUP, length), lambda b, group: (group, b)),
-        out_shape=jax.ShapeDtypeStruct((D, parts * length), jnp.bfloat16),
-        name="attend",
-    )(*attention_operands(mixed, gains, segment))
-
-
-def attend_back(mixed, gains, segment, grad):
-    parts, length = segment.shape
-    return pl.pallas_call(
-        attend_back_kernel,
-        grid=(parts, D // GROUP),
-        in_specs=attention_specs(length)
-        + [pl.BlockSpec((GROUP, length), lambda b, group: (group, b))],
-        out_specs=[
-            pl.BlockSpec((3, GROUP, length), lambda b, group: (0, group, b)),
-            pl.BlockSpec((1, 2, GROUP, 1), lambda b, group: (b, 0, group, 0)),
+        pool_kernel,
+        out_shape=[
+            jax.ShapeDtypeStruct(shape, jnp.bfloat16),
+            jax.ShapeDtypeStruct(shape, jnp.float32),
+            jax.ShapeDtypeStruct(shape, jnp.bfloat16),
         ],
+        in_specs=whole("vvvvv"),
+        out_specs=whole("vvv"),
+        compiler_params=pltpu.CompilerParams(vmem_limit_bytes=VMEM_LIMIT),
+        name="pool_forward",
+    )(state, gains, segment[:, :, None], segment[:, None, :], matrix)
+
+
+def contrast_kernel(
+    me,
+    images,
+    texts,
+    alive_columns,
+    alive_rows,
+    own_images,
+    own_live,
+    state,
+    gains,
+    rows,
+    columns,
+    matrix,
+    pooled_low,
+    embedded,
+    loss,
+    grad,
+    grad_matrix,
+    gain_out,
+    text_side,
+):
+    parts, length = (rows.shape[0], rows.shape[1])
+    everyone = images.shape[1]
+    count = jnp.zeros((1, 1), jnp.float32)
+    for b in range(parts):
+        count = count + jnp.sum(alive_columns[b], -1, keepdims=True)
+    factor = 1.0 / (2.0 * count)
+    first = me[0] * IMGS
+
+    def rows_of(scores, alive, live, start):
+        masked = jnp.where(alive > 0, scores, -1e30)
+        top = jnp.max(masked, -1, keepdims=True)
+        exponent = jnp.exp(masked - top)
+        total = jnp.sum(exponent, -1, keepdims=True)
+        line = lax.broadcasted_iota(jnp.int32, scores.shape, 0) + start
+        column = lax.broadcasted_iota(jnp.int32, scores.shape, 1)
+        target = (line == column).astype(jnp.float32)
+        diagonal = jnp.sum(scores * target, -1, keepdims=True)
+        term = (top + jnp.log(total) - diagonal) * live
+        delta = (exponent * (1.0 / total) - target) * live
+        return (term, (delta * factor * LOGIT_SCALE).astype(jnp.bfloat16))
+
+    loss[...] = jnp.zeros_like(loss)
+    grad_sum = jnp.zeros((D, D), jnp.float32)
+    gain_out[...] = jnp.zeros_like(gain_out)
+    for b in range(parts):
+        forward = LOGIT_SCALE * contract_last(own_images[b], texts[b])
+        term, forward_low = rows_of(forward, alive_columns[b], own_live[b], first)
+        loss[...] += jnp.sum(term, 0, keepdims=True) * factor
+        text_side[...] = jnp.zeros_like(text_side)
+
+        @pl.loop(0, everyone // TILE)
+        def _(t):
+            part = tile_of(t)
+            backward = LOGIT_SCALE * contract_last(texts[b, part], images[b])
+            term, backward_low = rows_of(
+                backward, alive_columns[b], alive_rows[b, part], t * TILE
+            )
+            line = lax.broadcasted_iota(jnp.int32, term.shape, 0) + t * TILE
+            here = jnp.logical_and(line >= first, line < first + IMGS)
+            loss[...] += jnp.sum(jnp.where(here, term, 0.0), 0, keepdims=True) * factor
+            text_side[...] += contract_first(backward_low, texts[b, part])
+
+        image_grad = jnp.dot(forward_low, texts[b], preferred_element_type=jnp.float32)
+        image_grad = image_grad + text_side[pl.ds(pl.multiple_of(first, IMGS), IMGS)]
+        value = embedded[b]
+        scale = unit_scale(value)
+        embed_low = (
+            (
+                image_grad * scale
+                - value * (scale * scale * scale) * jnp.mean(value * image_grad, -1, keepdims=True)
+            )
+            * (1.0 / math.sqrt(D))
+        ).astype(jnp.bfloat16)
+        grad_sum = grad_sum + contract_first(pooled_low[b], embed_low)
+        pooled_grad = contract_last(embed_low, matrix[...])
+        unit, norm_scale, final, marks, member, member_rows, share, spread_share, dead, _ = (
+            pool_sequence(
+                state[b * length : (b + 1) * length], gains[...], rows[b], columns[b]
+            )
+        )
+        token_grad = full_dot(member, pooled_grad)
+        share_grad = full_dot(final * token_grad, marks)
+        inside = full_dot(member, full_dot(member_rows, share * share_grad))
+        logit_grad = share * (share_grad - inside) * (1.0 / math.sqrt(HD))
+        spread_logit = full_dot_last(logit_grad, marks)
+        final_grad = (
+            spread_share * token_grad
+            + spread_logit * gains[2:3]
+            + jnp.sum(dead * pooled_grad, 0, keepdims=True) * (1.0 / length)
+        )
+        gain_out[0:1] += jnp.sum(final_grad * unit, 0, keepdims=True)
+        gain_out[1:2] += jnp.sum(final_grad, 0, keepdims=True)
+        gain_out[2:3] += jnp.sum(spread_logit * final, 0, keepdims=True)
+        delta = final_grad * gains[0:1]
+        delta = delta - jnp.mean(delta, -1, keepdims=True) - unit * jnp.mean(
+            delta * unit, -1, keepdims=True
+        )
+        grad[b * length : (b + 1) * length] = delta * norm_scale
+    grad_matrix[...] = grad_sum.astype(jnp.bfloat16)
+
+
+def contrast(me, images, texts, alive, own_images, live, state, gains, segment, matrix, pooled_low, embedded):
+    parts, everyone = alive.shape
+    loss, grad, grad_matrix, gain_grads = pl.pallas_call(
+        contrast_kernel,
         out_shape=[
-            jax.ShapeDtypeStruct((3, D, parts * length), jnp.bfloat16),
-            jax.ShapeDtypeStruct((parts, 2, D, 1), jnp.float32),
+            jax.ShapeDtypeStruct((8, 128), jnp.float32),
+            jax.ShapeDtypeStruct(state.shape, jnp.float32),
+            jax.ShapeDtypeStruct((D, D), jnp.bfloat16),
+            jax.ShapeDtypeStruct((8, D), jnp.float32),
         ],
-        name="attend_back",
-    )(*attention_operands(mixed, gains, segment), grad)
-
-
-def layer_forward(state, blocks, gains, segment):
-    heads_in, norm_one = jax.vjp(layer_norm, state, gains[0], gains[1])
-    heads_low = rounded(heads_in)
-    mixed = product(blocks[0].reshape(3 * D, D), heads_low, "rd,sd->rs")
-    attended_low = attend(mixed, gains, segment)
-    state = state + product(attended_low, blocks[1].reshape(D, D), "rs,rd->sd")
-    normed, norm_two = jax.vjp(layer_norm, state, gains[2], gains[3])
-    normed_low = rounded(normed)
-    hidden, gelu_back = jax.vjp(
-        jax.nn.gelu, product(normed_low, blocks[2].reshape(FF, D), "sd,rd->sr")
+        in_specs=[pl.BlockSpec(memory_space=pltpu.SMEM)] + whole("vvvvvvvvvvvvv"),
+        out_specs=whole("vvvv"),
+        scratch_shapes=[pltpu.VMEM((everyone, D), jnp.float32)],
+        compiler_params=pltpu.CompilerParams(vmem_limit_bytes=VMEM_LIMIT),
+        name="contrast",
+    )(
+        me.reshape(1),
+        images,
+        texts,
+        alive[:, None, :],
+        alive[:, :, None],
+        own_images,
+        live[:, :, None],
+        state,
+        gains,
+        segment[:, :, None],
+        segment[:, None, :],
+        matrix,
+        pooled_low,
+        embedded,
     )
-    hidden_low = rounded(hidden)
-    state = state + product(hidden_low, blocks[3].reshape(FF, D), "sr,rd->sd")
-    kept = (
-        norm_one,
-        heads_low,
-        mixed,
-        attended_low,
-        norm_two,
-        normed_low,
-        gelu_back,
-        hidden_low,
-    )
-    return (state, kept)
-
-
-def layer_backward(grad, kept, blocks, gains, segment):
-    norm_one, heads_low, mixed, attended_low, norm_two, normed_low, gelu_back, hidden_low = kept
-    down = blocks[3].reshape(FF, D)
-    upward = blocks[2].reshape(FF, D)
-    grad_low = rounded(grad)
-    grad_down = rounded(product(hidden_low, grad_low, "sr,sd->rd"))
-    (grad_hidden,) = gelu_back(product(grad_low, down, "sd,rd->sr"))
-    hidden_grad = rounded(grad_hidden)
-    grad_up = rounded(product(hidden_grad, normed_low, "sr,sd->rd"))
-    inner, gain_two, shift_two = norm_two(product(hidden_grad, upward, "sr,rd->sd"))
-    grad = grad + inner
-    grad_low = rounded(grad)
-    grad_out = rounded(product(attended_low, grad_low, "rs,sd->rd"))
-    attended_grad = rounded(product(blocks[1].reshape(D, D), grad_low, "rd,sd->rs"))
-    mixed_low, head_gains = attend_back(mixed, gains, segment, attended_grad)
-    head_gains = jnp.sum(head_gains[..., 0], 0)
-    grad_mixed = rounded(product(mixed_low, heads_low, "krs,sd->krd"))
-    inner, gain_one, shift_one = norm_one(
-        product(
-            mixed_low.reshape(3 * D, -1), blocks[0].reshape(3 * D, D), "rs,rd->sd"
-        )
-    )
-    grad = grad + inner
-    block_grads = [grad_mixed, grad_out, grad_up, grad_down]
-    gain_grads = jnp.concatenate(
-        [jnp.stack([gain_one, shift_one, gain_two, shift_two]), head_gains], 0
-    )
-    return (grad, block_grads, gain_grads)
-
-
-def contrast_rows(scores, alive, own_live, rows):
-    masked = jnp.where(alive[None, :] > 0, scores, -1e30)
-    top = jax.scipy.special.logsumexp(masked, axis=1, keepdims=True)
-    share = jnp.exp(masked - top)
-    columns = jnp.arange(scores.shape[1], dtype=jnp.int32)
-    target = (columns[None, :] == rows[:, None]).astype(jnp.float32)
-    diagonal = jnp.sum(scores * target, 1)
-    return ((top[:, 0] - diagonal) * own_live, (share - target) * own_live[:, None])
+    return (loss[0, 0], grad, grad_matrix, gain_grads[:3])
 
 
 def muon_groups():
@@ -1269,9 +1751,20 @@
     live = jnp.any(segments[:, 0, None, :] == slots[None, :, None], -1).astype(jnp.float32)
     depth = lax.axis_size("fsdp")
     captions = MB * IMGS
-    ids = jnp.broadcast_to(text_ids.reshape(1, captions, -1), (depth, captions, text_ids.shape[3]))
-    ids = swap(ids, 10)
-    stem, *first_blocks = fetch(weights, [(0, 1), (2, 3), (5, 1), (6, 4), (10, 4)], 1)
+    tokens = text_ids.shape[3]
+    own_ids = jnp.pad(text_ids.reshape(captions, tokens), ((0, 0), (0, 128 - tokens)))
+    early = [(0, 1), (2, 3), (5, 1), (6, 4), (10, 4), (1, 1)]
+    later = []
+    for index in range(1, LAYERS):
+        start = 2 + 12 * index
+        early = early + [(start, 3), (start + 3, 1)]
+        later = later + [(start + 4, 4), (start + 8, 4)]
+    (stem, *first_blocks), ids, later_part = fetch(weights, early, later, own_ids, 1)
+    early_blocks = first_blocks[5:]
+    pooling_matrix = first_blocks[4][0]
+    first_blocks = first_blocks[:4]
+    later_blocks = gather_later(later_part)
+    ids = ids[:, :, :tokens]
     flat_ids = ids.reshape(depth * captions, -1)
     share_rows = table.shape[0]
     picked = flat_ids - lax.axis_index("fsdp") * share_rows
@@ -1298,59 +1791,37 @@
         if index == 0:
             blocks = first_blocks
         else:
-            start = 2 + 12 * index
-            pieces = [(start, 3), (start + 3, 1), (start + 4, 4), (start + 8, 4)]
-            if index == 1:
-                pieces = pieces + [(1, 1)]
-            blocks = fetch(weights, pieces, 2 + index)
-            if index == 1:
-                pooling_matrix = blocks.pop()[0]
+            first = 8 * index - 8
+            blocks = early_blocks[2 * index - 2 : 2 * index] + [
+                later_blocks[first : first + 4],
+                later_blocks[first + 4 : first + 8],
+            ]
         state, kept = layer_forward(state, blocks, gains[6 * index : 6 * index + 6], segment)
         saved.append((kept, blocks))
-    final, norm_final = jax.vjp(layer_norm, state, gains[fin], gains[fin + 1])
-
-    def pool_all(values, query):
-        split = values.reshape(MB, -1, D)
-        return jnp.concatenate([pooling(segment[part])(split[part], query) for part in range(MB)])
-
-    pooled, pool_back = jax.vjp(pool_all, final, gains[fin + 2])
-    pooled_low = rounded(pooled)
-    embedded, unit_back = jax.vjp(unit_rows, product(pooled_low, pooling_matrix, "kr,rd->kd"))
-    image_low = rounded(embedded)
-    flags = jnp.broadcast_to(live.reshape(1, captions, 1), (1, captions, D)).astype(jnp.bfloat16)
-    both = jnp.concatenate([image_low[None], text_low[None], flags], 0).reshape(3 * captions, D)
-    whole = share(both, 8).reshape(-1, 3, MB, IMGS, D)
-    flags = whole[:, 2, :, :, 0].astype(jnp.float32)
-    count = jnp.sum(flags)
-    factor = 1.0 / (2.0 * count)
-    loss_part = jnp.float32(0.0)
-    image_grads = []
-    for part in range(MB):
-        images = whole[:, 0, part].reshape(-1, D)
-        texts = whole[:, 1, part].reshape(-1, D)
-        alive = flags[:, part].reshape(-1)
-        own_image = image_low[part * IMGS : (part + 1) * IMGS]
-        forward = LOGIT_SCALE * product(own_image, texts, "kd,nd->kn")
-        backward = LOGIT_SCALE * product(texts, images, "kd,nd->kn")
-        own = me * IMGS + jnp.arange(IMGS, dtype=jnp.int32)
-        everyone = jnp.arange(alive.shape[0], dtype=jnp.int32)
-        term_f, grad_f = contrast_rows(forward, alive, live[part], own)
-        term_b, grad_b = contrast_rows(backward, alive, alive, everyone)
-        own_terms = jnp.sum(jnp.where((everyone // IMGS) == me, term_b, 0.0))
-        loss_part = loss_part + (jnp.sum(term_f) + own_terms) * factor
-        forward_low = rounded(grad_f * factor * LOGIT_SCALE)
-        backward_low = rounded(
-            lax.dynamic_slice_in_dim(grad_b, me * IMGS, IMGS, 1) * factor * LOGIT_SCALE
-        )
-        image_grads.append(
-            product(forward_low, texts, "kn,nd->kd") + product(backward_low, texts, "nk,nd->kd")
-        )
-    image_grad = jnp.concatenate(image_grads, 0)
-    (embed_grad,) = unit_back(image_grad)
-    embed_low = rounded(embed_grad)
-    grad_pool = rounded(product(pooled_low, embed_low, "kr,kd->rd"))
-    final_grad, query_grad = pool_back(product(embed_low, pooling_matrix, "kd,rd->kr"))
-    grad, gain_final, shift_final = norm_final(final_grad)
+    pool_gains = jnp.pad(gains[fin : fin + 3], ((0, 5), (0, 0)))
+    pooled_low, embedded, image_low = pool_forward(state, pool_gains, segment, pooling_matrix)
+    own_flags = jnp.broadcast_to(live.reshape(captions, 1), (captions, 128)).astype(jnp.bfloat16)
+    both = jnp.stack([image_low.reshape(captions, D), text_low]).reshape(2 * captions, D)
+    gathered, flags = share([both, own_flags], 8)
+    gathered = gathered.reshape(-1, 2, MB, IMGS, D)
+    flags = flags.reshape(-1, MB, IMGS, 128)[..., 0].astype(jnp.float32)
+    images, texts = [
+        jnp.moveaxis(gathered[:, i], 0, 1).reshape(MB, -1, D) for i in range(2)
+    ]
+    loss_part, grad, grad_pool, pool_gain_grads = contrast(
+        me,
+        images,
+        texts,
+        jnp.moveaxis(flags, 0, 1).reshape(MB, -1),
+        image_low,
+        live,
+        state,
+        pool_gains,
+        segment,
+        pooling_matrix,
+        pooled_low,
+        embedded,
+    )
     gain_parts = [None] * LAYERS
     block_grads = [None] * LAYERS
     fast = depth == 4 and lanes == 8
@@ -1371,7 +1842,7 @@
     grad_cols = jnp.dot(cols_hot.T, grad, precision=HIGH)
     gains_grad = jnp.concatenate(
         gain_parts
-        + [jnp.stack([gain_final, shift_final, query_grad]), grad_rows, grad_cols],
+        + [pool_gain_grads, grad_rows, grad_cols],
         0,
     )
     plan, widths = lane_plan(lanes)

time: 900 us -> 854 us (0.949)
  matrix products: 160 us -> 17.5 us
  Pallas kernels: 630 us -> 718 us
    pallas_call x5 -> x7, Pallas kernels: 76.3 us -> 211 us  [the longest x2 97.1 us: layer_backward(): pl.pallas_call(backward_kernel, out_shape=[jax.ShapeDtypeStruct((tokens,...]
    dot_general x39 -> x4, matrix products: 135 us -> 4.29 us  [product(): return jnp.einsum(form, left, right, preferred_element_type=jnp.float32)]
    pallas_call x2 -> x1, Pallas kernels: 144 us -> 98.7 us  [fetch(): pl.pallas_call(functools.partial(fetch_kernel, chunks, [n for _, n in pie...]
    dot_general x10 -> x0, matrix products: 13.9 us -> none  [the longest x6 9.08 us: pooled_of(): jnp.einsum('khs,shd->khd', share, split, precision=HIGH).reshape(IMGS, -1)]
    reduce_sum x25 -> x2, other arithmetic: 13.9 us -> 3.39 us  [layer_backward(): jnp.sum(head_gains[..., 0], 0)]
    reduce_sum x1, other arithmetic: 13 us -> 22.4 us  [per_device(): jnp.sum((picked[:, :, None] == jnp.arange(share_rows, dtype=jnp.int32)[No...]
  transfers between devices with their start and end apart: 0 -> 1, of which waited for: 0 -> 0; matrix products, arithmetic and copies ran while one was open for 0% -> 6% of each run, Pallas kernels for 0% -> 5%
where the time goes in v4:
time: 854 us; the launch traced here: 847 us
  Pallas kernels  718 us (84%)
  other arithmetic  49.1 us (6%)
  local copies, waits for them, and re-layouts  39.7 us (5%)
  between operations  22.5 us (3%)
  matrix products  17.5 us (2%)
    pallas_call x2, Pallas kernels, reduce_grads(): pl.pallas_call(functools.partial(reduce_kernel, chunks, len(sources), len...  166 us
    pallas_call x1, Pallas kernels, fetch(): pl.pallas_call(functools.partial(fetch_kernel, chunks, [n for _, n in pie...  98.7 us
    pallas_call x2, Pallas kernels, layer_backward(): pl.pallas_call(backward_kernel, out_shape=[jax.ShapeDtypeStruct((tokens,...  97.1 us
    pallas_call x1, Pallas kernels, spread(): pl.pallas_call(spread_kernel, out_shape=jax.ShapeDtypeStruct(own.shape[:1...  70.3 us
    pallas_call x1, Pallas kernels, sum_grams(): pl.pallas_call(gram_kernel, out_shape=[jax.ShapeDtypeStruct(grams.shape,...  65.3 us
    pallas_call x2, Pallas kernels, layer_forward(): pl.pallas_call(forward_kernel, out_shape=[jax.ShapeDtypeStruct((tokens, D...  58.3 us
    pallas_call x1, Pallas kernels, update(): pl.pallas_call(update_kernel, grid_spec=pltpu.PrefetchScalarGridSpec(num_...  35.8 us
    pallas_call x1, Pallas kernels, schulz(): pl.pallas_call(schulz_kernel, out_shape=jax.ShapeDtypeStruct(rows.shape,...  31.7 us
  transfers between devices with their start and end apart: 1, of which 0 were waited for; matrix products, arithmetic and copies ran while one was open for 6% of the time, Pallas kernels for 5%

profile of v4, /device:TPU:0, one launch (start us, length us, event | category | flops | bytes accessed | tf_op | source)
XLA Modules:
  0.0 846.5 jit_solution(18219627038110310803)
XLA Ops:
  7.2 1.4 pad.22.ids
  8.6 98.7 %fetch_1.1 = (bf16[1,4,8,24,768]{4,3,2,1,0:T(8,128)(2,1)}, bf16[3,4,8,24,768]{4,3,2,1,0:T(8,128)(2,1)}, bf16[1,4,8,24,768]{4,3,2,1,0:T(8,128)(2,1)}, bf16[4,4,8,...) custom-call(f32[26,8,24,768]{3,2,1,0:T(8,128)} %bitcast.114, ...), custom_call_target="tpu_custom_call" | custom-call | tf_op jit(solution)/shard_map/fetch_1/pallas_call | solution.py:236
  107.9 0.8 broadcast_in_dim_squeeze.33.rows
  108.7 0.9 copy.56.gain_query
  109.7 0.9 copy.57.gain_key
  110.6 1.0 copy.59.gain_query
  111.6 0.9 copy.60.gain_key
  113.8 22.4 %convert_reduce_fusion = s32[64,8000]{1,0:T(8,128)S(1)} fusion(s32[64,16]{1,0:T(8,128)S(1)} %bitcast.151), kind=kLoop, calls=%fused_computation | loop fusion | flops 24064000 | bytes 2052096 | tf_op jit(solution)/shard_map/reduce_sum | solution.py:1771
  136.2 7.4 fusion.5
  143.6 15.1 %swap_11.1 = f32[4,16,768]{2,1,0:T(8,128)} custom-call(f32[4,16,768]{2,1,0:T(8,128)} %bitcast.149), custom_call_target="tpu_custom_call" | custom-call | tf_op jit(solution)/shard_map/swap_11/pallas_call | solution.py:369
  158.7 0.9 reduce_sum.84
  159.9 0.7 copy.68.own_live
  166.1 0.7 slice_select_fusion.1.gains
  166.8 0.8 fusion.9
  167.6 0.8 fusion.30
  168.4 2.0 fusion.1.state
  170.4 29.2 %layer_forward.2 = (f32[512,768]{1,0:T(8,128)}, f32[512,768]{1,0:T(8,128)}, f32[2304,512]{1,0:T(8,128)}, bf16[512,768]{1,0:T(8,128)(2,1)}, bf16[768,512]{1,0:T(8,128)(2,1)}, /*index=5*/bf16[512,768]{1,0:T(8,128)(2,1)}) custom-call(f32[512,768]{1,0:T(8,128)} %fusion.1.state, f32[8,768]{1,0:T(8,128)} %slice_select_fusion.1.gains, f32[768,1]{1,0:T(8,128)} %copy.56.gain_query, ...), custom_call_target="tpu_custom_call" | custom-call | tf_op jit(solution)/shard_map/layer_forward/pallas_call | solution.py:1207
  200.3 5.2 dynamic-slice_select_fusion.3
  205.6 8.1 fusion.24
  213.7 29.1 %layer_forward.3 = (f32[512,768]{1,0:T(8,128)}, f32[512,768]{1,0:T(8,128)}, f32[2304,512]{1,0:T(8,128)}, bf16[512,768]{1,0:T(8,128)(2,1)}, bf16[768,512]{1,0:T(8,128)(2,1)}, /*index=5*/bf16[512,768]{1,0:T(8,128)(2,1)}) custom-call(f32[512,768]{1,0:T(8,128)} %get-tuple-element.68.state, f32[8,768]{1,0:T(8,128)} %pad.24.gains, f32[768,1]{1,0:T(8,128)} %copy.59.gain_query, ...), custom_call_target="tpu_custom_call" | custom-call | tf_op jit(solution)/shard_map/layer_forward/pallas_call | solution.py:1207
  242.8 10.4 %pool_forward.1 = (bf16[2,8,768]{2,1,0:T(8,128)(2,1)}, f32[2,8,768]{2,1,0:T(8,128)}, bf16[2,8,768]{2,1,0:T(8,128)(2,1)}) custom-call(f32[512,768]{1,0:T(8,128)} %get-tuple-element.72.state, f32[8,768]{1,0:T(8,128)} %pad.25.gains, s32[2,256,1]{2,1,0:T(8,128)} %broadcast_in_dim_squeeze.33.rows, s32[2,1,256]{2,1,0:T(1,128)} %columns.11, bf16[768,768]{1,0:T(8,128)(2,1)} %bitcast.136), custom_call_target="tpu_custom_call" | custom-call | tf_op jit(solution)/shard_map/pool_forward/pallas_call | solution.py:1524
  253.3 1.4 pad_maximum_fusion.2
  254.6 0.7 broadcast_in_dim.13.refs_1_
  255.3 25.0 %share_8.1 = (bf16[8,4,32,768]{3,2,1,0:T(8,128)(2,1)}, bf16[8,4,16,128]{3,2,1,0:T(8,128)(2,1)}) custom-call(bf16[32,768]{1,0:T(8,128)(2,1)} %bitcast.150, bf16[16,128]{1,0:T(8,128)(2,1)} %broadcast_in_dim.13.refs_1_), custom_call_target="tpu_custom_call" | custom-call | tf_op jit(solution)/shard_map/share_8/pallas_call | solution.py:330
  280.3 1.3 copy.81
  281.7 0.9 broadcast_in_dim_reshape.9.alive_rows
  283.2 1.5 fusion.25
  284.6 1.2 copy_bitcast_fusion
  285.9 20.1 %contrast.1 = (f32[8,128]{1,0:T(8,128)}, f32[512,768]{1,0:T(8,128)}, bf16[768,768]{1,0:T(8,128)(2,1)}, f32[8,768]{1,0:T(8,128)}) custom-call(s32[1]{0:T(128)} %bitcast.me, bf16[2,256,768]{2,1,0:T(8,128)(2,1)} %get-tuple-element.157.images, bf16[2,256,768]{2,1,0:T(8,128)(2,1)} %get-tuple-element.156.texts, ...), custom_call_target="tpu_custom_call" | custom-call | tf_op jit(solution)/shard_map/contrast/pallas_call | solution.py:1642
  306.0 48.5 %layer_backward.2 = (f32[512,768]{1,0:T(8,128)}, f32[8,768]{1,0:T(8,128)}, f32[2,2,768,1]{3,2,1,0:T(8,128)}, bf16[2304,768]{1,0:T(8,128)(2,1)}, bf16[768,768]{1,...) custom-call(f32[512,768]{1,0:T(8,128)} %get-tuple-element.80.grad, ...), custom_call_target="tpu_custom_call" | custom-call | tf_op jit(solution)/shard_map/layer_backward/pallas_call | solution.py:1419
  354.5 48.7 %layer_backward.3 = (f32[512,768]{1,0:T(8,128)}, f32[8,768]{1,0:T(8,128)}, f32[2,2,768,1]{3,2,1,0:T(8,128)}, bf16[2304,768]{1,0:T(8,128)(2,1)}, bf16[768,768]{1,...) custom-call(f32[512,768]{1,0:T(8,128)} %get-tuple-element.86.grad, ...), custom_call_target="tpu_custom_call" | custom-call | tf_op jit(solution)/shard_map/layer_backward/pallas_call | solution.py:1419
  403.2 2.3 fusion.7
  405.4 0.8 fusion.8
  406.2 1.8 convolution_convert_fusion
  408.0 80.8 %reduce_5.1 = f32[13,24,768]{2,1,0:T(8,128)} custom-call(bf16[3,4,2,2,2,24,768]{6,5,4,3,2,1,0:T(8,128)(2,1)} %bitcast.139, bf16[1,4,2,2,2,24,768]{6,5,4,3,2,1,0:T(8,128)(2,1)} %bitcast.146, bf16[4,4,2,2,2,24,768]{6,5,4,3,2,1,0:T(8,128)(2,1)} %bitcast.132, bf16[4,4,2,2,2,24,768]{6,5,4,3,2,1,0:T(8,128)(2,1)} %bitcast.133, ...), custom_call_target="tpu_custom_call" | custom-call | tf_op jit(solution)/shard_map/reduce_5/pallas_call | solution.py:565
  488.8 2.3 fusion.26
  491.1 1.7 reduce_sum.87
  492.9 1.7 reduce_sum.88
  495.1 1.2 slice.212
  496.3 0.7 select_maximum_fusion
  497.0 0.8 reshape_reshape.33.refs_5_
  497.8 85.5 %reduce_4.1 = (f32[13,24,768]{2,1,0:T(8,128)}, f32[1,8,256]{2,1,0:T(8,128)}) custom-call(bf16[3,4,2,2,2,24,768]{6,5,4,3,2,1,0:T(8,128)(2,1)} %bitcast.140, bf16[1,4,2,2,2,24,768]{6,5,4,3,2,1,0:T(8,128)(2,1)} %bitcast.147, bf16[4,4,2,2,2,24,768]{6,5,4,3,2,1,0:T(8,128)(2,1)} %bitcast.134, bf16[4,4,2,2,2,24,768]{6,5,4,3,2,1,0:T(8,128)(2,1)} %bitcast.135, ...), custom_call_target="tpu_custom_call" | custom-call | tf_op jit(solution)/shard_map/reduce_4/pallas_call | solution.py:565
  583.2 2.3 fusion.27
  585.6 0.7 slice_dynamic-update-slice_fusion.1
  586.3 0.7 slice_dynamic-update-slice_fusion
  587.0 0.7 slice_dynamic-update-slice_fusion.3
  589.5 0.6 broadcast_dynamic-update-slice_fusion
  590.2 0.7 slice_dynamic-update-slice_fusion.2
  592.7 0.6 broadcast_dynamic-update-slice_fusion.1
  595.3 23.5 %meet_9.1 = (f32[8,4,16,256]{3,2,1,0:T(8,128)}, bf16[4,8,24,768]{3,2,1,0:T(8,128)(2,1)}) custom-call(f32[16,256]{1,0:T(8,128)} %concatenate.21.own, bf16[8,4,24,768]{3,2,1,0:T(8,128)(2,1)} %bitcast.51.parts), custom_call_target="tpu_custom_call" | custom-call | tf_op jit(solution)/shard_map/meet_9/pallas_call | solution.py:689
  618.8 1.0 slice_bitcast_fusion.2
  619.8 1.5 slice_reduce_fusion
  621.5 0.7 multiply_reduce_fusion.2
  623.6 0.7 mul.153
  625.8 0.9 copy-done.3
  626.7 1.8 fusion.22
  629.5 1.1 convolution_bitcast_fusion
  630.7 2.5 pad_maximum_fusion.gram
  633.2 1.0 pad_maximum_fusion.1.own
  634.2 65.3 %gram_12.1 = (f32[2,768,768]{2,1,0:T(8,128)}, bf16[26,8,24,768]{3,2,1,0:T(8,128)(2,1)}) custom-call(f32[2,768,768]{2,1,0:T(8,128)} %pad_maximum_fusion.gram, bf16[26,24,768]{2,1,0:T(8,128)(2,1)} %pad_maximum_fusion.1.own), custom_call_target="tpu_custom_call" | custom-call | tf_op jit(solution)/shard_map/gram_12/pallas_call | solution.py:861
  699.5 31.7 %schulz.1.own = bf16[4,192,768]{2,1,0:T(8,128)(2,1)} custom-call(s32[1]{0:T(128)} %dynamic_slice.52.two, f32[2,768,768]{2,1,0:T(8,128)} %get-tuple-element.113.gram, f32[4,192,768]{2,1,0:T(8,128)} %get-tuple-element.123.rows), custom_call_target="tpu_custom_call" | custom-call | tf_op jit(solution)/shard_map/schulz/pallas_call | solution.py:961
  731.3 70.3 %spread_13.1.turned = bf16[4,8,192,768]{3,2,1,0:T(8,128)(2,1)} custom-call(bf16[4,192,768]{2,1,0:T(8,128)(2,1)} %schulz.1.own), custom_call_target="tpu_custom_call" | custom-call | tf_op jit(solution)/shard_map/spread_13/pallas_call | solution.py:990
  801.6 1.0 multiply_subtract_fusion
  802.5 35.8 %update.1 = (f32[26,192,768]{2,1,0:T(8,128)}, f32[26,192,768]{2,1,0:T(8,128)}, bf16[26,192,768]{2,1,0:T(8,128)(2,1)}) custom-call(s32[52]{0:T(128)} %constant.119.clone.table, f32[26]{0:T(128)} %constant.120.clone.scale, f32[1]{0:T(128)} %bitcast.54.clip, f32[26,192,768]{2,1,0:T(8,128)} %momenta.1, bf16[26,192,768]{2,1,0:T(8,128)(2,1)} %bitcast.127, ...), custom_call_target="tpu_custom_call" | custom-call | tf_op jit(solution)/shard_map/update/pallas_call | solution.py:1019
  (94 shorter events, 12.7 us)
Async XLA Ops:
  7.2 160.4 %copy-start = (bf16[2,1,256,768]{3,2,1,0:T(8,128)(2,1)S(1)}, bf16[2,1,256,768]{3,2,1,0:T(8,128)(2,1)}, u32[]{:S(2)}) copy-start(bf16[2,1,256,768]{3,2,1,0:T(8,128)(2,1)} %param.19) | copy-start | bytes 2359300
  7.2 198.4 %all-gather.3.cloned.1.call-start = ((), (), s32[]{:S(2)}) async-start(), calls=%async_computation | async-start | bytes 9732096 | tf_op jit(solution)/shard_map/all_gather | solution.py:272
  8.6 98.8 %copy-start.5 = (f32[79,768]{1,0:T(8,128)S(1)}, f32[79,768]{1,0:T(8,128)}, u32[]{:S(2)}) copy-start(f32[79,768]{1,0:T(8,128)} %param.26) | copy-start | bytes 728068
  8.6 98.8 %copy-start.10 = (s32[2,1,256]{2,1,0:T(1,128)S(1)}, s32[2,1,256]{2,1,0:T(1,128)}, u32[]{:S(2)}) copy-start(s32[2,1,256]{2,1,0:T(1,128)} %columns.11) | copy-start | bytes 6148
  8.6 98.8 %copy-start.11 = (s32[2,1,4,256]{3,2,1,0:T(4,128)S(1)}, s32[2,1,4,256]{3,2,1,0:T(4,128)}, u32[]{:S(2)}) copy-start(s32[2,1,4,256]{3,2,1,0:T(4,128)} %param.20) | copy-start | bytes 24580
  107.3 6.4 copy-start.12
  136.1 25.2 %copy-start.18 = (s32[8,4]{1,0:T(8,128)S(1)}, s32[8,4]{1,0:T(8,128)}, u32[]{:S(2)}) copy-start(s32[8,4]{1,0:T(8,128)} %constant.117.clone) | copy-start | bytes 388
  136.1 28.4 %copy-start.21 = (s32[8]{0:T(128)S(1)}, s32[8]{0:T(128)}, u32[]{:S(2)}) copy-start(s32[8]{0:T(128)} %constant.118.clone) | copy-start | bytes 100
  136.2 29.9 %copy-start.19 = (pred[8]{0:T(512)(128)(4,1)S(1)}, pred[8]{0:T(512)(128)(4,1)}, u32[]{:S(2)}) copy-start(pred[8]{0:T(512)(128)(4,1)} %constant.88.clone.1) | copy-start | bytes 28
  143.6 24.1 %copy-start.20 = (bf16[1,4,8,24,768]{4,3,2,1,0:T(8,128)(2,1)S(1)}, bf16[1,4,8,24,768]{4,3,2,1,0:T(8,128)(2,1)}, u32[]{:S(2)}) copy-start(bf16[1,4,8,24,768]{4,3,2,1,0:T(8,128)(2,1)} %get-tuple-element.63) | copy-start | bytes 3538948
  170.4 29.2 %copy-start.17 = (pred[8,4]{1,0:T(8,128)(4,1)S(1)}, pred[8,4]{1,0:T(8,128)(4,1)}, u32[]{:S(2)}) copy-start(pred[8,4]{1,0:T(8,128)(4,1)} %constant.116.clone) | copy-start | bytes 100
  403.2 2.3 copy-start.2
  408.0 83.1 %copy-start.16 = (f32[8,768]{1,0:T(8,128)S(1)}, f32[8,768]{1,0:T(8,128)}, u32[]{:S(2)}) copy-start(f32[8,768]{1,0:T(8,128)} %get-tuple-element.97) | copy-start | bytes 73732
  488.8 4.1 copy-start.15
  491.1 3.4 copy-start.14
  583.2 11.4 %copy-start.13 = (f32[1,8,256]{2,1,0:T(8,128)S(1)}, f32[1,8,256]{2,1,0:T(8,128)}, u32[]{:S(2)}) copy-start(f32[1,8,256]{2,1,0:T(8,128)} %get-tuple-element.103) | copy-start | bytes 24580
  624.3 1.3 copy-start.4
  625.6 1.1 copy-start.3
  630.7 2.5 copy-start.9
  731.3 70.3 %copy-start.6 = (f32[79,768]{1,0:T(8,128)S(1)}, f32[79,768]{1,0:T(8,128)}, u32[]{:S(2)}) copy-start(f32[79,768]{1,0:T(8,128)} %mul.153) | copy-start | bytes 728068
  731.3 70.3 %copy-start.7 = (f32[79,768]{1,0:T(8,128)S(1)}, f32[79,768]{1,0:T(8,128)}, u32[]{:S(2)}) copy-start(f32[79,768]{1,0:T(8,128)} %param.28) | copy-start | bytes 728068
  731.3 70.3 %copy-start.8 = (f32[79,768]{1,0:T(8,128)S(1)}, f32[79,768]{1,0:T(8,128)}, u32[]{:S(2)}) copy-start(f32[79,768]{1,0:T(8,128)} %param.27) | copy-start | bytes 728068
  802.5 35.8 %copy-start.1 = (bf16[2,1,256,768]{3,2,1,0:T(8,128)(2,1)S(1)}, bf16[2,1,256,768]{3,2,1,0:T(8,128)(2,1)}, u32[]{:S(2)}) copy-start(bf16[2,1,256,768]{3,2,1,0:T(8,128)(2,1)} %param.19) | copy-start | bytes 2359300
Sparse Core Ops, SparseCore 0:
  107.5 90.9 all-gather.2

commit v5 on v4

--- a/solution.py
+++ b/solution.py
@@ -64,6 +64,11 @@
     )
 
 
+def whole(kinds):
+    memory = {"v": pltpu.VMEM, "a": pl.ANY}
+    return [pl.BlockSpec(memory_space=memory[kind]) for kind in kinds]
+
+
 def flip(index, bit):
     return index + bit - 2 * bit * lax.rem(index // bit, 2)
 
@@ -81,12 +86,30 @@
     return (d, z, [lax.rem(z + step, 4) for step in range(4)])
 
 
-def fetch_kernel(chunks, sizes, later, weights, ids, *refs):
+CAPTION_TILE = 400
+
+
+def fetch_kernel(chunks, sizes, weights, ids, table, *refs):
     outs = refs[: len(sizes)]
-    all_ids, slices = refs[len(sizes) : len(sizes) + 2]
-    full, low, held, load_sem, store_sem, send, recv, later_sem, id_send, id_recv = refs[
-        len(sizes) + 2 :
-    ]
+    text_sum = refs[len(sizes)]
+    (
+        full,
+        low,
+        all_ids,
+        pages,
+        found,
+        found_parts,
+        from_z,
+        load_sem,
+        store_sem,
+        send,
+        recv,
+        page_sem,
+        id_send,
+        id_recv,
+        part_send,
+        part_recv,
+    ) = refs[len(sizes) + 1 :]
     d, z, zs = places()
     sib, near_x, near_y = flip(d, 1), flip(d, 2), flip(d, 4)
     diagonal = flip(near_x, 4)
@@ -99,14 +122,14 @@
             )
         )
         loads[k].start()
-    later_loads = [
-        pltpu.make_async_copy(
-            weights.at[pl.ds(first, n), d], held.at[pl.ds(place, n)], later_sem.at[i]
-        )
-        for i, (first, place, n) in enumerate(later)
-    ]
-    for copy in later_loads:
-        copy.start()
+    page_count = table.shape[0] // CAPTION_TILE
+
+    def page(t):
+        return pltpu.make_async_copy(
+            table.at[tile_of(t, CAPTION_TILE)], pages.at[lax.rem(t, 2)], page_sem.at[lax.rem(t, 2)]
+        )
+
+    page(0).start()
     greet([(d, zs[1]), (d, zs[2]), (d, zs[3]), (sib, z), (near_x, z), (near_y, z)])
     pending = []
     all_ids[z] = ids[...]
@@ -162,12 +185,51 @@
             )
         )
         stores[k].start()
-    for copy in later_loads:
-        copy.wait()
-
-    @pl.loop(0, held.shape[0])
-    def _(i):
-        slices[i] = held[i].astype(slices.dtype)
+    for copy in id_copies:
+        copy.wait_recv()
+    marks = all_ids[0] + all_ids[1] + all_ids[2] + all_ids[3]
+    found[...] = jnp.zeros_like(found)
+
+    def look_up(t):
+        @pl.when(t + 1 < page_count)
+        def _():
+            page(t + 1).start()
+
+        page(t).wait()
+        row = lax.broadcasted_iota(jnp.int32, (CAPTION_TILE, marks.shape[1]), 0)
+        row = row + (z * table.shape[0] + t * CAPTION_TILE)
+        hits = jnp.zeros(row.shape, jnp.float32)
+        for token in range(marks.shape[0]):
+            hits = hits + jnp.where(row == marks[token : token + 1], 1.0, 0.0)
+        found[...] += contract_first(hits.astype(jnp.bfloat16), pages[lax.rem(t, 2)])
+
+    def look_up_span(first, last):
+        @pl.loop(first, last)
+        def _(t):
+            look_up(t)
+
+    share_of = -(-page_count // (len(chunks) - 1))
+    part_copies = []
+
+    def send_parts():
+        captions = found_parts.shape[1]
+        for owner in range(4):
+            found_parts[owner] = (
+                found[2 * owner * captions : (2 * owner + 1) * captions]
+                + found[(2 * owner + 1) * captions : (2 * owner + 2) * captions]
+            )
+        for o in (1, 2, 3):
+            part_copies.append(
+                pltpu.make_async_remote_copy(
+                    src_ref=found_parts.at[zs[o]],
+                    dst_ref=from_z.at[o - 1],
+                    send_sem=part_send.at[o - 1],
+                    recv_sem=part_recv.at[o - 1],
+                    device_id=(d, zs[o]),
+                    device_id_type=MESH,
+                )
+            )
+            part_copies[-1].start()
 
     along_x, along_y, turn_y, turn_x, last = {}, {}, {}, {}, []
     count = len(chunks)
@@ -194,6 +256,10 @@
                 along_y[k][o - 1].wait_recv()
                 turn_x[k].append(push(k, 11 + o, half, n - half, zz, near_y, (near_x, z)))
                 last.append(push(k, 20 + o, 0, n, zz, near_y, (sib, z)))
+        if step * share_of < page_count:
+            look_up_span(step * share_of, min((step + 1) * share_of, page_count))
+        if step == count - 1:
+            send_parts()
         if step >= 2:
             k, n = step - 2, chunks[step - 2][3]
             for o in (1, 2, 3):
@@ -208,20 +274,14 @@
     for copy in stores:
         copy.wait()
     for copy in id_copies:
+        copy.wait_send()
+    for copy in part_copies:
         copy.wait()
-
-
-def fetch(weights, pieces, later, ids, collective):
+    text_sum[...] = found_parts[z] + from_z[0] + from_z[1] + from_z[2]
+
+
+def fetch(weights, pieces, ids, table, captions, collective):
     depth, eighths = lax.axis_size("fsdp"), lax.axis_size("dp")
-    if depth != 4 or eighths != 8:
-        return (
-            [
-                lax.all_gather(rounded(weights[a : a + n]), "fsdp", axis=1, tiled=True)
-                for a, n in pieces
-            ],
-            lax.all_gather(ids, "fsdp", axis=0),
-            jnp.concatenate([rounded(weights[a : a + n]) for a, n in later], 0),
-        )
     blocks, rows, width = weights.shape
     part = (eighths, rows // eighths, width)
     chunks = []
@@ -229,31 +289,29 @@
         for first in range(0, n, 2):
             chunks.append((a + first, out, first, min(2, n - first)))
     total = sum(n for _, n in pieces)
-    later_places = []
-    for a, n in later:
-        later_places.append((a, sum(m for _, _, m in later_places), n))
-    later_total = sum(n for _, n in later)
     outs = pl.pallas_call(
-        functools.partial(fetch_kernel, chunks, [n for _, n in pieces], later_places),
+        functools.partial(fetch_kernel, chunks, [n for _, n in pieces]),
         out_shape=[
             jax.ShapeDtypeStruct((n, depth) + part, jnp.bfloat16) for _, n in pieces
         ]
-        + [
-            jax.ShapeDtypeStruct((depth,) + ids.shape, ids.dtype),
-            jax.ShapeDtypeStruct((later_total,) + part[1:], jnp.bfloat16),
-        ],
-        in_specs=[pl.BlockSpec(memory_space=pl.ANY), pl.BlockSpec(memory_space=pltpu.VMEM)],
-        out_specs=[pl.BlockSpec(memory_space=pl.ANY)] * len(pieces)
-        + [pl.BlockSpec(memory_space=pltpu.VMEM)] * 2,
+        + [jax.ShapeDtypeStruct((captions, width), jnp.float32)],
+        in_specs=whole("ava"),
+        out_specs=whole("a" * len(pieces) + "v"),
         scratch_shapes=[
             pltpu.VMEM((total,) + part, jnp.float32),
             pltpu.VMEM((total,) + part, jnp.bfloat16),
-            pltpu.VMEM((later_total,) + part[1:], jnp.float32),
+            pltpu.VMEM((depth,) + ids.shape, jnp.int32),
+            pltpu.VMEM((2, CAPTION_TILE, width), jnp.bfloat16),
+            pltpu.VMEM((2 * depth * captions, width), jnp.float32),
+            pltpu.VMEM((depth, captions, width), jnp.float32),
+            pltpu.VMEM((3, captions, width), jnp.float32),
             pltpu.SemaphoreType.DMA((len(chunks),)),
             pltpu.SemaphoreType.DMA((len(chunks),)),
             pltpu.SemaphoreType.DMA((len(chunks), 27)),
             pltpu.SemaphoreType.DMA((len(chunks), 27)),
-            pltpu.SemaphoreType.DMA((len(later),)),
+            pltpu.SemaphoreType.DMA((2,)),
+            pltpu.SemaphoreType.DMA((3,)),
+            pltpu.SemaphoreType.DMA((3,)),
             pltpu.SemaphoreType.DMA((3,)),
             pltpu.SemaphoreType.DMA((3,)),
         ],
@@ -261,8 +319,8 @@
             collective_id=collective, has_side_effects=True, vmem_limit_bytes=VMEM_LIMIT
         ),
         name=f"fetch_{collective}",
-    )(weights.reshape((blocks,) + part), ids)
-    return ([out.reshape(-1, width, width) for out in outs[:-2]], outs[-2], outs[-1])
+    )(weights.reshape((blocks,) + part), ids, table)
+    return ([out.reshape(-1, width, width) for out in outs[:-1]], outs[-1])
 
 
 def gather_later(own):
@@ -341,42 +399,6 @@
     )(*owns)
 
 
-def swap_kernel(parts, out, send, recv):
-    d, z, zs = places()
-    greet([(d, zs[1]), (d, zs[2]), (d, zs[3])])
-    out[z] = parts[z]
-    copies = []
-    for o in (1, 2, 3):
-        copies.append(
-            pltpu.make_async_remote_copy(
-                src_ref=parts.at[zs[o]],
-                dst_ref=out.at[z],
-                send_sem=send.at[o - 1],
-                recv_sem=recv.at[o - 1],
-                device_id=(d, zs[o]),
-                device_id_type=MESH,
-            )
-        )
-        copies[-1].start()
-    for copy in copies:
-        copy.wait()
-
-
-def swap(parts, collective):
-    depth = lax.axis_size("fsdp")
-    if depth != 4 or lax.axis_size("dp") != 8:
-        return lax.all_to_all(parts, "fsdp", 0, 0)
-    return pl.pallas_call(
-        swap_kernel,
-        out_shape=jax.ShapeDtypeStruct(parts.shape, parts.dtype),
-        in_specs=[pl.BlockSpec(memory_space=pltpu.VMEM)],
-        out_specs=pl.BlockSpec(memory_space=pltpu.VMEM),
-        scratch_shapes=[pltpu.SemaphoreType.DMA((3,)), pltpu.SemaphoreType.DMA((3,))],
-        compiler_params=pltpu.CompilerParams(collective_id=collective, has_side_effects=True),
-        name=f"swap_{collective}",
-    )(parts)
-
-
 class Reduction:
     def __init__(self, source, start, first, n, buffers, k, semaphores, spots):
         self.source, self.start, self.first, self.n, self.k = (source, start, first, n, k)
@@ -509,14 +531,117 @@
             copy.wait_send()
 
 
-def reduce_kernel(chunks, sources, sets, *refs):
+class Meeting:
+    def __init__(self, blocks_of, sources, refs):
+        self.blocks_of, self.sources = (blocks_of, sources)
+        self.small_out, self.stats_out, self.mine, self.low = refs[:4]
+        self.parts, self.stats, self.local_sem, self.send, self.recv = refs[4:9]
+        self.part_send, self.part_recv = refs[9:]
+
+    def push(self, slot, source, target, to, sems):
+        copy = pltpu.make_async_remote_copy(
+            src_ref=source,
+            dst_ref=target,
+            send_sem=sems[0].at[slot],
+            recv_sem=sems[1].at[slot],
+            device_id=to,
+            device_id_type=MESH,
+        )
+        copy.start()
+        return copy
+
+    def run(self, small, results, spots, others):
+        d, z, zs = spots[:3]
+        total = jnp.zeros(results[0].shape[1:], jnp.float32)
+        homes = {
+            int(block): (lane, place)
+            for lane, entry in enumerate(self.blocks_of)
+            for place, block in enumerate(entry)
+        }
+        for block, (source, index) in enumerate(self.sources):
+            value = results[source][index]
+            total = total + value * value
+            value = value.astype(self.low.dtype)
+            self.low[block] = value
+            lane, place = homes[block]
+            self.parts[lane, place] = value
+        for lane, entry in enumerate(self.blocks_of):
+            for place, block in enumerate(entry):
+                if block < 0:
+                    self.parts[lane, place] = jnp.zeros_like(self.parts[lane, place])
+        squares = jnp.sum(total, axis=(0, 1), keepdims=True)
+        self.stats[...] = jnp.broadcast_to(squares, self.stats.shape)
+        moved = [
+            self.push(
+                i,
+                self.parts.at[other],
+                self.mine.at[:, d],
+                (other, z),
+                (self.part_send, self.part_recv),
+            )
+            for i, other in enumerate(others)
+        ]
+        keep = pltpu.make_async_copy(self.parts.at[d], self.mine.at[:, d], self.local_sem)
+        keep.start()
+        pairs = [(small, self.small_out), (self.stats, self.stats_out)]
+        for own, out in pairs:
+            out[z, d] = own[...]
+        started = []
+
+        def push_all(slot, origin, to, first=False):
+            copies = []
+            for i, (own, out) in enumerate(pairs):
+                copies.append(
+                    self.push(
+                        slot,
+                        own if first else out.at[:, origin],
+                        out.at[z, origin] if first else out.at[:, origin],
+                        to,
+                        (self.send.at[i], self.recv.at[i]),
+                    )
+                )
+            started.extend(copies)
+            return copies
+
+        def arrive(copies):
+            for copy in copies:
+                copy.wait_recv()
+
+        first = [push_all(o - 1, d, (d, zs[o]), True) for o in (1, 2, 3)]
+        for copies in first:
+            arrive(copies)
+        second = [push_all(3 + i, d, (to, z)) for i, to in enumerate(others[:3])]
+        last = [push_all(6, d, (others[3], z))]
+        for i, origin in enumerate(others[:3]):
+            arrive(second[i])
+            last.append(push_all(7 + i, origin, (others[3], z)))
+        for copies in last:
+            arrive(copies)
+        arrive(moved)
+        for copy in started + moved:
+            copy.wait_send()
+        keep.wait()
+
+
+def reduce_kernel(chunks, sources, sets, meeting, *refs):
     ins = refs[:sources]
-    outs = refs[sources : sources + sets]
-    buffers = [refs[sources + sets + 6 * i : sources + sets + 6 * i + 6] for i in range(sets)]
-    semaphores = refs[sources + 7 * sets :]
+    refs = refs[sources:]
+    if meeting is not None:
+        earlier, refs = (refs[0], refs[1:])
+    outs = refs[:sets]
+    refs = refs[sets:]
+    if meeting is not None:
+        outside, refs = (refs[:4], refs[4:])
+    buffers = [refs[6 * i : 6 * i + 6] for i in range(sets)]
+    semaphores = refs[6 * sets : 6 * sets + 3]
     d, z, zs = places()
     spots = (d, z, zs, lax.rem(d // 2, 2), d // 4, lax.rem(d, 2))
-    greet([(d, zs[1]), (d, zs[2]), (d, zs[3]), (flip(d, 1), z), (flip(d, 2), z), (flip(d, 4), z)])
+    sib, near_x, near_y = (flip(d, 1), flip(d, 2), flip(d, 4))
+    diagonal = flip(near_x, 4)
+    others = [near_x, near_y, diagonal, sib, flip(near_x, 1), flip(near_y, 1), flip(diagonal, 1)]
+    if meeting is None:
+        others = [near_x, near_y, sib]
+    greet([(d, zs[1]), (d, zs[2]), (d, zs[3])] + [(other, z) for other in others])
     work = []
     for k, (source, start, first, n, which) in enumerate(chunks):
         work.append(
@@ -533,9 +658,12 @@
             work[step - 2].along_z()
         if step >= 3:
             work[step - 3].finish(outs[chunks[step - 3][4]])
-
-
-def reduce_grads(grads, small, collective):
+    if meeting is not None:
+        tail = Meeting(*meeting, tuple(outside) + tuple(refs[6 * sets + 3 :]))
+        tail.run(outs[1].at[0], (outs[0], earlier), spots, others)
+
+
+def reduce_grads(grads, collective, small=None, meeting=None, earlier=None):
     lanes, depth = lax.axis_size("dp"), lax.axis_size("fsdp")
     rows = D // (lanes * depth)
     tail = (depth, 2, 2, 2)
@@ -562,23 +690,43 @@
             pltpu.VMEM((n, depth) + shape, kind),
             pltpu.VMEM((n, 3) + shape, kind),
         ]
-    outs = pl.pallas_call(
-        functools.partial(reduce_kernel, chunks, len(sources), len(sets)),
-        out_shape=[jax.ShapeDtypeStruct((n,) + shape, jnp.float32) for n, shape, _ in sets],
-        in_specs=[pl.BlockSpec(memory_space=pl.ANY)] * len(sources),
-        out_specs=[pl.BlockSpec(memory_space=pltpu.VMEM)] * len(sets),
-        scratch_shapes=scratch
-        + [
-            pltpu.SemaphoreType.DMA((len(chunks),)),
-            pltpu.SemaphoreType.DMA((len(chunks), 8)),
-            pltpu.SemaphoreType.DMA((len(chunks), 8)),
-        ],
+    scratch += [
+        pltpu.SemaphoreType.DMA((len(chunks),)),
+        pltpu.SemaphoreType.DMA((len(chunks), 8)),
+        pltpu.SemaphoreType.DMA((len(chunks), 8)),
+    ]
+    out_shape = [jax.ShapeDtypeStruct((n,) + shape, jnp.float32) for n, shape, _ in sets]
+    count = len(sources)
+    if meeting is not None:
+        blocks_of, origins = meeting
+        most = len(blocks_of[0])
+        out_shape += [
+            jax.ShapeDtypeStruct((depth, lanes) + small.shape[1:], jnp.float32),
+            jax.ShapeDtypeStruct((depth, lanes, 8, 128), jnp.float32),
+            jax.ShapeDtypeStruct((most, lanes, rows, D), jnp.bfloat16),
+            jax.ShapeDtypeStruct((len(origins), rows, D), jnp.bfloat16),
+        ]
+        scratch += [
+            pltpu.VMEM((lanes, most, rows, D), jnp.bfloat16),
+            pltpu.VMEM((8, 128), jnp.float32),
+            pltpu.SemaphoreType.DMA,
+            pltpu.SemaphoreType.DMA((2, 10)),
+            pltpu.SemaphoreType.DMA((2, 10)),
+            pltpu.SemaphoreType.DMA((7,)),
+            pltpu.SemaphoreType.DMA((7,)),
+        ]
+        sources.append(earlier)
+    return pl.pallas_call(
+        functools.partial(reduce_kernel, chunks, count, len(sets), meeting),
+        out_shape=out_shape,
+        in_specs=whole("a" * count + "v" * (len(sources) - count)),
+        out_specs=whole("v" * len(out_shape)),
+        scratch_shapes=scratch,
         compiler_params=pltpu.CompilerParams(
             collective_id=collective, has_side_effects=True, vmem_limit_bytes=VMEM_LIMIT
         ),
         name=f"reduce_{collective}",
     )(*sources)
-    return (outs[0], outs[1] if small is not None else None)
 
 
 def spread_stages(own, out, local_sem, send, recv):
@@ -640,72 +788,6 @@
         keep.wait()
 
     return (begin, forward, collect, finish)
-
-
-def meet_kernel(own, parts, out, mine, local_sem, send, recv, part_send, part_recv):
-    d, z, zs = places()
-    sib, near_x, near_y = flip(d, 1), flip(d, 2), flip(d, 4)
-    diagonal = flip(near_x, 4)
-    others = [near_x, near_y, diagonal, sib, flip(near_x, 1), flip(near_y, 1), flip(diagonal, 1)]
-    greet([(d, zs[1]), (d, zs[2]), (d, zs[3])] + [(other, z) for other in others])
-    out[d, z] = own[...]
-
-    def push(slot, source, target, to, sems=(send, recv)):
-        copy = pltpu.make_async_remote_copy(
-            src_ref=source,
-            dst_ref=target,
-            send_sem=sems[0].at[slot],
-            recv_sem=sems[1].at[slot],
-            device_id=to,
-            device_id_type=MESH,
-        )
-        copy.start()
-        return copy
-
-    first = [push(o - 1, own, out.at[d, z], (d, zs[o])) for o in (1, 2, 3)]
-    moved = [
-        push(i, parts.at[other], mine.at[:, d], (other, z), (part_send, part_recv))
-        for i, other in enumerate(others)
-    ]
-    keep = pltpu.make_async_copy(parts.at[d], mine.at[:, d], local_sem)
-    keep.start()
-    for copy in first:
-        copy.wait_recv()
-    second = [push(3 + i, out.at[d], out.at[d], (to, z)) for i, to in enumerate(others[:3])]
-    last = [push(6, out.at[d], out.at[d], (sib, z))]
-    for i, origin in enumerate(others[:3]):
-        second[i].wait_recv()
-        last.append(push(7 + i, out.at[origin], out.at[origin], (sib, z)))
-    for copy in last + moved:
-        copy.wait_recv()
-    for copy in first + second + last + moved:
-        copy.wait_send()
-    keep.wait()
-
-
-def meet(own, parts, collective):
-    lanes, depth = lax.axis_size("dp"), lax.axis_size("fsdp")
-    rest = parts.shape[1:]
-    return pl.pallas_call(
-        meet_kernel,
-        out_shape=[
-            jax.ShapeDtypeStruct((lanes, depth) + own.shape, own.dtype),
-            jax.ShapeDtypeStruct(rest[:1] + (lanes,) + rest[1:], parts.dtype),
-        ],
-        in_specs=[pl.BlockSpec(memory_space=pltpu.VMEM)] * 2,
-        out_specs=[pl.BlockSpec(memory_space=pltpu.VMEM)] * 2,
-        scratch_shapes=[
-            pltpu.SemaphoreType.DMA,
-            pltpu.SemaphoreType.DMA((10,)),
-            pltpu.SemaphoreType.DMA((10,)),
-            pltpu.SemaphoreType.DMA((7,)),
-            pltpu.SemaphoreType.DMA((7,)),
-        ],
-        compiler_params=pltpu.CompilerParams(
-            collective_id=collective, has_side_effects=True, vmem_limit_bytes=VMEM_LIMIT
-        ),
-        name=f"meet_{collective}",
-    )(own, parts)
 
 
 GRAM_TILE = 128
@@ -1104,6 +1186,15 @@
     return copies
 
 
+def stand_up(row):
+    return jnp.broadcast_to(row, (8, row.shape[1])).T[:, :1]
+
+
+def slot_marks(segment, b):
+    row = segment[b : b + 1].astype(jnp.float32)
+    return (stand_up(row), row)
+
+
 def norm_rows(source, gains, first, target):
     gain, shift = (gains[first : first + 1], gains[first + 1 : first + 2])
 
@@ -1114,12 +1205,11 @@
 
 
 def forward_kernel(
+    spans,
+    base,
     state,
     gains,
-    gain_query,
-    gain_key,
-    rows,
-    columns,
+    segment,
     mixing,
     mixing_out,
     upward,
@@ -1135,21 +1225,29 @@
     up_held,
     down_held,
     hidden,
+    gain_query,
+    gain_key,
     sem,
 ):
+    mixing, mixing_out, upward, down = [
+        ref.at[pl.ds(*span)] for ref, span in zip((mixing, mixing_out, upward, down), spans)
+    ]
     loads = load_all(
         [(mixing, mixing_held), (mixing_out, out_held), (upward, up_held), (down, down_held)], sem
     )
-    norm_rows(state, gains, 0, heads_low)
+    gain_query[...] = stand_up(gains[base + 4 : base + 5])
+    gain_key[...] = stand_up(gains[base + 5 : base + 6])
+    norm_rows(state, gains, base, heads_low)
     loads[0].wait()
 
     @pl.loop(0, 3 * D // TILE)
     def _(t):
         mixed[tile_of(t)] = contract_last(mixing_held[tile_of(t)], heads_low[...])
 
-    parts, length = (rows.shape[0], rows.shape[1])
+    parts, length = segment.shape
     for b in range(parts):
-        same = rows[b] == columns[b]
+        column, row = slot_marks(segment, b)
+        same = column == row
         tokens = slice(b * length, (b + 1) * length)
 
         @pl.loop(0, D // GROUP)
@@ -1172,7 +1270,7 @@
     for t in range(state.shape[0] // TILE):
         part = slice(t * TILE, (t + 1) * TILE)
         middle[part] = state[part] + contract_first(attended[:, part], out_held[...])
-    norm_rows(middle, gains, 2, normed_low)
+    norm_rows(middle, gains, base + 2, normed_low)
     loads[2].wait()
 
     @pl.loop(0, FF // TILE)
@@ -1186,26 +1284,16 @@
         state_out[part] = middle[part] + contract_first(hidden[:, part], down_held[...])
 
 
-def attention_operands(gains, segment):
-    return (
-        jnp.pad(gains[:4], ((0, 4), (0, 0))),
-        gains[4][:, None],
-        gains[5][:, None],
-        segment[:, :, None],
-        segment[:, None, :],
-    )
-
-
-def whole(*memory):
-    kinds = {"v": pltpu.VMEM, "a": pl.ANY}
-    return [pl.BlockSpec(memory_space=kinds[kind]) for kind in memory[0]]
-
-
-def layer_forward(state, blocks, gains, segment):
+def layer_weights(blocks):
+    weights = [array.reshape(-1, D) for array, _, _ in blocks]
+    return (weights, [(first * D, number * D) for _, first, number in blocks])
+
+
+def layer_forward(state, blocks, gains, base, segment):
     tokens = state.shape[0]
-    weights = [block.reshape(-1, D) for block in blocks]
+    weights, spans = layer_weights(blocks)
     state_out, middle, mixed, heads_low, attended, normed_low = pl.pallas_call(
-        forward_kernel,
+        functools.partial(forward_kernel, spans, base),
         out_shape=[
             jax.ShapeDtypeStruct((tokens, D), jnp.float32),
             jax.ShapeDtypeStruct((tokens, D), jnp.float32),
@@ -1214,25 +1302,29 @@
             jax.ShapeDtypeStruct((D, tokens), jnp.bfloat16),
             jax.ShapeDtypeStruct((tokens, D), jnp.bfloat16),
         ],
-        in_specs=whole("vvvvvvaaaa"),
+        in_specs=whole("vvvaaaa"),
         out_specs=whole("vvvvvv"),
-        scratch_shapes=[pltpu.VMEM(weight.shape, jnp.bfloat16) for weight in weights]
-        + [pltpu.VMEM((FF, tokens), jnp.bfloat16), pltpu.SemaphoreType.DMA((4,))],
+        scratch_shapes=[pltpu.VMEM((number, D), jnp.bfloat16) for _, number in spans]
+        + [
+            pltpu.VMEM((FF, tokens), jnp.bfloat16),
+            pltpu.VMEM((D, 1), jnp.float32),
+            pltpu.VMEM((D, 1), jnp.float32),
+            pltpu.SemaphoreType.DMA((4,)),
+        ],
         compiler_params=pltpu.CompilerParams(vmem_limit_bytes=VMEM_LIMIT),
         name="layer_forward",
-    )(state, *attention_operands(gains, segment), *weights)
+    )(state, gains, segment, *weights)
     return (state_out, (state, middle, mixed, heads_low, attended, normed_low))
 
 
 def backward_kernel(
+    spans,
+    base,
     grad,
     middle,
     normed_low,
     gains,
-    gain_query,
-    gain_key,
-    rows,
-    columns,
+    segment,
     state,
     mixed,
     heads_low,
@@ -1265,9 +1357,14 @@
     made_down,
     made_mixing,
     made_out,
+    gain_query,
+    gain_key,
     sem,
     store_sem,
 ):
+    mixing, mixing_out, upward, down = [
+        ref.at[pl.ds(*span)] for ref, span in zip((mixing, mixing_out, upward, down), spans)
+    ]
     loads = load_all(
         [
             (upward, up_held),
@@ -1289,6 +1386,8 @@
     ]
     tokens = grad.shape[0]
     gain_out[...] = jnp.zeros_like(gain_out)
+    gain_query[...] = stand_up(gains[base + 4 : base + 5])
+    gain_key[...] = stand_up(gains[base + 5 : base + 6])
 
     @pl.loop(0, tokens // 64)
     def _(t):
@@ -1317,7 +1416,7 @@
         inner[part] = contract_first(hidden_grad[:, part], up_held[...])
 
     def norm_back(source, first, previous, target, target_low):
-        gain = gains[first : first + 1]
+        gain = gains[base + first : base + first + 1]
 
         @pl.loop(0, tokens // 64)
         def _(t):
@@ -1349,9 +1448,10 @@
 
     stores[2].start()
     loads[4].wait()
-    parts, length = (rows.shape[0], rows.shape[1])
+    parts, length = segment.shape
     for b in range(parts):
-        same = rows[b] == columns[b]
+        column, row = slot_marks(segment, b)
+        same = column == row
         span = slice(b * length, (b + 1) * length)
 
         @pl.loop(0, D // GROUP)
@@ -1411,20 +1511,20 @@
         copy.wait()
 
 
-def layer_backward(grad, kept, blocks, gains, segment):
+def layer_backward(grad, kept, blocks, gains, base, segment):
     state, middle, mixed, heads_low, attended, normed_low = kept
     tokens = grad.shape[0]
-    weights = [block.reshape(-1, D) for block in blocks]
+    weights, spans = layer_weights(blocks)
     low = jnp.bfloat16
     grad, gain_grads, head_gains, *block_grads = pl.pallas_call(
-        backward_kernel,
+        functools.partial(backward_kernel, spans, base),
         out_shape=[
             jax.ShapeDtypeStruct((tokens, D), jnp.float32),
             jax.ShapeDtypeStruct((8, D), jnp.float32),
             jax.ShapeDtypeStruct((segment.shape[0], 2, D, 1), jnp.float32),
         ]
-        + [jax.ShapeDtypeStruct(weight.shape, low) for weight in weights],
-        in_specs=whole("vvvvvvvvaaaaaaaa"),
+        + [jax.ShapeDtypeStruct((number, D), low) for _, number in spans],
+        in_specs=whole("vvvvvaaaaaaaa"),
         out_specs=whole("vvvaaaa"),
         scratch_shapes=[
             pltpu.VMEM(state.shape, jnp.float32),
@@ -1432,7 +1532,7 @@
             pltpu.VMEM(heads_low.shape, low),
             pltpu.VMEM(attended.shape, low),
         ]
-        + [pltpu.VMEM(weight.shape, low) for weight in weights]
+        + [pltpu.VMEM((number, D), low) for _, number in spans]
         + [
             pltpu.VMEM((tokens, D), low),
             pltpu.VMEM((tokens, D), jnp.float32),
@@ -1443,12 +1543,14 @@
             pltpu.VMEM((FF, D), low),
             pltpu.VMEM((3 * D, D), low),
             pltpu.VMEM((D, D), low),
+            pltpu.VMEM((D, 1), jnp.float32),
+            pltpu.VMEM((D, 1), jnp.float32),
             pltpu.SemaphoreType.DMA((8,)),
             pltpu.SemaphoreType.DMA((4,)),
         ],
         compiler_params=pltpu.CompilerParams(vmem_limit_bytes=60 * 1024 * 1024),
         name="layer_backward",
-    )(grad, middle, normed_low, *attention_operands(gains, segment), state, mixed, heads_low, attended, *weights)
+    )(grad, middle, normed_low, gains, segment, state, mixed, heads_low, attended, *weights)
     gain_grads = jnp.concatenate([gain_grads[:4], jnp.sum(head_gains[..., 0], 0)], 0)
     return (grad, block_grads, gain_grads)
 
@@ -1476,15 +1578,16 @@
     )
 
 
-def pool_sequence(state, gains, rows, columns):
+def pool_sequence(state, gains, marks_of):
     unit, scale = row_norm(state)
     final = unit * gains[0:1] + gains[1:2]
     marks = head_marks()
     logits = full_dot(final * gains[2:3], marks) * (1.0 / math.sqrt(HD))
+    rows, columns = marks_of
     slot = lax.broadcasted_iota(jnp.int32, (rows.shape[0], IMGS), 1)
-    member = (rows == slot).astype(jnp.float32)
+    member = (rows == slot.astype(jnp.float32)).astype(jnp.float32)
     slot = lax.broadcasted_iota(jnp.int32, (IMGS, columns.shape[1]), 0)
-    member_rows = (columns == slot).astype(jnp.float32)
+    member_rows = (columns == slot.astype(jnp.float32)).astype(jnp.float32)
     tops = jnp.zeros_like(logits)
     for k in range(IMGS):
         here = rows == k
@@ -1504,11 +1607,11 @@
     return lax.rsqrt(jnp.mean(value * value, -1, keepdims=True) + 1e-06)
 
 
-def pool_kernel(state, gains, rows, columns, matrix, pooled_low, embedded, image_low):
-    parts, length = (rows.shape[0], rows.shape[1])
+def pool_kernel(base, state, gains, segment, matrix, pooled_low, embedded, image_low):
+    parts, length = segment.shape
     for b in range(parts):
         pooled = pool_sequence(
-            state[b * length : (b + 1) * length], gains[...], rows[b], columns[b]
+            state[b * length : (b + 1) * length], gains[base : base + 3], slot_marks(segment, b)
         )[-1]
         pooled_low[b] = pooled.astype(jnp.bfloat16)
         value = jnp.dot(
@@ -1518,24 +1621,25 @@
         image_low[b] = (value * unit_scale(value) * (1.0 / math.sqrt(D))).astype(jnp.bfloat16)
 
 
-def pool_forward(state, gains, segment, matrix):
+def pool_forward(state, gains, base, segment, matrix):
     parts = segment.shape[0]
     shape = (parts, IMGS, D)
     return pl.pallas_call(
-        pool_kernel,
+        functools.partial(pool_kernel, base),
         out_shape=[
             jax.ShapeDtypeStruct(shape, jnp.bfloat16),
             jax.ShapeDtypeStruct(shape, jnp.float32),
             jax.ShapeDtypeStruct(shape, jnp.bfloat16),
         ],
-        in_specs=whole("vvvvv"),
+        in_specs=whole("vvvv"),
         out_specs=whole("vvv"),
         compiler_params=pltpu.CompilerParams(vmem_limit_bytes=VMEM_LIMIT),
         name="pool_forward",
-    )(state, gains, segment[:, :, None], segment[:, None, :], matrix)
+    )(state, gains, segment, matrix)
 
 
 def contrast_kernel(
+    base,
     me,
     images,
     texts,
@@ -1544,9 +1648,8 @@
     own_images,
     own_live,
     state,
-    gains,
-    rows,
-    columns,
+    all_gains,
+    segment,
     matrix,
     pooled_low,
     embedded,
@@ -1556,7 +1659,8 @@
     gain_out,
     text_side,
 ):
-    parts, length = (rows.shape[0], rows.shape[1])
+    parts, length = segment.shape
+    gains = all_gains[base : base + 3]
     everyone = images.shape[1]
     count = jnp.zeros((1, 1), jnp.float32)
     for b in range(parts):
@@ -1613,7 +1717,7 @@
         pooled_grad = contract_last(embed_low, matrix[...])
         unit, norm_scale, final, marks, member, member_rows, share, spread_share, dead, _ = (
             pool_sequence(
-                state[b * length : (b + 1) * length], gains[...], rows[b], columns[b]
+                state[b * length : (b + 1) * length], gains, slot_marks(segment, b)
             )
         )
         token_grad = full_dot(member, pooled_grad)
@@ -1637,17 +1741,17 @@
     grad_matrix[...] = grad_sum.astype(jnp.bfloat16)
 
 
-def contrast(me, images, texts, alive, own_images, live, state, gains, segment, matrix, pooled_low, embedded):
+def contrast(me, images, texts, alive, own_images, live, state, gains, base, segment, matrix, pooled_low, embedded):
     parts, everyone = alive.shape
     loss, grad, grad_matrix, gain_grads = pl.pallas_call(
-        contrast_kernel,
+        functools.partial(contrast_kernel, base),
         out_shape=[
             jax.ShapeDtypeStruct((8, 128), jnp.float32),
             jax.ShapeDtypeStruct(state.shape, jnp.float32),
             jax.ShapeDtypeStruct((D, D), jnp.bfloat16),
             jax.ShapeDtypeStruct((8, D), jnp.float32),
         ],
-        in_specs=[pl.BlockSpec(memory_space=pltpu.SMEM)] + whole("vvvvvvvvvvvvv"),
+        in_specs=[pl.BlockSpec(memory_space=pltpu.SMEM)] + whole("vvvvvvvvvvvv"),
         out_specs=whole("vvvv"),
         scratch_shapes=[pltpu.VMEM((everyone, D), jnp.float32)],
         compiler_params=pltpu.CompilerParams(vmem_limit_bytes=VMEM_LIMIT),
@@ -1662,8 +1766,7 @@
         live[:, :, None],
         state,
         gains,
-        segment[:, :, None],
-        segment[:, None, :],
+        segment,
         matrix,
         pooled_low,
         embedded,
@@ -1752,30 +1855,45 @@
     depth = lax.axis_size("fsdp")
     captions = MB * IMGS
     tokens = text_ids.shape[3]
-    own_ids = jnp.pad(text_ids.reshape(captions, tokens), ((0, 0), (0, 128 - tokens)))
+    fast = depth == 4 and lanes == 8
     early = [(0, 1), (2, 3), (5, 1), (6, 4), (10, 4), (1, 1)]
     later = []
     for index in range(1, LAYERS):
         start = 2 + 12 * index
         early = early + [(start, 3), (start + 3, 1)]
         later = later + [(start + 4, 4), (start + 8, 4)]
-    (stem, *first_blocks), ids, later_part = fetch(weights, early, later, own_ids, 1)
+    later_own = jnp.concatenate([weights[a : a + n] for a, n in later], 0)
+    if fast:
+        eighth = weights.shape[1] // lanes
+        later_own = lax.dynamic_slice_in_dim(later_own, lax.axis_index("dp") * eighth, eighth, 1)
+    later_blocks = gather_later(rounded(later_own))
+    if fast:
+        half = tokens // 2
+        own_ids = jnp.transpose(text_ids.reshape(captions, 2, half), (2, 1, 0)).reshape(half, -1)
+        place = jnp.arange(depth * 2 * captions, dtype=jnp.int32) // (2 * captions)
+        own_ids = jnp.where(
+            place[None] == lax.axis_index("fsdp"), jnp.tile(own_ids, (1, depth)), 0
+        )
+        (stem, *first_blocks), text_sum = fetch(weights, early, own_ids, table, captions, 1)
+    else:
+        stem, *first_blocks = [
+            lax.all_gather(rounded(weights[a : a + n]), "fsdp", axis=1, tiled=True)
+            for a, n in early
+        ]
+        ids = lax.all_gather(text_ids.reshape(captions, tokens), "fsdp", axis=0)
+        picked = ids.reshape(depth * captions, -1) - lax.axis_index("fsdp") * table.shape[0]
+        row = jnp.arange(table.shape[0], dtype=jnp.int32)
+        hits = jnp.sum((picked[:, :, None] == row[None, None, :]).astype(jnp.int32), 1)
+        text_sum = lax.psum_scatter(
+            jnp.dot(
+                rounded(hits.astype(jnp.float32)), table, preferred_element_type=jnp.float32
+            ).reshape(depth, captions, D),
+            "fsdp",
+            scatter_dimension=0,
+        )
     early_blocks = first_blocks[5:]
     pooling_matrix = first_blocks[4][0]
     first_blocks = first_blocks[:4]
-    later_blocks = gather_later(later_part)
-    ids = ids[:, :, :tokens]
-    flat_ids = ids.reshape(depth * captions, -1)
-    share_rows = table.shape[0]
-    picked = flat_ids - lax.axis_index("fsdp") * share_rows
-    hits = jnp.sum(
-        (picked[:, :, None] == jnp.arange(share_rows, dtype=jnp.int32)[None, None, :]).astype(
-            jnp.int32
-        ),
-        1,
-    )
-    parts = jnp.dot(rounded(hits.astype(jnp.float32)), table, preferred_element_type=jnp.float32)
-    text_sum = jnp.sum(swap(parts.reshape(depth, captions, D), 11), 0)
     text_low = rounded(unit_rows(text_sum / text_ids.shape[-1]))
     me = lax.axis_index(("dp", "fsdp"))
     segment = segments[:, 0]
@@ -1789,17 +1907,15 @@
     saved = []
     for index in range(LAYERS):
         if index == 0:
-            blocks = first_blocks
+            blocks = [(array, 0, array.shape[0]) for array in first_blocks]
         else:
             first = 8 * index - 8
-            blocks = early_blocks[2 * index - 2 : 2 * index] + [
-                later_blocks[first : first + 4],
-                later_blocks[first + 4 : first + 8],
-            ]
-        state, kept = layer_forward(state, blocks, gains[6 * index : 6 * index + 6], segment)
+            blocks = [
+                (array, 0, array.shape[0]) for array in early_blocks[2 * index - 2 : 2 * index]
+            ] + [(later_blocks, first, 4), (later_blocks, first + 4, 4)]
+        state, kept = layer_forward(state, blocks, gains, 6 * index, segment)
         saved.append((kept, blocks))
-    pool_gains = jnp.pad(gains[fin : fin + 3], ((0, 5), (0, 0)))
-    pooled_low, embedded, image_low = pool_forward(state, pool_gains, segment, pooling_matrix)
+    pooled_low, embedded, image_low = pool_forward(state, gains, fin, segment, pooling_matrix)
     own_flags = jnp.broadcast_to(live.reshape(captions, 1), (captions, 128)).astype(jnp.bfloat16)
     both = jnp.stack([image_low.reshape(captions, D), text_low]).reshape(2 * captions, D)
     gathered, flags = share([both, own_flags], 8)
@@ -1816,7 +1932,8 @@
         image_low,
         live,
         state,
-        pool_gains,
+        gains,
+        fin,
         segment,
         pooling_matrix,
         pooled_low,
@@ -1824,17 +1941,16 @@
     )
     gain_parts = [None] * LAYERS
     block_grads = [None] * LAYERS
-    fast = depth == 4 and lanes == 8
     slices = [None] * LAYERS
     for index in reversed(range(LAYERS)):
         kept, blocks = saved[index]
         grad, block_grads[index], gain_parts[index] = layer_backward(
-            grad, kept, blocks, gains[6 * index : 6 * index + 6], segment
+            grad, kept, blocks, gains, 6 * index, segment
         )
         if index == 1:
             block_grads[index].append(grad_pool)
         if fast and index > 0:
-            slices[index], _ = reduce_grads(block_grads[index], None, 4 + index)
+            (slices[index],) = reduce_grads(block_grads[index], 4 + index)
     grad_low = rounded(grad)
     grad_patch = rounded(product(grad_low, patch_low, "sr,sd->rd"))
     block_grads[0].append(grad_patch)
@@ -1855,30 +1971,22 @@
         width = 256
         small = jnp.concatenate([gains_grad.reshape(-1), loss_part[None]])
         small = jnp.pad(small, (0, lanes * depth * 8 * width - small.shape[0]))
-        slices[0], small = reduce_grads(
-            block_grads[0], small.reshape(lanes * depth, 8, width), 4
-        )
-        squares = jnp.sum(slices[0] * slices[0]) + jnp.sum(slices[1] * slices[1])
-        slices = [rounded(value) for value in slices]
-        slices = jnp.concatenate(
-            [slices[0][12:], slices[1][12:]] + [values[:12] for values in slices], 0
-        )
-        empty = jnp.zeros((1,) + slices.shape[1:], slices.dtype)
-        parts = jnp.concatenate(
-            [
-                slices[block : block + 1] if block >= 0 else empty
-                for block in lane_blocks(plan).reshape(-1)
-            ],
-            0,
-        ).reshape((lanes, -1) + slices.shape[1:])
-        squares = jnp.broadcast_to(squares, (8, width))
-        shared, mine = meet(jnp.concatenate([small[0], squares], 0), parts, 9)
-        flat = jnp.transpose(shared[:, :, :8], (1, 0, 2, 3)).reshape(-1)
+        blocks_here = lane_blocks(plan)
+        origins = [(0, 12), (1, 12)] + [
+            (index, block) for index in range(LAYERS) for block in range(12)
+        ]
+        slices[0], _, small, stats, mine, slices = reduce_grads(
+            block_grads[0],
+            4,
+            small.reshape(lanes * depth, 8, width),
+            (blocks_here, origins),
+            slices[1],
+        )
+        flat = small.reshape(-1)
         gains_grad, loss = (flat[: gains.size].reshape(gains.shape), flat[gains.size])
-        squares = jnp.sum(shared[:, :, 8, 0])
+        squares = jnp.sum(stats[:, :, 0, 0])
         norm = jnp.sqrt(squares + jnp.sum(gains_grad * gains_grad))
         clip = jnp.minimum(1.0, CLIP_LIMIT / (norm + 1e-06))
-        blocks_here = lane_blocks(plan)
         own_momenta = jnp.stack(
             [
                 jnp.where(

time: 854 us -> 818 us (0.958)
  other arithmetic: 49.1 us -> 20.5 us
  local copies, waits for them, and re-layouts: 39.7 us -> 17.5 us
  Pallas kernels: 718 us -> 738 us
    pallas_call x1, Pallas kernels: 98.7 us -> 134 us  [fetch(): pl.pallas_call(functools.partial(fetch_kernel, chunks, [n for _, n in pie...]
    reduce_sum x3 -> x1, other arithmetic: 24.8 us -> 1.54 us  [per_device(): squares = jnp.sum(stats[:, :, 0, 0])]
    pallas_call x10 -> x8, Pallas kernels: 391 us -> 371 us  [the longest x2 185 us: reduce_grads(): pl.pallas_call(functools.partial(reduce_kernel, chunks, count, len(sets),...]
    slice x7 -> x0, local copies, waits for them, and re-layouts: 9.45 us -> none  [the longest x1 8.12 us: per_device(): later_blocks[first + 4:first + 8]]
  transfers between devices with their start and end apart: 1 -> 1, of which waited for: 0 -> 0; matrix products, arithmetic and copies ran while one was open for 6% -> 2% of each run, Pallas kernels for 5% -> 20%
where the time goes in v5:
time: 818 us; the launch traced here: 808 us
  Pallas kernels  738 us (90%)
  between operations  21.5 us (3%)
  other arithmetic  20.5 us (3%)
  local copies, waits for them, and re-layouts  17.5 us (2%)
  matrix products  10.1 us (1%)
    pallas_call x2, Pallas kernels, reduce_grads(): pl.pallas_call(functools.partial(reduce_kernel, chunks, count, len(sets),...  185 us
    pallas_call x1, Pallas kernels, fetch(): pl.pallas_call(functools.partial(fetch_kernel, chunks, [n for _, n in pie...  134 us
    pallas_call x2, Pallas kernels, layer_backward(): pl.pallas_call(functools.partial(backward_kernel, spans, base), out_shape...  97 us
    pallas_call x1, Pallas kernels, spread(): pl.pallas_call(spread_kernel, out_shape=jax.ShapeDtypeStruct(own.shape[:1...  70.8 us
    pallas_call x1, Pallas kernels, sum_grams(): pl.pallas_call(gram_kernel, out_shape=[jax.ShapeDtypeStruct(grams.shape,...  67.4 us
    pallas_call x2, Pallas kernels, layer_forward(): pl.pallas_call(functools.partial(forward_kernel, spans, base), out_shape=...  58.3 us
    pallas_call x1, Pallas kernels, update(): pl.pallas_call(update_kernel, grid_spec=pltpu.PrefetchScalarGridSpec(num_...  35.8 us
    pallas_call x1, Pallas kernels, schulz(): pl.pallas_call(schulz_kernel, out_shape=jax.ShapeDtypeStruct(rows.shape,...  31.8 us
  transfers between devices with their start and end apart: 1, of which 0 were waited for; matrix products, arithmetic and copies ran while one was open for 2% of the time, Pallas kernels for 20%

profile of v5, /device:TPU:0, one launch (start us, length us, event | category | flops | bytes accessed | tf_op | source)
XLA Modules:
  0.0 807.7 jit_solution(2211716977305928232)
XLA Ops:
  7.2 0.0 all-gather.3.cloned.1.call-start
  7.3 2.6 concatenate.12
  10.0 0.7 dynamic-slice_convert_fusion
  10.7 0.1 reshape.237
  10.8 0.1 copy.41
  10.9 0.1 tile.10
  11.0 0.1 tile.12
  11.1 0.4 and_reduce_fusion
  11.5 0.1 fusion.17
  11.7 0.1 convert_element_type.60
  11.8 0.7 copy.48.own_live
  13.2 0.6 constant_dynamic-slice_fusion
  16.4 0.7 dynamic_slice.56.two
  17.8 0.6 broadcast_select_fusion.ids
  18.4 134.0 %fetch_1.1 = (bf16[1,4,8,24,768]{4,3,2,1,0:T(8,128)(2,1)}, bf16[3,4,8,24,768]{4,3,2,1,0:T(8,128)(2,1)}, bf16[1,4,8,24,768]{4,3,2,1,0:T(8,128)(2,1)}, bf16[4,4,8,...) custom-call(f32[26,8,24,768]{3,2,1,0:T(8,128)} %bitcast.100, ...), custom_call_target="tpu_custom_call" | custom-call | tf_op jit(solution)/shard_map/fetch_1/pallas_call | solution.py:292
  152.4 0.4 slice_divide_fusion
  152.8 0.8 fusion.8
  153.7 0.8 fusion.24
  154.5 2.0 fusion.1.state
  156.5 29.2 %layer_forward.2 = (f32[512,768]{1,0:T(8,128)}, f32[512,768]{1,0:T(8,128)}, f32[2304,512]{1,0:T(8,128)}, bf16[512,768]{1,0:T(8,128)(2,1)}, bf16[768,512]{1,0:T(8,128)(2,1)}, /*index=5*/bf16[512,768]{1,0:T(8,128)(2,1)}) custom-call(f32[512,768]{1,0:T(8,128)} %fusion.1.state, f32[79,768]{1,0:T(8,128)} %gains.9, s32[2,256]{1,0:T(2,128)} %bitcast.133, ...), custom_call_target="tpu_custom_call" | custom-call | tf_op jit(solution)/shard_map/layer_forward/pallas_call | solution.py:1295
  185.6 0.6 constant_dynamic-slice_fusion.1
  186.3 0.1 multiply_reduce_fusion.1
  186.4 4.4 dynamic-slice_select_fusion.3
  190.8 0.1 fusion.16
  190.9 29.2 %layer_forward.3 = (f32[512,768]{1,0:T(8,128)}, f32[512,768]{1,0:T(8,128)}, f32[2304,512]{1,0:T(8,128)}, bf16[512,768]{1,0:T(8,128)(2,1)}, bf16[768,512]{1,0:T(8,128)(2,1)}, /*index=5*/bf16[512,768]{1,0:T(8,128)(2,1)}) custom-call(f32[512,768]{1,0:T(8,128)} %get-tuple-element.67.state, f32[79,768]{1,0:T(8,128)} %gains.9, s32[2,256]{1,0:T(2,128)} %bitcast.134, ...), custom_call_target="tpu_custom_call" | custom-call | tf_op jit(solution)/shard_map/layer_forward/pallas_call | solution.py:1295
  220.0 10.4 %pool_forward.1 = (bf16[2,8,768]{2,1,0:T(8,128)(2,1)}, f32[2,8,768]{2,1,0:T(8,128)}, bf16[2,8,768]{2,1,0:T(8,128)(2,1)}) custom-call(f32[512,768]{1,0:T(8,128)} %get-tuple-element.70.state, f32[79,768]{1,0:T(8,128)} %gains.9, s32[2,256]{1,0:T(2,128)} %bitcast.135, bf16[768,768]{1,0:T(8,128)(2,1)} %bitcast.119), custom_call_target="tpu_custom_call" | custom-call | tf_op jit(solution)/shard_map/pool_forward/pallas_call | solution.py:1627
  230.5 1.4 pad_maximum_fusion.1
  231.8 0.7 broadcast_in_dim.38.refs_1_
  232.5 27.5 %share_8.1 = (bf16[8,4,32,768]{3,2,1,0:T(8,128)(2,1)}, bf16[8,4,16,128]{3,2,1,0:T(8,128)(2,1)}) custom-call(bf16[32,768]{1,0:T(8,128)(2,1)} %bitcast.131, bf16[16,128]{1,0:T(8,128)(2,1)} %broadcast_in_dim.38.refs_1_), custom_call_target="tpu_custom_call" | custom-call | tf_op jit(solution)/shard_map/share_8/pallas_call | solution.py:388
  260.0 1.3 copy.53
  261.4 0.9 broadcast_in_dim_reshape.9.alive_rows
  262.3 0.7 broadcast_in_dim_reshape.8.alive_columns
  262.9 1.5 fusion.23
  264.4 1.2 copy_bitcast_fusion
  265.7 20.3 %contrast.1 = (f32[8,128]{1,0:T(8,128)}, f32[512,768]{1,0:T(8,128)}, bf16[768,768]{1,0:T(8,128)(2,1)}, f32[8,768]{1,0:T(8,128)}) custom-call(s32[1]{0:T(128)} %bitcast.me, bf16[2,256,768]{2,1,0:T(8,128)(2,1)} %get-tuple-element.141.images, bf16[2,256,768]{2,1,0:T(8,128)(2,1)} %get-tuple-element.140.texts, ...), custom_call_target="tpu_custom_call" | custom-call | tf_op jit(solution)/shard_map/contrast/pallas_call | solution.py:1746
  285.9 48.5 %layer_backward.2 = (f32[512,768]{1,0:T(8,128)}, f32[8,768]{1,0:T(8,128)}, f32[2,2,768,1]{3,2,1,0:T(8,128)}, bf16[2304,768]{1,0:T(8,128)(2,1)}, bf16[768,768]{1,...) custom-call(f32[512,768]{1,0:T(8,128)} %get-tuple-element.78.grad, ...), custom_call_target="tpu_custom_call" | custom-call | tf_op jit(solution)/shard_map/layer_backward/pallas_call | solution.py:1519
  334.5 48.5 %layer_backward.3 = (f32[512,768]{1,0:T(8,128)}, f32[8,768]{1,0:T(8,128)}, f32[2,2,768,1]{3,2,1,0:T(8,128)}, bf16[2304,768]{1,0:T(8,128)(2,1)}, bf16[768,768]{1,...) custom-call(f32[512,768]{1,0:T(8,128)} %get-tuple-element.84.grad, ...), custom_call_target="tpu_custom_call" | custom-call | tf_op jit(solution)/shard_map/layer_backward/pallas_call | solution.py:1519
  383.0 2.3 fusion.6
  385.2 0.8 fusion.7
  386.0 1.8 convolution_convert_fusion
  387.9 1.7 reduce_sum.46
  389.6 1.7 reduce_sum.47
  391.3 0.5 concatenate.13
  391.8 1.2 slice.77
  393.0 0.7 select_maximum_fusion
  393.7 0.8 reshape_reshape.40.refs_5_
  394.5 80.5 %reduce_5.1.refs_6_ = f32[13,24,768]{2,1,0:T(8,128)} custom-call(bf16[3,4,2,2,2,24,768]{6,5,4,3,2,1,0:T(8,128)(2,1)} %bitcast.121, bf16[1,4,2,2,2,24,768]{6,5,4,3,2,1,0:T(8,128)(2,1)} %bitcast.128, bf16[4,4,2,2,2,24,768]{6,5,4,3,2,1,0:T(8,128)(2,1)} %bitcast.115, bf16[4,4,2,2,2,24,768]{6,5,4,3,2,1,0:T(8,128)(2,1)} %bitcast.116, ...), custom_call_target="tpu_custom_call" | custom-call | tf_op jit(solution)/shard_map/reduce_5/pallas_call | solution.py:719
  474.9 104.1 %reduce_4.1 = (f32[13,24,768]{2,1,0:T(8,128)}, f32[1,8,256]{2,1,0:T(8,128)}, f32[4,8,8,256]{3,2,1,0:T(8,128)}, f32[4,8,8,128]{3,2,1,0:T(8,128)}, bf16[4,8,24,768...) custom-call(bf16[3,4,2,2,2,24,768]{6,5,4,3,2,1,0:T(8,128)(2,1)} %bitcast.122, ...), custom_call_target="tpu_custom_call" | custom-call | tf_op jit(solution)/shard_map/reduce_4/pallas_call | solution.py:719
  579.1 1.1 copy.54
  580.2 0.7 multiply_reduce_fusion
  580.8 1.5 slice_reduce_fusion
  583.8 0.6 slice.97
  584.4 1.5 convert_multiply_fusion
  585.9 1.8 fusion.21
  587.7 0.5 convolution_bitcast_fusion.1
  588.2 0.5 slice.92
  588.7 0.1 slice_select_fusion
  588.8 1.1 convolution_bitcast_fusion
  589.9 2.5 pad_maximum_fusion.gram
  592.4 67.4 %gram_12.1 = (f32[2,768,768]{2,1,0:T(8,128)}, bf16[26,8,24,768]{3,2,1,0:T(8,128)(2,1)}) custom-call(f32[2,768,768]{2,1,0:T(8,128)} %pad_maximum_fusion.gram, bf16[26,24,768]{2,1,0:T(8,128)(2,1)} %get-tuple-element.109.own), custom_call_target="tpu_custom_call" | custom-call | tf_op jit(solution)/shard_map/gram_12/pallas_call | solution.py:943
  659.8 31.8 %schulz.1.own = bf16[4,192,768]{2,1,0:T(8,128)(2,1)} custom-call(s32[1]{0:T(128)} %dynamic_slice.56.two, f32[2,768,768]{2,1,0:T(8,128)} %get-tuple-element.111.gram, f32[4,192,768]{2,1,0:T(8,128)} %get-tuple-element.121.rows), custom_call_target="tpu_custom_call" | custom-call | tf_op jit(solution)/shard_map/schulz/pallas_call | solution.py:1043
  691.7 70.8 %spread_13.1.turned = bf16[4,8,192,768]{3,2,1,0:T(8,128)(2,1)} custom-call(bf16[4,192,768]{2,1,0:T(8,128)(2,1)} %schulz.1.own), custom_call_target="tpu_custom_call" | custom-call | tf_op jit(solution)/shard_map/spread_13/pallas_call | solution.py:1072
  762.5 1.0 multiply_subtract_fusion
  763.5 35.8 %update.1 = (f32[26,192,768]{2,1,0:T(8,128)}, f32[26,192,768]{2,1,0:T(8,128)}, bf16[26,192,768]{2,1,0:T(8,128)(2,1)}) custom-call(s32[52]{0:T(128)} %constant.132.clone.table, f32[26]{0:T(128)} %constant.133.clone.scale, f32[1]{0:T(128)} %bitcast.44.clip, f32[26,192,768]{2,1,0:T(8,128)} %momenta.1, bf16[26,192,768]{2,1,0:T(8,128)(2,1)} %bitcast.109, ...), custom_call_target="tpu_custom_call" | custom-call | tf_op jit(solution)/shard_map/update/pallas_call | solution.py:1101
  (57 shorter events, 0.3 us)
Async XLA Ops:
  7.2 146.5 %copy-start = (bf16[2,1,256,768]{3,2,1,0:T(8,128)(2,1)S(1)}, bf16[2,1,256,768]{3,2,1,0:T(8,128)(2,1)}, u32[]{:S(2)}) copy-start(bf16[2,1,256,768]{3,2,1,0:T(8,128)(2,1)} %param.19) | copy-start | bytes 2359300
  7.2 183.7 %all-gather.3.cloned.1.call-start = ((), (), s32[]{:S(2)}) async-start(), calls=%async_computation | async-start | bytes 9732096 | tf_op jit(solution)/shard_map/all_gather | solution.py:330
  7.2 3.5 copy-start.10
  7.3 3.8 copy-start.9
  7.3 4.2 copy-start.15
  7.3 5.9 copy-start.16
  7.3 9.1 %copy-start.18 = (s32[8]{0:T(128)S(1)}, s32[8]{0:T(128)}, u32[]{:S(2)}) copy-start(s32[8]{0:T(128)} %constant.131.clone) | copy-start | bytes 100
  11.5 140.9 %copy-start.8 = (s32[2,1,256]{2,0,1:T(2,128)}, s32[2,1,256]{2,0,1:T(2,128)S(1)}, u32[]{:S(2)}) copy-start(s32[2,1,256]{2,0,1:T(2,128)S(1)} %copy.58) | copy-start | bytes 6148
  18.4 134.5 %copy-start.2 = (f32[79,768]{1,0:T(8,128)S(1)}, f32[79,768]{1,0:T(8,128)}, u32[]{:S(2)}) copy-start(f32[79,768]{1,0:T(8,128)} %gains.9) | copy-start | bytes 728068
  152.4 1.3 copy-start.17
  156.5 29.2 %copy-start.14 = (pred[8,4]{1,0:T(8,128)(4,1)S(1)}, pred[8,4]{1,0:T(8,128)(4,1)}, u32[]{:S(2)}) copy-start(pred[8,4]{1,0:T(8,128)(4,1)} %constant.129.clone) | copy-start | bytes 100
  156.5 29.8 %copy-start.7 = (f32[16,768]{1,0:T(8,128)S(1)}, f32[16,768]{1,0:T(8,128)}, u32[]{:S(2)}) copy-start(f32[16,768]{1,0:T(8,128)} %get-tuple-element.73) | copy-start | bytes 147460
  383.0 2.3 copy-start.4
  386.0 1.9 copy-start.13
  386.0 1.9 copy-start.12
  387.9 3.4 copy-start.11
  691.7 70.8 %copy-start.3 = (f32[79,768]{1,0:T(8,128)S(1)}, f32[79,768]{1,0:T(8,128)}, u32[]{:S(2)}) copy-start(f32[79,768]{1,0:T(8,128)} %gains.9) | copy-start | bytes 728068
  691.7 70.8 %copy-start.5 = (f32[79,768]{1,0:T(8,128)S(1)}, f32[79,768]{1,0:T(8,128)}, u32[]{:S(2)}) copy-start(f32[79,768]{1,0:T(8,128)} %param.28) | copy-start | bytes 728068
  691.7 70.8 %copy-start.6 = (f32[79,768]{1,0:T(8,128)S(1)}, f32[79,768]{1,0:T(8,128)}, u32[]{:S(2)}) copy-start(f32[79,768]{1,0:T(8,128)} %param.27) | copy-start | bytes 728068
  763.4 35.8 %copy-start.1 = (bf16[2,1,256,768]{3,2,1,0:T(8,128)(2,1)S(1)}, bf16[2,1,256,768]{3,2,1,0:T(8,128)(2,1)}, u32[]{:S(2)}) copy-start(bf16[2,1,256,768]{3,2,1,0:T(8,128)(2,1)} %param.19) | copy-start | bytes 2359300
Sparse Core Ops, SparseCore 0:
  11.5 127.3 all-gather.2

commit v6 on v5

--- a/solution.py
+++ b/solution.py
@@ -793,271 +793,312 @@
 GRAM_TILE = 128
 
 
-def gram_kernel(gram, own, total, shards, left, right, onward, back, sems, local_sem, send, recv):
+def gram_kernel(
+    gram,
+    rows,
+    own,
+    total,
+    all_rows,
+    shards,
+    left,
+    right,
+    onward,
+    back,
+    sems,
+    local_sem,
+    send,
+    recv,
+    row_sems,
+):
     d, z, _ = places()
     up, down = (z + 1, z - 1)
     two = jnp.logical_and(lax.rem(d, 2) == 1, d // 4 == 1)
+    one = jnp.logical_not(two)
     sib, near_x, near_y = flip(d, 1), flip(d, 2), flip(d, 4)
     greet([(d, lax.rem(z + step, 4)) for step in (1, 2, 3)] + [(sib, z), (near_x, z), (near_y, z)])
     stages = spread_stages(own, shards, local_sem, send, recv)
-    stages[0]()
     count = D // GRAM_TILE
 
-    def at(ref, slot, j):
-        return ref.at[slot, pl.ds(j * GRAM_TILE, GRAM_TILE), pl.ds(j * GRAM_TILE, D - j * GRAM_TILE)]
-
-    def copy(source, target, slot, j, way, to):
+    def at(ref, j):
+        return ref.at[pl.ds(j * GRAM_TILE, GRAM_TILE), pl.ds(j * GRAM_TILE, D - j * GRAM_TILE)]
+
+    def copy(source, target, j, way, to):
         return pltpu.make_async_remote_copy(
-            src_ref=at(source, slot, j),
-            dst_ref=at(target, slot, j),
-            send_sem=sems.at[2 * way, slot, j],
-            recv_sem=sems.at[2 * way + 1, slot, j],
+            src_ref=at(source, j),
+            dst_ref=at(target, j),
+            send_sem=sems.at[2 * way, j],
+            recv_sem=sems.at[2 * way + 1, j],
             device_id=(d, to),
             device_id_type=MESH,
         )
 
-    def add(target, slot, j, *terms):
+    def add(target, j, *terms):
         @pl.loop(0, GRAM_TILE // 16)
         def _(i):
-            rows = pl.ds(pl.multiple_of(j * GRAM_TILE + i * 16, 16), 16)
+            part = pl.ds(pl.multiple_of(j * GRAM_TILE + i * 16, 16), 16)
             columns = pl.ds(j * GRAM_TILE, D - j * GRAM_TILE)
-            value = terms[0][slot, rows, columns]
+            value = terms[0][part, columns]
             for term in terms[1:]:
-                value = value + term[slot, rows, columns]
-            target[slot, rows, columns] = value
-
-    def ends(slot):
+                value = value + term[part, columns]
+            target[part, columns] = value
+
+    def ends():
         @pl.when(z == 0)
         def _():
             for j in range(count):
-                copy(gram, left, slot, j, 0, up).start()
+                copy(gram, left, j, 0, up).start()
 
         @pl.when(z == 3)
         def _():
             for j in range(count):
-                copy(gram, right, slot, j, 1, down).start()
-
-    def near(slot, j):
+                copy(gram, right, j, 1, down).start()
+
+    def near(j):
         @pl.when(z == 1)
         def _():
-            copy(onward, left, slot, j, 0, up).wait_recv()
-            add(onward, slot, j, gram, left)
-            copy(onward, left, slot, j, 0, up).start()
+            copy(onward, left, j, 0, up).wait_recv()
+            add(onward, j, gram, left)
+            copy(onward, left, j, 0, up).start()
 
         @pl.when(z == 2)
         def _():
-            copy(back, right, slot, j, 1, down).wait_recv()
-            add(back, slot, j, gram, right)
-            copy(back, right, slot, j, 1, down).start()
-
-    def far(slot, j):
+            copy(back, right, j, 1, down).wait_recv()
+            add(back, j, gram, right)
+            copy(back, right, j, 1, down).start()
+
+    def far(j):
         @pl.when(z == 1)
         def _():
-            copy(back, right, slot, j, 1, down).wait_recv()
-            add(back, slot, j, gram, right)
-            copy(back, right, slot, j, 1, down).start()
-            add(total, slot, j, onward, right)
+            copy(back, right, j, 1, down).wait_recv()
+            add(back, j, gram, right)
+            copy(back, right, j, 1, down).start()
+            add(total, j, onward, right)
 
         @pl.when(z == 2)
         def _():
-            copy(onward, left, slot, j, 0, up).wait_recv()
-            add(onward, slot, j, gram, left)
-            copy(onward, left, slot, j, 0, up).start()
-            add(total, slot, j, onward, right)
-
-    def close(slot, j):
+            copy(onward, left, j, 0, up).wait_recv()
+            add(onward, j, gram, left)
+            copy(onward, left, j, 0, up).start()
+            add(total, j, onward, right)
+
         @pl.when(z == 3)
         def _():
-            copy(gram, left, slot, j, 0, up).wait_recv()
-            add(total, slot, j, left, gram)
+            copy(gram, left, j, 0, up).wait_recv()
+            add(total, j, left, gram)
 
         @pl.when(z == 0)
         def _():
-            copy(gram, right, slot, j, 1, down).wait_recv()
-            add(total, slot, j, gram, right)
-
-    def finish(slot):
+            copy(gram, right, j, 1, down).wait_recv()
+            add(total, j, gram, right)
+
+        lines = slice(j * GRAM_TILE, (j + 1) * GRAM_TILE)
+        for k in range(j + 1, count):
+            columns = slice(k * GRAM_TILE, (k + 1) * GRAM_TILE)
+            total[columns, lines] = total[lines, columns].T
+
+    def finish():
         for j in range(count):
+
             @pl.when(z == 0)
             def _():
-                copy(gram, left, slot, j, 0, up).wait_send()
+                copy(gram, left, j, 0, up).wait_send()
 
             @pl.when(z == 3)
             def _():
-                copy(gram, right, slot, j, 1, down).wait_send()
+                copy(gram, right, j, 1, down).wait_send()
 
             @pl.when(jnp.logical_and(z > 0, z < 3))
             def _():
-                copy(onward, left, slot, j, 0, up).wait_send()
-                copy(back, right, slot, j, 1, down).wait_send()
-
-    def mirror(slot):
-        for i in range(count):
-            for j in range(i + 1, count):
-                block = total[slot, i * GRAM_TILE : (i + 1) * GRAM_TILE, j * GRAM_TILE : (j + 1) * GRAM_TILE]
-                total[slot, j * GRAM_TILE : (j + 1) * GRAM_TILE, i * GRAM_TILE : (i + 1) * GRAM_TILE] = block.T
-
-    ends(0)
+                copy(onward, left, j, 0, up).wait_send()
+                copy(back, right, j, 1, down).wait_send()
+
+    def pass_on(origin, way, to, source=None):
+        return pltpu.make_async_remote_copy(
+            src_ref=all_rows.at[origin] if source is None else source,
+            dst_ref=all_rows.at[origin],
+            send_sem=row_sems.at[2 * way, origin],
+            recv_sem=row_sems.at[2 * way + 1, origin],
+            device_id=(d, to),
+            device_id_type=MESH,
+        )
+
+    def line_of(here):
+        started = []
+        if here < 3:
+            started.append(pass_on(here, 0, here + 1, rows))
+            started[-1].start()
+        if here > 0:
+            started.append(pass_on(here, 1, here - 1, rows))
+            started[-1].start()
+        all_rows[here] = rows[...]
+        from_left = list(range(here - 1, -1, -1))
+        from_right = list(range(here + 1, 4))
+        for i in range(3):
+            if i < len(from_left):
+                pass_on(from_left[i], 0, here).wait_recv()
+                if here < 3:
+                    started.append(pass_on(from_left[i], 0, here + 1))
+                    started[-1].start()
+            if i < len(from_right):
+                pass_on(from_right[i], 1, here).wait_recv()
+                if here > 0:
+                    started.append(pass_on(from_right[i], 1, here - 1))
+                    started[-1].start()
+        return started
+
+    pl.when(one)(ends)
+    stages[0]()
+
+    @pl.when(one)
+    def _():
+        near(0)
+        near(1)
+        near(2)
+        far(0)
 
     @pl.when(two)
     def _():
-        ends(1)
-
-    def guarded(action, item):
-        if item[0] == 0:
-            action(*item)
-        else:
-            pl.when(two)(lambda: action(*item))
-
-    skew = 2
-    items = [(slot, j) for slot in (0, 1) for j in range(count)]
-    for step in range(len(items) + skew):
-        if step < len(items):
-            guarded(near, items[step])
-        if step >= skew:
-            guarded(far, items[step - skew])
-            guarded(close, items[step - skew])
-        if step == 3:
-            stages[1]()
-        if step == count + 1:
-            stages[2]()
-
-    mirror(0)
-
-    @pl.when(two)
+        for here in range(4):
+
+            @pl.when(z == here)
+            def _():
+                for started in line_of(here):
+                    started.wait_send()
+
+    stages[1]()
+
+    @pl.when(one)
     def _():
-        mirror(1)
-
-    finish(0)
-
-    @pl.when(two)
+        near(3)
+        far(1)
+        near(4)
+        far(2)
+
+    stages[2]()
+
+    @pl.when(one)
     def _():
-        finish(1)
+        near(5)
+        far(3)
+        far(4)
+        far(5)
+        finish()
 
     stages[3]()
 
 
-def sum_grams(grams, own, collective):
-    lanes = lax.axis_size("dp")
-    whole = pltpu.VMEM(grams.shape, jnp.float32)
+def sum_grams(gram, rows, own, collective):
+    lanes, depth = lax.axis_size("dp"), lax.axis_size("fsdp")
+    square = pltpu.VMEM(gram.shape, jnp.float32)
     return pl.pallas_call(
         gram_kernel,
         out_shape=[
-            jax.ShapeDtypeStruct(grams.shape, jnp.float32),
+            jax.ShapeDtypeStruct(gram.shape, jnp.float32),
+            jax.ShapeDtypeStruct((depth,) + rows.shape, rows.dtype),
             jax.ShapeDtypeStruct(own.shape[:1] + (lanes,) + own.shape[1:], own.dtype),
         ],
-        in_specs=[pl.BlockSpec(memory_space=pltpu.VMEM)] * 2,
-        out_specs=[
-            pl.BlockSpec(memory_space=pltpu.VMEM),
-            pl.BlockSpec(memory_space=pl.ANY),
-        ],
+        in_specs=whole("vvv"),
+        out_specs=whole("vva"),
         scratch_shapes=[
-            whole,
-            whole,
-            whole,
-            whole,
-            pltpu.SemaphoreType.DMA((4, grams.shape[0], D // GRAM_TILE)),
+            square,
+            square,
+            square,
+            square,
+            pltpu.SemaphoreType.DMA((4, D // GRAM_TILE)),
             pltpu.SemaphoreType.DMA,
             pltpu.SemaphoreType.DMA((14,)),
             pltpu.SemaphoreType.DMA((14,)),
+            pltpu.SemaphoreType.DMA((4, 4)),
         ],
         compiler_params=pltpu.CompilerParams(
             collective_id=collective, has_side_effects=True, vmem_limit_bytes=VMEM_LIMIT
         ),
         name=f"gram_{collective}",
-    )(grams, own)
-
-
-def schulz_kernel(two, gram, rows, out, state, state_low, change, current):
-    tile = 256
-
-    def chain(slot, first, places_here, step):
-        total = jnp.zeros((1, 1), jnp.float32)
-        for t in range(0, D, tile):
-            value = gram[slot, t : t + tile, :]
-            line = lax.broadcasted_iota(jnp.int32, value.shape, 0) + t
+    )(gram, rows, own)
+
+
+def schulz_kernel(two, gram, all_rows, rows, out, state, state_low, change, current):
+    def chains(parts):
+        for slot, first, number in parts:
+            if len(parts) == 1:
+                value = gram[...]
+            else:
+                value = jnp.zeros((D, D), jnp.float32)
+                for z in range(all_rows.shape[0]):
+                    piece = all_rows[z, slot]
+                    value = value + contract_first(piece, piece)
+            line = lax.broadcasted_iota(jnp.int32, value.shape, 0)
             column = lax.broadcasted_iota(jnp.int32, value.shape, 1)
-            total = total + jnp.sum(
-                jnp.where(line == column, value, 0.0), axis=(0, 1), keepdims=True
-            )
-        inverse = 1.0 / (jnp.sqrt(total) + 1e-07)
-
-        @pl.loop(0, D // tile)
-        def _(t):
-            part = pl.ds(pl.multiple_of(t * tile, tile), tile)
-            value = gram[slot, part, :] * (inverse * inverse)
-            state[part, :] = value
-            state_low[part, :] = value.astype(jnp.bfloat16)
-
-        for place in range(places_here):
-            current[first + place] = rows[first + place] * inverse
-
-        @pl.loop(0, NS_ITERS)
-        def _(turn):
-            @pl.loop(0, D // tile)
-            def _(t):
-                part = pl.ds(pl.multiple_of(t * tile, tile), tile)
+            total = jnp.sum(jnp.where(line == column, value, 0.0), axis=(0, 1), keepdims=True)
+            inverse = 1.0 / (jnp.sqrt(total) + 1e-07)
+            value = value * (inverse * inverse)
+            state[slot] = value
+            state_low[slot] = value.astype(jnp.bfloat16)
+            for place in range(first, first + number):
+                current[place] = rows[place] * inverse
+
+        def turn(last):
+            for slot, _, _ in parts:
                 square = jnp.dot(
-                    state_low[part, :], state_low[...], preferred_element_type=jnp.float32
+                    state_low[slot], state_low[slot], preferred_element_type=jnp.float32
                 )
-                change[part, :] = (COEF_B * state[part, :] + COEF_C * square).astype(jnp.bfloat16)
-
-            @pl.loop(first, first + places_here)
-            def _(place):
-                value = current[place]
-                current[place] = COEF_A * value + jnp.dot(
-                    value.astype(jnp.bfloat16), change[...], preferred_element_type=jnp.float32
-                )
-
-            @pl.when(turn < NS_ITERS - 1)
-            def _():
-                @pl.loop(0, D // tile)
-                def _(t):
-                    part = pl.ds(pl.multiple_of(t * tile, tile), tile)
-                    value = state[part, :]
-                    for _ in range(2):
-                        value = COEF_A * value + jnp.dot(
-                            value.astype(jnp.bfloat16),
-                            change[...],
-                            preferred_element_type=jnp.float32,
-                        )
-                    state[part, :] = value
-                    state_low[part, :] = value.astype(jnp.bfloat16)
-
-        for place in range(places_here):
-            out[first + place] = current[first + place].astype(jnp.bfloat16)
+                change[slot] = (COEF_B * state[slot] + COEF_C * square).astype(jnp.bfloat16)
+            for slot, first, number in parts:
+                for place in range(first, first + number):
+                    value = current[place]
+                    current[place] = COEF_A * value + jnp.dot(
+                        value.astype(jnp.bfloat16),
+                        change[slot],
+                        preferred_element_type=jnp.float32,
+                    )
+            if last:
+                return
+            for half in range(2):
+                for slot, _, _ in parts:
+                    value = COEF_A * state[slot] + jnp.dot(
+                        state_low[slot], change[slot], preferred_element_type=jnp.float32
+                    )
+                    state[slot] = value
+                    state_low[slot] = value.astype(jnp.bfloat16)
+
+        @pl.loop(0, NS_ITERS - 1)
+        def _(_):
+            turn(False)
+
+        turn(True)
+        for slot, first, number in parts:
+            for place in range(first, first + number):
+                out[place] = current[place].astype(jnp.bfloat16)
 
     @pl.when(two[0] == 0)
     def _():
-        chain(0, 0, 4, 0)
+        chains([(0, 0, 4)])
 
     @pl.when(two[0] == 1)
     def _():
-        chain(0, 0, 1, 0)
-        chain(1, 1, 1, 0)
+        chains([(0, 0, 1), (1, 1, 1)])
         for place in (2, 3):
             out[place] = jnp.zeros(out.shape[1:], jnp.bfloat16)
 
 
-def schulz(two, grams, rows):
+def schulz(two, gram, all_rows, rows):
     return pl.pallas_call(
         schulz_kernel,
         out_shape=jax.ShapeDtypeStruct(rows.shape, jnp.bfloat16),
         in_specs=[
             pl.BlockSpec(memory_space=pltpu.SMEM),
-            pl.BlockSpec(memory_space=pltpu.VMEM),
-            pl.BlockSpec(memory_space=pltpu.VMEM),
-        ],
+        ]
+        + whole("vvv"),
         out_specs=pl.BlockSpec(memory_space=pltpu.VMEM),
         scratch_shapes=[
-            pltpu.VMEM((D, D), jnp.float32),
-            pltpu.VMEM((D, D), jnp.bfloat16),
-            pltpu.VMEM((D, D), jnp.bfloat16),
+            pltpu.VMEM((2, D, D), jnp.float32),
+            pltpu.VMEM((2, D, D), jnp.bfloat16),
+            pltpu.VMEM((2, D, D), jnp.bfloat16),
             pltpu.VMEM(rows.shape, jnp.float32),
         ],
         compiler_params=pltpu.CompilerParams(vmem_limit_bytes=VMEM_LIMIT),
         name="schulz",
-    )(two, grams, rows)
+    )(two, gram, all_rows, rows)
 
 
 def spread_kernel(own, out, local_sem, send, recv):
@@ -1086,33 +1127,50 @@
     )(own)
 
 
-def update_kernel(table, scale, clip, momenta, grads, weights, turned, momenta_new, weights_new, weights_low):
-    b = pl.program_id(0)
-    momenta_new[...] = MOMENT * momenta[...] + clip[0] * grads[...].astype(jnp.float32)
-    value = weights[...] * (1.0 - MUON_RATE * MUON_DECAY) - scale[b] * turned[0].astype(jnp.float32)
-    weights_new[...] = value
-    weights_low[...] = value.astype(jnp.bfloat16)
+def update_kernel(
+    table,
+    scale,
+    clip,
+    momenta,
+    grads,
+    weights,
+    turned_first,
+    turned_second,
+    momenta_new,
+    weights_new,
+    weights_low,
+):
+    pair = pl.program_id(0)
+    for i, turned in enumerate((turned_first, turned_second)):
+        momenta_new[i] = MOMENT * momenta[i] + clip[0] * grads[i].astype(jnp.float32)
+        value = weights[i] * (1.0 - MUON_RATE * MUON_DECAY) - scale[2 * pair + i] * turned[
+            0, 0
+        ].astype(jnp.float32)
+        weights_new[i] = value
+        weights_low[i] = value.astype(jnp.bfloat16)
 
 
 def update(home, scale, clip, momenta, grads, weights, turned):
     blocks, rows, width = weights.shape
-    table = np.array([home[block][1] for block in range(blocks)] + [home[block][0] for block in range(blocks)], np.int32)
-    block = pl.BlockSpec((1, rows, width), lambda b, *_: (b, 0, 0))
+    table = np.array(
+        [home[block][1] for block in range(blocks)] + [home[block][0] for block in range(blocks)],
+        np.int32,
+    )
+    pair = pl.BlockSpec((2, rows, width), lambda b, *_: (b, 0, 0))
+
+    def turned_of(i):
+        return pl.BlockSpec(
+            (1, 1, rows, width),
+            lambda b, table, *_: (table[2 * b + i], table[blocks + 2 * b + i], 0, 0),
+        )
+
     return pl.pallas_call(
         update_kernel,
         grid_spec=pltpu.PrefetchScalarGridSpec(
             num_scalar_prefetch=3,
-            grid=(blocks,),
-            in_specs=[
-                block,
-                block,
-                block,
-                pl.BlockSpec(
-                    (1, 1, rows, width),
-                    lambda b, table, *_: (table[b], table[blocks + b], 0, 0),
-                ),
-            ],
-            out_specs=[block, block, block],
+            grid=(blocks // 2,),
+            in_specs=[pair, pair, pair, turned_of(0), turned_of(1)],
+            out_specs=[pair, pair, pair],
         ),
         out_shape=[
             jax.ShapeDtypeStruct(weights.shape, jnp.float32),
@@ -1121,7 +1179,16 @@
         ],
         compiler_params=pltpu.CompilerParams(vmem_limit_bytes=VMEM_LIMIT),
         name="update",
-    )(jnp.asarray(table), jnp.asarray(scale), clip.reshape(1), momenta, grads, weights, turned)
+    )(
+        jnp.asarray(table),
+        jnp.asarray(scale),
+        clip.reshape(1),
+        momenta,
+        grads,
+        weights,
+        turned,
+        turned,
+    )
 
 
 GROUP = 4 * HD
@@ -1153,7 +1220,8 @@
     return exponent * (1.0 / jnp.sum(exponent, 0, keepdims=True))
 
 
-TILE = 256
+TILE = 768
+TOKENS = 256
 SLOPE = math.sqrt(2.0 / math.pi)
 CUBIC = 0.044715
 
@@ -1267,8 +1335,8 @@
                 ).astype(jnp.bfloat16)
 
     loads[1].wait()
-    for t in range(state.shape[0] // TILE):
-        part = slice(t * TILE, (t + 1) * TILE)
+    for t in range(state.shape[0] // TOKENS):
+        part = slice(t * TOKENS, (t + 1) * TOKENS)
         middle[part] = state[part] + contract_first(attended[:, part], out_held[...])
     norm_rows(middle, gains, base + 2, normed_low)
     loads[2].wait()
@@ -1279,8 +1347,8 @@
         hidden[tile_of(t)] = gelu_parts(value)[0].astype(jnp.bfloat16)
 
     loads[3].wait()
-    for t in range(state.shape[0] // TILE):
-        part = slice(t * TILE, (t + 1) * TILE)
+    for t in range(state.shape[0] // TOKENS):
+        part = slice(t * TOKENS, (t + 1) * TOKENS)
         state_out[part] = middle[part] + contract_first(hidden[:, part], down_held[...])
 
 
@@ -1335,7 +1403,6 @@
     down,
     grad_out,
     gain_out,
-    head_gain_out,
     grad_mixing,
     grad_mixing_out,
     grad_up,
@@ -1359,6 +1426,7 @@
     made_out,
     gain_query,
     gain_key,
+    head_gains,
     sem,
     store_sem,
 ):
@@ -1386,6 +1454,7 @@
     ]
     tokens = grad.shape[0]
     gain_out[...] = jnp.zeros_like(gain_out)
+    head_gains[...] = jnp.zeros_like(head_gains)
     gain_query[...] = stand_up(gains[base + 4 : base + 5])
     gain_key[...] = stand_up(gains[base + 5 : base + 6])
 
@@ -1411,8 +1480,8 @@
 
     stores[0].start()
     stores[1].start()
-    for t in range(tokens // TILE):
-        part = slice(t * TILE, (t + 1) * TILE)
+    for t in range(tokens // TOKENS):
+        part = slice(t * TOKENS, (t + 1) * TOKENS)
         inner[part] = contract_first(hidden_grad[:, part], up_held[...])
 
     def norm_back(source, first, previous, target, target_low):
@@ -1484,13 +1553,16 @@
                         (key_grad, key_unit, key_scale, gain_key[part]),
                     )
                 ):
-                    head_gain_out[b, place, part] = jnp.sum(delta * unit, 1, keepdims=True)
+                    head_gains[place, part] += jnp.sum(delta * unit, 1, keepdims=True)
                     delta = delta * gain
                     delta = delta - jnp.mean(delta, 0, keepdims=True) - unit * jnp.mean(
                         delta * unit, 0, keepdims=True
                     )
                     mixed_low[where[place], span] = (delta * scale).astype(jnp.bfloat16)
 
+    for place in range(2):
+        column = jnp.broadcast_to(head_gains[place], (D, 128))
+        gain_out[4 + place : 5 + place] = column.T[:1]
     loads[5].wait()
 
     @pl.loop(0, 3 * D // TILE)
@@ -1502,8 +1574,8 @@
 
     stores[3].start()
     loads[6].wait()
-    for t in range(tokens // TILE):
-        part = slice(t * TILE, (t + 1) * TILE)
+    for t in range(tokens // TOKENS):
+        part = slice(t * TOKENS, (t + 1) * TOKENS)
         inner[part] = contract_first(mixed_low[:, part], mixing_held[...])
     loads[7].wait()
     norm_back(state_held, 0, grad_out, grad_out, None)
@@ -1516,16 +1588,15 @@
     tokens = grad.shape[0]
     weights, spans = layer_weights(blocks)
     low = jnp.bfloat16
-    grad, gain_grads, head_gains, *block_grads = pl.pallas_call(
+    grad, gain_grads, *block_grads = pl.pallas_call(
         functools.partial(backward_kernel, spans, base),
         out_shape=[
             jax.ShapeDtypeStruct((tokens, D), jnp.float32),
             jax.ShapeDtypeStruct((8, D), jnp.float32),
-            jax.ShapeDtypeStruct((segment.shape[0], 2, D, 1), jnp.float32),
         ]
         + [jax.ShapeDtypeStruct((number, D), low) for _, number in spans],
         in_specs=whole("vvvvvaaaaaaaa"),
-        out_specs=whole("vvvaaaa"),
+        out_specs=whole("vvaaaa"),
         scratch_shapes=[
             pltpu.VMEM(state.shape, jnp.float32),
             pltpu.VMEM(mixed.shape, jnp.float32),
@@ -1545,14 +1616,14 @@
             pltpu.VMEM((D, D), low),
             pltpu.VMEM((D, 1), jnp.float32),
             pltpu.VMEM((D, 1), jnp.float32),
+            pltpu.VMEM((2, D, 1), jnp.float32),
             pltpu.SemaphoreType.DMA((8,)),
             pltpu.SemaphoreType.DMA((4,)),
         ],
         compiler_params=pltpu.CompilerParams(vmem_limit_bytes=60 * 1024 * 1024),
         name="layer_backward",
     )(grad, middle, normed_low, gains, segment, state, mixed, heads_low, attended, *weights)
-    gain_grads = jnp.concatenate([gain_grads[:4], jnp.sum(head_gains[..., 0], 0)], 0)
-    return (grad, block_grads, gain_grads)
+    return (grad, block_grads, gain_grads[:6])
 
 
 HEAD_LANES = 128
@@ -1690,14 +1761,14 @@
         loss[...] += jnp.sum(term, 0, keepdims=True) * factor
         text_side[...] = jnp.zeros_like(text_side)
 
-        @pl.loop(0, everyone // TILE)
+        @pl.loop(0, everyone // TOKENS)
         def _(t):
-            part = tile_of(t)
+            part = tile_of(t, TOKENS)
             backward = LOGIT_SCALE * contract_last(texts[b, part], images[b])
             term, backward_low = rows_of(
-                backward, alive_columns[b], alive_rows[b, part], t * TILE
+                backward, alive_columns[b], alive_rows[b, part], t * TOKENS
             )
-            line = lax.broadcasted_iota(jnp.int32, term.shape, 0) + t * TILE
+            line = lax.broadcasted_iota(jnp.int32, term.shape, 0) + t * TOKENS
             here = jnp.logical_and(line >= first, line < first + IMGS)
             loss[...] += jnp.sum(jnp.where(here, term, 0.0), 0, keepdims=True) * factor
             text_side[...] += contract_first(backward_low, texts[b, part])
@@ -2002,17 +2073,9 @@
         own = MOMENT * own_momenta + clip * mine.reshape(own_momenta.shape).astype(jnp.float32)
         two = jnp.asarray(np.array([len(entry) > 1 for entry in plan], np.int32))[lane]
         own_low = rounded(own)
-        first_low = jnp.concatenate(
-            [own_low[:1], jnp.where(two > 0, jnp.bfloat16(0), own_low[1:])], 0
-        )
-        grams = jnp.stack(
-            [
-                product(first_low, first_low, "brd,bre->de"),
-                product(own_low[1], own_low[1], "rd,re->de"),
-            ]
-        )
-        grams, shard_grads = sum_grams(grams, slices, 12)
-        turned = spread(schulz(two.reshape(1), grams, own), 13)
+        gram = product(own_low, own_low, "brd,bre->de")
+        gram, all_rows, shard_grads = sum_grams(gram, own_low[:2], slices, 12)
+        turned = spread(schulz(two.reshape(1), gram, all_rows, own), 13)
         homes = {
             int(block): (lane_of, place)
             for lane_of, entry in enumerate(blocks_here)

time: 818 us -> 768 us (0.939)
  Pallas kernels: 738 us -> 693 us
    pallas_call x1, Pallas kernels: 70.8 us -> 55.4 us  [spread(): pl.pallas_call(spread_kernel, out_shape=jax.ShapeDtypeStruct(own.shape[:1...]
  transfers between devices with their start and end apart: 1 -> 1, of which waited for: 0 -> 0; matrix products, arithmetic and copies ran while one was open for 2% -> 2% of each run, Pallas kernels for 20% -> 21%
where the time goes in v6:
time: 768 us; the launch traced here: 758 us
  Pallas kernels  693 us (90%)
  between operations  20.7 us (3%)
  local copies, waits for them, and re-layouts  18.4 us (2%)
  other arithmetic  13.1 us (2%)
  matrix products  12.4 us (2%)
    pallas_call x2, Pallas kernels, reduce_grads(): pl.pallas_call(functools.partial(reduce_kernel, chunks, count, len(sets),...  185 us
    pallas_call x1, Pallas kernels, fetch(): pl.pallas_call(functools.partial(fetch_kernel, chunks, [n for _, n in pie...  135 us
    pallas_call x2, Pallas kernels, layer_backward(): pl.pallas_call(functools.partial(backward_kernel, spans, base), out_shape...  90.7 us
    pallas_call x1, Pallas kernels, sum_grams(): pl.pallas_call(gram_kernel, out_shape=[jax.ShapeDtypeStruct(gram.shape, j...  61.3 us
    pallas_call x1, Pallas kernels, spread(): pl.pallas_call(spread_kernel, out_shape=jax.ShapeDtypeStruct(own.shape[:1...  55.4 us
    pallas_call x2, Pallas kernels, layer_forward(): pl.pallas_call(functools.partial(forward_kernel, spans, base), out_shape=...  52.7 us
    pallas_call x1, Pallas kernels, update(): pl.pallas_call(update_kernel, grid_spec=pltpu.PrefetchScalarGridSpec(num_...  31 us
    pallas_call x1, Pallas kernels, share(): pl.pallas_call(functools.partial(share_kernel, count), out_shape=[jax.Sha...  27 us
  transfers between devices with their start and end apart: 1, of which 0 were waited for; matrix products, arithmetic and copies ran while one was open for 2% of the time, Pallas kernels for 21%

profile of v6, /device:TPU:0, one launch (start us, length us, event | category | flops | bytes accessed | tf_op | source)
XLA Modules:
  0.0 758.0 jit_solution(4363744526308788007)
XLA Ops:
  7.2 0.0 copy-start
  7.2 0.0 all-gather.3.cloned.1.call-start
  7.3 0.0 copy-start.18
  7.3 2.6 concatenate.11
  10.0 0.7 dynamic-slice_convert_fusion
  10.7 0.0 all-gather.3.cloned.1.call-update
  10.7 0.1 reshape.245
  10.8 0.1 copy.41
  10.9 0.1 tile.10
  11.0 0.1 tile.12
  11.1 0.4 and_reduce_fusion
  11.5 0.1 fusion.18
  11.7 0.1 convert_element_type.66
  11.8 0.7 copy.48.own_live
  13.2 0.6 constant_dynamic-slice_fusion
  16.4 0.7 dynamic_slice.56.two
  17.1 0.6 broadcast_select_fusion.ids
  17.7 135.1 %fetch_1.1 = (bf16[1,4,8,24,768]{4,3,2,1,0:T(8,128)(2,1)}, bf16[3,4,8,24,768]{4,3,2,1,0:T(8,128)(2,1)}, bf16[1,4,8,24,768]{4,3,2,1,0:T(8,128)(2,1)}, bf16[4,4,8,...) custom-call(f32[26,8,24,768]{3,2,1,0:T(8,128)} %bitcast.100, ...), custom_call_target="tpu_custom_call" | custom-call | tf_op jit(solution)/shard_map/fetch_1/pallas_call | solution.py:292
  152.8 0.4 slice_divide_fusion
  153.2 0.8 fusion.9
  154.0 2.1 fusion.24
  156.1 2.0 fusion.3.state
  158.1 26.3 %layer_forward.2 = (f32[512,768]{1,0:T(8,128)}, f32[512,768]{1,0:T(8,128)}, f32[2304,512]{1,0:T(8,128)}, bf16[512,768]{1,0:T(8,128)(2,1)}, bf16[768,512]{1,0:T(8,128)(2,1)}, /*index=5*/bf16[512,768]{1,0:T(8,128)(2,1)}) custom-call(f32[512,768]{1,0:T(8,128)} %fusion.3.state, f32[79,768]{1,0:T(8,128)} %gains.9, s32[2,256]{1,0:T(2,128)} %bitcast.137, ...), custom_call_target="tpu_custom_call" | custom-call | tf_op jit(solution)/shard_map/layer_forward/pallas_call | solution.py:1363
  184.4 0.6 constant_dynamic-slice_fusion.1
  185.0 0.1 multiply_reduce_fusion.1
  185.1 4.4 dynamic-slice_select_fusion.3
  189.5 0.1 fusion.17
  189.6 26.5 %layer_forward.3 = (f32[512,768]{1,0:T(8,128)}, f32[512,768]{1,0:T(8,128)}, f32[2304,512]{1,0:T(8,128)}, bf16[512,768]{1,0:T(8,128)(2,1)}, bf16[768,512]{1,0:T(8,128)(2,1)}, /*index=5*/bf16[512,768]{1,0:T(8,128)(2,1)}) custom-call(f32[512,768]{1,0:T(8,128)} %get-tuple-element.66.state, f32[79,768]{1,0:T(8,128)} %gains.9, s32[2,256]{1,0:T(2,128)} %bitcast.138, ...), custom_call_target="tpu_custom_call" | custom-call | tf_op jit(solution)/shard_map/layer_forward/pallas_call | solution.py:1363
  216.1 10.4 %pool_forward.1 = (bf16[2,8,768]{2,1,0:T(8,128)(2,1)}, f32[2,8,768]{2,1,0:T(8,128)}, bf16[2,8,768]{2,1,0:T(8,128)(2,1)}) custom-call(f32[512,768]{1,0:T(8,128)} %get-tuple-element.69.state, f32[79,768]{1,0:T(8,128)} %gains.9, s32[2,256]{1,0:T(2,128)} %bitcast.139, bf16[768,768]{1,0:T(8,128)(2,1)} %bitcast.119), custom_call_target="tpu_custom_call" | custom-call | tf_op jit(solution)/shard_map/pool_forward/pallas_call | solution.py:1698
  226.5 1.4 pad_maximum_fusion
  227.9 0.7 broadcast_in_dim.34.refs_1_
  228.5 27.0 %share_8.1 = (bf16[8,4,32,768]{3,2,1,0:T(8,128)(2,1)}, bf16[8,4,16,128]{3,2,1,0:T(8,128)(2,1)}) custom-call(bf16[32,768]{1,0:T(8,128)(2,1)} %bitcast.135, bf16[16,128]{1,0:T(8,128)(2,1)} %broadcast_in_dim.34.refs_1_), custom_call_target="tpu_custom_call" | custom-call | tf_op jit(solution)/shard_map/share_8/pallas_call | solution.py:388
  255.5 1.3 copy.54
  256.9 0.9 broadcast_in_dim_reshape.9.alive_rows
  257.7 0.7 broadcast_in_dim_reshape.8.alive_columns
  258.4 1.5 fusion.23
  259.9 1.3 copy_bitcast_fusion
  261.1 20.1 %contrast.1 = (f32[8,128]{1,0:T(8,128)}, f32[512,768]{1,0:T(8,128)}, bf16[768,768]{1,0:T(8,128)(2,1)}, f32[8,768]{1,0:T(8,128)}) custom-call(s32[1]{0:T(128)} %bitcast.me, bf16[2,256,768]{2,1,0:T(8,128)(2,1)} %get-tuple-element.137.images, bf16[2,256,768]{2,1,0:T(8,128)(2,1)} %get-tuple-element.136.texts, ...), custom_call_target="tpu_custom_call" | custom-call | tf_op jit(solution)/shard_map/contrast/pallas_call | solution.py:1817
  281.2 45.3 %layer_backward.2 = (f32[512,768]{1,0:T(8,128)}, f32[8,768]{1,0:T(8,128)}, bf16[2304,768]{1,0:T(8,128)(2,1)}, bf16[768,768]{1,0:T(8,128)(2,1)}, bf16[3072,768]{1,0:T(8,128)(2,1)}, /*index=5*/bf16[3072,768]{1,0:T(8,128)(2,1)}) custom-call(f32[512,768]{1,0:T(8,128)} %get-tuple-element.77.grad, f32[512,768]{1,0:T(8,128)} %get-tuple-element.78.middle, ...), custom_call_target="tpu_custom_call" | custom-call | tf_op jit(solution)/shard_map/layer_backward/pallas_call | solution.py:1591
  326.5 45.5 %layer_backward.3 = (f32[512,768]{1,0:T(8,128)}, f32[8,768]{1,0:T(8,128)}, bf16[2304,768]{1,0:T(8,128)(2,1)}, bf16[768,768]{1,0:T(8,128)(2,1)}, bf16[3072,768]{1,0:T(8,128)(2,1)}, /*index=5*/bf16[3072,768]{1,0:T(8,128)(2,1)}) custom-call(f32[512,768]{1,0:T(8,128)} %get-tuple-element.83.grad, f32[512,768]{1,0:T(8,128)} %get-tuple-element.84.middle, ...), custom_call_target="tpu_custom_call" | custom-call | tf_op jit(solution)/shard_map/layer_backward/pallas_call | solution.py:1591
  372.0 2.3 fusion.7
  374.3 0.8 fusion.8
  375.1 1.8 convolution_convert_fusion
  376.9 0.5 concatenate.12
  377.4 1.2 slice.70
  378.6 0.7 select_maximum_fusion
  379.3 0.8 reshape_reshape.40.refs_5_
  380.1 80.5 %reduce_5.1.refs_6_ = f32[13,24,768]{2,1,0:T(8,128)} custom-call(bf16[3,4,2,2,2,24,768]{6,5,4,3,2,1,0:T(8,128)(2,1)} %bitcast.121, bf16[1,4,2,2,2,24,768]{6,5,4,3,2,1,0:T(8,128)(2,1)} %bitcast.132, bf16[4,4,2,2,2,24,768]{6,5,4,3,2,1,0:T(8,128)(2,1)} %bitcast.115, bf16[4,4,2,2,2,24,768]{6,5,4,3,2,1,0:T(8,128)(2,1)} %bitcast.116, ...), custom_call_target="tpu_custom_call" | custom-call | tf_op jit(solution)/shard_map/reduce_5/pallas_call | solution.py:719
  460.6 104.1 %reduce_4.1 = (f32[13,24,768]{2,1,0:T(8,128)}, f32[1,8,256]{2,1,0:T(8,128)}, f32[4,8,8,256]{3,2,1,0:T(8,128)}, f32[4,8,8,128]{3,2,1,0:T(8,128)}, bf16[4,8,24,768...) custom-call(bf16[3,4,2,2,2,24,768]{6,5,4,3,2,1,0:T(8,128)(2,1)} %bitcast.122, ...), custom_call_target="tpu_custom_call" | custom-call | tf_op jit(solution)/shard_map/reduce_4/pallas_call | solution.py:719
  564.7 1.1 copy.55
  565.7 0.7 multiply_reduce_fusion
  566.4 1.5 slice_reduce_fusion
  569.4 0.6 slice.86
  570.0 0.5 slice.83
  570.5 1.5 convert_multiply_fusion
  572.0 0.3 fusion.2.rows
  572.3 0.9 slice.109.rows
  573.2 0.1 copy-done.6
  573.3 2.7 convolution_bitcast_fusion.gram
  576.0 61.3 %gram_12.1 = (f32[768,768]{1,0:T(8,128)}, bf16[4,2,192,768]{3,2,1,0:T(8,128)(2,1)}, bf16[26,8,24,768]{3,2,1,0:T(8,128)(2,1)}) custom-call(f32[768,768]{1,0:T(8,128)} %convolution_bitcast_fusion.gram, bf16[2,192,768]{2,1,0:T(8,128)(2,1)} %slice.109.rows, bf16[26,24,768]{2,1,0:T(8,128)(2,1)} %get-tuple-element.106.own), custom_call_target="tpu_custom_call" | custom-call | tf_op jit(solution)/shard_map/gram_12/pallas_call | solution.py:993
  637.3 24.9 %schulz.1.own = bf16[4,192,768]{2,1,0:T(8,128)(2,1)} custom-call(s32[1]{0:T(128)} %dynamic_slice.56.two, f32[768,768]{1,0:T(8,128)} %get-tuple-element.108.gram, bf16[4,2,192,768]{3,2,1,0:T(8,128)(2,1)} %get-tuple-element.109.all_rows, f32[4,192,768]{2,1,0:T(8,128)} %copy-done.5), custom_call_target="tpu_custom_call" | custom-call | tf_op jit(solution)/shard_map/schulz/pallas_call | solution.py:1085
  662.2 55.4 %spread_13.1.turned_first.turned_second = bf16[4,8,192,768]{3,2,1,0:T(8,128)(2,1)} custom-call(bf16[4,192,768]{2,1,0:T(8,128)(2,1)} %schulz.1.own), custom_call_target="tpu_custom_call" | custom-call | tf_op jit(solution)/shard_map/spread_13/pallas_call | solution.py:1113
  717.6 1.0 multiply_subtract_fusion
  718.6 31.0 %update.1 = (f32[26,192,768]{2,1,0:T(8,128)}, f32[26,192,768]{2,1,0:T(8,128)}, bf16[26,192,768]{2,1,0:T(8,128)(2,1)}) custom-call(s32[52]{0:T(128)} %constant.128.clone.table, f32[26]{0:T(128)} %constant.129.clone.scale, f32[1]{0:T(128)} %bitcast.44.clip, f32[26,192,768]{2,1,0:T(8,128)} %momenta.1, bf16[26,192,768]{2,1,0:T(8,128)(2,1)} %bitcast.109, ...), custom_call_target="tpu_custom_call" | custom-call | tf_op jit(solution)/shard_map/update/pallas_call | solution.py:1167
  (52 shorter events, 0.3 us)
Async XLA Ops:
  7.2 146.9 %copy-start = (bf16[2,1,256,768]{3,2,1,0:T(8,128)(2,1)S(1)}, bf16[2,1,256,768]{3,2,1,0:T(8,128)(2,1)}, u32[]{:S(2)}) copy-start(bf16[2,1,256,768]{3,2,1,0:T(8,128)(2,1)} %param.19) | copy-start | bytes 2359300
  7.2 182.4 %all-gather.3.cloned.1.call-start = ((), (), s32[]{:S(2)}) async-start(), calls=%async_computation | async-start | bytes 9732096 | tf_op jit(solution)/shard_map/all_gather | solution.py:330
  7.2 3.5 copy-start.14
  7.3 3.8 copy-start.11
  7.3 4.2 copy-start.17
  7.3 5.9 copy-start.18
  7.3 9.1 %copy-start.19 = (s32[8]{0:T(128)S(1)}, s32[8]{0:T(128)}, u32[]{:S(2)}) copy-start(s32[8]{0:T(128)} %constant.127.clone) | copy-start | bytes 100
  11.5 141.3 %copy-start.10 = (s32[2,1,256]{2,0,1:T(2,128)}, s32[2,1,256]{2,0,1:T(2,128)S(1)}, u32[]{:S(2)}) copy-start(s32[2,1,256]{2,0,1:T(2,128)S(1)} %copy.59) | copy-start | bytes 6148
  17.7 135.5 %copy-start.2 = (f32[79,768]{1,0:T(8,128)S(1)}, f32[79,768]{1,0:T(8,128)}, u32[]{:S(2)}) copy-start(f32[79,768]{1,0:T(8,128)} %gains.9) | copy-start | bytes 728068
  158.1 26.3 %copy-start.16 = (pred[8,4]{1,0:T(8,128)(4,1)S(1)}, pred[8,4]{1,0:T(8,128)(4,1)}, u32[]{:S(2)}) copy-start(pred[8,4]{1,0:T(8,128)(4,1)} %constant.125.clone) | copy-start | bytes 100
  158.1 26.9 %copy-start.9 = (f32[16,768]{1,0:T(8,128)S(1)}, f32[16,768]{1,0:T(8,128)}, u32[]{:S(2)}) copy-start(f32[16,768]{1,0:T(8,128)} %get-tuple-element.72) | copy-start | bytes 147460
  372.0 2.3 copy-start.4
  374.3 2.6 copy-start.15
  374.3 2.6 copy-start.12
  374.3 2.6 copy-start.13
  572.0 1.3 copy-start.6
  572.3 3.6 copy-start.5
  662.1 55.4 %copy-start.3 = (f32[79,768]{1,0:T(8,128)S(1)}, f32[79,768]{1,0:T(8,128)}, u32[]{:S(2)}) copy-start(f32[79,768]{1,0:T(8,128)} %gains.9) | copy-start | bytes 728068
  662.1 55.4 %copy-start.7 = (f32[79,768]{1,0:T(8,128)S(1)}, f32[79,768]{1,0:T(8,128)}, u32[]{:S(2)}) copy-start(f32[79,768]{1,0:T(8,128)} %param.28) | copy-start | bytes 728068
  662.1 55.5 %copy-start.8 = (f32[79,768]{1,0:T(8,128)S(1)}, f32[79,768]{1,0:T(8,128)}, u32[]{:S(2)}) copy-start(f32[79,768]{1,0:T(8,128)} %param.27) | copy-start | bytes 728068
  718.6 31.1 %copy-start.1 = (bf16[2,1,256,768]{3,2,1,0:T(8,128)(2,1)S(1)}, bf16[2,1,256,768]{3,2,1,0:T(8,128)(2,1)}, u32[]{:S(2)}) copy-start(bf16[2,1,256,768]{3,2,1,0:T(8,128)(2,1)} %param.19) | copy-start | bytes 2359300
Sparse Core Ops, SparseCore 0:
  11.5 130.0 all-gather.2

commit v7 on v6

--- a/solution.py
+++ b/solution.py
@@ -1191,7 +1191,7 @@
     )
 
 
-GROUP = 4 * HD
+GROUP = 6 * HD
 
 
 def normed_head(value, gain):
@@ -1213,9 +1213,8 @@
     )
 
 
-def head_shares(query_low, key_low, same):
-    scores = contract_first(key_low, query_low) * (1.0 / math.sqrt(HD))
-    scores = jnp.where(same, scores, -1e30)
+def shares_of(scores, same):
+    scores = jnp.where(same, scores * (1.0 / math.sqrt(HD)), -1e30)
     exponent = jnp.exp(scores - jnp.max(scores, 0, keepdims=True))
     return exponent * (1.0 / jnp.sum(exponent, 0, keepdims=True))
 
@@ -1320,6 +1319,7 @@
 
         @pl.loop(0, D // GROUP)
         def _(group):
+            held = []
             for head in range(GROUP // HD):
                 first = group * GROUP + head * HD
                 part = pl.ds(pl.multiple_of(first, HD), HD)
@@ -1329,9 +1329,12 @@
                 ]
                 query_low = normed_head(query, gain_query[part])[0].astype(jnp.bfloat16)
                 key_low = normed_head(key, gain_key[part])[0].astype(jnp.bfloat16)
-                share = head_shares(query_low, key_low, same).astype(jnp.bfloat16)
+                held.append((part, query_low, key_low, value.astype(jnp.bfloat16)))
+            scores = [contract_first(key_low, query_low) for _, query_low, key_low, _ in held]
+            shares = [shares_of(score, same).astype(jnp.bfloat16) for score in scores]
+            for (part, _, _, value_low), share in zip(held, shares):
                 attended[part, tokens] = jnp.dot(
-                    value.astype(jnp.bfloat16), share, preferred_element_type=jnp.float32
+                    value_low, share, preferred_element_type=jnp.float32
                 ).astype(jnp.bfloat16)
 
     loads[1].wait()
@@ -1525,36 +1528,41 @@
 
         @pl.loop(0, D // GROUP)
         def _(group):
+            held = []
             for head in range(GROUP // HD):
                 first = group * GROUP + head * HD
                 part = pl.ds(pl.multiple_of(first, HD), HD)
                 where = [pl.ds(pl.multiple_of(place * D + first, HD), HD) for place in range(3)]
                 query, key, value = [mixed_held[at, span] for at in where]
-                query_value, query_unit, query_scale = normed_head(query, gain_query[part])
-                key_value, key_unit, key_scale = normed_head(key, gain_key[part])
-                query_low = query_value.astype(jnp.bfloat16)
-                key_low = key_value.astype(jnp.bfloat16)
-                value_low = value.astype(jnp.bfloat16)
-                out_low = attended_grad[part, span]
-                share = head_shares(query_low, key_low, same)
+                query_low = normed_head(query, gain_query[part])[0].astype(jnp.bfloat16)
+                key_low = normed_head(key, gain_key[part])[0].astype(jnp.bfloat16)
+                held.append((part, where, query_low, key_low, value.astype(jnp.bfloat16)))
+            scores = [contract_first(key_low, query_low) for _, _, query_low, key_low, _ in held]
+            share_grads = [
+                contract_first(value_low, attended_grad[part, span])
+                for part, _, _, _, value_low in held
+            ]
+            shares = [shares_of(score, same) for score in scores]
+            score_lows = []
+            for share, share_grad in zip(shares, share_grads):
+                total = jnp.sum(share * share_grad, 0, keepdims=True)
+                score_lows.append(
+                    (share * (share_grad - total) * (1.0 / math.sqrt(HD))).astype(jnp.bfloat16)
+                )
+            for (part, where, query_low, key_low, _), share, score_low in zip(
+                held, shares, score_lows
+            ):
                 mixed_low[where[2], span] = contract_last(
-                    out_low, share.astype(jnp.bfloat16)
+                    attended_grad[part, span], share.astype(jnp.bfloat16)
                 ).astype(jnp.bfloat16)
-                share_grad = contract_first(value_low, out_low)
-                total = jnp.sum(share * share_grad, 0, keepdims=True)
-                score_low = (share * (share_grad - total) * (1.0 / math.sqrt(HD))).astype(
-                    jnp.bfloat16
+                deltas = (
+                    jnp.dot(key_low, score_low, preferred_element_type=jnp.float32),
+                    contract_last(query_low, score_low),
                 )
-                query_grad = jnp.dot(key_low, score_low, preferred_element_type=jnp.float32)
-                key_grad = contract_last(query_low, score_low)
-                for place, (delta, unit, scale, gain) in enumerate(
-                    (
-                        (query_grad, query_unit, query_scale, gain_query[part]),
-                        (key_grad, key_unit, key_scale, gain_key[part]),
-                    )
-                ):
+                for place, (delta, gains_here) in enumerate(zip(deltas, (gain_query, gain_key))):
+                    _, unit, scale = normed_head(mixed_held[where[place], span], gains_here[part])
                     head_gains[place, part] += jnp.sum(delta * unit, 1, keepdims=True)
-                    delta = delta * gain
+                    delta = delta * gains_here[part]
                     delta = delta - jnp.mean(delta, 0, keepdims=True) - unit * jnp.mean(
                         delta * unit, 0, keepdims=True
                     )

time: 768 us -> 751 us (0.978)
  Pallas kernels: 693 us -> 676 us
    pallas_call x2, Pallas kernels: 52.7 us -> 43.3 us  [layer_forward(): pl.pallas_call(functools.partial(forward_kernel, spans, base), out_shape=...]
    pallas_call x2, Pallas kernels: 90.7 us -> 82.8 us  [layer_backward(): pl.pallas_call(functools.partial(backward_kernel, spans, base), out_shape...]
where the time goes in v7:
time: 751 us; the launch traced here: 741 us
  Pallas kernels  676 us (90%)
  between operations  20.7 us (3%)
  local copies, waits for them, and re-layouts  18.4 us (2%)
  other arithmetic  13.1 us (2%)
  matrix products  12.4 us (2%)
    pallas_call x2, Pallas kernels, reduce_grads(): pl.pallas_call(functools.partial(reduce_kernel, chunks, count, len(sets),...  185 us
    pallas_call x1, Pallas kernels, fetch(): pl.pallas_call(functools.partial(fetch_kernel, chunks, [n for _, n in pie...  135 us
    pallas_call x2, Pallas kernels, layer_backward(): pl.pallas_call(functools.partial(backward_kernel, spans, base), out_shape...  82.8 us
    pallas_call x1, Pallas kernels, sum_grams(): pl.pallas_call(gram_kernel, out_shape=[jax.ShapeDtypeStruct(gram.shape, j...  61.3 us
    pallas_call x1, Pallas kernels, spread(): pl.pallas_call(spread_kernel, out_shape=jax.ShapeDtypeStruct(own.shape[:1...  55.4 us
    pallas_call x2, Pallas kernels, layer_forward(): pl.pallas_call(functools.partial(forward_kernel, spans, base), out_shape=...  43.3 us
    pallas_call x1, Pallas kernels, update(): pl.pallas_call(update_kernel, grid_spec=pltpu.PrefetchScalarGridSpec(num_...  31 us
    pallas_call x1, Pallas kernels, share(): pl.pallas_call(functools.partial(share_kernel, count), out_shape=[jax.Sha...  27 us
  transfers between devices with their start and end apart: 1, of which 0 were waited for; matrix products, arithmetic and copies ran while one was open for 2% of the time, Pallas kernels for 21%

profile of v7, /device:TPU:0, one launch (start us, length us, event | category | flops | bytes accessed | tf_op | source)
XLA Modules:
  0.0 740.6 jit_solution(10253356328210170611)
XLA Ops:
  7.2 0.0 copy-start
  7.2 0.0 all-gather.3.cloned.1.call-start
  7.3 0.0 copy-start.19
  7.3 2.6 concatenate.11
  10.0 0.7 dynamic-slice_convert_fusion
  10.7 0.0 all-gather.3.cloned.1.call-update
  10.7 0.1 reshape.245
  10.8 0.1 copy.41
  10.9 0.1 tile.10
  11.0 0.1 tile.12
  11.1 0.4 and_reduce_fusion
  11.5 0.1 fusion.18
  11.7 0.1 convert_element_type.66
  11.8 0.7 copy.48.own_live
  13.2 0.6 constant_dynamic-slice_fusion
  16.4 0.7 dynamic_slice.56.two
  17.1 0.6 broadcast_select_fusion.ids
  17.7 135.1 %fetch_1.1 = (bf16[1,4,8,24,768]{4,3,2,1,0:T(8,128)(2,1)}, bf16[3,4,8,24,768]{4,3,2,1,0:T(8,128)(2,1)}, bf16[1,4,8,24,768]{4,3,2,1,0:T(8,128)(2,1)}, bf16[4,4,8,...) custom-call(f32[26,8,24,768]{3,2,1,0:T(8,128)} %bitcast.100, ...), custom_call_target="tpu_custom_call" | custom-call | tf_op jit(solution)/shard_map/fetch_1/pallas_call | solution.py:292
  152.8 0.4 slice_divide_fusion
  153.2 0.8 fusion.9
  154.0 2.1 fusion.24
  156.1 2.0 fusion.3.state
  158.1 21.6 %layer_forward.2 = (f32[512,768]{1,0:T(8,128)}, f32[512,768]{1,0:T(8,128)}, f32[2304,512]{1,0:T(8,128)}, bf16[512,768]{1,0:T(8,128)(2,1)}, bf16[768,512]{1,0:T(8,128)(2,1)}, /*index=5*/bf16[512,768]{1,0:T(8,128)(2,1)}) custom-call(f32[512,768]{1,0:T(8,128)} %fusion.3.state, f32[79,768]{1,0:T(8,128)} %gains.9, s32[2,256]{1,0:T(2,128)} %bitcast.137, ...), custom_call_target="tpu_custom_call" | custom-call | tf_op jit(solution)/shard_map/layer_forward/pallas_call | solution.py:1366
  179.7 0.6 constant_dynamic-slice_fusion.1
  180.3 0.1 multiply_reduce_fusion.1
  180.4 4.4 dynamic-slice_select_fusion.3
  184.8 0.1 fusion.17
  184.9 21.8 %layer_forward.3 = (f32[512,768]{1,0:T(8,128)}, f32[512,768]{1,0:T(8,128)}, f32[2304,512]{1,0:T(8,128)}, bf16[512,768]{1,0:T(8,128)(2,1)}, bf16[768,512]{1,0:T(8,128)(2,1)}, /*index=5*/bf16[512,768]{1,0:T(8,128)(2,1)}) custom-call(f32[512,768]{1,0:T(8,128)} %get-tuple-element.66.state, f32[79,768]{1,0:T(8,128)} %gains.9, s32[2,256]{1,0:T(2,128)} %bitcast.138, ...), custom_call_target="tpu_custom_call" | custom-call | tf_op jit(solution)/shard_map/layer_forward/pallas_call | solution.py:1366
  206.7 10.4 %pool_forward.1 = (bf16[2,8,768]{2,1,0:T(8,128)(2,1)}, f32[2,8,768]{2,1,0:T(8,128)}, bf16[2,8,768]{2,1,0:T(8,128)(2,1)}) custom-call(f32[512,768]{1,0:T(8,128)} %get-tuple-element.69.state, f32[79,768]{1,0:T(8,128)} %gains.9, s32[2,256]{1,0:T(2,128)} %bitcast.139, bf16[768,768]{1,0:T(8,128)(2,1)} %bitcast.119), custom_call_target="tpu_custom_call" | custom-call | tf_op jit(solution)/shard_map/pool_forward/pallas_call | solution.py:1706
  217.1 1.4 pad_maximum_fusion
  218.5 0.7 broadcast_in_dim.34.refs_1_
  219.1 27.0 %share_8.1 = (bf16[8,4,32,768]{3,2,1,0:T(8,128)(2,1)}, bf16[8,4,16,128]{3,2,1,0:T(8,128)(2,1)}) custom-call(bf16[32,768]{1,0:T(8,128)(2,1)} %bitcast.135, bf16[16,128]{1,0:T(8,128)(2,1)} %broadcast_in_dim.34.refs_1_), custom_call_target="tpu_custom_call" | custom-call | tf_op jit(solution)/shard_map/share_8/pallas_call | solution.py:388
  246.1 1.3 copy.54
  247.5 0.9 broadcast_in_dim_reshape.9.alive_rows
  248.4 0.7 broadcast_in_dim_reshape.8.alive_columns
  249.0 1.5 fusion.23
  250.5 1.3 copy_bitcast_fusion
  251.8 20.1 %contrast.1 = (f32[8,128]{1,0:T(8,128)}, f32[512,768]{1,0:T(8,128)}, bf16[768,768]{1,0:T(8,128)(2,1)}, f32[8,768]{1,0:T(8,128)}) custom-call(s32[1]{0:T(128)} %bitcast.me, bf16[2,256,768]{2,1,0:T(8,128)(2,1)} %get-tuple-element.137.images, bf16[2,256,768]{2,1,0:T(8,128)(2,1)} %get-tuple-element.136.texts, ...), custom_call_target="tpu_custom_call" | custom-call | tf_op jit(solution)/shard_map/contrast/pallas_call | solution.py:1825
  271.8 41.2 %layer_backward.2 = (f32[512,768]{1,0:T(8,128)}, f32[8,768]{1,0:T(8,128)}, bf16[2304,768]{1,0:T(8,128)(2,1)}, bf16[768,768]{1,0:T(8,128)(2,1)}, bf16[3072,768]{1,0:T(8,128)(2,1)}, /*index=5*/bf16[3072,768]{1,0:T(8,128)(2,1)}) custom-call(f32[512,768]{1,0:T(8,128)} %get-tuple-element.77.grad, f32[512,768]{1,0:T(8,128)} %get-tuple-element.78.middle, ...), custom_call_target="tpu_custom_call" | custom-call | tf_op jit(solution)/shard_map/layer_backward/pallas_call | solution.py:1599
  313.1 41.6 %layer_backward.3 = (f32[512,768]{1,0:T(8,128)}, f32[8,768]{1,0:T(8,128)}, bf16[2304,768]{1,0:T(8,128)(2,1)}, bf16[768,768]{1,0:T(8,128)(2,1)}, bf16[3072,768]{1,0:T(8,128)(2,1)}, /*index=5*/bf16[3072,768]{1,0:T(8,128)(2,1)}) custom-call(f32[512,768]{1,0:T(8,128)} %get-tuple-element.83.grad, f32[512,768]{1,0:T(8,128)} %get-tuple-element.84.middle, ...), custom_call_target="tpu_custom_call" | custom-call | tf_op jit(solution)/shard_map/layer_backward/pallas_call | solution.py:1599
  354.6 2.3 fusion.7
  356.9 0.8 fusion.8
  357.7 1.8 convolution_convert_fusion
  359.6 0.5 concatenate.12
  360.1 1.2 slice.70
  361.3 0.7 select_maximum_fusion
  361.9 0.8 reshape_reshape.40.refs_5_
  362.7 80.5 %reduce_5.1.refs_6_ = f32[13,24,768]{2,1,0:T(8,128)} custom-call(bf16[3,4,2,2,2,24,768]{6,5,4,3,2,1,0:T(8,128)(2,1)} %bitcast.121, bf16[1,4,2,2,2,24,768]{6,5,4,3,2,1,0:T(8,128)(2,1)} %bitcast.132, bf16[4,4,2,2,2,24,768]{6,5,4,3,2,1,0:T(8,128)(2,1)} %bitcast.115, bf16[4,4,2,2,2,24,768]{6,5,4,3,2,1,0:T(8,128)(2,1)} %bitcast.116, ...), custom_call_target="tpu_custom_call" | custom-call | tf_op jit(solution)/shard_map/reduce_5/pallas_call | solution.py:719
  443.2 104.1 %reduce_4.1 = (f32[13,24,768]{2,1,0:T(8,128)}, f32[1,8,256]{2,1,0:T(8,128)}, f32[4,8,8,256]{3,2,1,0:T(8,128)}, f32[4,8,8,128]{3,2,1,0:T(8,128)}, bf16[4,8,24,768...) custom-call(bf16[3,4,2,2,2,24,768]{6,5,4,3,2,1,0:T(8,128)(2,1)} %bitcast.122, ...), custom_call_target="tpu_custom_call" | custom-call | tf_op jit(solution)/shard_map/reduce_4/pallas_call | solution.py:719
  547.3 1.1 copy.55
  548.4 0.7 multiply_reduce_fusion
  549.0 1.5 slice_reduce_fusion
  552.0 0.6 slice.86
  552.6 0.5 slice.83
  553.2 1.5 convert_multiply_fusion
  554.6 0.3 fusion.2.rows
  555.0 0.9 slice.109.rows
  555.8 0.1 copy-done.6
  555.9 2.7 convolution_bitcast_fusion.gram
  558.6 61.3 %gram_12.1 = (f32[768,768]{1,0:T(8,128)}, bf16[4,2,192,768]{3,2,1,0:T(8,128)(2,1)}, bf16[26,8,24,768]{3,2,1,0:T(8,128)(2,1)}) custom-call(f32[768,768]{1,0:T(8,128)} %convolution_bitcast_fusion.gram, bf16[2,192,768]{2,1,0:T(8,128)(2,1)} %slice.109.rows, bf16[26,24,768]{2,1,0:T(8,128)(2,1)} %get-tuple-element.106.own), custom_call_target="tpu_custom_call" | custom-call | tf_op jit(solution)/shard_map/gram_12/pallas_call | solution.py:993
  619.9 24.9 %schulz.1.own = bf16[4,192,768]{2,1,0:T(8,128)(2,1)} custom-call(s32[1]{0:T(128)} %dynamic_slice.56.two, f32[768,768]{1,0:T(8,128)} %get-tuple-element.108.gram, bf16[4,2,192,768]{3,2,1,0:T(8,128)(2,1)} %get-tuple-element.109.all_rows, f32[4,192,768]{2,1,0:T(8,128)} %copy-done.5), custom_call_target="tpu_custom_call" | custom-call | tf_op jit(solution)/shard_map/schulz/pallas_call | solution.py:1085
  644.8 55.4 %spread_13.1.turned_first.turned_second = bf16[4,8,192,768]{3,2,1,0:T(8,128)(2,1)} custom-call(bf16[4,192,768]{2,1,0:T(8,128)(2,1)} %schulz.1.own), custom_call_target="tpu_custom_call" | custom-call | tf_op jit(solution)/shard_map/spread_13/pallas_call | solution.py:1113
  700.2 1.0 multiply_subtract_fusion
  701.2 31.0 %update.1 = (f32[26,192,768]{2,1,0:T(8,128)}, f32[26,192,768]{2,1,0:T(8,128)}, bf16[26,192,768]{2,1,0:T(8,128)(2,1)}) custom-call(s32[52]{0:T(128)} %constant.128.clone.table, f32[26]{0:T(128)} %constant.129.clone.scale, f32[1]{0:T(128)} %bitcast.44.clip, f32[26,192,768]{2,1,0:T(8,128)} %momenta.1, bf16[26,192,768]{2,1,0:T(8,128)(2,1)} %bitcast.109, ...), custom_call_target="tpu_custom_call" | custom-call | tf_op jit(solution)/shard_map/update/pallas_call | solution.py:1167
  (52 shorter events, 0.3 us)
Async XLA Ops:
  7.2 146.9 %copy-start = (bf16[2,1,256,768]{3,2,1,0:T(8,128)(2,1)S(1)}, bf16[2,1,256,768]{3,2,1,0:T(8,128)(2,1)}, u32[]{:S(2)}) copy-start(bf16[2,1,256,768]{3,2,1,0:T(8,128)(2,1)} %param.19) | copy-start | bytes 2359300
  7.2 177.7 %all-gather.3.cloned.1.call-start = ((), (), s32[]{:S(2)}) async-start(), calls=%async_computation | async-start | bytes 9732096 | tf_op jit(solution)/shard_map/all_gather | solution.py:330
  7.2 3.5 copy-start.14
  7.3 3.8 copy-start.11
  7.3 4.2 copy-start.17
  7.3 5.9 copy-start.18
  7.3 9.1 %copy-start.19 = (s32[8]{0:T(128)S(1)}, s32[8]{0:T(128)}, u32[]{:S(2)}) copy-start(s32[8]{0:T(128)} %constant.127.clone) | copy-start | bytes 100
  11.5 141.3 %copy-start.10 = (s32[2,1,256]{2,0,1:T(2,128)}, s32[2,1,256]{2,0,1:T(2,128)S(1)}, u32[]{:S(2)}) copy-start(s32[2,1,256]{2,0,1:T(2,128)S(1)} %copy.59) | copy-start | bytes 6148
  17.7 135.5 %copy-start.2 = (f32[79,768]{1,0:T(8,128)S(1)}, f32[79,768]{1,0:T(8,128)}, u32[]{:S(2)}) copy-start(f32[79,768]{1,0:T(8,128)} %gains.9) | copy-start | bytes 728068
  158.1 21.6 %copy-start.16 = (pred[8,4]{1,0:T(8,128)(4,1)S(1)}, pred[8,4]{1,0:T(8,128)(4,1)}, u32[]{:S(2)}) copy-start(pred[8,4]{1,0:T(8,128)(4,1)} %constant.125.clone) | copy-start | bytes 100
  158.1 22.2 %copy-start.9 = (f32[16,768]{1,0:T(8,128)S(1)}, f32[16,768]{1,0:T(8,128)}, u32[]{:S(2)}) copy-start(f32[16,768]{1,0:T(8,128)} %get-tuple-element.72) | copy-start | bytes 147460
  354.6 2.3 copy-start.4
  356.9 2.6 copy-start.15
  356.9 2.6 copy-start.12
  356.9 2.6 copy-start.13
  554.6 1.3 copy-start.6
  555.0 3.6 copy-start.5
  644.8 55.4 %copy-start.3 = (f32[79,768]{1,0:T(8,128)S(1)}, f32[79,768]{1,0:T(8,128)}, u32[]{:S(2)}) copy-start(f32[79,768]{1,0:T(8,128)} %gains.9) | copy-start | bytes 728068
  644.8 55.4 %copy-start.7 = (f32[79,768]{1,0:T(8,128)S(1)}, f32[79,768]{1,0:T(8,128)}, u32[]{:S(2)}) copy-start(f32[79,768]{1,0:T(8,128)} %param.28) | copy-start | bytes 728068
  644.8 55.5 %copy-start.8 = (f32[79,768]{1,0:T(8,128)S(1)}, f32[79,768]{1,0:T(8,128)}, u32[]{:S(2)}) copy-start(f32[79,768]{1,0:T(8,128)} %param.27) | copy-start | bytes 728068
  701.2 31.1 %copy-start.1 = (bf16[2,1,256,768]{3,2,1,0:T(8,128)(2,1)S(1)}, bf16[2,1,256,768]{3,2,1,0:T(8,128)(2,1)}, u32[]{:S(2)}) copy-start(bf16[2,1,256,768]{3,2,1,0:T(8,128)(2,1)} %param.19) | copy-start | bytes 2359300
Sparse Core Ops, SparseCore 0:
  11.5 130.0 all-gather.2

commit v8 on v7

--- a/solution.py
+++ b/solution.py
@@ -89,9 +89,9 @@
 CAPTION_TILE = 400
 
 
-def fetch_kernel(chunks, sizes, weights, ids, table, *refs):
+def fetch_kernel(chunks, sizes, tokens, weights, ids, table, *refs):
     outs = refs[: len(sizes)]
-    text_sum = refs[len(sizes)]
+    texts = refs[len(sizes)]
     (
         full,
         low,
@@ -109,6 +109,9 @@
         id_recv,
         part_send,
         part_recv,
+        own_text,
+        text_send,
+        text_recv,
     ) = refs[len(sizes) + 1 :]
     d, z, zs = places()
     sib, near_x, near_y = flip(d, 1), flip(d, 2), flip(d, 4)
@@ -130,7 +133,9 @@
         )
 
     page(0).start()
-    greet([(d, zs[1]), (d, zs[2]), (d, zs[3]), (sib, z), (near_x, z), (near_y, z)])
+    greet(
+        [(d, zs[1]), (d, zs[2]), (d, zs[3]), (sib, z), (near_x, z), (near_y, z), (diagonal, z)]
+    )
     pending = []
     all_ids[z] = ids[...]
     id_copies = []
@@ -208,8 +213,43 @@
         def _(t):
             look_up(t)
 
-    share_of = -(-page_count // (len(chunks) - 1))
+    share_of = -(-page_count // (len(chunks) - 4))
     part_copies = []
+    text_copies = []
+
+    def push_text(slot, source, target, to):
+        text_copies.append(
+            pltpu.make_async_remote_copy(
+                src_ref=source,
+                dst_ref=target,
+                send_sem=text_send.at[slot],
+                recv_sem=text_recv.at[slot],
+                device_id=to,
+                device_id_type=MESH,
+            )
+        )
+        text_copies[-1].start()
+
+    def text_along_z():
+        for copy in part_copies:
+            copy.wait_recv()
+        value = (found_parts[z] + from_z[0] + from_z[1] + from_z[2]) * (1.0 / tokens)
+        value = unit_rows(value).astype(own_text.dtype)
+        own_text[...] = value
+        texts[d, z] = value
+        for o in (1, 2, 3):
+            push_text(o - 1, own_text, texts.at[d, z], (d, zs[o]))
+
+    def text_across_plane():
+        for copy in text_copies[:3]:
+            copy.wait_recv()
+        for i, to in enumerate((near_x, near_y, diagonal, sib)):
+            push_text(3 + i, texts.at[d], texts.at[d], (to, z))
+
+    def text_to_core():
+        for i, origin in enumerate((near_x, near_y, diagonal)):
+            text_copies[3 + i].wait_recv()
+            push_text(7 + i, texts.at[origin], texts.at[origin], (sib, z))
 
     def send_parts():
         captions = found_parts.shape[1]
@@ -258,8 +298,14 @@
                 last.append(push(k, 20 + o, 0, n, zz, near_y, (sib, z)))
         if step * share_of < page_count:
             look_up_span(step * share_of, min((step + 1) * share_of, page_count))
-        if step == count - 1:
-            send_parts()
+        for at, action in (
+            (count - 4, send_parts),
+            (count - 2, text_along_z),
+            (count - 1, text_across_plane),
+            (count + 1, text_to_core),
+        ):
+            if step == at:
+                action()
         if step >= 2:
             k, n = step - 2, chunks[step - 2][3]
             for o in (1, 2, 3):
@@ -276,11 +322,14 @@
     for copy in id_copies:
         copy.wait_send()
     for copy in part_copies:
-        copy.wait()
-    text_sum[...] = found_parts[z] + from_z[0] + from_z[1] + from_z[2]
-
-
-def fetch(weights, pieces, ids, table, captions, collective):
+        copy.wait_send()
+    for copy in text_copies[6:]:
+        copy.wait_recv()
+    for copy in text_copies:
+        copy.wait_send()
+
+
+def fetch(weights, pieces, ids, table, captions, tokens, collective):
     depth, eighths = lax.axis_size("fsdp"), lax.axis_size("dp")
     blocks, rows, width = weights.shape
     part = (eighths, rows // eighths, width)
@@ -290,11 +339,11 @@
             chunks.append((a + first, out, first, min(2, n - first)))
     total = sum(n for _, n in pieces)
     outs = pl.pallas_call(
-        functools.partial(fetch_kernel, chunks, [n for _, n in pieces]),
+        functools.partial(fetch_kernel, chunks, [n for _, n in pieces], tokens),
         out_shape=[
             jax.ShapeDtypeStruct((n, depth) + part, jnp.bfloat16) for _, n in pieces
         ]
-        + [jax.ShapeDtypeStruct((captions, width), jnp.float32)],
+        + [jax.ShapeDtypeStruct((eighths, depth, captions, width), jnp.bfloat16)],
         in_specs=whole("ava"),
         out_specs=whole("a" * len(pieces) + "v"),
         scratch_shapes=[
@@ -314,6 +363,9 @@
             pltpu.SemaphoreType.DMA((3,)),
             pltpu.SemaphoreType.DMA((3,)),
             pltpu.SemaphoreType.DMA((3,)),
+            pltpu.VMEM((captions, width), jnp.bfloat16),
+            pltpu.SemaphoreType.DMA((10,)),
+            pltpu.SemaphoreType.DMA((10,)),
         ],
         compiler_params=pltpu.CompilerParams(
             collective_id=collective, has_side_effects=True, vmem_limit_bytes=VMEM_LIMIT
@@ -1953,7 +2005,9 @@
         own_ids = jnp.where(
             place[None] == lax.axis_index("fsdp"), jnp.tile(own_ids, (1, depth)), 0
         )
-        (stem, *first_blocks), text_sum = fetch(weights, early, own_ids, table, captions, 1)
+        (stem, *first_blocks), texts = fetch(
+            weights, early, own_ids, table, captions, tokens, 1
+        )
     else:
         stem, *first_blocks = [
             lax.all_gather(rounded(weights[a : a + n]), "fsdp", axis=1, tiled=True)
@@ -1970,10 +2024,10 @@
             "fsdp",
             scatter_dimension=0,
         )
+        (texts,) = share([rounded(unit_rows(text_sum / tokens))], 7)
     early_blocks = first_blocks[5:]
     pooling_matrix = first_blocks[4][0]
     first_blocks = first_blocks[:4]
-    text_low = rounded(unit_rows(text_sum / text_ids.shape[-1]))
     me = lax.axis_index(("dp", "fsdp"))
     segment = segments[:, 0]
     rows_hot, cols_hot = jax.vmap(positions)(grid[:, 0])
@@ -1996,12 +2050,11 @@
         saved.append((kept, blocks))
     pooled_low, embedded, image_low = pool_forward(state, gains, fin, segment, pooling_matrix)
     own_flags = jnp.broadcast_to(live.reshape(captions, 1), (captions, 128)).astype(jnp.bfloat16)
-    both = jnp.stack([image_low.reshape(captions, D), text_low]).reshape(2 * captions, D)
-    gathered, flags = share([both, own_flags], 8)
-    gathered = gathered.reshape(-1, 2, MB, IMGS, D)
+    images, flags = share([image_low.reshape(captions, D), own_flags], 8)
     flags = flags.reshape(-1, MB, IMGS, 128)[..., 0].astype(jnp.float32)
     images, texts = [
-        jnp.moveaxis(gathered[:, i], 0, 1).reshape(MB, -1, D) for i in range(2)
+        jnp.moveaxis(value.reshape(-1, MB, IMGS, D), 0, 1).reshape(MB, -1, D)
+        for value in (images, texts)
     ]
     loss_part, grad, grad_pool, pool_gain_grads = contrast(
         me,

time: 751 us -> 746 us (level)
  transfers between devices with their start and end apart: 1 -> 1, of which waited for: 0 -> 0; matrix products, arithmetic and copies ran while one was open for 2% -> 2% of each run, Pallas kernels for 21% -> 22%
where the time goes in v8:
time: 746 us; the launch traced here: 736 us
  Pallas kernels  673 us (90%)
  between operations  20.7 us (3%)
  local copies, waits for them, and re-layouts  18.2 us (2%)
  matrix products  12.4 us (2%)
  other arithmetic  11.5 us (2%)
    pallas_call x2, Pallas kernels, reduce_grads(): pl.pallas_call(functools.partial(reduce_kernel, chunks, count, len(sets),...  185 us
    pallas_call x1, Pallas kernels, fetch(): pl.pallas_call(functools.partial(fetch_kernel, chunks, [n for _, n in pie...  139 us
    pallas_call x2, Pallas kernels, layer_backward(): pl.pallas_call(functools.partial(backward_kernel, spans, base), out_shape...  82.8 us
    pallas_call x1, Pallas kernels, sum_grams(): pl.pallas_call(gram_kernel, out_shape=[jax.ShapeDtypeStruct(gram.shape, j...  61.9 us
    pallas_call x1, Pallas kernels, spread(): pl.pallas_call(spread_kernel, out_shape=jax.ShapeDtypeStruct(own.shape[:1...  55.2 us
    pallas_call x2, Pallas kernels, layer_forward(): pl.pallas_call(functools.partial(forward_kernel, spans, base), out_shape=...  43.3 us
    pallas_call x1, Pallas kernels, update(): pl.pallas_call(update_kernel, grid_spec=pltpu.PrefetchScalarGridSpec(num_...  31 us
    pallas_call x1, Pallas kernels, schulz(): pl.pallas_call(schulz_kernel, out_shape=jax.ShapeDtypeStruct(rows.shape,...  24.8 us
  transfers between devices with their start and end apart: 1, of which 0 were waited for; matrix products, arithmetic and copies ran while one was open for 2% of the time, Pallas kernels for 22%

profile of v8, /device:TPU:0, one launch (start us, length us, event | category | flops | bytes accessed | tf_op | source)
XLA Modules:
  0.0 736.2 jit_solution(15304455724326226102)
XLA Ops:
  7.2 0.0 copy-start
  7.2 0.0 all-gather.3.cloned.1.call-start
  7.3 0.0 copy-start.17
  7.3 0.0 copy-start.18
  7.3 2.6 concatenate.11
  10.0 0.7 dynamic-slice_convert_fusion
  10.7 0.0 all-gather.3.cloned.1.call-update
  10.7 0.1 reshape.240
  10.8 0.1 copy.41
  10.9 0.1 tile.10
  11.0 0.1 tile.12
  11.1 0.4 and_reduce_fusion
  11.5 0.1 fusion.17
  11.7 0.1 convert_element_type.62
  11.8 0.7 copy.48.own_live
  13.2 0.6 constant_dynamic-slice_fusion
  16.4 0.6 dynamic_slice.56.two
  17.0 0.6 broadcast_select_fusion.ids
  17.6 138.7 %fetch_1.1 = (bf16[1,4,8,24,768]{4,3,2,1,0:T(8,128)(2,1)}, bf16[3,4,8,24,768]{4,3,2,1,0:T(8,128)(2,1)}, bf16[1,4,8,24,768]{4,3,2,1,0:T(8,128)(2,1)}, bf16[4,4,8,...) custom-call(f32[26,8,24,768]{3,2,1,0:T(8,128)} %bitcast.94, ...), custom_call_target="tpu_custom_call" | custom-call | tf_op jit(solution)/shard_map/fetch_1/pallas_call | solution.py:341
  156.3 0.4 slice_divide_fusion
  156.7 0.8 fusion.9
  157.6 2.1 fusion.22
  159.7 2.0 fusion.3.state
  161.6 21.6 %layer_forward.2 = (f32[512,768]{1,0:T(8,128)}, f32[512,768]{1,0:T(8,128)}, f32[2304,512]{1,0:T(8,128)}, bf16[512,768]{1,0:T(8,128)(2,1)}, bf16[768,512]{1,0:T(8,128)(2,1)}, /*index=5*/bf16[512,768]{1,0:T(8,128)(2,1)}) custom-call(f32[512,768]{1,0:T(8,128)} %fusion.3.state, f32[79,768]{1,0:T(8,128)} %gains.9, s32[2,256]{1,0:T(2,128)} %bitcast.131, ...), custom_call_target="tpu_custom_call" | custom-call | tf_op jit(solution)/shard_map/layer_forward/pallas_call | solution.py:1418
  183.2 0.6 constant_dynamic-slice_fusion.1
  183.8 4.4 dynamic-slice_select_fusion.3
  188.2 0.0 all-gather.3.cloned.1.call-done
  188.2 21.8 %layer_forward.3 = (f32[512,768]{1,0:T(8,128)}, f32[512,768]{1,0:T(8,128)}, f32[2304,512]{1,0:T(8,128)}, bf16[512,768]{1,0:T(8,128)(2,1)}, bf16[768,512]{1,0:T(8,128)(2,1)}, /*index=5*/bf16[512,768]{1,0:T(8,128)(2,1)}) custom-call(f32[512,768]{1,0:T(8,128)} %get-tuple-element.66.state, f32[79,768]{1,0:T(8,128)} %gains.9, s32[2,256]{1,0:T(2,128)} %bitcast.132, ...), custom_call_target="tpu_custom_call" | custom-call | tf_op jit(solution)/shard_map/layer_forward/pallas_call | solution.py:1418
  210.0 10.4 %pool_forward.1 = (bf16[2,8,768]{2,1,0:T(8,128)(2,1)}, f32[2,8,768]{2,1,0:T(8,128)}, bf16[2,8,768]{2,1,0:T(8,128)(2,1)}) custom-call(f32[512,768]{1,0:T(8,128)} %get-tuple-element.69.state, f32[79,768]{1,0:T(8,128)} %gains.9, s32[2,256]{1,0:T(2,128)} %bitcast.133, bf16[768,768]{1,0:T(8,128)(2,1)} %bitcast.113), custom_call_target="tpu_custom_call" | custom-call | tf_op jit(solution)/shard_map/pool_forward/pallas_call | solution.py:1758
  220.4 0.7 broadcast_in_dim.33.refs_1_
  221.1 20.5 %share_8.1 = (bf16[8,4,16,768]{3,2,1,0:T(8,128)(2,1)}, bf16[8,4,16,128]{3,2,1,0:T(8,128)(2,1)}) custom-call(bf16[16,768]{1,0:T(8,128)(2,1)} %bitcast.138, bf16[16,128]{1,0:T(8,128)(2,1)} %broadcast_in_dim.33.refs_1_), custom_call_target="tpu_custom_call" | custom-call | tf_op jit(solution)/shard_map/share_8/pallas_call | solution.py:440
  241.6 1.3 copy.52
  242.9 0.9 broadcast_in_dim_reshape.9.alive_rows
  243.8 0.7 broadcast_in_dim_reshape.8.alive_columns
  244.5 2.6 copy_bitcast_fusion
  247.1 20.1 %contrast.1 = (f32[8,128]{1,0:T(8,128)}, f32[512,768]{1,0:T(8,128)}, bf16[768,768]{1,0:T(8,128)(2,1)}, f32[8,768]{1,0:T(8,128)}) custom-call(s32[1]{0:T(128)} %bitcast.me, bf16[2,256,768]{2,1,0:T(8,128)(2,1)} %get-tuple-element.135.images, bf16[2,256,768]{2,1,0:T(8,128)(2,1)} %get-tuple-element.134.texts, ...), custom_call_target="tpu_custom_call" | custom-call | tf_op jit(solution)/shard_map/contrast/pallas_call | solution.py:1877
  267.2 41.2 %layer_backward.2 = (f32[512,768]{1,0:T(8,128)}, f32[8,768]{1,0:T(8,128)}, bf16[2304,768]{1,0:T(8,128)(2,1)}, bf16[768,768]{1,0:T(8,128)(2,1)}, bf16[3072,768]{1,0:T(8,128)(2,1)}, /*index=5*/bf16[3072,768]{1,0:T(8,128)(2,1)}) custom-call(f32[512,768]{1,0:T(8,128)} %get-tuple-element.77.grad, f32[512,768]{1,0:T(8,128)} %get-tuple-element.78.middle, ...), custom_call_target="tpu_custom_call" | custom-call | tf_op jit(solution)/shard_map/layer_backward/pallas_call | solution.py:1651
  308.4 41.6 %layer_backward.3 = (f32[512,768]{1,0:T(8,128)}, f32[8,768]{1,0:T(8,128)}, bf16[2304,768]{1,0:T(8,128)(2,1)}, bf16[768,768]{1,0:T(8,128)(2,1)}, bf16[3072,768]{1,0:T(8,128)(2,1)}, /*index=5*/bf16[3072,768]{1,0:T(8,128)(2,1)}) custom-call(f32[512,768]{1,0:T(8,128)} %get-tuple-element.83.grad, f32[512,768]{1,0:T(8,128)} %get-tuple-element.84.middle, ...), custom_call_target="tpu_custom_call" | custom-call | tf_op jit(solution)/shard_map/layer_backward/pallas_call | solution.py:1651
  350.0 2.3 fusion.7
  352.2 0.0 copy-start.11
  352.3 0.8 fusion.8
  353.0 1.8 convolution_convert_fusion
  354.9 0.5 concatenate.12
  355.4 1.2 slice.62
  356.6 0.7 select_maximum_fusion
  357.3 0.8 reshape_reshape.40.refs_5_
  358.0 81.0 %reduce_5.1.refs_6_ = f32[13,24,768]{2,1,0:T(8,128)} custom-call(bf16[3,4,2,2,2,24,768]{6,5,4,3,2,1,0:T(8,128)(2,1)} %bitcast.115, bf16[1,4,2,2,2,24,768]{6,5,4,3,2,1,0:T(8,128)(2,1)} %bitcast.125, bf16[4,4,2,2,2,24,768]{6,5,4,3,2,1,0:T(8,128)(2,1)} %bitcast.109, bf16[4,4,2,2,2,24,768]{6,5,4,3,2,1,0:T(8,128)(2,1)} %bitcast.110, ...), custom_call_target="tpu_custom_call" | custom-call | tf_op jit(solution)/shard_map/reduce_5/pallas_call | solution.py:771
  439.0 103.6 %reduce_4.1 = (f32[13,24,768]{2,1,0:T(8,128)}, f32[1,8,256]{2,1,0:T(8,128)}, f32[4,8,8,256]{3,2,1,0:T(8,128)}, f32[4,8,8,128]{3,2,1,0:T(8,128)}, bf16[4,8,24,768...) custom-call(bf16[3,4,2,2,2,24,768]{6,5,4,3,2,1,0:T(8,128)(2,1)} %bitcast.116, ...), custom_call_target="tpu_custom_call" | custom-call | tf_op jit(solution)/shard_map/reduce_4/pallas_call | solution.py:771
  542.6 1.1 copy.53
  543.7 0.7 multiply_reduce_fusion
  544.3 1.5 slice_reduce_fusion
  547.3 0.6 slice.76
  547.9 0.5 slice.73
  548.4 1.5 convert_multiply_fusion
  549.9 0.3 fusion.2.rows
  550.2 0.0 copy-start.5
  550.3 0.9 slice.99.rows
  551.1 0.1 copy-done.6
  551.2 2.7 convolution_bitcast_fusion.gram
  553.9 61.9 %gram_12.1 = (f32[768,768]{1,0:T(8,128)}, bf16[4,2,192,768]{3,2,1,0:T(8,128)(2,1)}, bf16[26,8,24,768]{3,2,1,0:T(8,128)(2,1)}) custom-call(f32[768,768]{1,0:T(8,128)} %convolution_bitcast_fusion.gram, bf16[2,192,768]{2,1,0:T(8,128)(2,1)} %slice.99.rows, bf16[26,24,768]{2,1,0:T(8,128)(2,1)} %get-tuple-element.106.own), custom_call_target="tpu_custom_call" | custom-call | tf_op jit(solution)/shard_map/gram_12/pallas_call | solution.py:1045
  615.8 24.8 %schulz.1.own = bf16[4,192,768]{2,1,0:T(8,128)(2,1)} custom-call(s32[1]{0:T(128)} %dynamic_slice.56.two, f32[768,768]{1,0:T(8,128)} %get-tuple-element.108.gram, bf16[4,2,192,768]{3,2,1,0:T(8,128)(2,1)} %get-tuple-element.109.all_rows, f32[4,192,768]{2,1,0:T(8,128)} %copy-done.5), custom_call_target="tpu_custom_call" | custom-call | tf_op jit(solution)/shard_map/schulz/pallas_call | solution.py:1137
  640.6 55.2 %spread_13.1.turned_first.turned_second = bf16[4,8,192,768]{3,2,1,0:T(8,128)(2,1)} custom-call(bf16[4,192,768]{2,1,0:T(8,128)(2,1)} %schulz.1.own), custom_call_target="tpu_custom_call" | custom-call | tf_op jit(solution)/shard_map/spread_13/pallas_call | solution.py:1165
  695.8 1.0 multiply_subtract_fusion
  696.8 31.0 %update.1 = (f32[26,192,768]{2,1,0:T(8,128)}, f32[26,192,768]{2,1,0:T(8,128)}, bf16[26,192,768]{2,1,0:T(8,128)(2,1)}) custom-call(s32[52]{0:T(128)} %constant.119.clone.table, f32[26]{0:T(128)} %constant.120.clone.scale, f32[1]{0:T(128)} %bitcast.41.clip, f32[26,192,768]{2,1,0:T(8,128)} %momenta.1, bf16[26,192,768]{2,1,0:T(8,128)(2,1)} %bitcast.103, ...), custom_call_target="tpu_custom_call" | custom-call | tf_op jit(solution)/shard_map/update/pallas_call | solution.py:1219
  (45 shorter events, 0.2 us)
Async XLA Ops:
  7.2 150.4 %copy-start = (bf16[2,1,256,768]{3,2,1,0:T(8,128)(2,1)S(1)}, bf16[2,1,256,768]{3,2,1,0:T(8,128)(2,1)}, u32[]{:S(2)}) copy-start(bf16[2,1,256,768]{3,2,1,0:T(8,128)(2,1)} %param.19) | copy-start | bytes 2359300
  7.2 181.0 %all-gather.3.cloned.1.call-start = ((), (), s32[]{:S(2)}) async-start(), calls=%async_computation | async-start | bytes 9732096 | tf_op jit(solution)/shard_map/all_gather | solution.py:382
  7.2 3.5 copy-start.13
  7.3 3.8 copy-start.10
  7.3 4.2 copy-start.16
  7.3 5.9 copy-start.17
  7.3 9.1 %copy-start.18 = (s32[8]{0:T(128)S(1)}, s32[8]{0:T(128)}, u32[]{:S(2)}) copy-start(s32[8]{0:T(128)} %constant.118.clone) | copy-start | bytes 100
  11.5 144.8 %copy-start.9 = (s32[2,1,256]{2,0,1:T(2,128)}, s32[2,1,256]{2,0,1:T(2,128)S(1)}, u32[]{:S(2)}) copy-start(s32[2,1,256]{2,0,1:T(2,128)S(1)} %copy.57) | copy-start | bytes 6148
  17.6 139.2 %copy-start.2 = (f32[79,768]{1,0:T(8,128)S(1)}, f32[79,768]{1,0:T(8,128)}, u32[]{:S(2)}) copy-start(f32[79,768]{1,0:T(8,128)} %gains.9) | copy-start | bytes 728068
  161.6 21.6 %copy-start.15 = (pred[8,4]{1,0:T(8,128)(4,1)S(1)}, pred[8,4]{1,0:T(8,128)(4,1)}, u32[]{:S(2)}) copy-start(pred[8,4]{1,0:T(8,128)(4,1)} %constant.116.clone) | copy-start | bytes 100
  350.0 2.3 copy-start.4
  352.2 2.6 copy-start.14
  352.2 2.6 copy-start.11
  352.3 2.6 copy-start.12
  549.9 1.3 copy-start.6
  550.2 3.6 copy-start.5
  640.6 55.2 %copy-start.3 = (f32[79,768]{1,0:T(8,128)S(1)}, f32[79,768]{1,0:T(8,128)}, u32[]{:S(2)}) copy-start(f32[79,768]{1,0:T(8,128)} %gains.9) | copy-start | bytes 728068
  640.6 55.2 %copy-start.7 = (f32[79,768]{1,0:T(8,128)S(1)}, f32[79,768]{1,0:T(8,128)}, u32[]{:S(2)}) copy-start(f32[79,768]{1,0:T(8,128)} %param.28) | copy-start | bytes 728068
  640.6 55.2 %copy-start.8 = (f32[79,768]{1,0:T(8,128)S(1)}, f32[79,768]{1,0:T(8,128)}, u32[]{:S(2)}) copy-start(f32[79,768]{1,0:T(8,128)} %param.27) | copy-start | bytes 728068
  696.8 31.1 %copy-start.1 = (bf16[2,1,256,768]{3,2,1,0:T(8,128)(2,1)S(1)}, bf16[2,1,256,768]{3,2,1,0:T(8,128)(2,1)}, u32[]{:S(2)}) copy-start(bf16[2,1,256,768]{3,2,1,0:T(8,128)(2,1)} %param.19) | copy-start | bytes 2359300
Sparse Core Ops, SparseCore 0:
  11.5 129.5 all-gather.2

commit v9 on v8

--- a/solution.py
+++ b/solution.py
@@ -723,10 +723,9 @@
     chunks = []
     first = 0
     for i, source in enumerate(sources):
-        for start in range(0, source.shape[0], 2):
-            n = min(2, source.shape[0] - start)
-            chunks.append((i, start, first, n, 0))
-            first += n
+        for start in range(source.shape[0]):
+            chunks.append((i, start, first, 1, 0))
+            first += 1
     sets = [(first, (rows, D), jnp.bfloat16)]
     if small is not None:
         sources.append(small.reshape((1,) + tail + small.shape[1:]))

time: 746 us -> 739 us (level)
  no operation moved by 1% of the time
where the time goes in v9:
time: 739 us; the launch traced here: 729 us
  Pallas kernels  666 us (90%)
  between operations  20.7 us (3%)
  local copies, waits for them, and re-layouts  18.2 us (2%)
  matrix products  12.4 us (2%)
  other arithmetic  11.5 us (2%)
    pallas_call x2, Pallas kernels, reduce_grads(): pl.pallas_call(functools.partial(reduce_kernel, chunks, count, len(sets),...  179 us
    pallas_call x1, Pallas kernels, fetch(): pl.pallas_call(functools.partial(fetch_kernel, chunks, [n for _, n in pie...  139 us
    pallas_call x2, Pallas kernels, layer_backward(): pl.pallas_call(functools.partial(backward_kernel, spans, base), out_shape...  82.7 us
    pallas_call x1, Pallas kernels, sum_grams(): pl.pallas_call(gram_kernel, out_shape=[jax.ShapeDtypeStruct(gram.shape, j...  60.4 us
    pallas_call x1, Pallas kernels, spread(): pl.pallas_call(spread_kernel, out_shape=jax.ShapeDtypeStruct(own.shape[:1...  55.5 us
    pallas_call x2, Pallas kernels, layer_forward(): pl.pallas_call(functools.partial(forward_kernel, spans, base), out_shape=...  43.3 us
    pallas_call x1, Pallas kernels, update(): pl.pallas_call(update_kernel, grid_spec=pltpu.PrefetchScalarGridSpec(num_...  31 us
    pallas_call x1, Pallas kernels, schulz(): pl.pallas_call(schulz_kernel, out_shape=jax.ShapeDtypeStruct(rows.shape,...  24.6 us
  transfers between devices with their start and end apart: 1, of which 0 were waited for; matrix products, arithmetic and copies ran while one was open for 2% of the time, Pallas kernels for 22%

profile of v9, /device:TPU:0, one launch (start us, length us, event | category | flops | bytes accessed | tf_op | source)
XLA Modules:
  0.0 729.0 jit_solution(13912738622935729355)
XLA Ops:
  7.2 0.0 copy-start
  7.2 0.0 all-gather.3.cloned.1.call-start
  7.3 0.0 copy-start.17
  7.3 0.0 copy-start.18
  7.3 2.6 concatenate.11
  10.0 0.7 dynamic-slice_convert_fusion
  10.7 0.0 all-gather.3.cloned.1.call-update
  10.7 0.1 reshape.240
  10.8 0.1 copy.41
  10.9 0.1 tile.10
  11.0 0.1 tile.12
  11.1 0.4 and_reduce_fusion
  11.5 0.1 fusion.17
  11.7 0.1 convert_element_type.62
  11.8 0.7 copy.48.own_live
  13.2 0.6 constant_dynamic-slice_fusion
  16.4 0.6 dynamic_slice.56.two
  17.0 0.6 broadcast_select_fusion.ids
  17.6 138.7 %fetch_1.1 = (bf16[1,4,8,24,768]{4,3,2,1,0:T(8,128)(2,1)}, bf16[3,4,8,24,768]{4,3,2,1,0:T(8,128)(2,1)}, bf16[1,4,8,24,768]{4,3,2,1,0:T(8,128)(2,1)}, bf16[4,4,8,...) custom-call(f32[26,8,24,768]{3,2,1,0:T(8,128)} %bitcast.94, ...), custom_call_target="tpu_custom_call" | custom-call | tf_op jit(solution)/shard_map/fetch_1/pallas_call | solution.py:341
  156.3 0.4 slice_divide_fusion
  156.7 0.8 fusion.9
  157.6 2.1 fusion.22
  159.7 2.0 fusion.3.state
  161.6 21.6 %layer_forward.2 = (f32[512,768]{1,0:T(8,128)}, f32[512,768]{1,0:T(8,128)}, f32[2304,512]{1,0:T(8,128)}, bf16[512,768]{1,0:T(8,128)(2,1)}, bf16[768,512]{1,0:T(8,128)(2,1)}, /*index=5*/bf16[512,768]{1,0:T(8,128)(2,1)}) custom-call(f32[512,768]{1,0:T(8,128)} %fusion.3.state, f32[79,768]{1,0:T(8,128)} %gains.9, s32[2,256]{1,0:T(2,128)} %bitcast.131, ...), custom_call_target="tpu_custom_call" | custom-call | tf_op jit(solution)/shard_map/layer_forward/pallas_call | solution.py:1417
  183.2 0.6 constant_dynamic-slice_fusion.1
  183.8 4.4 dynamic-slice_select_fusion.3
  188.2 0.0 all-gather.3.cloned.1.call-done
  188.2 21.8 %layer_forward.3 = (f32[512,768]{1,0:T(8,128)}, f32[512,768]{1,0:T(8,128)}, f32[2304,512]{1,0:T(8,128)}, bf16[512,768]{1,0:T(8,128)(2,1)}, bf16[768,512]{1,0:T(8,128)(2,1)}, /*index=5*/bf16[512,768]{1,0:T(8,128)(2,1)}) custom-call(f32[512,768]{1,0:T(8,128)} %get-tuple-element.66.state, f32[79,768]{1,0:T(8,128)} %gains.9, s32[2,256]{1,0:T(2,128)} %bitcast.132, ...), custom_call_target="tpu_custom_call" | custom-call | tf_op jit(solution)/shard_map/layer_forward/pallas_call | solution.py:1417
  210.0 10.4 %pool_forward.1 = (bf16[2,8,768]{2,1,0:T(8,128)(2,1)}, f32[2,8,768]{2,1,0:T(8,128)}, bf16[2,8,768]{2,1,0:T(8,128)(2,1)}) custom-call(f32[512,768]{1,0:T(8,128)} %get-tuple-element.69.state, f32[79,768]{1,0:T(8,128)} %gains.9, s32[2,256]{1,0:T(2,128)} %bitcast.133, bf16[768,768]{1,0:T(8,128)(2,1)} %bitcast.113), custom_call_target="tpu_custom_call" | custom-call | tf_op jit(solution)/shard_map/pool_forward/pallas_call | solution.py:1757
  220.4 0.7 broadcast_in_dim.33.refs_1_
  221.1 20.5 %share_8.1 = (bf16[8,4,16,768]{3,2,1,0:T(8,128)(2,1)}, bf16[8,4,16,128]{3,2,1,0:T(8,128)(2,1)}) custom-call(bf16[16,768]{1,0:T(8,128)(2,1)} %bitcast.138, bf16[16,128]{1,0:T(8,128)(2,1)} %broadcast_in_dim.33.refs_1_), custom_call_target="tpu_custom_call" | custom-call | tf_op jit(solution)/shard_map/share_8/pallas_call | solution.py:440
  241.6 1.3 copy.52
  242.9 0.9 broadcast_in_dim_reshape.9.alive_rows
  243.8 0.7 broadcast_in_dim_reshape.8.alive_columns
  244.5 2.6 copy_bitcast_fusion
  247.1 20.1 %contrast.1 = (f32[8,128]{1,0:T(8,128)}, f32[512,768]{1,0:T(8,128)}, bf16[768,768]{1,0:T(8,128)(2,1)}, f32[8,768]{1,0:T(8,128)}) custom-call(s32[1]{0:T(128)} %bitcast.me, bf16[2,256,768]{2,1,0:T(8,128)(2,1)} %get-tuple-element.135.images, bf16[2,256,768]{2,1,0:T(8,128)(2,1)} %get-tuple-element.134.texts, ...), custom_call_target="tpu_custom_call" | custom-call | tf_op jit(solution)/shard_map/contrast/pallas_call | solution.py:1876
  267.2 41.2 %layer_backward.2 = (f32[512,768]{1,0:T(8,128)}, f32[8,768]{1,0:T(8,128)}, bf16[2304,768]{1,0:T(8,128)(2,1)}, bf16[768,768]{1,0:T(8,128)(2,1)}, bf16[3072,768]{1,0:T(8,128)(2,1)}, /*index=5*/bf16[3072,768]{1,0:T(8,128)(2,1)}) custom-call(f32[512,768]{1,0:T(8,128)} %get-tuple-element.77.grad, f32[512,768]{1,0:T(8,128)} %get-tuple-element.78.middle, ...), custom_call_target="tpu_custom_call" | custom-call | tf_op jit(solution)/shard_map/layer_backward/pallas_call | solution.py:1650
  308.4 41.5 %layer_backward.3 = (f32[512,768]{1,0:T(8,128)}, f32[8,768]{1,0:T(8,128)}, bf16[2304,768]{1,0:T(8,128)(2,1)}, bf16[768,768]{1,0:T(8,128)(2,1)}, bf16[3072,768]{1,0:T(8,128)(2,1)}, /*index=5*/bf16[3072,768]{1,0:T(8,128)(2,1)}) custom-call(f32[512,768]{1,0:T(8,128)} %get-tuple-element.83.grad, f32[512,768]{1,0:T(8,128)} %get-tuple-element.84.middle, ...), custom_call_target="tpu_custom_call" | custom-call | tf_op jit(solution)/shard_map/layer_backward/pallas_call | solution.py:1650
  349.9 2.3 fusion.7
  352.2 0.0 copy-start.11
  352.2 0.8 fusion.8
  353.0 1.8 convolution_convert_fusion
  354.8 0.5 concatenate.12
  355.3 1.2 slice.62
  356.5 0.7 select_maximum_fusion
  357.2 0.8 reshape_reshape.40.refs_5_
  358.0 78.1 %reduce_5.1.refs_6_ = f32[13,24,768]{2,1,0:T(8,128)} custom-call(bf16[3,4,2,2,2,24,768]{6,5,4,3,2,1,0:T(8,128)(2,1)} %bitcast.115, bf16[1,4,2,2,2,24,768]{6,5,4,3,2,1,0:T(8,128)(2,1)} %bitcast.125, bf16[4,4,2,2,2,24,768]{6,5,4,3,2,1,0:T(8,128)(2,1)} %bitcast.109, bf16[4,4,2,2,2,24,768]{6,5,4,3,2,1,0:T(8,128)(2,1)} %bitcast.110, ...), custom_call_target="tpu_custom_call" | custom-call | tf_op jit(solution)/shard_map/reduce_5/pallas_call | solution.py:770
  436.1 100.7 %reduce_4.1 = (f32[13,24,768]{2,1,0:T(8,128)}, f32[1,8,256]{2,1,0:T(8,128)}, f32[4,8,8,256]{3,2,1,0:T(8,128)}, f32[4,8,8,128]{3,2,1,0:T(8,128)}, bf16[4,8,24,768...) custom-call(bf16[3,4,2,2,2,24,768]{6,5,4,3,2,1,0:T(8,128)(2,1)} %bitcast.116, ...), custom_call_target="tpu_custom_call" | custom-call | tf_op jit(solution)/shard_map/reduce_4/pallas_call | solution.py:770
  536.7 1.1 copy.53
  537.8 0.7 multiply_reduce_fusion
  538.5 1.5 slice_reduce_fusion
  541.5 0.6 slice.76
  542.1 0.5 slice.73
  542.6 1.5 convert_multiply_fusion
  544.1 0.3 fusion.2.rows
  544.4 0.0 copy-start.5
  544.4 0.9 slice.99.rows
  545.3 0.1 copy-done.6
  545.4 2.7 convolution_bitcast_fusion.gram
  548.1 60.4 %gram_12.1 = (f32[768,768]{1,0:T(8,128)}, bf16[4,2,192,768]{3,2,1,0:T(8,128)(2,1)}, bf16[26,8,24,768]{3,2,1,0:T(8,128)(2,1)}) custom-call(f32[768,768]{1,0:T(8,128)} %convolution_bitcast_fusion.gram, bf16[2,192,768]{2,1,0:T(8,128)(2,1)} %slice.99.rows, bf16[26,24,768]{2,1,0:T(8,128)(2,1)} %get-tuple-element.106.own), custom_call_target="tpu_custom_call" | custom-call | tf_op jit(solution)/shard_map/gram_12/pallas_call | solution.py:1044
  608.4 24.6 %schulz.1.own = bf16[4,192,768]{2,1,0:T(8,128)(2,1)} custom-call(s32[1]{0:T(128)} %dynamic_slice.56.two, f32[768,768]{1,0:T(8,128)} %get-tuple-element.108.gram, bf16[4,2,192,768]{3,2,1,0:T(8,128)(2,1)} %get-tuple-element.109.all_rows, f32[4,192,768]{2,1,0:T(8,128)} %copy-done.5), custom_call_target="tpu_custom_call" | custom-call | tf_op jit(solution)/shard_map/schulz/pallas_call | solution.py:1136
  633.0 55.5 %spread_13.1.turned_first.turned_second = bf16[4,8,192,768]{3,2,1,0:T(8,128)(2,1)} custom-call(bf16[4,192,768]{2,1,0:T(8,128)(2,1)} %schulz.1.own), custom_call_target="tpu_custom_call" | custom-call | tf_op jit(solution)/shard_map/spread_13/pallas_call | solution.py:1164
  688.6 1.0 multiply_subtract_fusion
  689.6 31.0 %update.1 = (f32[26,192,768]{2,1,0:T(8,128)}, f32[26,192,768]{2,1,0:T(8,128)}, bf16[26,192,768]{2,1,0:T(8,128)(2,1)}) custom-call(s32[52]{0:T(128)} %constant.119.clone.table, f32[26]{0:T(128)} %constant.120.clone.scale, f32[1]{0:T(128)} %bitcast.41.clip, f32[26,192,768]{2,1,0:T(8,128)} %momenta.1, bf16[26,192,768]{2,1,0:T(8,128)(2,1)} %bitcast.103, ...), custom_call_target="tpu_custom_call" | custom-call | tf_op jit(solution)/shard_map/update/pallas_call | solution.py:1218
  (45 shorter events, 0.2 us)
Async XLA Ops:
  7.2 150.4 %copy-start = (bf16[2,1,256,768]{3,2,1,0:T(8,128)(2,1)S(1)}, bf16[2,1,256,768]{3,2,1,0:T(8,128)(2,1)}, u32[]{:S(2)}) copy-start(bf16[2,1,256,768]{3,2,1,0:T(8,128)(2,1)} %param.19) | copy-start | bytes 2359300
  7.2 181.0 %all-gather.3.cloned.1.call-start = ((), (), s32[]{:S(2)}) async-start(), calls=%async_computation | async-start | bytes 9732096 | tf_op jit(solution)/shard_map/all_gather | solution.py:382
  7.2 3.5 copy-start.13
  7.3 3.8 copy-start.10
  7.3 4.2 copy-start.16
  7.3 5.9 copy-start.17
  7.3 9.1 %copy-start.18 = (s32[8]{0:T(128)S(1)}, s32[8]{0:T(128)}, u32[]{:S(2)}) copy-start(s32[8]{0:T(128)} %constant.118.clone) | copy-start | bytes 100
  11.5 144.8 %copy-start.9 = (s32[2,1,256]{2,0,1:T(2,128)}, s32[2,1,256]{2,0,1:T(2,128)S(1)}, u32[]{:S(2)}) copy-start(s32[2,1,256]{2,0,1:T(2,128)S(1)} %copy.57) | copy-start | bytes 6148
  17.6 139.2 %copy-start.2 = (f32[79,768]{1,0:T(8,128)S(1)}, f32[79,768]{1,0:T(8,128)}, u32[]{:S(2)}) copy-start(f32[79,768]{1,0:T(8,128)} %gains.9) | copy-start | bytes 728068
  161.6 21.6 %copy-start.15 = (pred[8,4]{1,0:T(8,128)(4,1)S(1)}, pred[8,4]{1,0:T(8,128)(4,1)}, u32[]{:S(2)}) copy-start(pred[8,4]{1,0:T(8,128)(4,1)} %constant.116.clone) | copy-start | bytes 100
  349.9 2.3 copy-start.4
  352.2 2.6 copy-start.14
  352.2 2.6 copy-start.11
  352.2 2.6 copy-start.12
  544.1 1.3 copy-start.6
  544.4 3.6 copy-start.5
  633.0 55.6 %copy-start.3 = (f32[79,768]{1,0:T(8,128)S(1)}, f32[79,768]{1,0:T(8,128)}, u32[]{:S(2)}) copy-start(f32[79,768]{1,0:T(8,128)} %gains.9) | copy-start | bytes 728068
  633.0 55.6 %copy-start.7 = (f32[79,768]{1,0:T(8,128)S(1)}, f32[79,768]{1,0:T(8,128)}, u32[]{:S(2)}) copy-start(f32[79,768]{1,0:T(8,128)} %param.28) | copy-start | bytes 728068
  633.0 55.6 %copy-start.8 = (f32[79,768]{1,0:T(8,128)S(1)}, f32[79,768]{1,0:T(8,128)}, u32[]{:S(2)}) copy-start(f32[79,768]{1,0:T(8,128)} %param.27) | copy-start | bytes 728068
  689.6 31.1 %copy-start.1 = (bf16[2,1,256,768]{3,2,1,0:T(8,128)(2,1)S(1)}, bf16[2,1,256,768]{3,2,1,0:T(8,128)(2,1)}, u32[]{:S(2)}) copy-start(bf16[2,1,256,768]{3,2,1,0:T(8,128)(2,1)} %param.19) | copy-start | bytes 2359300
Sparse Core Ops, SparseCore 0:
  11.5 129.5 all-gather.2
